TPU v7x, 32 devices: a whole 2x2x4 slice. The times are simulated.
32 devices in a mesh: mem: 8 (over z, y), lat: 4 (over x, core).
Axes of the slice: x: 2, y: 2, z: 4, core: 2. Of those that a mesh axis runs over, the one named last changes fastest.
Arguments:
- control: float32 [16, 4, 64, 1024], P('mem', None, 'lat'), may hold values from -6 to 6
- perturbations: bfloat16 [4, 2, 16, 4, 64, 1024], P(None, None, 'mem', None, 'lat'), may hold values from -3 to 3
- obs_weight: float32 [8, 2, 4, 64, 1024], P('mem', None, None, 'lat'), may hold values from 0.2 to 5
- slot_owner: int32 [4], replicated, may hold values from 0 to 7, as said below
- zonal_shift: int32 [64], P('lat'), may hold values from 0 to 1023
- zonal_taps: float32 [64, 17], P('lat'), may hold values from 0.05 to 0.5
- meridional_taps: float32 [64, 17], P('lat'), may hold values from 0.05 to 0.5
- level_mixing: float32 [64, 4, 4], P('lat'), may hold values from -3 to 3
Outputs:
- applied: float32 [16, 4, 64, 1024], P('mem', None, 'lat')
Inputs may be any that keep to these rules, and one draw needn't show every extreme that they name: `slot_owner`: the 4 entries are distinct; index 0 and index 8 - 1 of mem are always among them.
All inputs are finite; a program needn't handle non-finite values.
Results may differ from a plain program's by a relative error of at most 0.0003.
Values sent between devices are 32-bit elements; how exact they have to be, the bound alone decides.
No kernel may reach another device: no remote copies, remote signals or barrier semaphores. Data moves between devices by JAX's collectives and lax.ppermute only.
A program may use at most 64 MiB of HBM per device.

v0:
```python
import jax
import jax.numpy as jnp
from jax import lax
from jax.sharding import PartitionSpec as P

SLOTS = 4
LON = 1024
BAND = 17


highest_mode = lax.Precision.HIGHEST


def padded(cells, sides, width):
    for axis, dim in sides:
        count = lax.axis_size(axis)
        ends = count - 1
        head = lax.slice_in_dim(cells, 0, width, axis=dim)
        tail = lax.slice_in_dim(cells, cells.shape[dim] - width, cells.shape[dim], axis=dim)
        cells = jnp.concatenate(
            [
                lax.ppermute(tail, axis, [(i, (i + 1) % count) for i in range(ends)]),
                cells,
                lax.ppermute(head, axis, [((i + 1) % count, i) for i in range(ends)]),
            ],
            axis=dim,
        )
    return cells


def spread(value, axis, root):
    mine = lax.axis_index(axis) == root
    return lax.psum(jnp.where(mine, value, jnp.zeros_like(value)), axis)


def band_rim(field):
    return padded(field, (("lat", 2),), BAND // 2)


def zonal_matrix(shift, taps):
    width = LON
    inputs = jnp.arange(width, dtype=jnp.int32)[:, None]
    outputs = jnp.arange(width, dtype=jnp.int32)[None, :]
    distance = (inputs - outputs - shift + BAND // 2) % width
    matrix = jnp.zeros((width, width), jnp.float32)
    for tap_number in range(BAND):
        matrix = jnp.where(distance == tap_number, taps[tap_number], matrix)
    return matrix


def zonal_filter(field, shifts, taps, transposed):
    members, levels, band_rows, width = field.shape
    by_rows = jnp.transpose(field, (2, 0, 1, 3)).reshape(band_rows, members * levels, width)

    def one_row(packed):
        values, shift, row_taps = packed
        matrix = zonal_matrix(shift, row_taps)
        if transposed:
            return jnp.dot(
                values, matrix.T, precision=highest_mode, preferred_element_type=jnp.float32
            )
        return jnp.dot(values, matrix, precision=highest_mode, preferred_element_type=jnp.float32)

    result = lax.map(one_row, (by_rows, shifts, taps))
    return jnp.transpose(result.reshape(band_rows, members, levels, width), (1, 2, 0, 3))


def per_device(
    control,
    perturbations,
    obs_weight,
    slot_owner,
    zonal_shift,
    zonal_taps,
    meridional_taps,
    level_mixing,
):
    half_band = BAND // 2
    band_rows = control.shape[2]
    position = jnp.arange(band_rows + 2 * half_band, dtype=jnp.int32)[None, :]
    row_number = jnp.arange(band_rows, dtype=jnp.int32)[:, None]
    forward_band = jnp.zeros((band_rows, band_rows + 2 * half_band), jnp.float32)
    for tap_number in range(BAND):
        forward_band = forward_band + jnp.where(
            position - row_number == tap_number, meridional_taps[:, tap_number][:, None], 0.0
        )
    taps_haloed = padded(meridional_taps, (("lat", 0),), BAND // 2)
    adjoint_band = jnp.zeros((band_rows, band_rows + 2 * half_band), jnp.float32)
    for tap_number in range(BAND):
        adjoint_band = adjoint_band + jnp.where(
            row_number - position + 2 * half_band == tap_number,
            taps_haloed[:, tap_number][None, :],
            0.0,
        )
    section = zonal_filter(control, zonal_shift, zonal_taps, False)
    section = jnp.einsum(
        "jp,mlpx->mljx",
        forward_band,
        band_rim(section),
        precision=highest_mode,
        preferred_element_type=jnp.float32,
    )
    localized = jnp.einsum(
        "jab,mbjx->majx",
        level_mixing,
        section,
        precision=highest_mode,
        preferred_element_type=jnp.float32,
    )
    partial_value = jnp.sum(perturbations * localized[None, None], axis=2)
    copies = []
    for slot_number in range(SLOTS):
        copies.append(spread(obs_weight[0], "mem", slot_owner[slot_number]))
    weights = jnp.stack(copies)
    own_share = lax.psum_scatter(
        partial_value.reshape(-1, partial_value.shape[-1]), "mem", scatter_dimension=0, tiled=True
    )
    share_rows = own_share.shape[0]
    weight_rows = lax.dynamic_slice_in_dim(
        weights.reshape(-1, partial_value.shape[-1]),
        lax.axis_index("mem") * share_rows,
        share_rows,
        0,
    )
    gathered = lax.all_gather(weight_rows * own_share, "mem", axis=0, tiled=True)
    gradient = gathered.reshape(partial_value.shape)
    weighted = jnp.sum(perturbations * gradient[:, :, None], axis=(0, 1))
    back = jnp.einsum(
        "jab,majx->mbjx",
        level_mixing,
        weighted,
        precision=highest_mode,
        preferred_element_type=jnp.float32,
    )
    back = jnp.einsum(
        "jp,mlpx->mljx",
        adjoint_band,
        band_rim(back),
        precision=highest_mode,
        preferred_element_type=jnp.float32,
    )
    back = zonal_filter(back, zonal_shift, zonal_taps, True)
    return control + back


def solution(mesh):
    in_specs = (
        P("mem", None, "lat", None),
        P(None, None, "mem", None, "lat", None),
        P("mem", None, None, "lat", None),
        P(),
        P("lat"),
        P("lat", None),
        P("lat", None),
        P("lat", None, None),
    )
    out_specs = P("mem", None, "lat", None)
    return jax.shard_map(
        per_device, mesh=mesh, in_specs=in_specs, out_specs=out_specs, check_vma=False
    )
```

profile of v0, /device:TPU:1, one launch (start us, length us, event | category | flops | bytes accessed | tf_op | source)
XLA Modules:
  0.0 909.4 jit_solution(46037491019921897)
XLA Ops:
  6.5 1.5 fusion.459
  10.6 2.5 broadcast_select_fusion.3
  13.2 354.8 %while.24 = (s32[]{:T(128)}, f32[16,8,1024]{2,0,1:T(8,128)S(1)}, f32[16,8,1024]{2,0,1:T(8,128)S(1)}, s32[16]{0:T(128)S(1)}, f32[16,17]{1,0:T(8,128)}, /*index=5*/s32[]{:T(128)}, s32[]{:T(128)}) while((s32[]{:T(128)}, f32[16,8,1024]{2,0,1:T(8,128)S(1)}, f32[16,8,1024]{2,0,1:T(8,128)S(1)}, s32[16]{0:T(128)S(1)}, f32[16,17]{1,0:T(8,128)}, ...), condition=%wide.region_5.6_spmd, body=%wide.region_4.5_spmd.sunk | while | flops 150994944 | bytes 262589 | solution.py:64
  13.9 0.7 fusion.469
  15.3 19.9 %fusion.470 = f32[1,8,1024]{2,1,0:T(8,128)S(1)} fusion(f32[]{:T(128)} %bitcast.125, f32[]{:T(128)} %bitcast.126, f32[]{:T(128)} %bitcast.127, f32[]{:T(128)} %bitcast.128, f32[]{:T(128)} %bitcast.129, f32[]{:T(128)} %bitcast.130, f32[]{:T(128)} %bitcast.131, f32[]{:T(128)} %bitcast.132, f32[]{:T(128)} %bitcast.133, f32[]{:T(128)} %bitcast.134, ...), kind=kOutput, calls=%fused_computation.80.clone.1 | convolution fusion | flops 150994944 | bytes 65608 | tf_op jit(solution)/shard_map/while/body/eval_jaxpr/dot_general | solution.py:62
  37.5 19.9 %fusion.470 = f32[1,8,1024]{2,1,0:T(8,128)S(1)} fusion(f32[]{:T(128)} %bitcast.125, f32[]{:T(128)} %bitcast.126, f32[]{:T(128)} %bitcast.127, f32[]{:T(128)} %bitcast.128, f32[]{:T(128)} %bitcast.129, f32[]{:T(128)} %bitcast.130, f32[]{:T(128)} %bitcast.131, f32[]{:T(128)} %bitcast.132, f32[]{:T(128)} %bitcast.133, f32[]{:T(128)} %bitcast.134, ...), kind=kOutput, calls=%fused_computation.80.clone.1 | convolution fusion | flops 150994944 | bytes 65608 | tf_op jit(solution)/shard_map/while/body/eval_jaxpr/dot_general | solution.py:62
  59.6 19.9 %fusion.470 = f32[1,8,1024]{2,1,0:T(8,128)S(1)} fusion(f32[]{:T(128)} %bitcast.125, f32[]{:T(128)} %bitcast.126, f32[]{:T(128)} %bitcast.127, f32[]{:T(128)} %bitcast.128, f32[]{:T(128)} %bitcast.129, f32[]{:T(128)} %bitcast.130, f32[]{:T(128)} %bitcast.131, f32[]{:T(128)} %bitcast.132, f32[]{:T(128)} %bitcast.133, f32[]{:T(128)} %bitcast.134, ...), kind=kOutput, calls=%fused_computation.80.clone.1 | convolution fusion | flops 150994944 | bytes 65608 | tf_op jit(solution)/shard_map/while/body/eval_jaxpr/dot_general | solution.py:62
  80.4 0.7 fusion.469
  81.8 19.9 %fusion.470 = f32[1,8,1024]{2,1,0:T(8,128)S(1)} fusion(f32[]{:T(128)} %bitcast.125, f32[]{:T(128)} %bitcast.126, f32[]{:T(128)} %bitcast.127, f32[]{:T(128)} %bitcast.128, f32[]{:T(128)} %bitcast.129, f32[]{:T(128)} %bitcast.130, f32[]{:T(128)} %bitcast.131, f32[]{:T(128)} %bitcast.132, f32[]{:T(128)} %bitcast.133, f32[]{:T(128)} %bitcast.134, ...), kind=kOutput, calls=%fused_computation.80.clone.1 | convolution fusion | flops 150994944 | bytes 65608 | tf_op jit(solution)/shard_map/while/body/eval_jaxpr/dot_general | solution.py:62
  104.0 19.9 %fusion.470 = f32[1,8,1024]{2,1,0:T(8,128)S(1)} fusion(f32[]{:T(128)} %bitcast.125, f32[]{:T(128)} %bitcast.126, f32[]{:T(128)} %bitcast.127, f32[]{:T(128)} %bitcast.128, f32[]{:T(128)} %bitcast.129, f32[]{:T(128)} %bitcast.130, f32[]{:T(128)} %bitcast.131, f32[]{:T(128)} %bitcast.132, f32[]{:T(128)} %bitcast.133, f32[]{:T(128)} %bitcast.134, ...), kind=kOutput, calls=%fused_computation.80.clone.1 | convolution fusion | flops 150994944 | bytes 65608 | tf_op jit(solution)/shard_map/while/body/eval_jaxpr/dot_general | solution.py:62
  126.2 19.9 %fusion.470 = f32[1,8,1024]{2,1,0:T(8,128)S(1)} fusion(f32[]{:T(128)} %bitcast.125, f32[]{:T(128)} %bitcast.126, f32[]{:T(128)} %bitcast.127, f32[]{:T(128)} %bitcast.128, f32[]{:T(128)} %bitcast.129, f32[]{:T(128)} %bitcast.130, f32[]{:T(128)} %bitcast.131, f32[]{:T(128)} %bitcast.132, f32[]{:T(128)} %bitcast.133, f32[]{:T(128)} %bitcast.134, ...), kind=kOutput, calls=%fused_computation.80.clone.1 | convolution fusion | flops 150994944 | bytes 65608 | tf_op jit(solution)/shard_map/while/body/eval_jaxpr/dot_general | solution.py:62
  147.0 0.7 fusion.469
  148.3 19.9 %fusion.470 = f32[1,8,1024]{2,1,0:T(8,128)S(1)} fusion(f32[]{:T(128)} %bitcast.125, f32[]{:T(128)} %bitcast.126, f32[]{:T(128)} %bitcast.127, f32[]{:T(128)} %bitcast.128, f32[]{:T(128)} %bitcast.129, f32[]{:T(128)} %bitcast.130, f32[]{:T(128)} %bitcast.131, f32[]{:T(128)} %bitcast.132, f32[]{:T(128)} %bitcast.133, f32[]{:T(128)} %bitcast.134, ...), kind=kOutput, calls=%fused_computation.80.clone.1 | convolution fusion | flops 150994944 | bytes 65608 | tf_op jit(solution)/shard_map/while/body/eval_jaxpr/dot_general | solution.py:62
  170.5 19.9 %fusion.470 = f32[1,8,1024]{2,1,0:T(8,128)S(1)} fusion(f32[]{:T(128)} %bitcast.125, f32[]{:T(128)} %bitcast.126, f32[]{:T(128)} %bitcast.127, f32[]{:T(128)} %bitcast.128, f32[]{:T(128)} %bitcast.129, f32[]{:T(128)} %bitcast.130, f32[]{:T(128)} %bitcast.131, f32[]{:T(128)} %bitcast.132, f32[]{:T(128)} %bitcast.133, f32[]{:T(128)} %bitcast.134, ...), kind=kOutput, calls=%fused_computation.80.clone.1 | convolution fusion | flops 150994944 | bytes 65608 | tf_op jit(solution)/shard_map/while/body/eval_jaxpr/dot_general | solution.py:62
  192.7 19.9 %fusion.470 = f32[1,8,1024]{2,1,0:T(8,128)S(1)} fusion(f32[]{:T(128)} %bitcast.125, f32[]{:T(128)} %bitcast.126, f32[]{:T(128)} %bitcast.127, f32[]{:T(128)} %bitcast.128, f32[]{:T(128)} %bitcast.129, f32[]{:T(128)} %bitcast.130, f32[]{:T(128)} %bitcast.131, f32[]{:T(128)} %bitcast.132, f32[]{:T(128)} %bitcast.133, f32[]{:T(128)} %bitcast.134, ...), kind=kOutput, calls=%fused_computation.80.clone.1 | convolution fusion | flops 150994944 | bytes 65608 | tf_op jit(solution)/shard_map/while/body/eval_jaxpr/dot_general | solution.py:62
  213.5 0.7 fusion.469
  214.8 19.9 %fusion.470 = f32[1,8,1024]{2,1,0:T(8,128)S(1)} fusion(f32[]{:T(128)} %bitcast.125, f32[]{:T(128)} %bitcast.126, f32[]{:T(128)} %bitcast.127, f32[]{:T(128)} %bitcast.128, f32[]{:T(128)} %bitcast.129, f32[]{:T(128)} %bitcast.130, f32[]{:T(128)} %bitcast.131, f32[]{:T(128)} %bitcast.132, f32[]{:T(128)} %bitcast.133, f32[]{:T(128)} %bitcast.134, ...), kind=kOutput, calls=%fused_computation.80.clone.1 | convolution fusion | flops 150994944 | bytes 65608 | tf_op jit(solution)/shard_map/while/body/eval_jaxpr/dot_general | solution.py:62
  237.0 19.9 %fusion.470 = f32[1,8,1024]{2,1,0:T(8,128)S(1)} fusion(f32[]{:T(128)} %bitcast.125, f32[]{:T(128)} %bitcast.126, f32[]{:T(128)} %bitcast.127, f32[]{:T(128)} %bitcast.128, f32[]{:T(128)} %bitcast.129, f32[]{:T(128)} %bitcast.130, f32[]{:T(128)} %bitcast.131, f32[]{:T(128)} %bitcast.132, f32[]{:T(128)} %bitcast.133, f32[]{:T(128)} %bitcast.134, ...), kind=kOutput, calls=%fused_computation.80.clone.1 | convolution fusion | flops 150994944 | bytes 65608 | tf_op jit(solution)/shard_map/while/body/eval_jaxpr/dot_general | solution.py:62
  257.8 0.7 fusion.469
  259.2 19.9 %fusion.470 = f32[1,8,1024]{2,1,0:T(8,128)S(1)} fusion(f32[]{:T(128)} %bitcast.125, f32[]{:T(128)} %bitcast.126, f32[]{:T(128)} %bitcast.127, f32[]{:T(128)} %bitcast.128, f32[]{:T(128)} %bitcast.129, f32[]{:T(128)} %bitcast.130, f32[]{:T(128)} %bitcast.131, f32[]{:T(128)} %bitcast.132, f32[]{:T(128)} %bitcast.133, f32[]{:T(128)} %bitcast.134, ...), kind=kOutput, calls=%fused_computation.80.clone.1 | convolution fusion | flops 150994944 | bytes 65608 | tf_op jit(solution)/shard_map/while/body/eval_jaxpr/dot_general | solution.py:62
  280.0 0.7 fusion.469
  281.4 19.9 %fusion.470 = f32[1,8,1024]{2,1,0:T(8,128)S(1)} fusion(f32[]{:T(128)} %bitcast.125, f32[]{:T(128)} %bitcast.126, f32[]{:T(128)} %bitcast.127, f32[]{:T(128)} %bitcast.128, f32[]{:T(128)} %bitcast.129, f32[]{:T(128)} %bitcast.130, f32[]{:T(128)} %bitcast.131, f32[]{:T(128)} %bitcast.132, f32[]{:T(128)} %bitcast.133, f32[]{:T(128)} %bitcast.134, ...), kind=kOutput, calls=%fused_computation.80.clone.1 | convolution fusion | flops 150994944 | bytes 65608 | tf_op jit(solution)/shard_map/while/body/eval_jaxpr/dot_general | solution.py:62
  303.5 19.9 %fusion.470 = f32[1,8,1024]{2,1,0:T(8,128)S(1)} fusion(f32[]{:T(128)} %bitcast.125, f32[]{:T(128)} %bitcast.126, f32[]{:T(128)} %bitcast.127, f32[]{:T(128)} %bitcast.128, f32[]{:T(128)} %bitcast.129, f32[]{:T(128)} %bitcast.130, f32[]{:T(128)} %bitcast.131, f32[]{:T(128)} %bitcast.132, f32[]{:T(128)} %bitcast.133, f32[]{:T(128)} %bitcast.134, ...), kind=kOutput, calls=%fused_computation.80.clone.1 | convolution fusion | flops 150994944 | bytes 65608 | tf_op jit(solution)/shard_map/while/body/eval_jaxpr/dot_general | solution.py:62
  324.3 0.7 fusion.469
  325.7 19.9 %fusion.470 = f32[1,8,1024]{2,1,0:T(8,128)S(1)} fusion(f32[]{:T(128)} %bitcast.125, f32[]{:T(128)} %bitcast.126, f32[]{:T(128)} %bitcast.127, f32[]{:T(128)} %bitcast.128, f32[]{:T(128)} %bitcast.129, f32[]{:T(128)} %bitcast.130, f32[]{:T(128)} %bitcast.131, f32[]{:T(128)} %bitcast.132, f32[]{:T(128)} %bitcast.133, f32[]{:T(128)} %bitcast.134, ...), kind=kOutput, calls=%fused_computation.80.clone.1 | convolution fusion | flops 150994944 | bytes 65608 | tf_op jit(solution)/shard_map/while/body/eval_jaxpr/dot_general | solution.py:62
  347.9 19.9 %fusion.470 = f32[1,8,1024]{2,1,0:T(8,128)S(1)} fusion(f32[]{:T(128)} %bitcast.125, f32[]{:T(128)} %bitcast.126, f32[]{:T(128)} %bitcast.127, f32[]{:T(128)} %bitcast.128, f32[]{:T(128)} %bitcast.129, f32[]{:T(128)} %bitcast.130, f32[]{:T(128)} %bitcast.131, f32[]{:T(128)} %bitcast.132, f32[]{:T(128)} %bitcast.133, f32[]{:T(128)} %bitcast.134, ...), kind=kOutput, calls=%fused_computation.80.clone.1 | convolution fusion | flops 150994944 | bytes 65608 | tf_op jit(solution)/shard_map/while/body/eval_jaxpr/dot_general | solution.py:62
  368.0 0.7 fusion.457
  368.7 4.6 collective-permute-start.2
  373.3 1.9 collective-permute-start.3
  375.9 1.1 collective-permute-done.2
  377.0 4.2 collective-permute-done.3
  381.1 1.7 convolution_bitcast_fusion.2
  382.9 1.3 convolution_bitcast_fusion.1
  384.6 1.9 fusion.200
  386.5 3.1 pad_maximum_fusion
  389.6 63.3 %reduce-scatter.2.cloned.1.call-done = f32[64,1024]{1,0:T(8,128)} async-done(((f32[512,1024]{1,0:T(8,128)}), f32[64,1024]{1,0:T(8,128)}) %reduce-scatter.2.cloned.1.call-update) | async-done | bytes 262160 | tf_op jit(solution)/shard_map/reduce_scatter | solution.py:115
  452.9 1.8 dynamic-slice_multiply_fusion
  454.7 5.5 collective-permute-start
  460.2 1.9 collective-permute-start.1
  462.2 41.9 %all-gather.2.cloned.1.call-done = f32[512,1024]{1,0:T(8,128)} async-done(((f32[64,1024]{1,0:T(8,128)}), f32[512,1024]{1,0:T(8,128)}) %all-gather.2.cloned.1.call-update) | async-done | bytes 2097168 | tf_op jit(solution)/shard_map/all_gather | solution.py:125
  504.1 2.2 fusion.201
  506.3 1.3 convolution_bitcast_fusion
  507.7 4.8 collective-permute-start.4
  512.5 2.1 collective-permute-start.5
  515.8 4.4 collective-permute-done.5
  520.4 1.2 fusion.207
  521.7 380.3 %while.25 = (s32[]{:T(128)}, f32[16,8,1024]{2,0,1:T(8,128)S(1)}, f32[16,8,1024]{2,0,1:T(8,128)S(1)}, s32[16]{0:T(128)S(1)}, f32[16,17]{1,0:T(8,128)}, /*index=5*/s32[]{:T(128)}, s32[]{:T(128)}) while((s32[]{:T(128)}, f32[16,8,1024]{2,0,1:T(8,128)S(1)}, f32[16,8,1024]{2,0,1:T(8,128)S(1)}, s32[16]{0:T(128)S(1)}, f32[16,17]{1,0:T(8,128)}, ...), condition=%wide.region_10.11_spmd, body=%wide.region_9.10_spmd.sunk | while | flops 150994944 | bytes 262589 | solution.py:64
  523.8 21.4 %fusion.473 = f32[1,8,1024]{2,1,0:T(8,128)S(1)} fusion(f32[]{:T(128)} %bitcast.145, f32[]{:T(128)} %bitcast.146, f32[]{:T(128)} %bitcast.147, f32[]{:T(128)} %bitcast.148, f32[]{:T(128)} %bitcast.149, f32[]{:T(128)} %bitcast.150, f32[]{:T(128)} %bitcast.151, f32[]{:T(128)} %bitcast.152, f32[]{:T(128)} %bitcast.153, f32[]{:T(128)} %bitcast.154, ...), kind=kOutput, calls=%fused_computation.184.clone.1 | convolution fusion | flops 150994944 | bytes 65608 | tf_op jit(solution)/shard_map/while/body/eval_jaxpr/dot_general | solution.py:59
  547.6 21.4 %fusion.473 = f32[1,8,1024]{2,1,0:T(8,128)S(1)} fusion(f32[]{:T(128)} %bitcast.145, f32[]{:T(128)} %bitcast.146, f32[]{:T(128)} %bitcast.147, f32[]{:T(128)} %bitcast.148, f32[]{:T(128)} %bitcast.149, f32[]{:T(128)} %bitcast.150, f32[]{:T(128)} %bitcast.151, f32[]{:T(128)} %bitcast.152, f32[]{:T(128)} %bitcast.153, f32[]{:T(128)} %bitcast.154, ...), kind=kOutput, calls=%fused_computation.184.clone.1 | convolution fusion | flops 150994944 | bytes 65608 | tf_op jit(solution)/shard_map/while/body/eval_jaxpr/dot_general | solution.py:59
  571.3 21.4 %fusion.473 = f32[1,8,1024]{2,1,0:T(8,128)S(1)} fusion(f32[]{:T(128)} %bitcast.145, f32[]{:T(128)} %bitcast.146, f32[]{:T(128)} %bitcast.147, f32[]{:T(128)} %bitcast.148, f32[]{:T(128)} %bitcast.149, f32[]{:T(128)} %bitcast.150, f32[]{:T(128)} %bitcast.151, f32[]{:T(128)} %bitcast.152, f32[]{:T(128)} %bitcast.153, f32[]{:T(128)} %bitcast.154, ...), kind=kOutput, calls=%fused_computation.184.clone.1 | convolution fusion | flops 150994944 | bytes 65608 | tf_op jit(solution)/shard_map/while/body/eval_jaxpr/dot_general | solution.py:59
  595.1 21.4 %fusion.473 = f32[1,8,1024]{2,1,0:T(8,128)S(1)} fusion(f32[]{:T(128)} %bitcast.145, f32[]{:T(128)} %bitcast.146, f32[]{:T(128)} %bitcast.147, f32[]{:T(128)} %bitcast.148, f32[]{:T(128)} %bitcast.149, f32[]{:T(128)} %bitcast.150, f32[]{:T(128)} %bitcast.151, f32[]{:T(128)} %bitcast.152, f32[]{:T(128)} %bitcast.153, f32[]{:T(128)} %bitcast.154, ...), kind=kOutput, calls=%fused_computation.184.clone.1 | convolution fusion | flops 150994944 | bytes 65608 | tf_op jit(solution)/shard_map/while/body/eval_jaxpr/dot_general | solution.py:59
  618.9 21.4 %fusion.473 = f32[1,8,1024]{2,1,0:T(8,128)S(1)} fusion(f32[]{:T(128)} %bitcast.145, f32[]{:T(128)} %bitcast.146, f32[]{:T(128)} %bitcast.147, f32[]{:T(128)} %bitcast.148, f32[]{:T(128)} %bitcast.149, f32[]{:T(128)} %bitcast.150, f32[]{:T(128)} %bitcast.151, f32[]{:T(128)} %bitcast.152, f32[]{:T(128)} %bitcast.153, f32[]{:T(128)} %bitcast.154, ...), kind=kOutput, calls=%fused_computation.184.clone.1 | convolution fusion | flops 150994944 | bytes 65608 | tf_op jit(solution)/shard_map/while/body/eval_jaxpr/dot_general | solution.py:59
  642.7 21.4 %fusion.473 = f32[1,8,1024]{2,1,0:T(8,128)S(1)} fusion(f32[]{:T(128)} %bitcast.145, f32[]{:T(128)} %bitcast.146, f32[]{:T(128)} %bitcast.147, f32[]{:T(128)} %bitcast.148, f32[]{:T(128)} %bitcast.149, f32[]{:T(128)} %bitcast.150, f32[]{:T(128)} %bitcast.151, f32[]{:T(128)} %bitcast.152, f32[]{:T(128)} %bitcast.153, f32[]{:T(128)} %bitcast.154, ...), kind=kOutput, calls=%fused_computation.184.clone.1 | convolution fusion | flops 150994944 | bytes 65608 | tf_op jit(solution)/shard_map/while/body/eval_jaxpr/dot_general | solution.py:59
  666.4 21.4 %fusion.473 = f32[1,8,1024]{2,1,0:T(8,128)S(1)} fusion(f32[]{:T(128)} %bitcast.145, f32[]{:T(128)} %bitcast.146, f32[]{:T(128)} %bitcast.147, f32[]{:T(128)} %bitcast.148, f32[]{:T(128)} %bitcast.149, f32[]{:T(128)} %bitcast.150, f32[]{:T(128)} %bitcast.151, f32[]{:T(128)} %bitcast.152, f32[]{:T(128)} %bitcast.153, f32[]{:T(128)} %bitcast.154, ...), kind=kOutput, calls=%fused_computation.184.clone.1 | convolution fusion | flops 150994944 | bytes 65608 | tf_op jit(solution)/shard_map/while/body/eval_jaxpr/dot_general | solution.py:59
  690.2 21.4 %fusion.473 = f32[1,8,1024]{2,1,0:T(8,128)S(1)} fusion(f32[]{:T(128)} %bitcast.145, f32[]{:T(128)} %bitcast.146, f32[]{:T(128)} %bitcast.147, f32[]{:T(128)} %bitcast.148, f32[]{:T(128)} %bitcast.149, f32[]{:T(128)} %bitcast.150, f32[]{:T(128)} %bitcast.151, f32[]{:T(128)} %bitcast.152, f32[]{:T(128)} %bitcast.153, f32[]{:T(128)} %bitcast.154, ...), kind=kOutput, calls=%fused_computation.184.clone.1 | convolution fusion | flops 150994944 | bytes 65608 | tf_op jit(solution)/shard_map/while/body/eval_jaxpr/dot_general | solution.py:59
  714.0 21.4 %fusion.473 = f32[1,8,1024]{2,1,0:T(8,128)S(1)} fusion(f32[]{:T(128)} %bitcast.145, f32[]{:T(128)} %bitcast.146, f32[]{:T(128)} %bitcast.147, f32[]{:T(128)} %bitcast.148, f32[]{:T(128)} %bitcast.149, f32[]{:T(128)} %bitcast.150, f32[]{:T(128)} %bitcast.151, f32[]{:T(128)} %bitcast.152, f32[]{:T(128)} %bitcast.153, f32[]{:T(128)} %bitcast.154, ...), kind=kOutput, calls=%fused_computation.184.clone.1 | convolution fusion | flops 150994944 | bytes 65608 | tf_op jit(solution)/shard_map/while/body/eval_jaxpr/dot_general | solution.py:59
  737.7 21.4 %fusion.473 = f32[1,8,1024]{2,1,0:T(8,128)S(1)} fusion(f32[]{:T(128)} %bitcast.145, f32[]{:T(128)} %bitcast.146, f32[]{:T(128)} %bitcast.147, f32[]{:T(128)} %bitcast.148, f32[]{:T(128)} %bitcast.149, f32[]{:T(128)} %bitcast.150, f32[]{:T(128)} %bitcast.151, f32[]{:T(128)} %bitcast.152, f32[]{:T(128)} %bitcast.153, f32[]{:T(128)} %bitcast.154, ...), kind=kOutput, calls=%fused_computation.184.clone.1 | convolution fusion | flops 150994944 | bytes 65608 | tf_op jit(solution)/shard_map/while/body/eval_jaxpr/dot_general | solution.py:59
  761.5 21.4 %fusion.473 = f32[1,8,1024]{2,1,0:T(8,128)S(1)} fusion(f32[]{:T(128)} %bitcast.145, f32[]{:T(128)} %bitcast.146, f32[]{:T(128)} %bitcast.147, f32[]{:T(128)} %bitcast.148, f32[]{:T(128)} %bitcast.149, f32[]{:T(128)} %bitcast.150, f32[]{:T(128)} %bitcast.151, f32[]{:T(128)} %bitcast.152, f32[]{:T(128)} %bitcast.153, f32[]{:T(128)} %bitcast.154, ...), kind=kOutput, calls=%fused_computation.184.clone.1 | convolution fusion | flops 150994944 | bytes 65608 | tf_op jit(solution)/shard_map/while/body/eval_jaxpr/dot_general | solution.py:59
  785.3 21.4 %fusion.473 = f32[1,8,1024]{2,1,0:T(8,128)S(1)} fusion(f32[]{:T(128)} %bitcast.145, f32[]{:T(128)} %bitcast.146, f32[]{:T(128)} %bitcast.147, f32[]{:T(128)} %bitcast.148, f32[]{:T(128)} %bitcast.149, f32[]{:T(128)} %bitcast.150, f32[]{:T(128)} %bitcast.151, f32[]{:T(128)} %bitcast.152, f32[]{:T(128)} %bitcast.153, f32[]{:T(128)} %bitcast.154, ...), kind=kOutput, calls=%fused_computation.184.clone.1 | convolution fusion | flops 150994944 | bytes 65608 | tf_op jit(solution)/shard_map/while/body/eval_jaxpr/dot_general | solution.py:59
  809.1 21.4 %fusion.473 = f32[1,8,1024]{2,1,0:T(8,128)S(1)} fusion(f32[]{:T(128)} %bitcast.145, f32[]{:T(128)} %bitcast.146, f32[]{:T(128)} %bitcast.147, f32[]{:T(128)} %bitcast.148, f32[]{:T(128)} %bitcast.149, f32[]{:T(128)} %bitcast.150, f32[]{:T(128)} %bitcast.151, f32[]{:T(128)} %bitcast.152, f32[]{:T(128)} %bitcast.153, f32[]{:T(128)} %bitcast.154, ...), kind=kOutput, calls=%fused_computation.184.clone.1 | convolution fusion | flops 150994944 | bytes 65608 | tf_op jit(solution)/shard_map/while/body/eval_jaxpr/dot_general | solution.py:59
  832.8 21.4 %fusion.473 = f32[1,8,1024]{2,1,0:T(8,128)S(1)} fusion(f32[]{:T(128)} %bitcast.145, f32[]{:T(128)} %bitcast.146, f32[]{:T(128)} %bitcast.147, f32[]{:T(128)} %bitcast.148, f32[]{:T(128)} %bitcast.149, f32[]{:T(128)} %bitcast.150, f32[]{:T(128)} %bitcast.151, f32[]{:T(128)} %bitcast.152, f32[]{:T(128)} %bitcast.153, f32[]{:T(128)} %bitcast.154, ...), kind=kOutput, calls=%fused_computation.184.clone.1 | convolution fusion | flops 150994944 | bytes 65608 | tf_op jit(solution)/shard_map/while/body/eval_jaxpr/dot_general | solution.py:59
  856.6 21.4 %fusion.473 = f32[1,8,1024]{2,1,0:T(8,128)S(1)} fusion(f32[]{:T(128)} %bitcast.145, f32[]{:T(128)} %bitcast.146, f32[]{:T(128)} %bitcast.147, f32[]{:T(128)} %bitcast.148, f32[]{:T(128)} %bitcast.149, f32[]{:T(128)} %bitcast.150, f32[]{:T(128)} %bitcast.151, f32[]{:T(128)} %bitcast.152, f32[]{:T(128)} %bitcast.153, f32[]{:T(128)} %bitcast.154, ...), kind=kOutput, calls=%fused_computation.184.clone.1 | convolution fusion | flops 150994944 | bytes 65608 | tf_op jit(solution)/shard_map/while/body/eval_jaxpr/dot_general | solution.py:59
  880.4 21.4 %fusion.473 = f32[1,8,1024]{2,1,0:T(8,128)S(1)} fusion(f32[]{:T(128)} %bitcast.145, f32[]{:T(128)} %bitcast.146, f32[]{:T(128)} %bitcast.147, f32[]{:T(128)} %bitcast.148, f32[]{:T(128)} %bitcast.149, f32[]{:T(128)} %bitcast.150, f32[]{:T(128)} %bitcast.151, f32[]{:T(128)} %bitcast.152, f32[]{:T(128)} %bitcast.153, f32[]{:T(128)} %bitcast.154, ...), kind=kOutput, calls=%fused_computation.184.clone.1 | convolution fusion | flops 150994944 | bytes 65608 | tf_op jit(solution)/shard_map/while/body/eval_jaxpr/dot_general | solution.py:59
  902.0 0.9 add.237
  (217 shorter events, 70.1 us)
Async XLA Ops:
  6.5 380.0 %all-reduce.3.cloned.1.call-start = ((), (), s32[]{:S(2)}) async-start(), calls=%async_computation.3 | async-start | bytes 4194304 | tf_op jit(solution)/shard_map/psum | solution.py:33
  10.5 2.6 copy-start.2
  10.6 2.6 copy-start.4
  13.1 439.8 %reduce-scatter.2.cloned.1.call-start = ((), (), s32[]{:S(2)}) async-start(), calls=%async_computation.1 | async-start | bytes 2359296 | tf_op jit(solution)/shard_map/reduce_scatter | solution.py:115
  13.2 362.1 %copy-start.3 = (f32[16,4,4]{0,2,1:T(4,128)S(1)}, f32[16,4,4]{0,2,1:T(4,128)}, u32[]{:S(2)}) copy-start(f32[16,4,4]{0,2,1:T(4,128)} %param.19) | copy-start | bytes 3076
  13.2 362.2 %copy-start.1 = (f32[16,17]{1,0:T(8,128)S(1)}, f32[16,17]{1,0:T(8,128)}, u32[]{:S(2)}) copy-start(f32[16,17]{1,0:T(8,128)} %param.18) | copy-start | bytes 3268
  368.7 15.8 %copy-start = (bf16[4,2,2,4,16,1024]{5,4,3,2,1,0:T(8,128)(2,1)S(1)}, bf16[4,2,2,4,16,1024]{5,4,3,2,1,0:T(8,128)(2,1)}, u32[]{:S(2)}) copy-start(bf16[4,2,2,4,16,1024]{5,4,3,2,1,0:T(8,128)(2,1)} %param.13) | copy-start | bytes 6291460
  368.7 8.3 collective-permute-start.2
  373.3 7.8 collective-permute-start.3
  386.5 117.6 %all-gather.2.cloned.1.call-start = ((), (), s32[]{:S(2)}) async-start(), calls=%async_computation.2 | async-start | bytes 2359296 | tf_op jit(solution)/shard_map/all_gather | solution.py:125
  454.7 7.4 collective-permute-start
  460.2 54.4 %collective-permute-start.1 = (f32[8,17]{1,0:T(8,128)S(1)}, f32[8,17]{1,0:T(8,128)S(1)}, u32[]{:S(2)}, u32[]{:S(2)}) collective-permute-start(f32[8,17]{1,0:T(8,128)S(1)} %get-tuple-element.254), channel_id=1, source_target_pairs={{1,0},{2,1},{3,2},{5,4},{6,5},{7,6},{9,8},{10,9},{11,10},{13,12},{... | collective-permute-start | bytes 1640 | tf_op jit(solution)/shard_map/ppermute | solution.py:24
  507.7 8.1 collective-permute-start.4
  512.5 7.7 collective-permute-start.5
Sparse Core Ops, SparseCore 0:
  13.2 104.7 all-reduce.2
  386.6 66.2 reduce-scatter.1
  455.0 49.0 all-gather.1
where the time goes:
time: 916 us; the launch traced here: 909 us
  matrix products  667 us (73%)
  waiting for transfers between devices  116 us (13%)
  local copies, waits for them, and re-layouts  76.2 us (8%)
  starting transfers between devices  20.9 us (2%)
  between operations  15.9 us (2%)
  other arithmetic  12.5 us (1%)
    dot_general x16, matrix products, one_row(): jnp.dot(values, matrix.T, precision=highest_mode, preferred_element_type=...  343 us
    dot_general x16, matrix products, one_row(): jnp.dot(values, matrix, precision=highest_mode, preferred_element_type=jn...  318 us
    reduce_scatter x1, waiting for transfers between devices, per_device(): lax.psum_scatter(partial_value.reshape(-1, partial_value.shape[-1]), 'mem...  63.3 us
    dynamic_slice x96, local copies, waits for them, and re-layouts, zonal_filter(): result = lax.map(one_row, (by_rows, shifts, taps))  43.6 us
    all_gather x1, waiting for transfers between devices, per_device(): lax.all_gather(weight_rows * own_share, 'mem', axis=0, tiled=True)  41.9 us
    slice x32, local copies, waits for them, and re-layouts, zonal_matrix(): matrix = jnp.where(distance == tap_number, taps[tap_number], matrix)  22.9 us
  transfers between devices with their start and end apart: 9, of which 6 were waited for; matrix products, arithmetic and copies ran while one was open for 40% of the time, Pallas kernels for 0%

commit v1 on v0

v1 whole, which is shorter than its diff:
```python
import functools

import jax
import jax.numpy as jnp
from jax import lax
from jax.experimental import pallas as pl
from jax.experimental.pallas import tpu as pltpu
from jax.sharding import PartitionSpec as P

SLOTS = 4
BAND = 17
HALF = BAND // 2
LANES = 128
F32 = jnp.float32
BF16 = jnp.bfloat16

VMEM = pl.BlockSpec(memory_space=pltpu.VMEM)
SMEM = pl.BlockSpec(memory_space=pltpu.SMEM)

PARITY, HAS_X, OWN_Y, WEIGHT_FROM, SLOT = 0, 1, 2, 3, 4
TABLE = 8


def call(body, outs, name, cost, *operands, specs, scratch=()):
    return pl.pallas_call(
        body,
        out_shape=outs,
        in_specs=list(specs),
        out_specs=jax.tree.map(lambda _: VMEM, outs),
        scratch_shapes=list(scratch),
        compiler_params=pltpu.CompilerParams(vmem_limit_bytes=48 << 20),
        cost_estimate=pl.CostEstimate(flops=cost, bytes_accessed=cost, transcendentals=0),
        name=name,
    )(*operands)


def shape(*dims, dtype=F32):
    return jax.ShapeDtypeStruct(dims, dtype)


def shifted(columns, amount):
    lane = lax.broadcasted_iota(jnp.int32, columns[0].shape, 1)
    turned = [pltpu.roll(c, amount, 1) for c in columns]
    return [
        jnp.where(lane < amount, turned[i - 1], turned[i]) for i in range(len(columns))
    ]


def circle_filter(columns, amount, tap):
    count = len(columns)
    lane = lax.broadcasted_iota(jnp.int32, columns[0].shape, 1)
    fine = amount & (LANES - 1)
    source = (lane - fine) & (LANES - 1)
    turned = [
        jnp.take_along_axis(c, source, axis=1, mode="promise_in_bounds") for c in columns
    ]
    wraps = lane < fine
    columns = [jnp.where(wraps, turned[i - 1], turned[i]) for i in range(count)]
    step = 1
    while step < count:
        moved = (amount & (step * LANES)) != 0
        columns = [jnp.where(moved, columns[i - step], columns[i]) for i in range(count)]
        step *= 2
    near = [columns]
    for offset in range(1, 4):
        near.append(shifted(columns, offset))
    total = [tap(BAND - 1) * c for c in columns]
    for group in range((BAND - 1) // 4 - 1, -1, -1):
        total = shifted(total, 4)
        for offset in range(4):
            factor = tap(4 * group + offset)
            total = [t + factor * c for t, c in zip(total, near[offset])]
    return total


def row_shifts(shift_ref, first):
    row = lax.broadcasted_iota(jnp.int32, (8, LANES), 0)
    amounts = jnp.zeros((8, LANES), jnp.int32)
    for r in range(8):
        amounts = jnp.where(row == r, shift_ref[first + r], amounts)
    return amounts


def spread_taps(taps_ref, first, tap_ref):
    block = taps_ref[pl.ds(first, 8), :]
    for k in range(BAND):
        tap_ref[k] = jnp.broadcast_to(block[:, k : k + 1], (8, LANES))


def tiles(width):
    return [slice(i * LANES, (i + 1) * LANES) for i in range(width // LANES)]


def zonal_forward(table, shift_ref, taps_ref, control, near_core, near_x, tap_ref):
    members, levels, _, width = control.shape
    for which, out in enumerate((near_core, near_x)):
        first = pl.multiple_of((1 - table[PARITY] if which == 0 else table[PARITY]) * 8, 8)
        amount = (width - HALF - row_shifts(shift_ref, first)) & (width - 1)
        spread_taps(taps_ref, first, tap_ref)

        def step(unit, carry, out=out, first=first, amount=amount):
            m, l = unit // levels, unit % levels
            columns = [control[m, l, pl.ds(first, 8), cut] for cut in tiles(width)]
            result = circle_filter(columns, amount, lambda k: tap_ref[BAND - 1 - k])
            for cut, value in zip(tiles(width), result):
                out[m, l, :, cut] = value
            return carry

        lax.fori_loop(0, members * levels, step, 0)


def zonal_adjoint(
    table, shift_ref, taps_ref, control, own_core, own_x, got_core, got_x, out, tap_ref
):
    members, levels, _, width = control.shape
    for which, (own, got) in enumerate(((own_core, got_core), (own_x, got_x))):
        first = pl.multiple_of((1 - table[PARITY] if which == 0 else table[PARITY]) * 8, 8)
        amount = (row_shifts(shift_ref, first) - HALF) & (width - 1)
        spread_taps(taps_ref, first, tap_ref)

        def step(unit, carry, own=own, got=got, first=first, amount=amount):
            m, l = unit // levels, unit % levels
            columns = [own[m, l, :, cut] + got[m, l, :, cut] for cut in tiles(width)]
            result = circle_filter(columns, amount, lambda k: tap_ref[k])
            for cut, value in zip(tiles(width), result):
                out[m, l, pl.ds(first, 8), cut] = control[m, l, pl.ds(first, 8), cut] + value
            return carry

        lax.fori_loop(0, members * levels, step, 0)


def build_matrix(table, taps_ref, mixing_ref, matrix, transposed):
    band_rows, levels = taps_ref.shape[0], mixing_ref.shape[1]
    rows, columns = matrix.shape
    odd = table[PARITY]
    column = lax.broadcasted_iota(jnp.int32, (band_rows, columns), 1)
    row = lax.broadcasted_iota(jnp.int32, (band_rows, columns), 0)
    block, level, inner = column // (8 * levels), (column // 8) % levels, column % 8
    even_start = jnp.where(block == 0, 16, jnp.where(block == 1, 8, jnp.where(block == 2, 24, 0)))
    odd_start = jnp.where(block == 0, 8, jnp.where(block == 1, 16, jnp.where(block == 2, 0, 24)))
    reach = jnp.where(odd == 1, odd_start, even_start) + inner - row
    band = jnp.zeros((band_rows, columns), F32)
    for k in range(BAND):
        band = jnp.where(reach == k, taps_ref[:, k : k + 1], band)
    band = jnp.where((block == 3) & (table[HAS_X] == 0), 0.0, band)
    for a in range(levels):
        mixing = mixing_ref[a * band_rows : (a + 1) * band_rows, :]
        factor = jnp.zeros((band_rows, columns), F32)
        for b in range(levels):
            factor = jnp.where(level == b, mixing[:, b : b + 1], factor)
        matrix[a * band_rows : (a + 1) * band_rows, :] = factor * band
    transposed[...] = matrix[...].T


def halves(value):
    high = value.astype(BF16)
    return high, (value - high.astype(F32)).astype(BF16)


def product(left, right):
    (lh, ll), (rh, rl) = left, right
    dot = functools.partial(jnp.dot, preferred_element_type=F32)
    return dot(lh, rh) + (dot(lh, rl) + dot(ll, rh))


CHUNK = 256


def localize(matrix, parts, out):
    members, levels, band_rows, width = out.shape
    left = halves(matrix[...])
    for m in range(members):
        for c in range(0, width, CHUNK):
            cut = slice(c, c + CHUNK)
            stack = jnp.concatenate(
                [p[m, l, :, cut] for p in parts for l in range(levels)], axis=0
            )
            result = product(left, halves(stack))
            for l in range(levels):
                out[m, l, :, cut] = result[l * band_rows : (l + 1) * band_rows]


def delocalize(matrix, weighted, parts):
    members, levels, band_rows, width = weighted.shape
    left = halves(matrix[...])
    for m in range(members):
        for c in range(0, width, CHUNK):
            cut = slice(c, c + CHUNK)
            stack = jnp.concatenate([weighted[m, l, :, cut] for l in range(levels)], axis=0)
            result = product(left, halves(stack))
            for p, part in enumerate(parts):
                for l in range(levels):
                    start = (p * levels + l) * 8
                    part[m, l, :, cut] = result[start : start + 8]


def increment(ens, localized, slot, field, l):
    total = None
    for m in range(localized.shape[0]):
        term = ens[slot, field, m, l].astype(F32) * localized[m, l]
        total = term if total is None else total + term
    return total


def first_body(step, table, matrix, a, b, c, d, ens, localized, send):
    localize(matrix, (a, b, c, d), localized)
    for l in range(localized.shape[1]):
        send[l] = increment(ens, localized, table[SLOT + step], 1 - table[OWN_Y], l)


def send_body(steps, table, ens, localized, *sends):
    for step, send in zip(steps, sends):
        for l in range(localized.shape[1]):
            send[l] = increment(ens, localized, table[SLOT + step], 1 - table[OWN_Y], l)


def meet_body(step, table, ens, localized, got, out):
    for l in range(localized.shape[1]):
        out[l] = increment(ens, localized, table[SLOT + step], table[OWN_Y], l) + got[l]


def last_body(table, ens, localized, got_y, got_1, got_2, got_3, own, from_y, from_low, from_high, out):
    for l in range(localized.shape[1]):
        out[l] = (
            increment(ens, localized, table[SLOT], table[OWN_Y], l)
            + got_y[l]
            + (got_1[l] + got_2[l] + got_3[l])
        )
    source = table[WEIGHT_FROM]

    @pl.when(source == 0)
    def _():
        out[...] = out[...] * own[0, table[OWN_Y]]

    for code, weight in ((1, from_y), (2, from_low), (3, from_high)):

        @pl.when(source == code)
        def _(weight=weight):
            out[...] = out[...] * weight[...]


def spread_body(pieces, first, final, table, ens, *refs):
    refs = list(refs)
    grads = [refs.pop(0) for _ in pieces]
    before = None if first else refs.pop(0)
    matrix = refs.pop(0) if final else None
    out = refs[-1] if final else refs[0]
    members, levels = out.shape[:2]
    for m in range(members):
        for l in range(levels):
            total = None if before is None else before[m, l]
            for (step, other), grad in zip(pieces, grads):
                field = 1 - table[OWN_Y] if other else table[OWN_Y]
                term = ens[table[SLOT + step], field, m, l].astype(F32) * grad[l]
                total = term if total is None else total + term
            out[m, l] = total
    if final:
        delocalize(matrix, out, refs[:4])


def all_increments(ens, localized, out):
    for slot in range(out.shape[0]):
        for field in range(out.shape[1]):
            for l in range(out.shape[2]):
                out[slot, field, l] = increment(ens, localized, slot, field, l)


def localize_body(matrix, a, b, c, d, localized):
    localize(matrix, (a, b, c, d), localized)


def all_weighted(ens, grad, matrix, a, b, c, d, out):
    members, levels = out.shape[:2]
    for m in range(members):
        for l in range(levels):
            total = None
            for slot in range(ens.shape[0]):
                for field in range(ens.shape[1]):
                    term = ens[slot, field, m, l].astype(F32) * grad[slot, field, l]
                    total = term if total is None else total + term
            out[m, l] = total
    delocalize(matrix, out, (a, b, c, d))


def per_device(
    z_count,
    control,
    perturbations,
    obs_weight,
    slot_owner,
    zonal_shift,
    zonal_taps,
    meridional_taps,
    level_mixing,
):
    members, levels, band_rows, width = control.shape
    mem_count, lat_count = lax.axis_size("mem"), lax.axis_size("lat")
    lat, mem = lax.axis_index("lat"), lax.axis_index("mem")
    parity = lat % 2
    has_x = jnp.where((lat > 0) & (lat < lat_count - 1), 1, 0)
    direct = z_count > 0
    field_shape = (members, levels, band_rows, width)
    half_shape = (members, levels, 8, width)
    core_pairs = [(i, i ^ 1) for i in range(lat_count)]
    x_pairs = [(i, i + 1) for i in range(1, lat_count - 1, 2)]
    x_pairs += [(j, i) for i, j in x_pairs]
    swap_core = lambda v: lax.ppermute(v, "lat", core_pairs)
    swap_x = lambda v: lax.ppermute(v, "lat", x_pairs)

    z, y = mem // 2, mem % 2
    if direct:
        rank = jnp.sum((slot_owner[None, :] < slot_owner[:, None]).astype(jnp.int32), axis=1)
        place = (z + jnp.arange(SLOTS, dtype=jnp.int32)) % SLOTS
        at_place = (rank[None, :] == place[:, None]).astype(jnp.int32)
        slots = jnp.sum(at_place * jnp.arange(SLOTS, dtype=jnp.int32)[None, :], axis=1)
        owners = jnp.sum(at_place * slot_owner[None, :], axis=1)
        own_z, own_y = owners[0] // 2, owners[0] % 2
        source = jnp.where(
            own_z == z, jnp.where(own_y == y, 0, 1), jnp.where(own_z < z, 2, 3)
        )
    else:
        slots, source = jnp.arange(SLOTS, dtype=jnp.int32), jnp.int32(0)
    table = jnp.concatenate(
        [jnp.stack([parity, has_x, y, source]).astype(jnp.int32), slots]
    )

    if direct:
        y_pairs = [(i, i ^ 1) for i in range(mem_count)]
        swap_y = lambda v: lax.ppermute(v, "mem", y_pairs)
        turn_z = lambda v, s: lax.ppermute(
            v, "mem", [(i, (i + 2 * s) % mem_count) for i in range(mem_count)]
        )
        weight_y = swap_y(lax.dynamic_index_in_dim(obs_weight[0], 1 - y, 0, False))

    near_core, near_x = call(
        zonal_forward, (shape(*half_shape),) * 2, "zonal", 1 << 20,
        table, zonal_shift, zonal_taps, control,
        specs=(SMEM, SMEM, VMEM, VMEM), scratch=[pltpu.VMEM((BAND, 8, LANES), F32)],
    )
    far_core, far_x = swap_core(near_core), swap_x(near_x)
    mixing = jnp.transpose(level_mixing, (1, 0, 2)).reshape(levels * band_rows, levels)
    matrix, transposed = call(
        build_matrix,
        (shape(levels * band_rows, 32 * levels), shape(32 * levels, levels * band_rows)),
        "matrix", 1 << 16, table, meridional_taps, mixing, specs=(SMEM, VMEM, VMEM),
    )
    parts = (near_core, near_x, far_core, far_x)
    piece = shape(levels, band_rows, width)

    if direct:
        order = (2, 1, 3)
        localized, first = call(
            functools.partial(first_body, order[0]), (shape(*field_shape), piece),
            "first", 1 << 20, table, matrix, *parts, perturbations,
            specs=(SMEM,) + (VMEM,) * 6,
        )
        sent = {order[0]: first}
        rest = order[1:] + (0,)
        others = call(
            functools.partial(send_body, rest), (piece,) * len(rest), "send", 1 << 20,
            table, perturbations, localized, specs=(SMEM, VMEM, VMEM),
        )
        sent.update(zip(rest, others))
        got = {s: swap_y(sent[s]) for s in order + (0,)}
        own_weight = lax.dynamic_index_in_dim(obs_weight[0], y, 0, False)
        up = jnp.where(owners[1] % 2 == y, own_weight, weight_y)
        down = jnp.where(owners[3] % 2 == y, own_weight, weight_y)
        ends = z_count - 1
        raised = [(2 * i + j, 2 * i + 2 + j) for i in range(ends - 1) for j in range(2)]
        lowered = [(2 * i + 2 + j, 2 * i + j) for i in range(1, ends) for j in range(2)]
        from_low = lax.ppermute(up, "mem", raised)
        from_high = lax.ppermute(down, "mem", lowered)
        arrived = {}
        for s in order:
            total = call(
                functools.partial(meet_body, s), piece, "meet%d" % s, 1 << 19,
                table, perturbations, localized, got[s], specs=(SMEM,) + (VMEM,) * 3,
            )
            arrived[s] = turn_z(total, s)
        grad = call(
            last_body, piece, "last", 1 << 19, table, perturbations, localized, got[0],
            arrived[1], arrived[2], arrived[3], obs_weight, weight_y, from_low, from_high,
            specs=(SMEM,) + (VMEM,) * 10,
        )
        own = {0: grad}
        for s in order:
            own[s] = turn_z(grad, s)
        other = {s: swap_y(own[s]) for s in (0,) + order}
        back = lambda s: (-s) % SLOTS
        weighted = None
        for group in (((0, 0),), ((0, 1), (2, 0)), ((1, 0), (2, 1)), ((3, 0), (1, 1)), ((3, 1),)):
            final = group == ((3, 1),)
            grads = [other[s] if o else own[s] for s, o in group]
            pieces = tuple((back(s), o) for s, o in group)
            before = () if weighted is None else (weighted,)
            extra = (transposed,) if final else ()
            result = call(
                functools.partial(spread_body, pieces, weighted is None, final),
                (shape(*half_shape),) * 4 + (shape(*field_shape),) if final else shape(*field_shape),
                "spread%d" % group[0][0], 1 << 19,
                table, perturbations, *grads, *before, *extra,
                specs=(SMEM,) + (VMEM,) * (1 + len(grads) + len(before) + len(extra)),
            )
            weighted = result
        own_core, own_x, to_core, to_x = result[:4]
    else:
        localized = call(
            localize_body, shape(*field_shape), "localize", 1 << 20, matrix, *parts,
            specs=(VMEM,) * 5,
        )
        partial = call(
            all_increments, shape(SLOTS, perturbations.shape[1], levels, band_rows, width),
            "increments", 1 << 20, perturbations, localized, specs=(VMEM,) * 2,
        )
        weights = jnp.stack(
            [
                lax.psum(jnp.where(mem == slot_owner[t], obs_weight[0], 0.0), "mem")
                for t in range(SLOTS)
            ]
        )
        share = lax.psum_scatter(
            partial.reshape(-1, width), "mem", scatter_dimension=0, tiled=True
        )
        share_rows = share.shape[0]
        weight_rows = lax.dynamic_slice_in_dim(
            weights.reshape(-1, width), mem * share_rows, share_rows, 0
        )
        gathered = lax.all_gather(weight_rows * share, "mem", axis=0, tiled=True)
        own_core, own_x, to_core, to_x, _ = call(
            all_weighted, (shape(*half_shape),) * 4 + (shape(*field_shape),), "weighted",
            1 << 20, perturbations, gathered.reshape(partial.shape), transposed,
            specs=(VMEM,) * 3,
        )
    got_core, got_x = swap_core(to_core), swap_x(to_x)
    return call(
        zonal_adjoint, shape(*field_shape), "zonal_adjoint", 1 << 20,
        table, zonal_shift, zonal_taps, control, own_core, own_x, got_core, got_x,
        specs=(SMEM, SMEM) + (VMEM,) * 6, scratch=[pltpu.VMEM((BAND, 8, LANES), F32)],
    )


def solution(mesh):
    z_count = SLOTS if mesh.shape["mem"] == 2 * SLOTS else 0
    in_specs = (
        P("mem", None, "lat", None),
        P(None, None, "mem", None, "lat", None),
        P("mem", None, None, "lat", None),
        P(),
        P("lat"),
        P("lat", None),
        P("lat", None),
        P("lat", None, None),
    )
    out_specs = P("mem", None, "lat", None)
    return jax.shard_map(
        functools.partial(per_device, z_count),
        mesh=mesh, in_specs=in_specs, out_specs=out_specs, check_vma=False,
    )
```

time: 916 us -> 132 us (0.14)
  matrix products: 667 us -> 0 us
  local copies, waits for them, and re-layouts: 76.2 us -> 11.2 us
  waiting for transfers between devices: 116 us -> 55 us
  Pallas kernels: 0 us -> 28 us
  other arithmetic: 12.5 us -> 1.84 us
    dot_general x36 -> x0, matrix products: 667 us -> none  [the longest x16 343 us: one_row(): jnp.dot(values, matrix.T, precision=highest_mode, preferred_element_type=...]
    reduce_scatter x1 -> x0, waiting for transfers between devices: 63.3 us -> none  [per_device(): lax.psum_scatter(partial_value.reshape(-1, partial_value.shape[-1]), 'mem...]
    ppermute x6 -> x21, waiting for transfers between devices: 10.4 us -> 55 us  [the longest x6 33.4 us: per_device(): lax.ppermute(v, 'mem', [(i, (i + 2 * s) % mem_count) for i in range(mem_c...]
    dynamic_slice x96 -> x0, local copies, waits for them, and re-layouts: 43.6 us -> none  [zonal_filter(): result = lax.map(one_row, (by_rows, shifts, taps))]
    all_gather x1 -> x0, waiting for transfers between devices: 41.9 us -> none  [per_device(): lax.all_gather(weight_rows * own_share, 'mem', axis=0, tiled=True)]
    pallas_call x0 -> x14, Pallas kernels: none -> 28 us  [call(): pl.pallas_call(body, out_shape=outs, in_specs=list(specs), out_specs=jax....]
    slice x38 -> x1, local copies, waits for them, and re-layouts: 26.1 us -> 0.68 us  [per_device(): down = jnp.where(owners[3] % 2 == y, own_weight, weight_y)]
    ppermute x6 -> x21, starting transfers between devices: 20.9 us -> 28.3 us  [the longest x6 10.5 us: per_device(): lax.ppermute(v, 'mem', [(i, (i + 2 * s) % mem_count) for i in range(mem_c...]
  transfers between devices with their start and end apart: 9 -> 21, of which waited for: 6 -> 10; matrix products, arithmetic and copies ran while one was open for 40% -> 2% of each run, Pallas kernels for 0% -> 6%
where the time goes in v1:
time: 132 us; the launch traced here: 131 us
  waiting for transfers between devices  55 us (42%)
  starting transfers between devices  28.3 us (21%)
  Pallas kernels  28 us (21%)
  local copies, waits for them, and re-layouts  11.2 us (8%)
  between operations  7.07 us (5%)
  other arithmetic  1.84 us (1%)
    ppermute x6, waiting for transfers between devices, per_device(): lax.ppermute(v, 'mem', [(i, (i + 2 * s) % mem_count) for i in range(mem_c...  33.4 us
    pallas_call x14, Pallas kernels, call(): pl.pallas_call(body, out_shape=outs, in_specs=list(specs), out_specs=jax....  28 us
    ppermute x9, waiting for transfers between devices, per_device(): swap_y = lambda v: lax.ppermute(v, 'mem', y_pairs)  15.8 us
    ppermute x6, starting transfers between devices, per_device(): lax.ppermute(v, 'mem', [(i, (i + 2 * s) % mem_count) for i in range(mem_c...  10.5 us
    unnamed x28, local copies, waits for them, and re-layouts  8 us
    ppermute x2, starting transfers between devices, per_device(): swap_x = lambda v: lax.ppermute(v, 'lat', x_pairs)  6.37 us
    ppermute x9, starting transfers between devices, per_device(): swap_y = lambda v: lax.ppermute(v, 'mem', y_pairs)  6.04 us
    ppermute x2, waiting for transfers between devices, per_device(): swap_x = lambda v: lax.ppermute(v, 'lat', x_pairs)  5.75 us
  transfers between devices with their start and end apart: 21, of which 10 were waited for; matrix products, arithmetic and copies ran while one was open for 2% of the time, Pallas kernels for 6%

profile of v1, /device:TPU:1, one launch (start us, length us, event | category | flops | bytes accessed | tf_op | source)
XLA Modules:
  0.0 131.5 jit_solution(16333581609420523744)
XLA Ops:
  0.0 0.9 convert_reduce_fusion
  0.9 0.9 fusion.1
  1.8 0.7 fusion.3
  5.1 0.1 concatenate.3.table
  5.2 1.0 copy-done.2
  6.3 0.7 copy-done.9
  7.0 0.7 copy-done.12
  7.6 7.4 %zonal.1 = (f32[2,4,8,1024]{3,2,1,0:T(8,128)S(1)}, f32[2,4,8,1024]{3,2,1,0:T(8,128)S(1)}) custom-call(s32[8]{0:T(128)S(1)} %concatenate.3.table, s32[16]{0:T(128)S(1)} %copy-done.12, f32[16,17]{1,0:T(8,128)S(1)} %copy-done.9, f32[2,4,16,1024]{3,2,1,0:T(8,128)S(1)} %copy-done.2), custom_call_target="tpu_custom_call" | custom-call | flops 1048576 | bytes 1048576 | tf_op jit(solution)/shard_map/zonal/pallas_call | solution.py:25
  15.0 0.1 collective-permute-start
  15.1 4.5 %collective-permute-start.1 = (f32[2,4,8,1024]{3,2,1,0:T(8,128)S(1)}, f32[2,4,8,1024]{3,2,1,0:T(8,128)S(1)}, u32[]{:S(2)}, u32[]{:S(2)}) collective-permute-start(f32[2,4,8,1024]{3,2,1,0:T(8,128)S(1)} %get-tuple-element.20.b), channel_id=1, source_target_pairs={{1,2},{2,1},{5,6},{6,5},{9,10},{10,9},{13,14},{14,13},{17,18},{18,... | collective-permute-start | bytes 786440 | tf_op jit(solution)/shard_map/ppermute | solution.py:308
  19.6 1.7 %dynamic-slice_bitcast_fusion = f32[4,16,1024]{2,1,0:T(8,128)} fusion(f32[1,2,4,16,1024]{4,3,2,1,0:T(8,128)} %own.1, s32[]{:T(128)S(6)} %select_n.85), kind=kLoop, calls=%fused_computation.2 | loop fusion | bytes 524292 | tf_op jit(solution)/shard_map/jit(dynamic_index_in_dim)/squeeze | solution.py:333
  21.3 1.2 collective-permute-start.9
  22.5 0.8 copy.10
  23.3 0.7 copy-done.11
  24.0 0.8 matrix.1
  24.8 0.0 copy-start.5
  24.8 0.7 copy-done.5
  25.5 0.7 copy-done.7
  26.2 1.6 %copy-done = bf16[4,2,2,4,16,1024]{5,4,3,2,1,0:T(8,128)(2,1)S(1)} copy-done((bf16[4,2,2,4,16,1024]{5,4,3,2,1,0:T(8,128)(2,1)S(1)}, bf16[4,2,2,4,16,1024]{5,4,3,2,1,0:T(8,128)(2,1)}, u32[]{:S(2)}) %copy-start) | copy-done | bytes 2097176
  27.8 0.9 copy-done.6
  28.7 0.9 copy-done.8
  29.7 1.6 %first.1 = (f32[2,4,16,1024]{3,2,1,0:T(8,128)S(1)}, f32[4,16,1024]{2,1,0:T(8,128)}) custom-call(s32[8]{0:T(128)S(1)} %concatenate.3.table, f32[64,128]{1,0:T(8,128)S(1)} %get-tuple-element.18.matrix, f32[2,4,8,1024]{3,2,1,0:T(8,128)S(1)} %get-tuple-element.19.a, f32[2,4,8,1024]{3,2,1,0:T(8,128)S(1)} %get-tuple-element.20.b, f32[2,4,8,1024]{3,2,1,0:T(8,128)S(1)} %copy-done.6, ...), custom_call_target="tpu_custom_call" | custom-call | flops 1048576 | bytes 1048576 | tf_op jit(solution)/shard_map/first/pallas_call | solution.py:25
  31.3 1.6 %send.1 = (f32[4,16,1024]{2,1,0:T(8,128)}, f32[4,16,1024]{2,1,0:T(8,128)}, f32[4,16,1024]{2,1,0:T(8,128)}) custom-call(s32[8]{0:T(128)S(1)} %concatenate.3.table, bf16[4,2,2,4,16,1024]{5,4,3,2,1,0:T(8,128)(2,1)S(1)} %copy-done.1, f32[2,4,16,1024]{3,2,1,0:T(8,128)S(1)} %get-tuple-element.21.localized), custom_call_target="tpu_custom_call" | custom-call | flops 1048576 | bytes 1048576 | tf_op jit(solution)/shard_map/send/pallas_call | solution.py:25
  32.9 0.3 collective-permute-start.7
  33.1 1.2 collective-permute-start.5
  34.4 0.3 collective-permute-start.3
  34.6 1.2 collective-permute-start.2
  40.0 0.1 bitcast_select_fusion
  40.1 3.2 %collective-permute-start.10 = (f32[4,16,1024]{2,1,0:T(8,128)S(1)}, f32[4,16,1024]{2,1,0:T(8,128)S(1)}, u32[]{:S(2)}, u32[]{:S(2)}) collective-permute-start(f32[4,16,1024]{2,1,0:T(8,128)S(1)} %get-tuple-element.34), channel_id=1, source_target_pairs={{0,8},{4,12},{8,16},{12,20},{1,9},{5,13},{9,17},{13,21},{2,10},{6,... | collective-permute-start | bytes 786440 | tf_op jit(solution)/shard_map/ppermute | solution.py:371
  43.3 0.7 collective-permute-start.11
  44.0 1.0 meet3.1
  45.0 2.2 %collective-permute-done.5.got = f32[4,16,1024]{2,1,0:T(8,128)} collective-permute-done((f32[4,16,1024]{2,1,0:T(8,128)}, f32[4,16,1024]{2,1,0:T(8,128)}, u32[]{:S(2)}, u32[]{:S(2)}) %collective-permute-start.5) | collective-permute-done | bytes 262176 | tf_op jit(solution)/shard_map/ppermute | solution.py:329
  47.2 3.3 %collective-permute-start.8 = (f32[4,16,1024]{2,1,0:T(8,128)S(1)}, f32[4,16,1024]{2,1,0:T(8,128)S(1)}, u32[]{:S(2)}, u32[]{:S(2)}) collective-permute-start(f32[4,16,1024]{2,1,0:T(8,128)S(1)} %meet3.1), channel_id=1, source_target_pairs={{0,24},{4,28},{8,0},{12,4},{16,8},{20,12},{24,16},{28,20},{1,25},{... | collective-permute-start | bytes 786440 | tf_op jit(solution)/shard_map/ppermute | solution.py:330
  50.5 1.0 meet2.1
  51.6 1.3 collective-permute-done.3.got
  52.8 2.3 %collective-permute-start.6 = (f32[4,16,1024]{2,1,0:T(8,128)S(1)}, f32[4,16,1024]{2,1,0:T(8,128)S(1)}, u32[]{:S(2)}, u32[]{:S(2)}) collective-permute-start(f32[4,16,1024]{2,1,0:T(8,128)S(1)} %meet2.1), channel_id=1, source_target_pairs={{0,16},{4,20},{8,24},{12,28},{16,0},{20,4},{24,8},{28,12},{1,17},{... | collective-permute-start | bytes 786440 | tf_op jit(solution)/shard_map/ppermute | solution.py:330
  55.1 1.0 meet1.1
  56.2 0.3 collective-permute-done.2.got_y
  56.5 1.5 %collective-permute-start.4 = (f32[4,16,1024]{2,1,0:T(8,128)S(1)}, f32[4,16,1024]{2,1,0:T(8,128)S(1)}, u32[]{:S(2)}, u32[]{:S(2)}) collective-permute-start(f32[4,16,1024]{2,1,0:T(8,128)S(1)} %meet1.1), channel_id=1, source_target_pairs={{0,8},{4,12},{8,16},{12,20},{16,24},{20,28},{24,0},{28,4},{1,9},{5... | collective-permute-start | bytes 786440 | tf_op jit(solution)/shard_map/ppermute | solution.py:330
  58.0 18.6 %collective-permute-done.6.got_2 = f32[4,16,1024]{2,1,0:T(8,128)S(1)} collective-permute-done((f32[4,16,1024]{2,1,0:T(8,128)S(1)}, f32[4,16,1024]{2,1,0:T(8,128)S(1)}, u32[]{:S(2)}, u32[]{:S(2)}) %collective-permute-start.6) | collective-permute-done | bytes 262176 | tf_op jit(solution)/shard_map/ppermute | solution.py:330
  76.6 1.1 last.1.refs_0_
  77.8 0.1 collective-permute-start.16
  77.8 0.1 collective-permute-start.14
  77.9 3.3 %collective-permute-start.12 = (f32[4,16,1024]{2,1,0:T(8,128)S(1)}, f32[4,16,1024]{2,1,0:T(8,128)S(1)}, u32[]{:S(2)}, u32[]{:S(2)}) collective-permute-start(f32[4,16,1024]{2,1,0:T(8,128)S(1)} %last.1.refs_0_), channel_id=1, source_target_pairs={{0,24},{4,28},{8,0},{12,4},{16,8},{20,12},{24,16},{28,20},{1,25},{... | collective-permute-start | bytes 786440 | tf_op jit(solution)/shard_map/ppermute | solution.py:330
  81.2 0.2 collective-permute-start.18
  81.4 12.7 %collective-permute-done.16.refs_1_ = f32[4,16,1024]{2,1,0:T(8,128)S(1)} collective-permute-done((f32[4,16,1024]{2,1,0:T(8,128)S(1)}, f32[4,16,1024]{2,1,0:T(8,128)S(1)}, u32[]{:S(2)}, u32[]{:S(2)}) %collective-permute-start.16) | collective-permute-done | bytes 262176 | tf_op jit(solution)/shard_map/ppermute | solution.py:330
  94.0 0.2 collective-permute-start.17
  94.3 1.2 collective-permute-start.15
  95.5 2.1 %collective-permute-done.12.refs_0_ = f32[4,16,1024]{2,1,0:T(8,128)S(1)} collective-permute-done((f32[4,16,1024]{2,1,0:T(8,128)S(1)}, f32[4,16,1024]{2,1,0:T(8,128)S(1)}, u32[]{:S(2)}, u32[]{:S(2)}) %collective-permute-start.12) | collective-permute-done | bytes 262176 | tf_op jit(solution)/shard_map/ppermute | solution.py:330
  97.6 0.2 collective-permute-start.13
  97.8 0.6 spread0.2.refs_2_
  98.4 0.7 spread0.3.refs_2_
  99.1 2.2 %collective-permute-done.17.refs_1_ = f32[4,16,1024]{2,1,0:T(8,128)S(1)} collective-permute-done((f32[4,16,1024]{2,1,0:T(8,128)S(1)}, f32[4,16,1024]{2,1,0:T(8,128)S(1)}, u32[]{:S(2)}, u32[]{:S(2)}) %collective-permute-start.17) | collective-permute-done | bytes 262176 | tf_op jit(solution)/shard_map/ppermute | solution.py:329
  101.3 0.7 spread1.1.refs_2_
  102.0 4.9 %collective-permute-done.15.refs_1_ = f32[4,16,1024]{2,1,0:T(8,128)S(1)} collective-permute-done((f32[4,16,1024]{2,1,0:T(8,128)S(1)}, f32[4,16,1024]{2,1,0:T(8,128)S(1)}, u32[]{:S(2)}, u32[]{:S(2)}) %collective-permute-start.15) | collective-permute-done | bytes 262176 | tf_op jit(solution)/shard_map/ppermute | solution.py:329
  106.9 0.7 spread3.2.refs_1_
  107.6 0.0 copy-start.3
  107.7 0.0 copy-start.13
  107.7 4.9 %collective-permute-done.13.refs_0_ = f32[4,16,1024]{2,1,0:T(8,128)S(1)} collective-permute-done((f32[4,16,1024]{2,1,0:T(8,128)S(1)}, f32[4,16,1024]{2,1,0:T(8,128)S(1)}, u32[]{:S(2)}, u32[]{:S(2)}) %collective-permute-start.13) | collective-permute-done | bytes 262176 | tf_op jit(solution)/shard_map/ppermute | solution.py:329
  112.6 1.6 %spread3.3 = (f32[2,4,8,1024]{3,2,1,0:T(8,128)S(1)}, f32[2,4,8,1024]{3,2,1,0:T(8,128)S(1)}, f32[2,4,8,1024]{3,2,1,0:T(8,128)S(1)}, f32[2,4,8,1024]{3,2,1,0:T(8,128)S(1)}, f32[2,4,16,1024]{3,2,1,0:T(8,128)}) custom-call(s32[8]{0:T(128)S(1)} %concatenate.3.table, bf16[4,2,2,4,16,1024]{5,4,3,2,1,0:T(8,128)(2,1)S(1)} %copy-done.1, ...), custom_call_target="tpu_custom_call" | custom-call | flops 524288 | bytes 524288 | tf_op jit(solution)/shard_map/spread3/pallas_call | solution.py:25
  114.2 1.4 %collective-permute-start.19 = (f32[2,4,8,1024]{3,2,1,0:T(8,128)S(1)}, f32[2,4,8,1024]{3,2,1,0:T(8,128)S(1)}, u32[]{:S(2)}, u32[]{:S(2)}) collective-permute-start(f32[2,4,8,1024]{3,2,1,0:T(8,128)S(1)} %get-tuple-element.29), channel_id=1, source_target_pairs={{0,1},{1,0},{2,3},{3,2},{4,5},{5,4},{6,7},{7,6},{8,9},{9,8},{10,11... | collective-permute-start | bytes 786440 | tf_op jit(solution)/shard_map/ppermute | solution.py:307
  115.6 1.9 %collective-permute-start.20 = (f32[2,4,8,1024]{3,2,1,0:T(8,128)S(1)}, f32[2,4,8,1024]{3,2,1,0:T(8,128)S(1)}, u32[]{:S(2)}, u32[]{:S(2)}) collective-permute-start(f32[2,4,8,1024]{3,2,1,0:T(8,128)S(1)} %get-tuple-element.30), channel_id=1, source_target_pairs={{1,2},{2,1},{5,6},{6,5},{9,10},{10,9},{13,14},{14,13},{17,18},{18,... | collective-permute-start | bytes 786440 | tf_op jit(solution)/shard_map/ppermute | solution.py:308
  117.5 5.8 %collective-permute-done.20.got_x = f32[2,4,8,1024]{3,2,1,0:T(8,128)S(1)} collective-permute-done((f32[2,4,8,1024]{3,2,1,0:T(8,128)S(1)}, f32[2,4,8,1024]{3,2,1,0:T(8,128)S(1)}, u32[]{:S(2)}, u32[]{:S(2)}) %collective-permute-start.20) | collective-permute-done | bytes 262176 | tf_op jit(solution)/shard_map/ppermute | solution.py:308
  123.3 8.2 %zonal_adjoint.1 = f32[2,4,16,1024]{3,2,1,0:T(8,128)} custom-call(s32[8]{0:T(128)S(1)} %concatenate.3.table, s32[16]{0:T(128)S(1)} %copy-done.13, f32[16,17]{1,0:T(8,128)S(1)} %copy-done.10, f32[2,4,16,1024]{3,2,1,0:T(8,128)S(1)} %copy-done.3, f32[2,4,8,1024]{3,2,1,0:T(8,128)S(1)} %get-tuple-element.27.own_core, ...), custom_call_target="tpu_custom_call" | custom-call | flops 1048576 | bytes 1048576 | tf_op jit(solution)/shard_map/zonal_adjoint/pallas_call | solution.py:25
  (28 shorter events, 0.1 us)
Async XLA Ops:
  5.2 1.0 copy-start.2
  6.3 0.7 copy-start.9
  7.0 0.7 copy-start.12
  15.0 9.8 %collective-permute-start = (f32[2,4,8,1024]{3,2,1,0:T(8,128)S(1)}, f32[2,4,8,1024]{3,2,1,0:T(8,128)S(1)}, u32[]{:S(2)}, u32[]{:S(2)}) collective-permute-start(f32[2,4,8,1024]{3,2,1,0:T(8,128)S(1)} %get-tuple-element.19.a), channel_id=1, source_target_pairs={{0,1},{1,0},{2,3},{3,2},{4,5},{5,4},{6,7},{7,6},{8,9},{9,8},{10,11... | collective-permute-start | bytes 786440 | tf_op jit(solution)/shard_map/ppermute | solution.py:307
  15.1 10.4 %collective-permute-start.1 = (f32[2,4,8,1024]{3,2,1,0:T(8,128)S(1)}, f32[2,4,8,1024]{3,2,1,0:T(8,128)S(1)}, u32[]{:S(2)}, u32[]{:S(2)}) collective-permute-start(f32[2,4,8,1024]{3,2,1,0:T(8,128)S(1)} %get-tuple-element.20.b), channel_id=1, source_target_pairs={{1,2},{2,1},{5,6},{6,5},{9,10},{10,9},{13,14},{14,13},{17,18},{18,... | collective-permute-start | bytes 786440 | tf_op jit(solution)/shard_map/ppermute | solution.py:308
  21.3 18.7 %collective-permute-start.9 = (f32[4,16,1024]{2,1,0:T(8,128)}, f32[4,16,1024]{2,1,0:T(8,128)S(1)}, u32[]{:S(2)}, u32[]{:S(2)}) collective-permute-start(f32[4,16,1024]{2,1,0:T(8,128)} %dynamic-slice_bitcast_fusion), channel_id=1, source_target_pairs={{0,4},{4,0},{8,12},{12,8},{16,20},{20,16},{24,28},{28,24},{1,5},{5... | collective-permute-start | bytes 786440 | tf_op jit(solution)/shard_map/ppermute | solution.py:329
  23.3 0.7 copy-start.11
  24.8 0.7 copy-start.5
  25.5 0.7 copy-start.7
  26.2 1.6 %copy-start = (bf16[4,2,2,4,16,1024]{5,4,3,2,1,0:T(8,128)(2,1)S(1)}, bf16[4,2,2,4,16,1024]{5,4,3,2,1,0:T(8,128)(2,1)}, u32[]{:S(2)}) copy-start(bf16[4,2,2,4,16,1024]{5,4,3,2,1,0:T(8,128)(2,1)} %ens.21) | copy-start | bytes 6291460
  27.8 0.9 copy-start.6
  28.7 0.9 copy-start.8
  29.7 1.6 %copy-start.1 = (bf16[4,2,2,4,16,1024]{5,4,3,2,1,0:T(8,128)(2,1)S(1)}, bf16[4,2,2,4,16,1024]{5,4,3,2,1,0:T(8,128)(2,1)}, u32[]{:S(2)}) copy-start(bf16[4,2,2,4,16,1024]{5,4,3,2,1,0:T(8,128)(2,1)} %ens.21) | copy-start | bytes 6291460
  31.3 8.7 %copy-start.4 = (f32[1,2,4,16,1024]{4,3,2,1,0:T(8,128)S(1)}, f32[1,2,4,16,1024]{4,3,2,1,0:T(8,128)}, u32[]{:S(2)}) copy-start(f32[1,2,4,16,1024]{4,3,2,1,0:T(8,128)} %own.1) | copy-start | bytes 1572868
  32.9 10.4 %collective-permute-start.7 = (f32[4,16,1024]{2,1,0:T(8,128)}, f32[4,16,1024]{2,1,0:T(8,128)}, u32[]{:S(2)}, u32[]{:S(2)}) collective-permute-start(f32[4,16,1024]{2,1,0:T(8,128)} %get-tuple-element.25), channel_id=1, source_target_pairs={{0,4},{4,0},{8,12},{12,8},{16,20},{20,16},{24,28},{28,24},{1,5},{5... | collective-permute-start | bytes 786440 | tf_op jit(solution)/shard_map/ppermute | solution.py:329
  33.1 14.1 %collective-permute-start.5 = (f32[4,16,1024]{2,1,0:T(8,128)}, f32[4,16,1024]{2,1,0:T(8,128)}, u32[]{:S(2)}, u32[]{:S(2)}) collective-permute-start(f32[4,16,1024]{2,1,0:T(8,128)} %get-tuple-element.24), channel_id=1, source_target_pairs={{0,4},{4,0},{8,12},{12,8},{16,20},{20,16},{24,28},{28,24},{1,5},{5... | collective-permute-start | bytes 786440 | tf_op jit(solution)/shard_map/ppermute | solution.py:329
  34.4 18.5 %collective-permute-start.3 = (f32[4,16,1024]{2,1,0:T(8,128)}, f32[4,16,1024]{2,1,0:T(8,128)}, u32[]{:S(2)}, u32[]{:S(2)}) collective-permute-start(f32[4,16,1024]{2,1,0:T(8,128)} %get-tuple-element.23), channel_id=1, source_target_pairs={{0,4},{4,0},{8,12},{12,8},{16,20},{20,16},{24,28},{28,24},{1,5},{5... | collective-permute-start | bytes 786440 | tf_op jit(solution)/shard_map/ppermute | solution.py:329
  34.6 21.9 %collective-permute-start.2 = (f32[4,16,1024]{2,1,0:T(8,128)}, f32[4,16,1024]{2,1,0:T(8,128)}, u32[]{:S(2)}, u32[]{:S(2)}) collective-permute-start(f32[4,16,1024]{2,1,0:T(8,128)} %get-tuple-element.22), channel_id=1, source_target_pairs={{0,4},{4,0},{8,12},{12,8},{16,20},{20,16},{24,28},{28,24},{1,5},{5... | collective-permute-start | bytes 786440 | tf_op jit(solution)/shard_map/ppermute | solution.py:329
  40.1 17.9 %collective-permute-start.10 = (f32[4,16,1024]{2,1,0:T(8,128)S(1)}, f32[4,16,1024]{2,1,0:T(8,128)S(1)}, u32[]{:S(2)}, u32[]{:S(2)}) collective-permute-start(f32[4,16,1024]{2,1,0:T(8,128)S(1)} %get-tuple-element.34), channel_id=1, source_target_pairs={{0,8},{4,12},{8,16},{12,20},{1,9},{5,13},{9,17},{13,21},{2,10},{6,... | collective-permute-start | bytes 786440 | tf_op jit(solution)/shard_map/ppermute | solution.py:371
  43.3 14.7 %collective-permute-start.11 = (f32[4,16,1024]{2,1,0:T(8,128)S(1)}, f32[4,16,1024]{2,1,0:T(8,128)S(1)}, u32[]{:S(2)}, u32[]{:S(2)}) collective-permute-start(f32[4,16,1024]{2,1,0:T(8,128)S(1)} %get-tuple-element.33), channel_id=1, source_target_pairs={{16,8},{20,12},{24,16},{28,20},{17,9},{21,13},{25,17},{29,21},{18,... | collective-permute-start | bytes 786440 | tf_op jit(solution)/shard_map/ppermute | solution.py:372
  47.2 10.8 %collective-permute-start.8 = (f32[4,16,1024]{2,1,0:T(8,128)S(1)}, f32[4,16,1024]{2,1,0:T(8,128)S(1)}, u32[]{:S(2)}, u32[]{:S(2)}) collective-permute-start(f32[4,16,1024]{2,1,0:T(8,128)S(1)} %meet3.1), channel_id=1, source_target_pairs={{0,24},{4,28},{8,0},{12,4},{16,8},{20,12},{24,16},{28,20},{1,25},{... | collective-permute-start | bytes 786440 | tf_op jit(solution)/shard_map/ppermute | solution.py:330
  52.8 23.8 %collective-permute-start.6 = (f32[4,16,1024]{2,1,0:T(8,128)S(1)}, f32[4,16,1024]{2,1,0:T(8,128)S(1)}, u32[]{:S(2)}, u32[]{:S(2)}) collective-permute-start(f32[4,16,1024]{2,1,0:T(8,128)S(1)} %meet2.1), channel_id=1, source_target_pairs={{0,16},{4,20},{8,24},{12,28},{16,0},{20,4},{24,8},{28,12},{1,17},{... | collective-permute-start | bytes 786440 | tf_op jit(solution)/shard_map/ppermute | solution.py:330
  56.5 20.1 %collective-permute-start.4 = (f32[4,16,1024]{2,1,0:T(8,128)S(1)}, f32[4,16,1024]{2,1,0:T(8,128)S(1)}, u32[]{:S(2)}, u32[]{:S(2)}) collective-permute-start(f32[4,16,1024]{2,1,0:T(8,128)S(1)} %meet1.1), channel_id=1, source_target_pairs={{0,8},{4,12},{8,16},{12,20},{16,24},{20,28},{24,0},{28,4},{1,9},{5... | collective-permute-start | bytes 786440 | tf_op jit(solution)/shard_map/ppermute | solution.py:330
  77.8 16.3 %collective-permute-start.16 = (f32[4,16,1024]{2,1,0:T(8,128)S(1)}, f32[4,16,1024]{2,1,0:T(8,128)S(1)}, u32[]{:S(2)}, u32[]{:S(2)}) collective-permute-start(f32[4,16,1024]{2,1,0:T(8,128)S(1)} %last.1.refs_0_), channel_id=1, source_target_pairs={{0,16},{4,20},{8,24},{12,28},{16,0},{20,4},{24,8},{28,12},{1,17},{... | collective-permute-start | bytes 786440 | tf_op jit(solution)/shard_map/ppermute | solution.py:330
  77.8 16.4 %collective-permute-start.14 = (f32[4,16,1024]{2,1,0:T(8,128)S(1)}, f32[4,16,1024]{2,1,0:T(8,128)S(1)}, u32[]{:S(2)}, u32[]{:S(2)}) collective-permute-start(f32[4,16,1024]{2,1,0:T(8,128)S(1)} %last.1.refs_0_), channel_id=1, source_target_pairs={{0,8},{4,12},{8,16},{12,20},{16,24},{20,28},{24,0},{28,4},{1,9},{5... | collective-permute-start | bytes 786440 | tf_op jit(solution)/shard_map/ppermute | solution.py:330
  77.9 19.7 %collective-permute-start.12 = (f32[4,16,1024]{2,1,0:T(8,128)S(1)}, f32[4,16,1024]{2,1,0:T(8,128)S(1)}, u32[]{:S(2)}, u32[]{:S(2)}) collective-permute-start(f32[4,16,1024]{2,1,0:T(8,128)S(1)} %last.1.refs_0_), channel_id=1, source_target_pairs={{0,24},{4,28},{8,0},{12,4},{16,8},{20,12},{24,16},{28,20},{1,25},{... | collective-permute-start | bytes 786440 | tf_op jit(solution)/shard_map/ppermute | solution.py:330
  81.2 17.3 %collective-permute-start.18 = (f32[4,16,1024]{2,1,0:T(8,128)S(1)}, f32[4,16,1024]{2,1,0:T(8,128)S(1)}, u32[]{:S(2)}, u32[]{:S(2)}) collective-permute-start(f32[4,16,1024]{2,1,0:T(8,128)S(1)} %last.1.refs_0_), channel_id=1, source_target_pairs={{0,4},{4,0},{8,12},{12,8},{16,20},{20,16},{24,28},{28,24},{1,5},{5... | collective-permute-start | bytes 786440 | tf_op jit(solution)/shard_map/ppermute | solution.py:329
  94.0 7.3 %collective-permute-start.17 = (f32[4,16,1024]{2,1,0:T(8,128)S(1)}, f32[4,16,1024]{2,1,0:T(8,128)S(1)}, u32[]{:S(2)}, u32[]{:S(2)}) collective-permute-start(f32[4,16,1024]{2,1,0:T(8,128)S(1)} %collective-permute-done.16.refs_1_), channel_id=1, source_target_pairs={{0,4},{4,0},{8,12},{12,8},{16,20},{20,16},{24,28},{28,24},{1,5},{5... | collective-permute-start | bytes 786440 | tf_op jit(solution)/shard_map/ppermute | solution.py:329
  94.3 12.7 %collective-permute-start.15 = (f32[4,16,1024]{2,1,0:T(8,128)S(1)}, f32[4,16,1024]{2,1,0:T(8,128)S(1)}, u32[]{:S(2)}, u32[]{:S(2)}) collective-permute-start(f32[4,16,1024]{2,1,0:T(8,128)S(1)} %collective-permute-done.14.refs_0_), channel_id=1, source_target_pairs={{0,4},{4,0},{8,12},{12,8},{16,20},{20,16},{24,28},{28,24},{1,5},{5... | collective-permute-start | bytes 786440 | tf_op jit(solution)/shard_map/ppermute | solution.py:329
  97.6 15.0 %collective-permute-start.13 = (f32[4,16,1024]{2,1,0:T(8,128)S(1)}, f32[4,16,1024]{2,1,0:T(8,128)S(1)}, u32[]{:S(2)}, u32[]{:S(2)}) collective-permute-start(f32[4,16,1024]{2,1,0:T(8,128)S(1)} %collective-permute-done.12.refs_0_), channel_id=1, source_target_pairs={{0,4},{4,0},{8,12},{12,8},{16,20},{20,16},{24,28},{28,24},{1,5},{5... | collective-permute-start | bytes 786440 | tf_op jit(solution)/shard_map/ppermute | solution.py:329
  107.6 15.6 %copy-start.3 = (f32[2,4,16,1024]{3,2,1,0:T(8,128)S(1)}, f32[2,4,16,1024]{3,2,1,0:T(8,128)}, u32[]{:S(2)}) copy-start(f32[2,4,16,1024]{3,2,1,0:T(8,128)} %control.3) | copy-start | bytes 1572868
  107.7 15.6 %copy-start.10 = (f32[16,17]{1,0:T(8,128)S(1)}, f32[16,17]{1,0:T(8,128)}, u32[]{:S(2)}) copy-start(f32[16,17]{1,0:T(8,128)} %taps_ref.5) | copy-start | bytes 3268
  107.7 15.6 %copy-start.13 = (s32[16]{0:T(128)S(1)}, s32[16]{0:T(128)}, u32[]{:S(2)}) copy-start(s32[16]{0:T(128)} %shift_ref.3) | copy-start | bytes 196
  114.2 3.3 %collective-permute-start.19 = (f32[2,4,8,1024]{3,2,1,0:T(8,128)S(1)}, f32[2,4,8,1024]{3,2,1,0:T(8,128)S(1)}, u32[]{:S(2)}, u32[]{:S(2)}) collective-permute-start(f32[2,4,8,1024]{3,2,1,0:T(8,128)S(1)} %get-tuple-element.29), channel_id=1, source_target_pairs={{0,1},{1,0},{2,3},{3,2},{4,5},{5,4},{6,7},{7,6},{8,9},{9,8},{10,11... | collective-permute-start | bytes 786440 | tf_op jit(solution)/shard_map/ppermute | solution.py:307
  115.6 7.7 %collective-permute-start.20 = (f32[2,4,8,1024]{3,2,1,0:T(8,128)S(1)}, f32[2,4,8,1024]{3,2,1,0:T(8,128)S(1)}, u32[]{:S(2)}, u32[]{:S(2)}) collective-permute-start(f32[2,4,8,1024]{3,2,1,0:T(8,128)S(1)} %get-tuple-element.30), channel_id=1, source_target_pairs={{1,2},{2,1},{5,6},{6,5},{9,10},{10,9},{13,14},{14,13},{17,18},{18,... | collective-permute-start | bytes 786440 | tf_op jit(solution)/shard_map/ppermute | solution.py:308

commit v2 on v1

--- a/solution.py
+++ b/solution.py
@@ -16,22 +16,57 @@
 
 VMEM = pl.BlockSpec(memory_space=pltpu.VMEM)
 SMEM = pl.BlockSpec(memory_space=pltpu.SMEM)
-
-PARITY, HAS_X, OWN_Y, WEIGHT_FROM, SLOT = 0, 1, 2, 3, 4
-TABLE = 8
-
-
-def call(body, outs, name, cost, *operands, specs, scratch=()):
+ANY = pl.BlockSpec(memory_space=pl.ANY)
+
+
+def call(body, outs, name, cost, *operands, specs, scratch=(), after=()):
+    count, extra = len(operands), len(after)
+
+    def kernel(*refs):
+        body(*refs[:count], *refs[count + extra :])
+
     return pl.pallas_call(
-        body,
+        kernel,
         out_shape=outs,
-        in_specs=list(specs),
+        in_specs=list(specs) + [ANY] * extra,
         out_specs=jax.tree.map(lambda _: VMEM, outs),
         scratch_shapes=list(scratch),
-        compiler_params=pltpu.CompilerParams(vmem_limit_bytes=48 << 20),
+        compiler_params=pltpu.CompilerParams(vmem_limit_bytes=16 << 20),
         cost_estimate=pl.CostEstimate(flops=cost, bytes_accessed=cost, transcendentals=0),
         name=name,
-    )(*operands)
+    )(*operands, *after)
+
+
+def parity():
+    return lax.axis_index("lat") & 1
+
+
+def own_y():
+    return lax.axis_index("mem") & 1
+
+
+def own_z():
+    return lax.axis_index("mem") >> 1
+
+
+def entry_at(owners, step, value):
+    place = (own_z() + step) & (SLOTS - 1)
+    found = jnp.int32(0)
+    for t in range(SLOTS):
+        rank = jnp.int32(0)
+        for u in range(SLOTS):
+            if u != t:
+                rank += jnp.where(owners[u] < owners[t], 1, 0)
+        found = jnp.where(rank == place, value(t), found)
+    return found
+
+
+def slot_at(owners, step):
+    return entry_at(owners, step, lambda t: jnp.int32(t))
+
+
+def owner_at(owners, step):
+    return entry_at(owners, step, lambda t: owners[t])
 
 
 def shape(*dims, dtype=F32):
@@ -91,48 +126,56 @@
     return [slice(i * LANES, (i + 1) * LANES) for i in range(width // LANES)]
 
 
-def zonal_forward(table, shift_ref, taps_ref, control, near_core, near_x, tap_ref):
+def half_start(which):
+    odd = parity()
+    return pl.multiple_of((1 - odd if which == 0 else odd) * 8, 8)
+
+
+def zonal_forward(which, shift_ref, taps_ref, control, out, tap_ref):
     members, levels, _, width = control.shape
-    for which, out in enumerate((near_core, near_x)):
-        first = pl.multiple_of((1 - table[PARITY] if which == 0 else table[PARITY]) * 8, 8)
-        amount = (width - HALF - row_shifts(shift_ref, first)) & (width - 1)
-        spread_taps(taps_ref, first, tap_ref)
-
-        def step(unit, carry, out=out, first=first, amount=amount):
-            m, l = unit // levels, unit % levels
+    first = half_start(which)
+    amount = (width - HALF - row_shifts(shift_ref, first)) & (width - 1)
+    spread_taps(taps_ref, first, tap_ref)
+
+    def step(m, carry):
+        for l in range(levels):
             columns = [control[m, l, pl.ds(first, 8), cut] for cut in tiles(width)]
             result = circle_filter(columns, amount, lambda k: tap_ref[BAND - 1 - k])
             for cut, value in zip(tiles(width), result):
                 out[m, l, :, cut] = value
-            return carry
-
-        lax.fori_loop(0, members * levels, step, 0)
-
-
-def zonal_adjoint(
-    table, shift_ref, taps_ref, control, own_core, own_x, got_core, got_x, out, tap_ref
-):
+        return carry
+
+    lax.fori_loop(0, members, step, 0)
+
+
+def zonal_adjoint(which, shift_ref, taps_ref, control, own, got, *refs):
+    other, out, tap_ref = (None, *refs) if which == 0 else refs
     members, levels, _, width = control.shape
-    for which, (own, got) in enumerate(((own_core, got_core), (own_x, got_x))):
-        first = pl.multiple_of((1 - table[PARITY] if which == 0 else table[PARITY]) * 8, 8)
-        amount = (row_shifts(shift_ref, first) - HALF) & (width - 1)
-        spread_taps(taps_ref, first, tap_ref)
-
-        def step(unit, carry, own=own, got=got, first=first, amount=amount):
-            m, l = unit // levels, unit % levels
+    first = half_start(which)
+    amount = (row_shifts(shift_ref, first) - HALF) & (width - 1)
+    spread_taps(taps_ref, first, tap_ref)
+
+    def step(m, carry):
+        for l in range(levels):
             columns = [own[m, l, :, cut] + got[m, l, :, cut] for cut in tiles(width)]
             result = circle_filter(columns, amount, lambda k: tap_ref[k])
             for cut, value in zip(tiles(width), result):
-                out[m, l, pl.ds(first, 8), cut] = control[m, l, pl.ds(first, 8), cut] + value
-            return carry
-
-        lax.fori_loop(0, members * levels, step, 0)
-
-
-def build_matrix(table, taps_ref, mixing_ref, matrix, transposed):
+                total = control[m, l, pl.ds(first, 8), cut] + value
+                if which == 0:
+                    out[m, l, :, cut] = total
+                else:
+                    out[m, l, pl.ds(first, 8), cut] = total
+                    out[m, l, pl.ds(8 - first, 8), cut] = other[m, l, :, cut]
+        return carry
+
+    lax.fori_loop(0, members, step, 0)
+
+
+def build_matrix(lat_count, taps_ref, mixing_ref, matrix, transposed):
     band_rows, levels = taps_ref.shape[0], mixing_ref.shape[1]
     rows, columns = matrix.shape
-    odd = table[PARITY]
+    odd, lat = parity(), lax.axis_index("lat")
+    alone = (lat == 0) | (lat == lat_count - 1)
     column = lax.broadcasted_iota(jnp.int32, (band_rows, columns), 1)
     row = lax.broadcasted_iota(jnp.int32, (band_rows, columns), 0)
     block, level, inner = column // (8 * levels), (column // 8) % levels, column % 8
@@ -142,7 +185,7 @@
     band = jnp.zeros((band_rows, columns), F32)
     for k in range(BAND):
         band = jnp.where(reach == k, taps_ref[:, k : k + 1], band)
-    band = jnp.where((block == 3) & (table[HAS_X] == 0), 0.0, band)
+    band = jnp.where((block == 3) & alone, 0.0, band)
     for a in range(levels):
         mixing = mixing_ref[a * band_rows : (a + 1) * band_rows, :]
         factor = jnp.zeros((band_rows, columns), F32)
@@ -202,56 +245,73 @@
     return total
 
 
-def first_body(step, table, matrix, a, b, c, d, ens, localized, send):
+def weight_out(obs, out):
+    pltpu.sync_copy(obs.at[0, 1 - own_y()], out)
+
+
+def weight_pick(owners, obs, from_y, mine, up, down):
+    for step, out in ((0, mine), (1, up), (SLOTS - 1, down)):
+        held = (owner_at(owners, step) & 1) == own_y()
+
+        @pl.when(held)
+        def _(out=out):
+            pltpu.sync_copy(obs.at[0, own_y()], out)
+
+        @pl.when(jnp.logical_not(held))
+        def _(out=out):
+            out[...] = from_y[...]
+
+
+def first_body(step, owners, matrix, a, b, c, d, ens, localized, send):
     localize(matrix, (a, b, c, d), localized)
+    slot = slot_at(owners, step)
     for l in range(localized.shape[1]):
-        send[l] = increment(ens, localized, table[SLOT + step], 1 - table[OWN_Y], l)
-
-
-def send_body(steps, table, ens, localized, *sends):
+        send[l] = increment(ens, localized, slot, 1 - own_y(), l)
+
+
+def send_body(steps, owners, ens, localized, *sends):
     for step, send in zip(steps, sends):
+        slot = slot_at(owners, step)
         for l in range(localized.shape[1]):
-            send[l] = increment(ens, localized, table[SLOT + step], 1 - table[OWN_Y], l)
-
-
-def meet_body(step, table, ens, localized, got, out):
+            send[l] = increment(ens, localized, slot, 1 - own_y(), l)
+
+
+def meet_body(step, owners, ens, localized, got, out):
+    slot = slot_at(owners, step)
     for l in range(localized.shape[1]):
-        out[l] = increment(ens, localized, table[SLOT + step], table[OWN_Y], l) + got[l]
-
-
-def last_body(table, ens, localized, got_y, got_1, got_2, got_3, own, from_y, from_low, from_high, out):
-    for l in range(localized.shape[1]):
-        out[l] = (
-            increment(ens, localized, table[SLOT], table[OWN_Y], l)
-            + got_y[l]
-            + (got_1[l] + got_2[l] + got_3[l])
-        )
-    source = table[WEIGHT_FROM]
-
-    @pl.when(source == 0)
-    def _():
-        out[...] = out[...] * own[0, table[OWN_Y]]
-
-    for code, weight in ((1, from_y), (2, from_low), (3, from_high)):
-
-        @pl.when(source == code)
+        out[l] = increment(ens, localized, slot, own_y(), l) + got[l]
+
+
+def last_body(owners, ens, localized, got_y, got_1, got_2, got_3, mine, from_low, from_high, out):
+    slot, place = slot_at(owners, 0), owner_at(owners, 0) >> 1
+    for code, weight in enumerate((mine, from_low, from_high)):
+        here = (place == own_z(), place < own_z(), place > own_z())[code]
+
+        @pl.when(here)
         def _(weight=weight):
-            out[...] = out[...] * weight[...]
-
-
-def spread_body(pieces, first, final, table, ens, *refs):
+            for l in range(localized.shape[1]):
+                out[l] = weight[l] * (
+                    increment(ens, localized, slot, own_y(), l)
+                    + got_y[l]
+                    + (got_1[l] + got_2[l] + got_3[l])
+                )
+
+
+def spread_body(pieces, first, final, owners, ens, *refs):
     refs = list(refs)
     grads = [refs.pop(0) for _ in pieces]
     before = None if first else refs.pop(0)
     matrix = refs.pop(0) if final else None
     out = refs[-1] if final else refs[0]
     members, levels = out.shape[:2]
+    places = [
+        (slot_at(owners, step), 1 - own_y() if other else own_y()) for step, other in pieces
+    ]
     for m in range(members):
         for l in range(levels):
             total = None if before is None else before[m, l]
-            for (step, other), grad in zip(pieces, grads):
-                field = 1 - table[OWN_Y] if other else table[OWN_Y]
-                term = ens[table[SLOT + step], field, m, l].astype(F32) * grad[l]
+            for (slot, field), grad in zip(places, grads):
+                term = ens[slot, field, m, l].astype(F32) * grad[l]
                 total = term if total is None else total + term
             out[m, l] = total
     if final:
@@ -295,92 +355,85 @@
 ):
     members, levels, band_rows, width = control.shape
     mem_count, lat_count = lax.axis_size("mem"), lax.axis_size("lat")
-    lat, mem = lax.axis_index("lat"), lax.axis_index("mem")
-    parity = lat % 2
-    has_x = jnp.where((lat > 0) & (lat < lat_count - 1), 1, 0)
+    mem = lax.axis_index("mem")
     direct = z_count > 0
     field_shape = (members, levels, band_rows, width)
     half_shape = (members, levels, 8, width)
+    piece = shape(levels, band_rows, width)
     core_pairs = [(i, i ^ 1) for i in range(lat_count)]
     x_pairs = [(i, i + 1) for i in range(1, lat_count - 1, 2)]
     x_pairs += [(j, i) for i, j in x_pairs]
     swap_core = lambda v: lax.ppermute(v, "lat", core_pairs)
     swap_x = lambda v: lax.ppermute(v, "lat", x_pairs)
-
-    z, y = mem // 2, mem % 2
-    if direct:
-        rank = jnp.sum((slot_owner[None, :] < slot_owner[:, None]).astype(jnp.int32), axis=1)
-        place = (z + jnp.arange(SLOTS, dtype=jnp.int32)) % SLOTS
-        at_place = (rank[None, :] == place[:, None]).astype(jnp.int32)
-        slots = jnp.sum(at_place * jnp.arange(SLOTS, dtype=jnp.int32)[None, :], axis=1)
-        owners = jnp.sum(at_place * slot_owner[None, :], axis=1)
-        own_z, own_y = owners[0] // 2, owners[0] % 2
-        source = jnp.where(
-            own_z == z, jnp.where(own_y == y, 0, 1), jnp.where(own_z < z, 2, 3)
-        )
-    else:
-        slots, source = jnp.arange(SLOTS, dtype=jnp.int32), jnp.int32(0)
-    table = jnp.concatenate(
-        [jnp.stack([parity, has_x, y, source]).astype(jnp.int32), slots]
-    )
-
+    tap_room = [pltpu.VMEM((BAND, 8, LANES), F32)]
+
+    ahead = ()
     if direct:
         y_pairs = [(i, i ^ 1) for i in range(mem_count)]
         swap_y = lambda v: lax.ppermute(v, "mem", y_pairs)
         turn_z = lambda v, s: lax.ppermute(
             v, "mem", [(i, (i + 2 * s) % mem_count) for i in range(mem_count)]
         )
-        weight_y = swap_y(lax.dynamic_index_in_dim(obs_weight[0], 1 - y, 0, False))
-
-    near_core, near_x = call(
-        zonal_forward, (shape(*half_shape),) * 2, "zonal", 1 << 20,
-        table, zonal_shift, zonal_taps, control,
-        specs=(SMEM, SMEM, VMEM, VMEM), scratch=[pltpu.VMEM((BAND, 8, LANES), F32)],
-    )
-    far_core, far_x = swap_core(near_core), swap_x(near_x)
+        weight_sent = call(weight_out, piece, "weight_out", 1 << 18, obs_weight, specs=(ANY,))
+        weight_y = swap_y(weight_sent)
+        ahead = (weight_sent,)
+
+    def forward(which, after):
+        return call(
+            functools.partial(zonal_forward, which), shape(*half_shape), "zonal%d" % which,
+            1 << 19, zonal_shift, zonal_taps, control, specs=(SMEM, VMEM, VMEM),
+            scratch=tap_room, after=after,
+        )
+
+    near_x = forward(1, ahead)
+    far_x = swap_x(near_x)
+    near_core = forward(0, (near_x,))
+    far_core = swap_core(near_core)
     mixing = jnp.transpose(level_mixing, (1, 0, 2)).reshape(levels * band_rows, levels)
     matrix, transposed = call(
-        build_matrix,
+        functools.partial(build_matrix, lat_count),
         (shape(levels * band_rows, 32 * levels), shape(32 * levels, levels * band_rows)),
-        "matrix", 1 << 16, table, meridional_taps, mixing, specs=(SMEM, VMEM, VMEM),
+        "matrix", 1 << 16, meridional_taps, mixing, specs=(VMEM, VMEM), after=(near_core,),
     )
     parts = (near_core, near_x, far_core, far_x)
-    piece = shape(levels, band_rows, width)
 
     if direct:
+        ends = z_count - 1
+        raised = [(2 * i + j, 2 * i + 2 + j) for i in range(ends - 1) for j in range(2)]
+        lowered = [(2 * i + 2 + j, 2 * i + j) for i in range(1, ends) for j in range(2)]
+        mine, up, down = call(
+            weight_pick, (piece,) * 3, "weight_pick", 1 << 18, slot_owner, obs_weight, weight_y,
+            specs=(SMEM, ANY, VMEM), after=(matrix,),
+        )
+        from_low = lax.ppermute(up, "mem", raised)
+        from_high = lax.ppermute(down, "mem", lowered)
         order = (2, 1, 3)
         localized, first = call(
             functools.partial(first_body, order[0]), (shape(*field_shape), piece),
-            "first", 1 << 20, table, matrix, *parts, perturbations,
-            specs=(SMEM,) + (VMEM,) * 6,
+            "first", 1 << 20, slot_owner, matrix, *parts, perturbations,
+            specs=(SMEM,) + (VMEM,) * 6, after=(up,),
         )
         sent = {order[0]: first}
         rest = order[1:] + (0,)
         others = call(
             functools.partial(send_body, rest), (piece,) * len(rest), "send", 1 << 20,
-            table, perturbations, localized, specs=(SMEM, VMEM, VMEM),
+            slot_owner, perturbations, localized, specs=(SMEM, VMEM, VMEM),
         )
         sent.update(zip(rest, others))
         got = {s: swap_y(sent[s]) for s in order + (0,)}
-        own_weight = lax.dynamic_index_in_dim(obs_weight[0], y, 0, False)
-        up = jnp.where(owners[1] % 2 == y, own_weight, weight_y)
-        down = jnp.where(owners[3] % 2 == y, own_weight, weight_y)
-        ends = z_count - 1
-        raised = [(2 * i + j, 2 * i + 2 + j) for i in range(ends - 1) for j in range(2)]
-        lowered = [(2 * i + 2 + j, 2 * i + j) for i in range(1, ends) for j in range(2)]
-        from_low = lax.ppermute(up, "mem", raised)
-        from_high = lax.ppermute(down, "mem", lowered)
-        arrived = {}
+        arrived, before = {}, ()
         for s in order:
             total = call(
                 functools.partial(meet_body, s), piece, "meet%d" % s, 1 << 19,
-                table, perturbations, localized, got[s], specs=(SMEM,) + (VMEM,) * 3,
+                slot_owner, perturbations, localized, got[s],
+                specs=(SMEM,) + (VMEM,) * 3, after=before,
             )
             arrived[s] = turn_z(total, s)
+            before = (total,)
         grad = call(
-            last_body, piece, "last", 1 << 19, table, perturbations, localized, got[0],
-            arrived[1], arrived[2], arrived[3], obs_weight, weight_y, from_low, from_high,
-            specs=(SMEM,) + (VMEM,) * 10,
+            last_body, piece, "last", 1 << 19, slot_owner, perturbations, localized, got[0],
+            arrived[1], arrived[2], arrived[3], mine, from_low, from_high,
+            specs=(SMEM,) + (VMEM,) * 9,
         )
         own = {0: grad}
         for s in order:
@@ -398,7 +451,7 @@
                 functools.partial(spread_body, pieces, weighted is None, final),
                 (shape(*half_shape),) * 4 + (shape(*field_shape),) if final else shape(*field_shape),
                 "spread%d" % group[0][0], 1 << 19,
-                table, perturbations, *grads, *before, *extra,
+                slot_owner, perturbations, *grads, *before, *extra,
                 specs=(SMEM,) + (VMEM,) * (1 + len(grads) + len(before) + len(extra)),
             )
             weighted = result
@@ -431,11 +484,16 @@
             1 << 20, perturbations, gathered.reshape(partial.shape), transposed,
             specs=(VMEM,) * 3,
         )
-    got_core, got_x = swap_core(to_core), swap_x(to_x)
+    got_x, got_core = swap_x(to_x), swap_core(to_core)
+    half = call(
+        functools.partial(zonal_adjoint, 0), shape(*half_shape), "adjoint0", 1 << 19,
+        zonal_shift, zonal_taps, control, own_core, got_core,
+        specs=(SMEM,) + (VMEM,) * 4, scratch=tap_room,
+    )
     return call(
-        zonal_adjoint, shape(*field_shape), "zonal_adjoint", 1 << 20,
-        table, zonal_shift, zonal_taps, control, own_core, own_x, got_core, got_x,
-        specs=(SMEM, SMEM) + (VMEM,) * 6, scratch=[pltpu.VMEM((BAND, 8, LANES), F32)],
+        functools.partial(zonal_adjoint, 1), shape(*field_shape), "adjoint1", 1 << 19,
+        zonal_shift, zonal_taps, control, own_x, got_x, half,
+        specs=(SMEM,) + (VMEM,) * 5, scratch=tap_room,
     )
 
 

time: 132 us -> 115 us (0.87)
  Pallas kernels: 28 us -> 18 us
  between operations: 7.07 us -> 0.27 us
  waiting for transfers between devices: 55 us -> 58.5 us
  local copies, waits for them, and re-layouts: 11.2 us -> 9.03 us
  other arithmetic: 1.84 us -> 0 us
    pallas_call x14 -> x18, Pallas kernels: 28 us -> 18 us  [call(): pl.pallas_call(kernel, out_shape=outs, in_specs=list(specs) + [ANY] * ext...]
    ppermute x9, waiting for transfers between devices: 15.8 us -> 23.5 us  [per_device(): swap_y = lambda v: lax.ppermute(v, 'mem', y_pairs)]
    ppermute x6, waiting for transfers between devices: 33.4 us -> 31 us  [per_device(): lax.ppermute(v, 'mem', [(i, (i + 2 * s) % mem_count) for i in range(mem_c...]
    ppermute x2, waiting for transfers between devices: 5.75 us -> 3.97 us  [per_device(): swap_x = lambda v: lax.ppermute(v, 'lat', x_pairs)]
    reduce_sum x2 -> x0, other arithmetic: 1.78 us -> none  [the longest x1 0.91 us: per_device(): jnp.sum((slot_owner[None, :] < slot_owner[:, None]).astype(jnp.int32), ax...]
    squeeze x1 -> x0, local copies, waits for them, and re-layouts: 1.68 us -> none  [per_device(): weight_y = swap_y(lax.dynamic_index_in_dim(obs_weight[0], 1 - y, 0, False))]
    ppermute x2, starting transfers between devices: 6.37 us -> 4.93 us  [per_device(): swap_x = lambda v: lax.ppermute(v, 'lat', x_pairs)]
    unnamed x28 -> x30, local copies, waits for them, and re-layouts: 8 us -> 8.24 us
  transfers between devices with their start and end apart: 21 -> 21, of which waited for: 10 -> 11; matrix products, arithmetic and copies ran while one was open for 2% -> 1% of each run, Pallas kernels for 6% -> 10%
where the time goes in v2:
time: 115 us; the launch traced here: 114 us
  waiting for transfers between devices  58.5 us (51%)
  starting transfers between devices  28.4 us (25%)
  Pallas kernels  18 us (16%)
  local copies, waits for them, and re-layouts  9.03 us (8%)
    ppermute x6, waiting for transfers between devices, per_device(): lax.ppermute(v, 'mem', [(i, (i + 2 * s) % mem_count) for i in range(mem_c...  31 us
    ppermute x9, waiting for transfers between devices, per_device(): swap_y = lambda v: lax.ppermute(v, 'mem', y_pairs)  23.5 us
    pallas_call x18, Pallas kernels, call(): pl.pallas_call(kernel, out_shape=outs, in_specs=list(specs) + [ANY] * ext...  18 us
    ppermute x6, starting transfers between devices, per_device(): lax.ppermute(v, 'mem', [(i, (i + 2 * s) % mem_count) for i in range(mem_c...  10 us
    unnamed x30, local copies, waits for them, and re-layouts  8.24 us
    ppermute x9, starting transfers between devices, per_device(): swap_y = lambda v: lax.ppermute(v, 'mem', y_pairs)  7.23 us
    ppermute x2, starting transfers between devices, per_device(): swap_x = lambda v: lax.ppermute(v, 'lat', x_pairs)  4.93 us
    ppermute x2, waiting for transfers between devices, per_device(): swap_x = lambda v: lax.ppermute(v, 'lat', x_pairs)  3.97 us
  transfers between devices with their start and end apart: 21, of which 11 were waited for; matrix products, arithmetic and copies ran while one was open for 1% of the time, Pallas kernels for 10%

profile of v2, /device:TPU:1, one launch (start us, length us, event | category | flops | bytes accessed | tf_op | source)
XLA Modules:
  0.0 114.1 jit_solution(5961682331541717346)
XLA Ops:
  0.0 1.0 copy-done.4
  1.1 2.1 %collective-permute-start.2 = (f32[4,16,1024]{2,1,0:T(8,128)S(1)}, f32[4,16,1024]{2,1,0:T(8,128)}, u32[]{:S(2)}, u32[]{:S(2)}) collective-permute-start(f32[4,16,1024]{2,1,0:T(8,128)S(1)} %weight_out.1.refs_3_), channel_id=1, source_target_pairs={{0,4},{4,0},{8,12},{12,8},{16,20},{20,16},{24,28},{28,24},{1,5},{5... | collective-permute-start | bytes 786440 | tf_op jit(solution)/shard_map/ppermute | solution.py:373
  3.2 1.0 copy-done.1
  4.2 0.7 copy-done.6
  4.9 0.7 copy-done.12
  5.6 1.8 %zonal1.1.refs_3_ = f32[2,4,8,1024]{3,2,1,0:T(8,128)S(1)} custom-call(s32[16]{0:T(128)S(1)} %copy-done.12, f32[16,17]{1,0:T(8,128)S(1)} %copy-done.6, f32[2,4,16,1024]{3,2,1,0:T(8,128)S(1)} %copy-done.1, f32[4,16,1024]{2,1,0:T(8,128)S(1)} %weight_out.1.refs_3_), custom_call_target="tpu_custom_call" | custom-call | flops 524288 | bytes 524288 | tf_op jit(solution)/shard_map/zonal1/pallas_call | solution.py:28
  7.4 1.0 copy-done.2
  8.5 0.7 copy-done.7
  9.2 0.7 copy-done.13
  9.8 1.8 %zonal0.1.refs_2_ = f32[2,4,8,1024]{3,2,1,0:T(8,128)S(1)} custom-call(s32[16]{0:T(128)S(1)} %copy-done.13, f32[16,17]{1,0:T(8,128)S(1)} %copy-done.7, f32[2,4,16,1024]{3,2,1,0:T(8,128)S(1)} %copy-done.2, f32[2,4,8,1024]{3,2,1,0:T(8,128)S(1)} %zonal1.1.refs_3_), custom_call_target="tpu_custom_call" | custom-call | flops 524288 | bytes 524288 | tf_op jit(solution)/shard_map/zonal0/pallas_call | solution.py:28
  11.6 1.0 collective-permute-start
  12.6 3.0 %collective-permute-start.1 = (f32[2,4,8,1024]{3,2,1,0:T(8,128)S(1)}, f32[2,4,8,1024]{3,2,1,0:T(8,128)S(1)}, u32[]{:S(2)}, u32[]{:S(2)}) collective-permute-start(f32[2,4,8,1024]{3,2,1,0:T(8,128)S(1)} %zonal1.1.refs_3_), channel_id=1, source_target_pairs={{1,2},{2,1},{5,6},{6,5},{9,10},{10,9},{13,14},{14,13},{17,18},{18,... | collective-permute-start | bytes 786440 | tf_op jit(solution)/shard_map/ppermute | solution.py:367
  15.7 0.8 copy.9
  16.5 0.7 copy-done.11
  17.2 0.2 matrix.1
  17.4 0.0 copy-start.5
  17.4 1.0 copy-done.5
  18.5 0.7 copy-done.9
  19.1 1.1 weight_pick.1
  20.2 0.1 collective-permute-done.1.refs_5_
  20.3 0.9 first.1
  21.3 0.0 copy-start.10
  21.3 0.3 collective-permute-start.5
  21.5 0.8 send.1
  22.3 1.3 %collective-permute-start.4 = (f32[4,16,1024]{2,1,0:T(8,128)S(1)}, f32[4,16,1024]{2,1,0:T(8,128)S(1)}, u32[]{:S(2)}, u32[]{:S(2)}) collective-permute-start(f32[4,16,1024]{2,1,0:T(8,128)S(1)} %get-tuple-element.23), channel_id=1, source_target_pairs={{0,4},{4,0},{8,12},{12,8},{16,20},{20,16},{24,28},{28,24},{1,5},{5... | collective-permute-start | bytes 786440 | tf_op jit(solution)/shard_map/ppermute | solution.py:373
  23.6 0.2 collective-permute-start.8
  23.8 1.3 %collective-permute-start.3 = (f32[4,16,1024]{2,1,0:T(8,128)S(1)}, f32[4,16,1024]{2,1,0:T(8,128)S(1)}, u32[]{:S(2)}, u32[]{:S(2)}) collective-permute-start(f32[4,16,1024]{2,1,0:T(8,128)S(1)} %get-tuple-element.22), channel_id=1, source_target_pairs={{0,4},{4,0},{8,12},{12,8},{16,20},{20,16},{24,28},{28,24},{1,5},{5... | collective-permute-start | bytes 786440 | tf_op jit(solution)/shard_map/ppermute | solution.py:373
  25.1 3.2 %collective-permute-start.10 = (f32[4,16,1024]{2,1,0:T(8,128)S(1)}, f32[4,16,1024]{2,1,0:T(8,128)S(1)}, u32[]{:S(2)}, u32[]{:S(2)}) collective-permute-start(f32[4,16,1024]{2,1,0:T(8,128)S(1)} %get-tuple-element.20.refs_7_), channel_id=1, source_target_pairs={{0,8},{4,12},{8,16},{12,20},{1,9},{5,13},{9,17},{13,21},{2,10},{6,... | collective-permute-start | bytes 786440 | tf_op jit(solution)/shard_map/ppermute | solution.py:408
  28.3 1.4 %collective-permute-done.5.refs_3_ = f32[4,16,1024]{2,1,0:T(8,128)S(1)} collective-permute-done((f32[4,16,1024]{2,1,0:T(8,128)S(1)}, f32[4,16,1024]{2,1,0:T(8,128)S(1)}, u32[]{:S(2)}, u32[]{:S(2)}) %collective-permute-start.5) | collective-permute-done | bytes 262176 | tf_op jit(solution)/shard_map/ppermute | solution.py:373
  29.7 0.7 collective-permute-start.11
  30.4 0.6 meet2.1.refs_4_
  31.0 4.3 %collective-permute-done.4.refs_3_ = f32[4,16,1024]{2,1,0:T(8,128)S(1)} collective-permute-done((f32[4,16,1024]{2,1,0:T(8,128)S(1)}, f32[4,16,1024]{2,1,0:T(8,128)S(1)}, u32[]{:S(2)}, u32[]{:S(2)}) %collective-permute-start.4) | collective-permute-done | bytes 262176 | tf_op jit(solution)/shard_map/ppermute | solution.py:373
  35.3 0.6 meet1.1.refs_4_
  36.0 1.4 %collective-permute-start.6 = (f32[4,16,1024]{2,1,0:T(8,128)S(1)}, f32[4,16,1024]{2,1,0:T(8,128)S(1)}, u32[]{:S(2)}, u32[]{:S(2)}) collective-permute-start(f32[4,16,1024]{2,1,0:T(8,128)S(1)} %meet1.1.refs_4_), channel_id=1, source_target_pairs={{0,8},{4,12},{8,16},{12,20},{16,24},{20,28},{24,0},{28,4},{1,9},{5... | collective-permute-start | bytes 786440 | tf_op jit(solution)/shard_map/ppermute | solution.py:374
  37.3 3.6 %collective-permute-done.8.refs_3_ = f32[4,16,1024]{2,1,0:T(8,128)S(1)} collective-permute-done((f32[4,16,1024]{2,1,0:T(8,128)S(1)}, f32[4,16,1024]{2,1,0:T(8,128)S(1)}, u32[]{:S(2)}, u32[]{:S(2)}) %collective-permute-start.8) | collective-permute-done | bytes 262176 | tf_op jit(solution)/shard_map/ppermute | solution.py:373
  41.0 0.6 meet3.1
  41.6 3.4 %collective-permute-start.9 = (f32[4,16,1024]{2,1,0:T(8,128)S(1)}, f32[4,16,1024]{2,1,0:T(8,128)S(1)}, u32[]{:S(2)}, u32[]{:S(2)}) collective-permute-start(f32[4,16,1024]{2,1,0:T(8,128)S(1)} %meet3.1), channel_id=1, source_target_pairs={{0,24},{4,28},{8,0},{12,4},{16,8},{20,12},{24,16},{28,20},{1,25},{... | collective-permute-start | bytes 786440 | tf_op jit(solution)/shard_map/ppermute | solution.py:374
  45.0 1.9 %collective-permute-start.7 = (f32[4,16,1024]{2,1,0:T(8,128)S(1)}, f32[4,16,1024]{2,1,0:T(8,128)S(1)}, u32[]{:S(2)}, u32[]{:S(2)}) collective-permute-start(f32[4,16,1024]{2,1,0:T(8,128)S(1)} %meet2.1.refs_4_), channel_id=1, source_target_pairs={{0,16},{4,20},{8,24},{12,28},{16,0},{20,4},{24,8},{28,12},{1,17},{... | collective-permute-start | bytes 786440 | tf_op jit(solution)/shard_map/ppermute | solution.py:374
  46.9 3.6 %collective-permute-done.9.refs_6_ = f32[4,16,1024]{2,1,0:T(8,128)S(1)} collective-permute-done((f32[4,16,1024]{2,1,0:T(8,128)S(1)}, f32[4,16,1024]{2,1,0:T(8,128)S(1)}, u32[]{:S(2)}, u32[]{:S(2)}) %collective-permute-start.9) | collective-permute-done | bytes 262176 | tf_op jit(solution)/shard_map/ppermute | solution.py:374
  50.5 10.8 %collective-permute-done.7.refs_5_ = f32[4,16,1024]{2,1,0:T(8,128)S(1)} collective-permute-done((f32[4,16,1024]{2,1,0:T(8,128)S(1)}, f32[4,16,1024]{2,1,0:T(8,128)S(1)}, u32[]{:S(2)}, u32[]{:S(2)}) %collective-permute-start.7) | collective-permute-done | bytes 262176 | tf_op jit(solution)/shard_map/ppermute | solution.py:374
  61.3 0.7 last.1.refs_2_
  62.0 0.1 collective-permute-start.16
  62.1 2.4 %collective-permute-start.14 = (f32[4,16,1024]{2,1,0:T(8,128)S(1)}, f32[4,16,1024]{2,1,0:T(8,128)S(1)}, u32[]{:S(2)}, u32[]{:S(2)}) collective-permute-start(f32[4,16,1024]{2,1,0:T(8,128)S(1)} %last.1.refs_2_), channel_id=1, source_target_pairs={{0,8},{4,12},{8,16},{12,20},{16,24},{20,28},{24,0},{28,4},{1,9},{5... | collective-permute-start | bytes 786440 | tf_op jit(solution)/shard_map/ppermute | solution.py:374
  64.5 1.0 collective-permute-start.12
  65.4 0.3 collective-permute-start.18
  65.7 16.6 %collective-permute-done.16.refs_3_ = f32[4,16,1024]{2,1,0:T(8,128)S(1)} collective-permute-done((f32[4,16,1024]{2,1,0:T(8,128)S(1)}, f32[4,16,1024]{2,1,0:T(8,128)S(1)}, u32[]{:S(2)}, u32[]{:S(2)}) %collective-permute-start.16) | collective-permute-done | bytes 262176 | tf_op jit(solution)/shard_map/ppermute | solution.py:374
  82.3 0.3 collective-permute-start.17
  82.6 1.2 %collective-permute-start.15 = (f32[4,16,1024]{2,1,0:T(8,128)S(1)}, f32[4,16,1024]{2,1,0:T(8,128)S(1)}, u32[]{:S(2)}, u32[]{:S(2)}) collective-permute-start(f32[4,16,1024]{2,1,0:T(8,128)S(1)} %collective-permute-done.14.refs_2_), channel_id=1, source_target_pairs={{0,4},{4,0},{8,12},{12,8},{16,20},{20,16},{24,28},{28,24},{1,5},{5... | collective-permute-start | bytes 786440 | tf_op jit(solution)/shard_map/ppermute | solution.py:373
  83.8 0.3 collective-permute-start.13
  84.0 0.6 spread0.2.refs_4_
  84.7 0.7 spread0.3.refs_4_
  85.4 4.4 %collective-permute-done.17.refs_3_ = f32[4,16,1024]{2,1,0:T(8,128)S(1)} collective-permute-done((f32[4,16,1024]{2,1,0:T(8,128)S(1)}, f32[4,16,1024]{2,1,0:T(8,128)S(1)}, u32[]{:S(2)}, u32[]{:S(2)}) %collective-permute-start.17) | collective-permute-done | bytes 262176 | tf_op jit(solution)/shard_map/ppermute | solution.py:373
  89.7 0.7 spread1.1.refs_4_
  90.5 4.9 %collective-permute-done.15.refs_3_ = f32[4,16,1024]{2,1,0:T(8,128)S(1)} collective-permute-done((f32[4,16,1024]{2,1,0:T(8,128)S(1)}, f32[4,16,1024]{2,1,0:T(8,128)S(1)}, u32[]{:S(2)}, u32[]{:S(2)}) %collective-permute-start.15) | collective-permute-done | bytes 262176 | tf_op jit(solution)/shard_map/ppermute | solution.py:373
  95.4 0.7 spread3.2.refs_3_
  96.1 0.0 copy-start.3
  96.1 0.0 copy-start.8
  96.1 4.9 %collective-permute-done.13.refs_2_ = f32[4,16,1024]{2,1,0:T(8,128)S(1)} collective-permute-done((f32[4,16,1024]{2,1,0:T(8,128)S(1)}, f32[4,16,1024]{2,1,0:T(8,128)S(1)}, u32[]{:S(2)}, u32[]{:S(2)}) %collective-permute-start.13) | collective-permute-done | bytes 262176 | tf_op jit(solution)/shard_map/ppermute | solution.py:373
  101.0 1.7 %spread3.3 = (f32[2,4,8,1024]{3,2,1,0:T(8,128)S(1)}, f32[2,4,8,1024]{3,2,1,0:T(8,128)S(1)}, f32[2,4,8,1024]{3,2,1,0:T(8,128)S(1)}, f32[2,4,8,1024]{3,2,1,0:T(8,128)S(1)}, f32[2,4,16,1024]{3,2,1,0:T(8,128)}) custom-call(s32[4]{0:T(128)S(1)} %copy-done.10, bf16[4,2,2,4,16,1024]{5,4,3,2,1,0:T(8,128)(2,1)S(1)} %copy-done, ...), custom_call_target="tpu_custom_call" | custom-call | flops 524288 | bytes 524288 | tf_op jit(solution)/shard_map/spread3/pallas_call | solution.py:28
  102.6 1.3 %collective-permute-start.20 = (f32[2,4,8,1024]{3,2,1,0:T(8,128)S(1)}, f32[2,4,8,1024]{3,2,1,0:T(8,128)S(1)}, u32[]{:S(2)}, u32[]{:S(2)}) collective-permute-start(f32[2,4,8,1024]{3,2,1,0:T(8,128)S(1)} %get-tuple-element.32), channel_id=1, source_target_pairs={{0,1},{1,0},{2,3},{3,2},{4,5},{5,4},{6,7},{7,6},{8,9},{9,8},{10,11... | collective-permute-start | bytes 786440 | tf_op jit(solution)/shard_map/ppermute | solution.py:366
  103.9 1.9 %collective-permute-start.19 = (f32[2,4,8,1024]{3,2,1,0:T(8,128)S(1)}, f32[2,4,8,1024]{3,2,1,0:T(8,128)S(1)}, u32[]{:S(2)}, u32[]{:S(2)}) collective-permute-start(f32[2,4,8,1024]{3,2,1,0:T(8,128)S(1)} %get-tuple-element.30), channel_id=1, source_target_pairs={{1,2},{2,1},{5,6},{6,5},{9,10},{10,9},{13,14},{14,13},{17,18},{18,... | collective-permute-start | bytes 786440 | tf_op jit(solution)/shard_map/ppermute | solution.py:367
  105.9 1.8 %adjoint0.1.refs_5_ = f32[2,4,8,1024]{3,2,1,0:T(8,128)S(1)} custom-call(s32[16]{0:T(128)S(1)} %copy-done.14, f32[16,17]{1,0:T(8,128)S(1)} %copy-done.8, f32[2,4,16,1024]{3,2,1,0:T(8,128)S(1)} %copy-done.3, f32[2,4,8,1024]{3,2,1,0:T(8,128)S(1)} %get-tuple-element.31.refs_3_, f32[2,4,8,1024]{3,2,1,0:T(8,128)S(1)} %collective-permute-done.20.refs_4_), custom_call_target="tpu_custom_call" | custom-call | flops 524288 | bytes 524288 | tf_op jit(solution)/shard_map/adjoint0/pallas_call | solution.py:28
  107.7 3.9 %collective-permute-done.19.refs_4_ = f32[2,4,8,1024]{3,2,1,0:T(8,128)S(1)} collective-permute-done((f32[2,4,8,1024]{3,2,1,0:T(8,128)S(1)}, f32[2,4,8,1024]{3,2,1,0:T(8,128)S(1)}, u32[]{:S(2)}, u32[]{:S(2)}) %collective-permute-start.19) | collective-permute-done | bytes 262176 | tf_op jit(solution)/shard_map/ppermute | solution.py:367
  111.6 2.5 %adjoint1.1 = f32[2,4,16,1024]{3,2,1,0:T(8,128)} custom-call(s32[16]{0:T(128)S(1)} %copy-done.14, f32[16,17]{1,0:T(8,128)S(1)} %copy-done.8, f32[2,4,16,1024]{3,2,1,0:T(8,128)S(1)} %copy-done.3, f32[2,4,8,1024]{3,2,1,0:T(8,128)S(1)} %get-tuple-element.29.refs_3_, f32[2,4,8,1024]{3,2,1,0:T(8,128)S(1)} %collective-permute-done.19.refs_4_, ...), custom_call_target="tpu_custom_call" | custom-call | flops 524288 | bytes 524288 | tf_op jit(solution)/shard_map/adjoint1/pallas_call | solution.py:28
  (27 shorter events, 0.1 us)
Async XLA Ops:
  0.0 1.0 copy-start.4
  1.0 19.3 %copy-start = (bf16[4,2,2,4,16,1024]{5,4,3,2,1,0:T(8,128)(2,1)S(1)}, bf16[4,2,2,4,16,1024]{5,4,3,2,1,0:T(8,128)(2,1)}, u32[]{:S(2)}) copy-start(bf16[4,2,2,4,16,1024]{5,4,3,2,1,0:T(8,128)(2,1)} %refs_1_.27) | copy-start | bytes 6291460
  1.1 16.4 %collective-permute-start.2 = (f32[4,16,1024]{2,1,0:T(8,128)S(1)}, f32[4,16,1024]{2,1,0:T(8,128)}, u32[]{:S(2)}, u32[]{:S(2)}) collective-permute-start(f32[4,16,1024]{2,1,0:T(8,128)S(1)} %weight_out.1.refs_3_), channel_id=1, source_target_pairs={{0,4},{4,0},{8,12},{12,8},{16,20},{20,16},{24,28},{28,24},{1,5},{5... | collective-permute-start | bytes 786440 | tf_op jit(solution)/shard_map/ppermute | solution.py:373
  3.2 1.0 copy-start.1
  4.2 0.7 copy-start.6
  4.9 0.7 copy-start.12
  7.4 1.0 copy-start.2
  8.5 0.7 copy-start.7
  9.2 0.7 copy-start.13
  11.6 8.6 %collective-permute-start = (f32[2,4,8,1024]{3,2,1,0:T(8,128)S(1)}, f32[2,4,8,1024]{3,2,1,0:T(8,128)S(1)}, u32[]{:S(2)}, u32[]{:S(2)}) collective-permute-start(f32[2,4,8,1024]{3,2,1,0:T(8,128)S(1)} %zonal0.1.refs_2_), channel_id=1, source_target_pairs={{0,1},{1,0},{2,3},{3,2},{4,5},{5,4},{6,7},{7,6},{8,9},{9,8},{10,11... | collective-permute-start | bytes 786440 | tf_op jit(solution)/shard_map/ppermute | solution.py:366
  12.6 7.7 %collective-permute-start.1 = (f32[2,4,8,1024]{3,2,1,0:T(8,128)S(1)}, f32[2,4,8,1024]{3,2,1,0:T(8,128)S(1)}, u32[]{:S(2)}, u32[]{:S(2)}) collective-permute-start(f32[2,4,8,1024]{3,2,1,0:T(8,128)S(1)} %zonal1.1.refs_3_), channel_id=1, source_target_pairs={{1,2},{2,1},{5,6},{6,5},{9,10},{10,9},{13,14},{14,13},{17,18},{18,... | collective-permute-start | bytes 786440 | tf_op jit(solution)/shard_map/ppermute | solution.py:367
  16.5 0.7 copy-start.11
  17.4 1.0 copy-start.5
  18.5 0.7 copy-start.9
  21.3 9.1 %copy-start.10 = (s32[4]{0:T(128)S(1)}, s32[4]{0:T(128)}, u32[]{:S(2)}) copy-start(s32[4]{0:T(128)} %refs_0_.33) | copy-start | bytes 52
  21.3 8.5 %collective-permute-start.5 = (f32[4,16,1024]{2,1,0:T(8,128)S(1)}, f32[4,16,1024]{2,1,0:T(8,128)S(1)}, u32[]{:S(2)}, u32[]{:S(2)}) collective-permute-start(f32[4,16,1024]{2,1,0:T(8,128)S(1)} %get-tuple-element.24), channel_id=1, source_target_pairs={{0,4},{4,0},{8,12},{12,8},{16,20},{20,16},{24,28},{28,24},{1,5},{5... | collective-permute-start | bytes 786440 | tf_op jit(solution)/shard_map/ppermute | solution.py:373
  22.3 13.0 %collective-permute-start.4 = (f32[4,16,1024]{2,1,0:T(8,128)S(1)}, f32[4,16,1024]{2,1,0:T(8,128)S(1)}, u32[]{:S(2)}, u32[]{:S(2)}) collective-permute-start(f32[4,16,1024]{2,1,0:T(8,128)S(1)} %get-tuple-element.23), channel_id=1, source_target_pairs={{0,4},{4,0},{8,12},{12,8},{16,20},{20,16},{24,28},{28,24},{1,5},{5... | collective-permute-start | bytes 786440 | tf_op jit(solution)/shard_map/ppermute | solution.py:373
  23.6 17.3 %collective-permute-start.8 = (f32[4,16,1024]{2,1,0:T(8,128)S(1)}, f32[4,16,1024]{2,1,0:T(8,128)S(1)}, u32[]{:S(2)}, u32[]{:S(2)}) collective-permute-start(f32[4,16,1024]{2,1,0:T(8,128)S(1)} %get-tuple-element.25), channel_id=1, source_target_pairs={{0,4},{4,0},{8,12},{12,8},{16,20},{20,16},{24,28},{28,24},{1,5},{5... | collective-permute-start | bytes 786440 | tf_op jit(solution)/shard_map/ppermute | solution.py:373
  23.8 21.1 %collective-permute-start.3 = (f32[4,16,1024]{2,1,0:T(8,128)S(1)}, f32[4,16,1024]{2,1,0:T(8,128)S(1)}, u32[]{:S(2)}, u32[]{:S(2)}) collective-permute-start(f32[4,16,1024]{2,1,0:T(8,128)S(1)} %get-tuple-element.22), channel_id=1, source_target_pairs={{0,4},{4,0},{8,12},{12,8},{16,20},{20,16},{24,28},{28,24},{1,5},{5... | collective-permute-start | bytes 786440 | tf_op jit(solution)/shard_map/ppermute | solution.py:373
  25.1 21.8 %collective-permute-start.10 = (f32[4,16,1024]{2,1,0:T(8,128)S(1)}, f32[4,16,1024]{2,1,0:T(8,128)S(1)}, u32[]{:S(2)}, u32[]{:S(2)}) collective-permute-start(f32[4,16,1024]{2,1,0:T(8,128)S(1)} %get-tuple-element.20.refs_7_), channel_id=1, source_target_pairs={{0,8},{4,12},{8,16},{12,20},{1,9},{5,13},{9,17},{13,21},{2,10},{6,... | collective-permute-start | bytes 786440 | tf_op jit(solution)/shard_map/ppermute | solution.py:408
  29.7 17.2 %collective-permute-start.11 = (f32[4,16,1024]{2,1,0:T(8,128)S(1)}, f32[4,16,1024]{2,1,0:T(8,128)S(1)}, u32[]{:S(2)}, u32[]{:S(2)}) collective-permute-start(f32[4,16,1024]{2,1,0:T(8,128)S(1)} %get-tuple-element.27), channel_id=1, source_target_pairs={{16,8},{20,12},{24,16},{28,20},{17,9},{21,13},{25,17},{29,21},{18,... | collective-permute-start | bytes 786440 | tf_op jit(solution)/shard_map/ppermute | solution.py:409
  36.0 14.6 %collective-permute-start.6 = (f32[4,16,1024]{2,1,0:T(8,128)S(1)}, f32[4,16,1024]{2,1,0:T(8,128)S(1)}, u32[]{:S(2)}, u32[]{:S(2)}) collective-permute-start(f32[4,16,1024]{2,1,0:T(8,128)S(1)} %meet1.1.refs_4_), channel_id=1, source_target_pairs={{0,8},{4,12},{8,16},{12,20},{16,24},{20,28},{24,0},{28,4},{1,9},{5... | collective-permute-start | bytes 786440 | tf_op jit(solution)/shard_map/ppermute | solution.py:374
  41.6 8.9 %collective-permute-start.9 = (f32[4,16,1024]{2,1,0:T(8,128)S(1)}, f32[4,16,1024]{2,1,0:T(8,128)S(1)}, u32[]{:S(2)}, u32[]{:S(2)}) collective-permute-start(f32[4,16,1024]{2,1,0:T(8,128)S(1)} %meet3.1), channel_id=1, source_target_pairs={{0,24},{4,28},{8,0},{12,4},{16,8},{20,12},{24,16},{28,20},{1,25},{... | collective-permute-start | bytes 786440 | tf_op jit(solution)/shard_map/ppermute | solution.py:374
  45.0 16.4 %collective-permute-start.7 = (f32[4,16,1024]{2,1,0:T(8,128)S(1)}, f32[4,16,1024]{2,1,0:T(8,128)S(1)}, u32[]{:S(2)}, u32[]{:S(2)}) collective-permute-start(f32[4,16,1024]{2,1,0:T(8,128)S(1)} %meet2.1.refs_4_), channel_id=1, source_target_pairs={{0,16},{4,20},{8,24},{12,28},{16,0},{20,4},{24,8},{28,12},{1,17},{... | collective-permute-start | bytes 786440 | tf_op jit(solution)/shard_map/ppermute | solution.py:374
  62.0 20.3 %collective-permute-start.16 = (f32[4,16,1024]{2,1,0:T(8,128)S(1)}, f32[4,16,1024]{2,1,0:T(8,128)S(1)}, u32[]{:S(2)}, u32[]{:S(2)}) collective-permute-start(f32[4,16,1024]{2,1,0:T(8,128)S(1)} %last.1.refs_2_), channel_id=1, source_target_pairs={{0,16},{4,20},{8,24},{12,28},{16,0},{20,4},{24,8},{28,12},{1,17},{... | collective-permute-start | bytes 786440 | tf_op jit(solution)/shard_map/ppermute | solution.py:374
  62.1 20.5 %collective-permute-start.14 = (f32[4,16,1024]{2,1,0:T(8,128)S(1)}, f32[4,16,1024]{2,1,0:T(8,128)S(1)}, u32[]{:S(2)}, u32[]{:S(2)}) collective-permute-start(f32[4,16,1024]{2,1,0:T(8,128)S(1)} %last.1.refs_2_), channel_id=1, source_target_pairs={{0,8},{4,12},{8,16},{12,20},{16,24},{20,28},{24,0},{28,4},{1,9},{5... | collective-permute-start | bytes 786440 | tf_op jit(solution)/shard_map/ppermute | solution.py:374
  64.5 19.3 %collective-permute-start.12 = (f32[4,16,1024]{2,1,0:T(8,128)S(1)}, f32[4,16,1024]{2,1,0:T(8,128)S(1)}, u32[]{:S(2)}, u32[]{:S(2)}) collective-permute-start(f32[4,16,1024]{2,1,0:T(8,128)S(1)} %last.1.refs_2_), channel_id=1, source_target_pairs={{0,24},{4,28},{8,0},{12,4},{16,8},{20,12},{24,16},{28,20},{1,25},{... | collective-permute-start | bytes 786440 | tf_op jit(solution)/shard_map/ppermute | solution.py:374
  65.4 19.3 %collective-permute-start.18 = (f32[4,16,1024]{2,1,0:T(8,128)S(1)}, f32[4,16,1024]{2,1,0:T(8,128)S(1)}, u32[]{:S(2)}, u32[]{:S(2)}) collective-permute-start(f32[4,16,1024]{2,1,0:T(8,128)S(1)} %last.1.refs_2_), channel_id=1, source_target_pairs={{0,4},{4,0},{8,12},{12,8},{16,20},{20,16},{24,28},{28,24},{1,5},{5... | collective-permute-start | bytes 786440 | tf_op jit(solution)/shard_map/ppermute | solution.py:373
  82.3 7.4 %collective-permute-start.17 = (f32[4,16,1024]{2,1,0:T(8,128)S(1)}, f32[4,16,1024]{2,1,0:T(8,128)S(1)}, u32[]{:S(2)}, u32[]{:S(2)}) collective-permute-start(f32[4,16,1024]{2,1,0:T(8,128)S(1)} %collective-permute-done.16.refs_3_), channel_id=1, source_target_pairs={{0,4},{4,0},{8,12},{12,8},{16,20},{20,16},{24,28},{28,24},{1,5},{5... | collective-permute-start | bytes 786440 | tf_op jit(solution)/shard_map/ppermute | solution.py:373
  82.6 12.8 %collective-permute-start.15 = (f32[4,16,1024]{2,1,0:T(8,128)S(1)}, f32[4,16,1024]{2,1,0:T(8,128)S(1)}, u32[]{:S(2)}, u32[]{:S(2)}) collective-permute-start(f32[4,16,1024]{2,1,0:T(8,128)S(1)} %collective-permute-done.14.refs_2_), channel_id=1, source_target_pairs={{0,4},{4,0},{8,12},{12,8},{16,20},{20,16},{24,28},{28,24},{1,5},{5... | collective-permute-start | bytes 786440 | tf_op jit(solution)/shard_map/ppermute | solution.py:373
  83.8 17.2 %collective-permute-start.13 = (f32[4,16,1024]{2,1,0:T(8,128)S(1)}, f32[4,16,1024]{2,1,0:T(8,128)S(1)}, u32[]{:S(2)}, u32[]{:S(2)}) collective-permute-start(f32[4,16,1024]{2,1,0:T(8,128)S(1)} %collective-permute-done.12.refs_2_), channel_id=1, source_target_pairs={{0,4},{4,0},{8,12},{12,8},{16,20},{20,16},{24,28},{28,24},{1,5},{5... | collective-permute-start | bytes 786440 | tf_op jit(solution)/shard_map/ppermute | solution.py:373
  96.1 9.8 %copy-start.3 = (f32[2,4,16,1024]{3,2,1,0:T(8,128)S(1)}, f32[2,4,16,1024]{3,2,1,0:T(8,128)}, u32[]{:S(2)}) copy-start(f32[2,4,16,1024]{3,2,1,0:T(8,128)} %refs_2_.7) | copy-start | bytes 1572868
  96.1 9.8 %copy-start.8 = (f32[16,17]{1,0:T(8,128)S(1)}, f32[16,17]{1,0:T(8,128)}, u32[]{:S(2)}) copy-start(f32[16,17]{1,0:T(8,128)} %refs_1_.29) | copy-start | bytes 3268
  96.1 9.8 %copy-start.14 = (s32[16]{0:T(128)S(1)}, s32[16]{0:T(128)}, u32[]{:S(2)}) copy-start(s32[16]{0:T(128)} %refs_0_.35) | copy-start | bytes 196
  102.6 3.2 %collective-permute-start.20 = (f32[2,4,8,1024]{3,2,1,0:T(8,128)S(1)}, f32[2,4,8,1024]{3,2,1,0:T(8,128)S(1)}, u32[]{:S(2)}, u32[]{:S(2)}) collective-permute-start(f32[2,4,8,1024]{3,2,1,0:T(8,128)S(1)} %get-tuple-element.32), channel_id=1, source_target_pairs={{0,1},{1,0},{2,3},{3,2},{4,5},{5,4},{6,7},{7,6},{8,9},{9,8},{10,11... | collective-permute-start | bytes 786440 | tf_op jit(solution)/shard_map/ppermute | solution.py:366
  103.9 7.7 %collective-permute-start.19 = (f32[2,4,8,1024]{3,2,1,0:T(8,128)S(1)}, f32[2,4,8,1024]{3,2,1,0:T(8,128)S(1)}, u32[]{:S(2)}, u32[]{:S(2)}) collective-permute-start(f32[2,4,8,1024]{3,2,1,0:T(8,128)S(1)} %get-tuple-element.30), channel_id=1, source_target_pairs={{1,2},{2,1},{5,6},{6,5},{9,10},{10,9},{13,14},{14,13},{17,18},{18,... | collective-permute-start | bytes 786440 | tf_op jit(solution)/shard_map/ppermute | solution.py:367

commit v3 on v2

--- a/solution.py
+++ b/solution.py
@@ -17,6 +17,7 @@
 VMEM = pl.BlockSpec(memory_space=pltpu.VMEM)
 SMEM = pl.BlockSpec(memory_space=pltpu.SMEM)
 ANY = pl.BlockSpec(memory_space=pl.ANY)
+HBM = pl.BlockSpec(memory_space=pltpu.HBM)
 
 
 def call(body, outs, name, cost, *operands, specs, scratch=(), after=()):
@@ -108,18 +109,18 @@
     return total
 
 
-def row_shifts(shift_ref, first):
+def row_shifts(shifts, first):
     row = lax.broadcasted_iota(jnp.int32, (8, LANES), 0)
     amounts = jnp.zeros((8, LANES), jnp.int32)
     for r in range(8):
-        amounts = jnp.where(row == r, shift_ref[first + r], amounts)
+        amounts = jnp.where(row == r, shifts[first + r], amounts)
     return amounts
 
 
-def spread_taps(taps_ref, first, tap_ref):
-    block = taps_ref[pl.ds(first, 8), :]
+def spread_taps(taps, first, spread):
+    block = taps[pl.ds(first, 8), :]
     for k in range(BAND):
-        tap_ref[k] = jnp.broadcast_to(block[:, k : k + 1], (8, LANES))
+        spread[k] = jnp.broadcast_to(block[:, k : k + 1], (8, LANES))
 
 
 def tiles(width):
@@ -131,16 +132,14 @@
     return pl.multiple_of((1 - odd if which == 0 else odd) * 8, 8)
 
 
-def zonal_forward(which, shift_ref, taps_ref, control, out, tap_ref):
+def zonal_forward(first, shifts, taps, control, out):
     members, levels, _, width = control.shape
-    first = half_start(which)
-    amount = (width - HALF - row_shifts(shift_ref, first)) & (width - 1)
-    spread_taps(taps_ref, first, tap_ref)
+    amount = (width - HALF - shifts[...]) & (width - 1)
 
     def step(m, carry):
         for l in range(levels):
             columns = [control[m, l, pl.ds(first, 8), cut] for cut in tiles(width)]
-            result = circle_filter(columns, amount, lambda k: tap_ref[BAND - 1 - k])
+            result = circle_filter(columns, amount, lambda k: taps[BAND - 1 - k])
             for cut, value in zip(tiles(width), result):
                 out[m, l, :, cut] = value
         return carry
@@ -148,17 +147,51 @@
     lax.fori_loop(0, members, step, 0)
 
 
-def zonal_adjoint(which, shift_ref, taps_ref, control, own, got, *refs):
-    other, out, tap_ref = (None, *refs) if which == 0 else refs
+def front_body(names, *refs):
+    r = dict(zip(names, refs))
+    sems = r["sems"]
+    first_x, first_core = half_start(1), half_start(0)
+    rows_x, rows_core = pl.ds(first_x, 8), pl.ds(first_core, 8)
+    moves = [
+        (r["shift"], r["shift_s"]),
+        (r["taps"], r["taps_v"]),
+        (r["control"].at[:, :, rows_x], r["control_v"].at[:, :, rows_x]),
+    ]
+    moves.append((r["control"].at[:, :, rows_core], r["control_v"].at[:, :, rows_core]))
+    moves.append((r["meridional"], r["meridional_v"]))
+    if "obs" in r:
+        moves.append((r["obs"].at[0], r["obs_v"]))
+    moves.append((r["ens"], r["ens_v"]))
+    copies = [pltpu.make_async_copy(a, b, sems.at[i]) for i, (a, b) in enumerate(moves)]
+    for copy in copies:
+        copy.start()
+    for copy in copies[:3]:
+        copy.wait()
+    r["shift_x"][...] = row_shifts(r["shift_s"], first_x)
+    r["shift_core"][...] = row_shifts(r["shift_s"], first_core)
+    spread_taps(r["taps_v"], first_x, r["taps_x"])
+    zonal_forward(first_x, r["shift_x"], r["taps_x"], r["control_v"], r["near_x"])
+    for copy in copies[3:]:
+        copy.wait()
+
+
+def core_body(shifts, taps_v, control, out, taps):
+    first = half_start(0)
+    spread_taps(taps_v, first, taps)
+    zonal_forward(first, shifts, taps, control, out)
+
+
+def zonal_adjoint(which, shifts, taps_v, control, own, got, *refs):
+    other, out, taps = (None, *refs) if which == 0 else refs
     members, levels, _, width = control.shape
     first = half_start(which)
-    amount = (row_shifts(shift_ref, first) - HALF) & (width - 1)
-    spread_taps(taps_ref, first, tap_ref)
+    amount = (shifts[...] - HALF) & (width - 1)
+    spread_taps(taps_v, first, taps)
 
     def step(m, carry):
         for l in range(levels):
             columns = [own[m, l, :, cut] + got[m, l, :, cut] for cut in tiles(width)]
-            result = circle_filter(columns, amount, lambda k: tap_ref[k])
+            result = circle_filter(columns, amount, lambda k: taps[k])
             for cut, value in zip(tiles(width), result):
                 total = control[m, l, pl.ds(first, 8), cut] + value
                 if which == 0:
@@ -245,32 +278,30 @@
     return total
 
 
-def weight_out(obs, out):
-    pltpu.sync_copy(obs.at[0, 1 - own_y()], out)
-
-
-def weight_pick(owners, obs, from_y, mine, up, down):
-    for step, out in ((0, mine), (1, up), (SLOTS - 1, down)):
-        held = (owner_at(owners, step) & 1) == own_y()
-
-        @pl.when(held)
-        def _(out=out):
-            pltpu.sync_copy(obs.at[0, own_y()], out)
-
-        @pl.when(jnp.logical_not(held))
-        def _(out=out):
-            out[...] = from_y[...]
-
-
-def first_body(step, owners, matrix, a, b, c, d, ens, localized, send):
+def weight_pick(owners, here, low, high, mine, across):
+    place = owner_at(owners, 0) >> 1
+    for found, weights in (
+        (place == own_z(), here), (place < own_z(), low), (place > own_z(), high)
+    ):
+
+        @pl.when(found)
+        def _(weights=weights):
+            mine[...] = weights[own_y()]
+            across[...] = weights[1 - own_y()]
+
+
+def first_body(step, owners_hbm, matrix, a, b, c, d, ens, localized, send, owners, sem):
+    copy = pltpu.make_async_copy(owners_hbm, owners, sem)
+    copy.start()
     localize(matrix, (a, b, c, d), localized)
+    copy.wait()
     slot = slot_at(owners, step)
     for l in range(localized.shape[1]):
         send[l] = increment(ens, localized, slot, 1 - own_y(), l)
 
 
-def send_body(steps, owners, ens, localized, *sends):
-    for step, send in zip(steps, sends):
+def send_body(owners, ens, localized, pair, single):
+    for step, send in ((1, pair.at[0]), (3, pair.at[1]), (0, single)):
         slot = slot_at(owners, step)
         for l in range(localized.shape[1]):
             send[l] = increment(ens, localized, slot, 1 - own_y(), l)
@@ -282,10 +313,15 @@
         out[l] = increment(ens, localized, slot, own_y(), l) + got[l]
 
 
-def last_body(owners, ens, localized, got_y, got_1, got_2, got_3, mine, from_low, from_high, out):
-    slot, place = slot_at(owners, 0), owner_at(owners, 0) >> 1
-    for code, weight in enumerate((mine, from_low, from_high)):
-        here = (place == own_z(), place < own_z(), place > own_z())[code]
+def meet_pair_body(owners, ens, localized, got, *outs):
+    for i, (step, out) in enumerate(zip((1, 3), outs)):
+        meet_body(step, owners, ens, localized, got.at[i], out)
+
+
+def last_body(owners, ens, localized, got_y, got_1, got_2, got_3, mine, from_y, out):
+    slot = slot_at(owners, 0)
+    held = (owner_at(owners, 0) & 1) == own_y()
+    for here, weight in ((held, mine), (jnp.logical_not(held), from_y)):
 
         @pl.when(here)
         def _(weight=weight):
@@ -366,83 +402,102 @@
     swap_core = lambda v: lax.ppermute(v, "lat", core_pairs)
     swap_x = lambda v: lax.ppermute(v, "lat", x_pairs)
     tap_room = [pltpu.VMEM((BAND, 8, LANES), F32)]
-
-    ahead = ()
+    ins = {
+        "shift": zonal_shift, "taps": zonal_taps, "control": control,
+        "meridional": meridional_taps, "ens": perturbations,
+    }
+    results = {
+        "near_x": shape(*half_shape), "control_v": shape(*field_shape),
+        "taps_v": shape(*zonal_taps.shape), "meridional_v": shape(*meridional_taps.shape),
+        "shift_x": shape(8, LANES, dtype=jnp.int32),
+        "shift_core": shape(8, LANES, dtype=jnp.int32),
+        "ens_v": shape(*perturbations.shape, dtype=BF16),
+    }
+    if direct:
+        ins["obs"] = obs_weight
+        results["obs_v"] = shape(*obs_weight.shape[1:])
+    names = (*ins, *results, "taps_x", "shift_s", "sems")
+    made = call(
+        functools.partial(front_body, names), tuple(results.values()), "front", 1 << 19,
+        *(pltpu.with_memory_space_constraint(v, pltpu.HBM) for v in ins.values()),
+        specs=(HBM,) * len(ins),
+        scratch=[
+            *tap_room, pltpu.SMEM(zonal_shift.shape, jnp.int32), pltpu.SemaphoreType.DMA((7,)),
+        ],
+    )
+    made = dict(zip(results, made))
+    near_x, control_v, ens = made["near_x"], made["control_v"], made["ens_v"]
+    far_x = swap_x(near_x)
     if direct:
         y_pairs = [(i, i ^ 1) for i in range(mem_count)]
         swap_y = lambda v: lax.ppermute(v, "mem", y_pairs)
         turn_z = lambda v, s: lax.ppermute(
             v, "mem", [(i, (i + 2 * s) % mem_count) for i in range(mem_count)]
         )
-        weight_sent = call(weight_out, piece, "weight_out", 1 << 18, obs_weight, specs=(ANY,))
-        weight_y = swap_y(weight_sent)
-        ahead = (weight_sent,)
-
-    def forward(which, after):
-        return call(
-            functools.partial(zonal_forward, which), shape(*half_shape), "zonal%d" % which,
-            1 << 19, zonal_shift, zonal_taps, control, specs=(SMEM, VMEM, VMEM),
-            scratch=tap_room, after=after,
-        )
-
-    near_x = forward(1, ahead)
-    far_x = swap_x(near_x)
-    near_core = forward(0, (near_x,))
+        ends = z_count - 1
+        raised = [(2 * i + j, 2 * i + 2 + j) for i in range(ends - 1) for j in range(2)]
+        lowered = [(2 * i + 2 + j, 2 * i + j) for i in range(1, ends) for j in range(2)]
+        from_low = lax.ppermute(made["obs_v"], "mem", raised)
+        from_high = lax.ppermute(made["obs_v"], "mem", lowered)
+    near_core = call(
+        core_body, shape(*half_shape), "core", 1 << 19, made["shift_core"], made["taps_v"],
+        control_v, specs=(VMEM,) * 3, scratch=tap_room,
+    )
     far_core = swap_core(near_core)
     mixing = jnp.transpose(level_mixing, (1, 0, 2)).reshape(levels * band_rows, levels)
     matrix, transposed = call(
         functools.partial(build_matrix, lat_count),
         (shape(levels * band_rows, 32 * levels), shape(32 * levels, levels * band_rows)),
-        "matrix", 1 << 16, meridional_taps, mixing, specs=(VMEM, VMEM), after=(near_core,),
+        "matrix", 1 << 16, made["meridional_v"], mixing, specs=(VMEM, VMEM), after=(near_core, far_x),
     )
     parts = (near_core, near_x, far_core, far_x)
 
     if direct:
-        ends = z_count - 1
-        raised = [(2 * i + j, 2 * i + 2 + j) for i in range(ends - 1) for j in range(2)]
-        lowered = [(2 * i + 2 + j, 2 * i + j) for i in range(1, ends) for j in range(2)]
-        mine, up, down = call(
-            weight_pick, (piece,) * 3, "weight_pick", 1 << 18, slot_owner, obs_weight, weight_y,
-            specs=(SMEM, ANY, VMEM), after=(matrix,),
-        )
-        from_low = lax.ppermute(up, "mem", raised)
-        from_high = lax.ppermute(down, "mem", lowered)
-        order = (2, 1, 3)
         localized, first = call(
-            functools.partial(first_body, order[0]), (shape(*field_shape), piece),
-            "first", 1 << 20, slot_owner, matrix, *parts, perturbations,
-            specs=(SMEM,) + (VMEM,) * 6, after=(up,),
-        )
-        sent = {order[0]: first}
-        rest = order[1:] + (0,)
-        others = call(
-            functools.partial(send_body, rest), (piece,) * len(rest), "send", 1 << 20,
-            slot_owner, perturbations, localized, specs=(SMEM, VMEM, VMEM),
-        )
-        sent.update(zip(rest, others))
-        got = {s: swap_y(sent[s]) for s in order + (0,)}
-        arrived, before = {}, ()
-        for s in order:
-            total = call(
-                functools.partial(meet_body, s), piece, "meet%d" % s, 1 << 19,
-                slot_owner, perturbations, localized, got[s],
-                specs=(SMEM,) + (VMEM,) * 3, after=before,
-            )
-            arrived[s] = turn_z(total, s)
-            before = (total,)
+            functools.partial(first_body, 2), (shape(*field_shape), piece),
+            "first", 1 << 20, slot_owner, matrix, *parts, ens,
+            specs=(HBM,) + (VMEM,) * 6,
+            scratch=[pltpu.SMEM((SLOTS,), jnp.int32), pltpu.SemaphoreType.DMA],
+        )
+        got_two = swap_y(first)
+        pair, single = call(
+            send_body, (shape(2, levels, band_rows, width), piece), "send", 1 << 20,
+            slot_owner, ens, localized, specs=(SMEM, VMEM, VMEM), after=(from_low, from_high),
+        )
+        pair, got_two = lax.optimization_barrier((pair, got_two))
+        got_pair = swap_y(pair)
+        two = call(
+            functools.partial(meet_body, 2), piece, "meet2", 1 << 19,
+            slot_owner, ens, localized, got_two, specs=(SMEM,) + (VMEM,) * 3,
+        )
+        arrived = {2: turn_z(two, 2)}
+        mine, across = call(
+            weight_pick, (piece,) * 2, "weight_pick", 1 << 18, slot_owner, made["obs_v"],
+            from_low, from_high, specs=(SMEM,) + (VMEM,) * 3, after=(two,),
+        )
+        one, three = call(
+            meet_pair_body, (piece,) * 2, "meet13", 1 << 19,
+            slot_owner, ens, localized, got_pair, specs=(SMEM,) + (VMEM,) * 3,
+            after=(two, across),
+        )
+        arrived[1], arrived[3] = turn_z(one, 1), turn_z(three, 3)
+        single, across, _ = lax.optimization_barrier((single, across, got_pair))
+        got_own, from_y = swap_y(single), swap_y(across)
         grad = call(
-            last_body, piece, "last", 1 << 19, slot_owner, perturbations, localized, got[0],
-            arrived[1], arrived[2], arrived[3], mine, from_low, from_high,
-            specs=(SMEM,) + (VMEM,) * 9,
-        )
-        own = {0: grad}
-        for s in order:
-            own[s] = turn_z(grad, s)
-        other = {s: swap_y(own[s]) for s in (0,) + order}
+            last_body, piece, "last", 1 << 19, slot_owner, ens, localized, got_own,
+            arrived[1], arrived[2], arrived[3], mine, from_y,
+            specs=(SMEM,) + (VMEM,) * 8,
+        )
+        own = {0: grad, 1: turn_z(grad, 1), 3: turn_z(grad, 3)}
+        other = {0: swap_y(grad)}
+        later, own[1], own[3], other[0] = lax.optimization_barrier((grad, own[1], own[3], other[0]))
+        own[2] = turn_z(later, 2)
+        other.update({s: swap_y(own[s]) for s in (1, 3, 2)})
         back = lambda s: (-s) % SLOTS
         weighted = None
-        for group in (((0, 0),), ((0, 1), (2, 0)), ((1, 0), (2, 1)), ((3, 0), (1, 1)), ((3, 1),)):
-            final = group == ((3, 1),)
+        groups = (((0, 0),), ((0, 1), (1, 0), (3, 0)), ((1, 1), (3, 1), (2, 0)), ((2, 1),))
+        for group in groups:
+            final = group == groups[-1]
             grads = [other[s] if o else own[s] for s, o in group]
             pieces = tuple((back(s), o) for s, o in group)
             before = () if weighted is None else (weighted,)
@@ -451,7 +506,7 @@
                 functools.partial(spread_body, pieces, weighted is None, final),
                 (shape(*half_shape),) * 4 + (shape(*field_shape),) if final else shape(*field_shape),
                 "spread%d" % group[0][0], 1 << 19,
-                slot_owner, perturbations, *grads, *before, *extra,
+                slot_owner, ens, *grads, *before, *extra,
                 specs=(SMEM,) + (VMEM,) * (1 + len(grads) + len(before) + len(extra)),
             )
             weighted = result
@@ -462,8 +517,8 @@
             specs=(VMEM,) * 5,
         )
         partial = call(
-            all_increments, shape(SLOTS, perturbations.shape[1], levels, band_rows, width),
-            "increments", 1 << 20, perturbations, localized, specs=(VMEM,) * 2,
+            all_increments, shape(SLOTS, ens.shape[1], levels, band_rows, width),
+            "increments", 1 << 20, ens, localized, specs=(VMEM,) * 2,
         )
         weights = jnp.stack(
             [
@@ -481,19 +536,19 @@
         gathered = lax.all_gather(weight_rows * share, "mem", axis=0, tiled=True)
         own_core, own_x, to_core, to_x, _ = call(
             all_weighted, (shape(*half_shape),) * 4 + (shape(*field_shape),), "weighted",
-            1 << 20, perturbations, gathered.reshape(partial.shape), transposed,
+            1 << 20, ens, gathered.reshape(partial.shape), transposed,
             specs=(VMEM,) * 3,
         )
     got_x, got_core = swap_x(to_x), swap_core(to_core)
     half = call(
         functools.partial(zonal_adjoint, 0), shape(*half_shape), "adjoint0", 1 << 19,
-        zonal_shift, zonal_taps, control, own_core, got_core,
-        specs=(SMEM,) + (VMEM,) * 4, scratch=tap_room,
+        made["shift_core"], made["taps_v"], control_v, own_core, got_core,
+        specs=(VMEM,) * 5, scratch=tap_room,
     )
     return call(
         functools.partial(zonal_adjoint, 1), shape(*field_shape), "adjoint1", 1 << 19,
-        zonal_shift, zonal_taps, control, own_x, got_x, half,
-        specs=(SMEM,) + (VMEM,) * 5, scratch=tap_room,
+        made["shift_x"], made["taps_v"], control_v, own_x, got_x, half,
+        specs=(VMEM,) * 6, scratch=tap_room,
     )
 
 

time: 115 us -> 103 us (0.90)
  waiting for transfers between devices: 58.5 us -> 48.2 us
  local copies, waits for them, and re-layouts: 9.03 us -> 0.11 us
  starting transfers between devices: 28.4 us -> 36.5 us
    ppermute x9 -> x8, waiting for transfers between devices: 23.5 us -> 13.9 us  [per_device(): swap_y = lambda v: lax.ppermute(v, 'mem', y_pairs)]
    unnamed x30 -> x4, local copies, waits for them, and re-layouts: 8.24 us -> 0.01 us
    ppermute x6, waiting for transfers between devices: 31 us -> 23.9 us  [per_device(): lax.ppermute(v, 'mem', [(i, (i + 2 * s) % mem_count) for i in range(mem_c...]
    ppermute x2, waiting for transfers between devices: 0.01 us -> 6.85 us  [the longest x1 6.85 us: per_device(): from_low = lax.ppermute(made['obs_v'], 'mem', raised)]
    ppermute x6, starting transfers between devices: 10 us -> 13.5 us  [per_device(): lax.ppermute(v, 'mem', [(i, (i + 2 * s) % mem_count) for i in range(mem_c...]
    ppermute x2, starting transfers between devices: 4.93 us -> 7.41 us  [per_device(): swap_x = lambda v: lax.ppermute(v, 'lat', x_pairs)]
    ppermute x9 -> x8, starting transfers between devices: 7.23 us -> 9.04 us  [per_device(): swap_y = lambda v: lax.ppermute(v, 'mem', y_pairs)]
    ppermute x2, starting transfers between devices: 3.87 us -> 5.31 us  [the longest x1 4.62 us: per_device(): from_low = lax.ppermute(made['obs_v'], 'mem', raised)]
  transfers between devices with their start and end apart: 21 -> 20, of which waited for: 11 -> 9; matrix products, arithmetic and copies ran while one was open for 1% -> 0% of each run, Pallas kernels for 10% -> 9%
where the time goes in v3:
time: 103 us
  waiting for transfers between devices  48.2 us (47%)
  starting transfers between devices  36.5 us (35%)
  Pallas kernels  17.5 us (17%)
    ppermute x6, waiting for transfers between devices, per_device(): lax.ppermute(v, 'mem', [(i, (i + 2 * s) % mem_count) for i in range(mem_c...  23.9 us
    pallas_call x15, Pallas kernels, call(): pl.pallas_call(kernel, out_shape=outs, in_specs=list(specs) + [ANY] * ext...  17.5 us
    ppermute x8, waiting for transfers between devices, per_device(): swap_y = lambda v: lax.ppermute(v, 'mem', y_pairs)  13.9 us
    ppermute x6, starting transfers between devices, per_device(): lax.ppermute(v, 'mem', [(i, (i + 2 * s) % mem_count) for i in range(mem_c...  13.5 us
    ppermute x8, starting transfers between devices, per_device(): swap_y = lambda v: lax.ppermute(v, 'mem', y_pairs)  9.04 us
    ppermute x2, starting transfers between devices, per_device(): swap_x = lambda v: lax.ppermute(v, 'lat', x_pairs)  7.41 us
    ppermute x1, waiting for transfers between devices, per_device(): from_low = lax.ppermute(made['obs_v'], 'mem', raised)  6.85 us
    ppermute x1, starting transfers between devices, per_device(): from_low = lax.ppermute(made['obs_v'], 'mem', raised)  4.62 us
  transfers between devices with their start and end apart: 20, of which 9 were waited for; matrix products, arithmetic and copies ran while one was open for 0% of the time, Pallas kernels for 9%

profile of v3, /device:TPU:1, one launch (start us, length us, event | category | flops | bytes accessed | tf_op | source)
XLA Modules:
  0.0 102.5 jit_solution(17540896699139068713)
XLA Ops:
  0.0 0.0 copy-start.1
  0.0 0.0 copy-start
  0.0 3.2 %front.1 = (f32[2,4,8,1024]{3,2,1,0:T(8,128)}, f32[2,4,16,1024]{3,2,1,0:T(8,128)S(1)}, f32[16,17]{1,0:T(8,128)S(1)}, f32[16,17]{1,0:T(8,128)S(1)}, s32[8,128]{1,...) custom-call(s32[16]{0:T(128)} %refs_0_.11, ...), custom_call_target="tpu_custom_call" | custom-call | flops 524288 | bytes 524288 | tf_op jit(solution)/shard_map/front/pallas_call | solution.py:29
  3.2 4.5 %collective-permute-start = (f32[2,4,8,1024]{3,2,1,0:T(8,128)}, f32[2,4,8,1024]{3,2,1,0:T(8,128)}, u32[]{:S(2)}, u32[]{:S(2)}) collective-permute-start(f32[2,4,8,1024]{3,2,1,0:T(8,128)} %get-tuple-element.41.refs_3_), channel_id=1, source_target_pairs={{1,2},{2,1},{5,6},{6,5},{9,10},{10,9},{13,14},{14,13},{17,18},{18,... | collective-permute-start | bytes 786440 | tf_op jit(solution)/shard_map/ppermute | solution.py:403
  7.7 1.3 %core.1.refs_2_ = f32[2,4,8,1024]{3,2,1,0:T(8,128)S(1)} custom-call(s32[8,128]{1,0:T(8,128)S(1)} %get-tuple-element.40.refs_0_, f32[16,17]{1,0:T(8,128)S(1)} %get-tuple-element.36.refs_1_, f32[2,4,16,1024]{3,2,1,0:T(8,128)S(1)} %get-tuple-element.37.refs_2_), custom_call_target="tpu_custom_call" | custom-call | flops 524288 | bytes 524288 | tf_op jit(solution)/shard_map/core/pallas_call | solution.py:29
  9.0 0.1 collective-permute-start.1
  9.1 0.7 collective-permute-start.3
  9.8 4.6 %collective-permute-start.2 = (f32[2,4,16,1024]{3,2,1,0:T(8,128)}, f32[2,4,16,1024]{3,2,1,0:T(8,128)}, u32[]{:S(2)}, u32[]{:S(2)}) collective-permute-start(f32[2,4,16,1024]{3,2,1,0:T(8,128)} %get-tuple-element.44.refs_1_), channel_id=1, source_target_pairs={{0,8},{4,12},{8,16},{12,20},{1,9},{5,13},{9,17},{13,21},{2,10},{6,... | collective-permute-start | bytes 1572872 | tf_op jit(solution)/shard_map/ppermute | solution.py:440
  14.4 0.0 copy-done.1
  14.4 0.1 copy.9
  14.5 0.0 collective-permute-done.refs_3_.refs_5_
  14.5 0.2 matrix.1
  14.8 0.0 collective-permute-done.1.refs_4_
  14.8 0.0 copy-done
  14.8 1.7 %first.1 = (f32[2,4,16,1024]{3,2,1,0:T(8,128)S(1)}, f32[4,16,1024]{2,1,0:T(8,128)S(1)}) custom-call(s32[4]{0:T(128)S(1)} %copy-done, f32[64,128]{1,0:T(8,128)S(1)} %get-tuple-element.42.refs_1_, f32[2,4,8,1024]{3,2,1,0:T(8,128)S(1)} %core.1.refs_2_, f32[2,4,8,1024]{3,2,1,0:T(8,128)} %get-tuple-element.41.refs_3_, ...), custom_call_target="tpu_custom_call" | custom-call | flops 1048576 | bytes 1048576 | tf_op jit(solution)/shard_map/first/pallas_call | solution.py:29
  16.6 1.3 %collective-permute-start.4 = (f32[4,16,1024]{2,1,0:T(8,128)S(1)}, f32[4,16,1024]{2,1,0:T(8,128)S(1)}, u32[]{:S(2)}, u32[]{:S(2)}) collective-permute-start(f32[4,16,1024]{2,1,0:T(8,128)S(1)} %get-tuple-element.47), channel_id=1, source_target_pairs={{0,4},{4,0},{8,12},{12,8},{16,20},{20,16},{24,28},{28,24},{1,5},{5... | collective-permute-start | bytes 786440 | tf_op jit(solution)/shard_map/ppermute | solution.py:433
  17.9 0.0 collective-permute-done.3.refs_4_.refs_3_
  17.9 6.8 %collective-permute-done.2.refs_3_.refs_2_ = f32[2,4,16,1024]{3,2,1,0:T(8,128)} collective-permute-done((f32[2,4,16,1024]{3,2,1,0:T(8,128)}, f32[2,4,16,1024]{3,2,1,0:T(8,128)}, u32[]{:S(2)}, u32[]{:S(2)}) %collective-permute-start.2) | collective-permute-done | bytes 524320 | tf_op jit(solution)/shard_map/ppermute | solution.py:440
  24.7 0.8 send.1
  25.5 0.0 collective-permute-done.4.refs_3_
  25.5 1.3 %collective-permute-start.5 = (f32[2,4,16,1024]{3,2,1,0:T(8,128)S(1)}, f32[2,4,16,1024]{3,2,1,0:T(8,128)S(1)}, u32[]{:S(2)}, u32[]{:S(2)}) collective-permute-start(f32[2,4,16,1024]{3,2,1,0:T(8,128)S(1)} %get-tuple-element.50), channel_id=1, source_target_pairs={{0,4},{4,0},{8,12},{12,8},{16,20},{20,16},{24,28},{28,24},{1,5},{5... | collective-permute-start | bytes 1572872 | tf_op jit(solution)/shard_map/ppermute | solution.py:433
  26.8 0.6 meet2.1.refs_4_
  27.4 3.7 %collective-permute-start.8 = (f32[4,16,1024]{2,1,0:T(8,128)S(1)}, f32[4,16,1024]{2,1,0:T(8,128)S(1)}, u32[]{:S(2)}, u32[]{:S(2)}) collective-permute-start(f32[4,16,1024]{2,1,0:T(8,128)S(1)} %meet2.1.refs_4_), channel_id=1, source_target_pairs={{0,16},{4,20},{8,24},{12,28},{16,0},{20,4},{24,8},{28,12},{1,17},{... | collective-permute-start | bytes 786440 | tf_op jit(solution)/shard_map/ppermute | solution.py:434
  31.2 1.3 %weight_pick.1 = (f32[4,16,1024]{2,1,0:T(8,128)S(1)}, f32[4,16,1024]{2,1,0:T(8,128)S(1)}) custom-call(s32[4]{0:T(128)S(1)} %copy-done, f32[2,4,16,1024]{3,2,1,0:T(8,128)} %get-tuple-element.44.refs_1_, f32[2,4,16,1024]{3,2,1,0:T(8,128)} %collective-permute-done.2.refs_3_.refs_2_, f32[2,4,16,1024]{3,2,1,0:T(8,128)S(1)} %collective-permute-done.3.refs_4_.refs_3_, ...), custom_call_target="tpu_custom_call" | custom-call | flops 262144 | bytes 262144 | tf_op jit(solution)/shard_map/weight_pick/pallas_call | solution.py:29
  32.5 5.2 %collective-permute-done.5.refs_3_ = f32[2,4,16,1024]{3,2,1,0:T(8,128)S(1)} collective-permute-done((f32[2,4,16,1024]{3,2,1,0:T(8,128)S(1)}, f32[2,4,16,1024]{3,2,1,0:T(8,128)S(1)}, u32[]{:S(2)}, u32[]{:S(2)}) %collective-permute-start.5) | collective-permute-done | bytes 524320 | tf_op jit(solution)/shard_map/ppermute | solution.py:433
  37.6 0.7 meet13.1
  38.3 2.3 %collective-permute-start.7 = (f32[4,16,1024]{2,1,0:T(8,128)S(1)}, f32[4,16,1024]{2,1,0:T(8,128)S(1)}, u32[]{:S(2)}, u32[]{:S(2)}) collective-permute-start(f32[4,16,1024]{2,1,0:T(8,128)S(1)} %get-tuple-element.52), channel_id=1, source_target_pairs={{0,8},{4,12},{8,16},{12,20},{16,24},{20,28},{24,0},{28,4},{1,9},{5... | collective-permute-start | bytes 786440 | tf_op jit(solution)/shard_map/ppermute | solution.py:434
  40.6 1.1 %collective-permute-start.9 = (f32[4,16,1024]{2,1,0:T(8,128)S(1)}, f32[4,16,1024]{2,1,0:T(8,128)S(1)}, u32[]{:S(2)}, u32[]{:S(2)}) collective-permute-start(f32[4,16,1024]{2,1,0:T(8,128)S(1)} %get-tuple-element.53), channel_id=1, source_target_pairs={{0,24},{4,28},{8,0},{12,4},{16,8},{20,12},{24,16},{28,20},{1,25},{... | collective-permute-start | bytes 786440 | tf_op jit(solution)/shard_map/ppermute | solution.py:434
  41.6 1.2 %collective-permute-start.6 = (f32[4,16,1024]{2,1,0:T(8,128)S(1)}, f32[4,16,1024]{2,1,0:T(8,128)S(1)}, u32[]{:S(2)}, u32[]{:S(2)}) collective-permute-start(f32[4,16,1024]{2,1,0:T(8,128)S(1)} %get-tuple-element.51), channel_id=1, source_target_pairs={{0,4},{4,0},{8,12},{12,8},{16,20},{20,16},{24,28},{28,24},{1,5},{5... | collective-permute-start | bytes 786440 | tf_op jit(solution)/shard_map/ppermute | solution.py:433
  42.9 0.2 collective-permute-start.10
  43.1 0.0 collective-permute-done.8.refs_5_
  43.1 2.7 %collective-permute-done.7.refs_4_ = f32[4,16,1024]{2,1,0:T(8,128)S(1)} collective-permute-done((f32[4,16,1024]{2,1,0:T(8,128)S(1)}, f32[4,16,1024]{2,1,0:T(8,128)S(1)}, u32[]{:S(2)}, u32[]{:S(2)}) %collective-permute-start.7) | collective-permute-done | bytes 262176 | tf_op jit(solution)/shard_map/ppermute | solution.py:434
  45.8 8.9 %collective-permute-done.9.refs_6_ = f32[4,16,1024]{2,1,0:T(8,128)S(1)} collective-permute-done((f32[4,16,1024]{2,1,0:T(8,128)S(1)}, f32[4,16,1024]{2,1,0:T(8,128)S(1)}, u32[]{:S(2)}, u32[]{:S(2)}) %collective-permute-start.9) | collective-permute-done | bytes 262176 | tf_op jit(solution)/shard_map/ppermute | solution.py:434
  54.8 0.0 collective-permute-done.6.refs_3_
  54.8 0.0 collective-permute-done.10.refs_8_
  54.8 0.7 last.1.refs_2_
  55.5 0.4 collective-permute-start.13
  55.8 0.0 collective-permute-start.12
  55.8 1.5 %collective-permute-start.11 = (f32[4,16,1024]{2,1,0:T(8,128)S(1)}, f32[4,16,1024]{2,1,0:T(8,128)S(1)}, u32[]{:S(2)}, u32[]{:S(2)}) collective-permute-start(f32[4,16,1024]{2,1,0:T(8,128)S(1)} %last.1.refs_2_), channel_id=1, source_target_pairs={{0,8},{4,12},{8,16},{12,20},{16,24},{20,28},{24,0},{28,4},{1,9},{5... | collective-permute-start | bytes 786440 | tf_op jit(solution)/shard_map/ppermute | solution.py:434
  57.3 4.8 %collective-permute-done.13.refs_2_ = f32[4,16,1024]{2,1,0:T(8,128)S(1)} collective-permute-done((f32[4,16,1024]{2,1,0:T(8,128)S(1)}, f32[4,16,1024]{2,1,0:T(8,128)S(1)}, u32[]{:S(2)}, u32[]{:S(2)}) %collective-permute-start.13) | collective-permute-done | bytes 262176 | tf_op jit(solution)/shard_map/ppermute | solution.py:433
  62.1 2.5 %collective-permute-done.12.refs_4_ = f32[4,16,1024]{2,1,0:T(8,128)S(1)} collective-permute-done((f32[4,16,1024]{2,1,0:T(8,128)S(1)}, f32[4,16,1024]{2,1,0:T(8,128)S(1)}, u32[]{:S(2)}, u32[]{:S(2)}) %collective-permute-start.12) | collective-permute-done | bytes 262176 | tf_op jit(solution)/shard_map/ppermute | solution.py:434
  64.6 0.0 collective-permute-done.11.refs_3_
  64.6 4.9 %collective-permute-start.14 = (f32[4,16,1024]{2,1,0:T(8,128)S(1)}, f32[4,16,1024]{2,1,0:T(8,128)S(1)}, u32[]{:S(2)}, u32[]{:S(2)}) collective-permute-start(f32[4,16,1024]{2,1,0:T(8,128)S(1)} %last.1.refs_2_), channel_id=1, source_target_pairs={{0,16},{4,20},{8,24},{12,28},{16,0},{20,4},{24,8},{28,12},{1,17},{... | collective-permute-start | bytes 786440 | tf_op jit(solution)/shard_map/ppermute | solution.py:434
  69.6 2.2 %collective-permute-start.16 = (f32[4,16,1024]{2,1,0:T(8,128)S(1)}, f32[4,16,1024]{2,1,0:T(8,128)S(1)}, u32[]{:S(2)}, u32[]{:S(2)}) collective-permute-start(f32[4,16,1024]{2,1,0:T(8,128)S(1)} %collective-permute-done.11.refs_3_), channel_id=1, source_target_pairs={{0,4},{4,0},{8,12},{12,8},{16,20},{20,16},{24,28},{28,24},{1,5},{5... | collective-permute-start | bytes 786440 | tf_op jit(solution)/shard_map/ppermute | solution.py:433
  71.8 0.0 collective-permute-start.17
  71.8 9.8 %collective-permute-done.14.refs_4_ = f32[4,16,1024]{2,1,0:T(8,128)S(1)} collective-permute-done((f32[4,16,1024]{2,1,0:T(8,128)S(1)}, f32[4,16,1024]{2,1,0:T(8,128)S(1)}, u32[]{:S(2)}, u32[]{:S(2)}) %collective-permute-start.14) | collective-permute-done | bytes 262176 | tf_op jit(solution)/shard_map/ppermute | solution.py:434
  81.6 2.4 %collective-permute-start.15 = (f32[4,16,1024]{2,1,0:T(8,128)S(1)}, f32[4,16,1024]{2,1,0:T(8,128)S(1)}, u32[]{:S(2)}, u32[]{:S(2)}) collective-permute-start(f32[4,16,1024]{2,1,0:T(8,128)S(1)} %collective-permute-done.14.refs_4_), channel_id=1, source_target_pairs={{0,4},{4,0},{8,12},{12,8},{16,20},{20,16},{24,28},{28,24},{1,5},{5... | collective-permute-start | bytes 786440 | tf_op jit(solution)/shard_map/ppermute | solution.py:433
  84.0 0.6 spread0.2.refs_5_
  84.6 0.8 spread0.3.refs_5_
  85.4 0.0 collective-permute-done.16.refs_2_
  85.4 0.0 collective-permute-done.17.refs_3_
  85.4 0.7 spread1.1.refs_3_
  86.1 3.9 %collective-permute-done.15.refs_2_ = f32[4,16,1024]{2,1,0:T(8,128)S(1)} collective-permute-done((f32[4,16,1024]{2,1,0:T(8,128)S(1)}, f32[4,16,1024]{2,1,0:T(8,128)S(1)}, u32[]{:S(2)}, u32[]{:S(2)}) %collective-permute-start.15) | collective-permute-done | bytes 262176 | tf_op jit(solution)/shard_map/ppermute | solution.py:433
  90.0 1.6 %spread2.1 = (f32[2,4,8,1024]{3,2,1,0:T(8,128)S(1)}, f32[2,4,8,1024]{3,2,1,0:T(8,128)S(1)}, f32[2,4,8,1024]{3,2,1,0:T(8,128)S(1)}, f32[2,4,8,1024]{3,2,1,0:T(8,128)S(1)}, f32[2,4,16,1024]{3,2,1,0:T(8,128)}) custom-call(s32[4]{0:T(128)S(1)} %copy-done, bf16[4,2,2,4,16,1024]{5,4,3,2,1,0:T(8,128)(2,1)S(1)} %get-tuple-element.38.refs_6_.refs_1_, ...), custom_call_target="tpu_custom_call" | custom-call | flops 524288 | bytes 524288 | tf_op jit(solution)/shard_map/spread2/pallas_call | solution.py:29
  91.7 1.2 %collective-permute-start.19 = (f32[2,4,8,1024]{3,2,1,0:T(8,128)S(1)}, f32[2,4,8,1024]{3,2,1,0:T(8,128)S(1)}, u32[]{:S(2)}, u32[]{:S(2)}) collective-permute-start(f32[2,4,8,1024]{3,2,1,0:T(8,128)S(1)} %get-tuple-element.64), channel_id=1, source_target_pairs={{0,1},{1,0},{2,3},{3,2},{4,5},{5,4},{6,7},{7,6},{8,9},{9,8},{10,11... | collective-permute-start | bytes 786440 | tf_op jit(solution)/shard_map/ppermute | solution.py:402
  92.9 2.9 %collective-permute-start.18 = (f32[2,4,8,1024]{3,2,1,0:T(8,128)S(1)}, f32[2,4,8,1024]{3,2,1,0:T(8,128)S(1)}, u32[]{:S(2)}, u32[]{:S(2)}) collective-permute-start(f32[2,4,8,1024]{3,2,1,0:T(8,128)S(1)} %get-tuple-element.62), channel_id=1, source_target_pairs={{1,2},{2,1},{5,6},{6,5},{9,10},{10,9},{13,14},{14,13},{17,18},{18,... | collective-permute-start | bytes 786440 | tf_op jit(solution)/shard_map/ppermute | solution.py:403
  95.8 0.0 collective-permute-done.19.refs_4_
  95.8 1.3 %adjoint0.1.refs_5_ = f32[2,4,8,1024]{3,2,1,0:T(8,128)S(1)} custom-call(s32[8,128]{1,0:T(8,128)S(1)} %get-tuple-element.40.refs_0_, f32[16,17]{1,0:T(8,128)S(1)} %get-tuple-element.36.refs_1_, f32[2,4,16,1024]{3,2,1,0:T(8,128)S(1)} %get-tuple-element.37.refs_2_, f32[2,4,8,1024]{3,2,1,0:T(8,128)S(1)} %get-tuple-element.63.refs_3_, ...), custom_call_target="tpu_custom_call" | custom-call | flops 524288 | bytes 524288 | tf_op jit(solution)/shard_map/adjoint0/pallas_call | solution.py:29
  97.1 3.5 %collective-permute-done.18.refs_4_ = f32[2,4,8,1024]{3,2,1,0:T(8,128)S(1)} collective-permute-done((f32[2,4,8,1024]{3,2,1,0:T(8,128)S(1)}, f32[2,4,8,1024]{3,2,1,0:T(8,128)S(1)}, u32[]{:S(2)}, u32[]{:S(2)}) %collective-permute-start.18) | collective-permute-done | bytes 262176 | tf_op jit(solution)/shard_map/ppermute | solution.py:403
  100.5 2.0 %adjoint1.1 = f32[2,4,16,1024]{3,2,1,0:T(8,128)} custom-call(s32[8,128]{1,0:T(8,128)S(1)} %get-tuple-element.35.refs_0_, f32[16,17]{1,0:T(8,128)S(1)} %get-tuple-element.36.refs_1_, f32[2,4,16,1024]{3,2,1,0:T(8,128)S(1)} %get-tuple-element.37.refs_2_, f32[2,4,8,1024]{3,2,1,0:T(8,128)S(1)} %get-tuple-element.61.refs_3_, ...), custom_call_target="tpu_custom_call" | custom-call | flops 524288 | bytes 524288 | tf_op jit(solution)/shard_map/adjoint1/pallas_call | solution.py:29
Async XLA Ops:
  0.0 14.4 %copy-start.1 = (f32[16,4,4]{0,2,1:T(4,128)S(1)}, f32[16,4,4]{0,2,1:T(4,128)}, u32[]{:S(2)}) copy-start(f32[16,4,4]{0,2,1:T(4,128)} %param.15) | copy-start | bytes 3076
  0.0 14.8 %copy-start = (s32[4]{0:T(128)S(1)}, s32[4]{0:T(128)}, u32[]{:S(2)}) copy-start(s32[4]{0:T(128)} %refs_0_.21) | copy-start | bytes 52
  3.2 11.3 %collective-permute-start = (f32[2,4,8,1024]{3,2,1,0:T(8,128)}, f32[2,4,8,1024]{3,2,1,0:T(8,128)}, u32[]{:S(2)}, u32[]{:S(2)}) collective-permute-start(f32[2,4,8,1024]{3,2,1,0:T(8,128)} %get-tuple-element.41.refs_3_), channel_id=1, source_target_pairs={{1,2},{2,1},{5,6},{6,5},{9,10},{10,9},{13,14},{14,13},{17,18},{18,... | collective-permute-start | bytes 786440 | tf_op jit(solution)/shard_map/ppermute | solution.py:403
  9.0 5.8 %collective-permute-start.1 = (f32[2,4,8,1024]{3,2,1,0:T(8,128)S(1)}, f32[2,4,8,1024]{3,2,1,0:T(8,128)}, u32[]{:S(2)}, u32[]{:S(2)}) collective-permute-start(f32[2,4,8,1024]{3,2,1,0:T(8,128)S(1)} %core.1.refs_2_), channel_id=1, source_target_pairs={{0,1},{1,0},{2,3},{3,2},{4,5},{5,4},{6,7},{7,6},{8,9},{9,8},{10,11... | collective-permute-start | bytes 786440 | tf_op jit(solution)/shard_map/ppermute | solution.py:402
  9.1 8.8 %collective-permute-start.3 = (f32[2,4,16,1024]{3,2,1,0:T(8,128)}, f32[2,4,16,1024]{3,2,1,0:T(8,128)S(1)}, u32[]{:S(2)}, u32[]{:S(2)}) collective-permute-start(f32[2,4,16,1024]{3,2,1,0:T(8,128)} %get-tuple-element.44.refs_1_), channel_id=1, source_target_pairs={{16,8},{20,12},{24,16},{28,20},{17,9},{21,13},{25,17},{29,21},{18,... | collective-permute-start | bytes 1572872 | tf_op jit(solution)/shard_map/ppermute | solution.py:441
  9.8 14.9 %collective-permute-start.2 = (f32[2,4,16,1024]{3,2,1,0:T(8,128)}, f32[2,4,16,1024]{3,2,1,0:T(8,128)}, u32[]{:S(2)}, u32[]{:S(2)}) collective-permute-start(f32[2,4,16,1024]{3,2,1,0:T(8,128)} %get-tuple-element.44.refs_1_), channel_id=1, source_target_pairs={{0,8},{4,12},{8,16},{12,20},{1,9},{5,13},{9,17},{13,21},{2,10},{6,... | collective-permute-start | bytes 1572872 | tf_op jit(solution)/shard_map/ppermute | solution.py:440
  16.6 8.9 %collective-permute-start.4 = (f32[4,16,1024]{2,1,0:T(8,128)S(1)}, f32[4,16,1024]{2,1,0:T(8,128)S(1)}, u32[]{:S(2)}, u32[]{:S(2)}) collective-permute-start(f32[4,16,1024]{2,1,0:T(8,128)S(1)} %get-tuple-element.47), channel_id=1, source_target_pairs={{0,4},{4,0},{8,12},{12,8},{16,20},{20,16},{24,28},{28,24},{1,5},{5... | collective-permute-start | bytes 786440 | tf_op jit(solution)/shard_map/ppermute | solution.py:433
  25.5 12.1 %collective-permute-start.5 = (f32[2,4,16,1024]{3,2,1,0:T(8,128)S(1)}, f32[2,4,16,1024]{3,2,1,0:T(8,128)S(1)}, u32[]{:S(2)}, u32[]{:S(2)}) collective-permute-start(f32[2,4,16,1024]{3,2,1,0:T(8,128)S(1)} %get-tuple-element.50), channel_id=1, source_target_pairs={{0,4},{4,0},{8,12},{12,8},{16,20},{20,16},{24,28},{28,24},{1,5},{5... | collective-permute-start | bytes 1572872 | tf_op jit(solution)/shard_map/ppermute | solution.py:433
  27.4 15.7 %collective-permute-start.8 = (f32[4,16,1024]{2,1,0:T(8,128)S(1)}, f32[4,16,1024]{2,1,0:T(8,128)S(1)}, u32[]{:S(2)}, u32[]{:S(2)}) collective-permute-start(f32[4,16,1024]{2,1,0:T(8,128)S(1)} %meet2.1.refs_4_), channel_id=1, source_target_pairs={{0,16},{4,20},{8,24},{12,28},{16,0},{20,4},{24,8},{28,12},{1,17},{... | collective-permute-start | bytes 786440 | tf_op jit(solution)/shard_map/ppermute | solution.py:434
  38.3 7.5 %collective-permute-start.7 = (f32[4,16,1024]{2,1,0:T(8,128)S(1)}, f32[4,16,1024]{2,1,0:T(8,128)S(1)}, u32[]{:S(2)}, u32[]{:S(2)}) collective-permute-start(f32[4,16,1024]{2,1,0:T(8,128)S(1)} %get-tuple-element.52), channel_id=1, source_target_pairs={{0,8},{4,12},{8,16},{12,20},{16,24},{20,28},{24,0},{28,4},{1,9},{5... | collective-permute-start | bytes 786440 | tf_op jit(solution)/shard_map/ppermute | solution.py:434
  40.6 14.2 %collective-permute-start.9 = (f32[4,16,1024]{2,1,0:T(8,128)S(1)}, f32[4,16,1024]{2,1,0:T(8,128)S(1)}, u32[]{:S(2)}, u32[]{:S(2)}) collective-permute-start(f32[4,16,1024]{2,1,0:T(8,128)S(1)} %get-tuple-element.53), channel_id=1, source_target_pairs={{0,24},{4,28},{8,0},{12,4},{16,8},{20,12},{24,16},{28,20},{1,25},{... | collective-permute-start | bytes 786440 | tf_op jit(solution)/shard_map/ppermute | solution.py:434
  41.6 13.1 %collective-permute-start.6 = (f32[4,16,1024]{2,1,0:T(8,128)S(1)}, f32[4,16,1024]{2,1,0:T(8,128)S(1)}, u32[]{:S(2)}, u32[]{:S(2)}) collective-permute-start(f32[4,16,1024]{2,1,0:T(8,128)S(1)} %get-tuple-element.51), channel_id=1, source_target_pairs={{0,4},{4,0},{8,12},{12,8},{16,20},{20,16},{24,28},{28,24},{1,5},{5... | collective-permute-start | bytes 786440 | tf_op jit(solution)/shard_map/ppermute | solution.py:433
  42.9 11.9 %collective-permute-start.10 = (f32[4,16,1024]{2,1,0:T(8,128)S(1)}, f32[4,16,1024]{2,1,0:T(8,128)S(1)}, u32[]{:S(2)}, u32[]{:S(2)}) collective-permute-start(f32[4,16,1024]{2,1,0:T(8,128)S(1)} %get-tuple-element.55.refs_5_), channel_id=1, source_target_pairs={{0,4},{4,0},{8,12},{12,8},{16,20},{20,16},{24,28},{28,24},{1,5},{5... | collective-permute-start | bytes 786440 | tf_op jit(solution)/shard_map/ppermute | solution.py:433
  55.5 6.7 %collective-permute-start.13 = (f32[4,16,1024]{2,1,0:T(8,128)S(1)}, f32[4,16,1024]{2,1,0:T(8,128)S(1)}, u32[]{:S(2)}, u32[]{:S(2)}) collective-permute-start(f32[4,16,1024]{2,1,0:T(8,128)S(1)} %last.1.refs_2_), channel_id=1, source_target_pairs={{0,4},{4,0},{8,12},{12,8},{16,20},{20,16},{24,28},{28,24},{1,5},{5... | collective-permute-start | bytes 786440 | tf_op jit(solution)/shard_map/ppermute | solution.py:433
  55.8 8.8 %collective-permute-start.12 = (f32[4,16,1024]{2,1,0:T(8,128)S(1)}, f32[4,16,1024]{2,1,0:T(8,128)S(1)}, u32[]{:S(2)}, u32[]{:S(2)}) collective-permute-start(f32[4,16,1024]{2,1,0:T(8,128)S(1)} %last.1.refs_2_), channel_id=1, source_target_pairs={{0,24},{4,28},{8,0},{12,4},{16,8},{20,12},{24,16},{28,20},{1,25},{... | collective-permute-start | bytes 786440 | tf_op jit(solution)/shard_map/ppermute | solution.py:434
  55.8 8.8 %collective-permute-start.11 = (f32[4,16,1024]{2,1,0:T(8,128)S(1)}, f32[4,16,1024]{2,1,0:T(8,128)S(1)}, u32[]{:S(2)}, u32[]{:S(2)}) collective-permute-start(f32[4,16,1024]{2,1,0:T(8,128)S(1)} %last.1.refs_2_), channel_id=1, source_target_pairs={{0,8},{4,12},{8,16},{12,20},{16,24},{20,28},{24,0},{28,4},{1,9},{5... | collective-permute-start | bytes 786440 | tf_op jit(solution)/shard_map/ppermute | solution.py:434
  64.6 16.9 %collective-permute-start.14 = (f32[4,16,1024]{2,1,0:T(8,128)S(1)}, f32[4,16,1024]{2,1,0:T(8,128)S(1)}, u32[]{:S(2)}, u32[]{:S(2)}) collective-permute-start(f32[4,16,1024]{2,1,0:T(8,128)S(1)} %last.1.refs_2_), channel_id=1, source_target_pairs={{0,16},{4,20},{8,24},{12,28},{16,0},{20,4},{24,8},{28,12},{1,17},{... | collective-permute-start | bytes 786440 | tf_op jit(solution)/shard_map/ppermute | solution.py:434
  69.6 15.8 %collective-permute-start.16 = (f32[4,16,1024]{2,1,0:T(8,128)S(1)}, f32[4,16,1024]{2,1,0:T(8,128)S(1)}, u32[]{:S(2)}, u32[]{:S(2)}) collective-permute-start(f32[4,16,1024]{2,1,0:T(8,128)S(1)} %collective-permute-done.11.refs_3_), channel_id=1, source_target_pairs={{0,4},{4,0},{8,12},{12,8},{16,20},{20,16},{24,28},{28,24},{1,5},{5... | collective-permute-start | bytes 786440 | tf_op jit(solution)/shard_map/ppermute | solution.py:433
  71.8 13.6 %collective-permute-start.17 = (f32[4,16,1024]{2,1,0:T(8,128)S(1)}, f32[4,16,1024]{2,1,0:T(8,128)S(1)}, u32[]{:S(2)}, u32[]{:S(2)}) collective-permute-start(f32[4,16,1024]{2,1,0:T(8,128)S(1)} %collective-permute-done.12.refs_4_), channel_id=1, source_target_pairs={{0,4},{4,0},{8,12},{12,8},{16,20},{20,16},{24,28},{28,24},{1,5},{5... | collective-permute-start | bytes 786440 | tf_op jit(solution)/shard_map/ppermute | solution.py:433
  81.6 8.4 %collective-permute-start.15 = (f32[4,16,1024]{2,1,0:T(8,128)S(1)}, f32[4,16,1024]{2,1,0:T(8,128)S(1)}, u32[]{:S(2)}, u32[]{:S(2)}) collective-permute-start(f32[4,16,1024]{2,1,0:T(8,128)S(1)} %collective-permute-done.14.refs_4_), channel_id=1, source_target_pairs={{0,4},{4,0},{8,12},{12,8},{16,20},{20,16},{24,28},{28,24},{1,5},{5... | collective-permute-start | bytes 786440 | tf_op jit(solution)/shard_map/ppermute | solution.py:433
  91.7 4.1 %collective-permute-start.19 = (f32[2,4,8,1024]{3,2,1,0:T(8,128)S(1)}, f32[2,4,8,1024]{3,2,1,0:T(8,128)S(1)}, u32[]{:S(2)}, u32[]{:S(2)}) collective-permute-start(f32[2,4,8,1024]{3,2,1,0:T(8,128)S(1)} %get-tuple-element.64), channel_id=1, source_target_pairs={{0,1},{1,0},{2,3},{3,2},{4,5},{5,4},{6,7},{7,6},{8,9},{9,8},{10,11... | collective-permute-start | bytes 786440 | tf_op jit(solution)/shard_map/ppermute | solution.py:402
  92.9 7.7 %collective-permute-start.18 = (f32[2,4,8,1024]{3,2,1,0:T(8,128)S(1)}, f32[2,4,8,1024]{3,2,1,0:T(8,128)S(1)}, u32[]{:S(2)}, u32[]{:S(2)}) collective-permute-start(f32[2,4,8,1024]{3,2,1,0:T(8,128)S(1)} %get-tuple-element.62), channel_id=1, source_target_pairs={{1,2},{2,1},{5,6},{6,5},{9,10},{10,9},{13,14},{14,13},{17,18},{18,... | collective-permute-start | bytes 786440 | tf_op jit(solution)/shard_map/ppermute | solution.py:403

commit v4 on v3

--- a/solution.py
+++ b/solution.py
@@ -51,7 +51,7 @@
 
 
 def entry_at(owners, step, value):
-    place = (own_z() + step) & (SLOTS - 1)
+    place = own_z() ^ step
     found = jnp.int32(0)
     for t in range(SLOTS):
         rank = jnp.int32(0)
@@ -278,10 +278,12 @@
     return total
 
 
-def weight_pick(owners, here, low, high, mine, across):
+def weight_pick(owners, here, side, middle, mine, across):
     place = owner_at(owners, 0) >> 1
     for found, weights in (
-        (place == own_z(), here), (place < own_z(), low), (place > own_z(), high)
+        (place == own_z(), here),
+        (place == own_z() ^ 1, side),
+        (place == own_z() ^ 3, middle),
     ):
 
         @pl.when(found)
@@ -432,13 +434,11 @@
         y_pairs = [(i, i ^ 1) for i in range(mem_count)]
         swap_y = lambda v: lax.ppermute(v, "mem", y_pairs)
         turn_z = lambda v, s: lax.ppermute(
-            v, "mem", [(i, (i + 2 * s) % mem_count) for i in range(mem_count)]
-        )
-        ends = z_count - 1
-        raised = [(2 * i + j, 2 * i + 2 + j) for i in range(ends - 1) for j in range(2)]
-        lowered = [(2 * i + 2 + j, 2 * i + j) for i in range(1, ends) for j in range(2)]
-        from_low = lax.ppermute(made["obs_v"], "mem", raised)
-        from_high = lax.ppermute(made["obs_v"], "mem", lowered)
+            v, "mem", [(i, i ^ 2 * s) for i in range(mem_count)]
+        )
+        middle = [(i, i ^ 6) for i in range(2, mem_count - 2)]
+        from_side = turn_z(made["obs_v"], 1)
+        from_middle = lax.ppermute(made["obs_v"], "mem", middle)
     near_core = call(
         core_body, shape(*half_shape), "core", 1 << 19, made["shift_core"], made["taps_v"],
         control_v, specs=(VMEM,) * 3, scratch=tap_room,
@@ -462,7 +462,7 @@
         got_two = swap_y(first)
         pair, single = call(
             send_body, (shape(2, levels, band_rows, width), piece), "send", 1 << 20,
-            slot_owner, ens, localized, specs=(SMEM, VMEM, VMEM), after=(from_low, from_high),
+            slot_owner, ens, localized, specs=(SMEM, VMEM, VMEM), after=(from_side, from_middle),
         )
         pair, got_two = lax.optimization_barrier((pair, got_two))
         got_pair = swap_y(pair)
@@ -473,7 +473,7 @@
         arrived = {2: turn_z(two, 2)}
         mine, across = call(
             weight_pick, (piece,) * 2, "weight_pick", 1 << 18, slot_owner, made["obs_v"],
-            from_low, from_high, specs=(SMEM,) + (VMEM,) * 3, after=(two,),
+            from_side, from_middle, specs=(SMEM,) + (VMEM,) * 3, after=(two,),
         )
         one, three = call(
             meet_pair_body, (piece,) * 2, "meet13", 1 << 19,
@@ -493,13 +493,12 @@
         later, own[1], own[3], other[0] = lax.optimization_barrier((grad, own[1], own[3], other[0]))
         own[2] = turn_z(later, 2)
         other.update({s: swap_y(own[s]) for s in (1, 3, 2)})
-        back = lambda s: (-s) % SLOTS
         weighted = None
         groups = (((0, 0),), ((0, 1), (1, 0), (3, 0)), ((1, 1), (3, 1), (2, 0)), ((2, 1),))
         for group in groups:
             final = group == groups[-1]
             grads = [other[s] if o else own[s] for s, o in group]
-            pieces = tuple((back(s), o) for s, o in group)
+            pieces = tuple(group)
             before = () if weighted is None else (weighted,)
             extra = (transposed,) if final else ()
             result = call(

time: 103 us -> 101 us (0.981)
  starting transfers between devices: 36.5 us -> 29.4 us
  waiting for transfers between devices: 48.2 us -> 53.5 us
    ppermute x8, starting transfers between devices: 18.8 us -> 9.82 us  [the longest x7 9.12 us: per_device(): lax.ppermute(v, 'mem', [(i, i ^ 2 * s) for i in range(mem_count)])]
    ppermute x8, waiting for transfers between devices: 30.8 us -> 36.2 us  [the longest x7 36.2 us: per_device(): lax.ppermute(v, 'mem', [(i, i ^ 2 * s) for i in range(mem_count)])]
    ppermute x2, starting transfers between devices: 7.41 us -> 9.56 us  [per_device(): swap_x = lambda v: lax.ppermute(v, 'lat', x_pairs)]
    ppermute x8, starting transfers between devices: 9.04 us -> 7.07 us  [per_device(): swap_y = lambda v: lax.ppermute(v, 'mem', y_pairs)]
    ppermute x2, starting transfers between devices: 1.28 us -> 2.96 us  [per_device(): swap_core = lambda v: lax.ppermute(v, 'lat', core_pairs)]
  transfers between devices with their start and end apart: 20 -> 20, of which waited for: 9 -> 11; matrix products, arithmetic and copies ran while one was open for 0% -> 0% of each run, Pallas kernels for 9% -> 9%
where the time goes in v4:
time: 101 us
  waiting for transfers between devices  53.5 us (53%)
  starting transfers between devices  29.4 us (29%)
  Pallas kernels  17.5 us (17%)
    ppermute x7, waiting for transfers between devices, per_device(): lax.ppermute(v, 'mem', [(i, i ^ 2 * s) for i in range(mem_count)])  36.2 us
    pallas_call x15, Pallas kernels, call(): pl.pallas_call(kernel, out_shape=outs, in_specs=list(specs) + [ANY] * ext...  17.5 us
    ppermute x8, waiting for transfers between devices, per_device(): swap_y = lambda v: lax.ppermute(v, 'mem', y_pairs)  14.5 us
    ppermute x2, starting transfers between devices, per_device(): swap_x = lambda v: lax.ppermute(v, 'lat', x_pairs)  9.56 us
    ppermute x7, starting transfers between devices, per_device(): lax.ppermute(v, 'mem', [(i, i ^ 2 * s) for i in range(mem_count)])  9.12 us
    ppermute x8, starting transfers between devices, per_device(): swap_y = lambda v: lax.ppermute(v, 'mem', y_pairs)  7.07 us
    ppermute x2, starting transfers between devices, per_device(): swap_core = lambda v: lax.ppermute(v, 'lat', core_pairs)  2.96 us
    ppermute x2, waiting for transfers between devices, per_device(): swap_x = lambda v: lax.ppermute(v, 'lat', x_pairs)  2.75 us
  transfers between devices with their start and end apart: 20, of which 11 were waited for; matrix products, arithmetic and copies ran while one was open for 0% of the time, Pallas kernels for 9%

profile of v4, /device:TPU:1, one launch (start us, length us, event | category | flops | bytes accessed | tf_op | source)
XLA Modules:
  0.0 100.7 jit_solution(4873922659365123465)
XLA Ops:
  0.0 0.0 copy-start.1
  0.0 0.0 copy-start
  0.0 3.2 %front.1 = (f32[2,4,8,1024]{3,2,1,0:T(8,128)}, f32[2,4,16,1024]{3,2,1,0:T(8,128)S(1)}, f32[16,17]{1,0:T(8,128)S(1)}, f32[16,17]{1,0:T(8,128)S(1)}, s32[8,128]{1,...) custom-call(s32[16]{0:T(128)} %refs_0_.11, ...), custom_call_target="tpu_custom_call" | custom-call | flops 524288 | bytes 524288 | tf_op jit(solution)/shard_map/front/pallas_call | solution.py:29
  3.2 4.5 %collective-permute-start = (f32[2,4,8,1024]{3,2,1,0:T(8,128)}, f32[2,4,8,1024]{3,2,1,0:T(8,128)}, u32[]{:S(2)}, u32[]{:S(2)}) collective-permute-start(f32[2,4,8,1024]{3,2,1,0:T(8,128)} %get-tuple-element.41.refs_3_), channel_id=1, source_target_pairs={{1,2},{2,1},{5,6},{6,5},{9,10},{10,9},{13,14},{14,13},{17,18},{18,... | collective-permute-start | bytes 786440 | tf_op jit(solution)/shard_map/ppermute | solution.py:405
  7.7 1.3 %core.1.refs_2_ = f32[2,4,8,1024]{3,2,1,0:T(8,128)S(1)} custom-call(s32[8,128]{1,0:T(8,128)S(1)} %get-tuple-element.40.refs_0_, f32[16,17]{1,0:T(8,128)S(1)} %get-tuple-element.36.refs_1_, f32[2,4,16,1024]{3,2,1,0:T(8,128)S(1)} %get-tuple-element.37.refs_2_), custom_call_target="tpu_custom_call" | custom-call | flops 524288 | bytes 524288 | tf_op jit(solution)/shard_map/core/pallas_call | solution.py:29
  9.0 0.1 collective-permute-start.1
  9.1 0.7 collective-permute-start.3
  9.8 3.9 %collective-permute-start.2 = (f32[2,4,16,1024]{3,2,1,0:T(8,128)}, f32[2,4,16,1024]{3,2,1,0:T(8,128)}, u32[]{:S(2)}, u32[]{:S(2)}) collective-permute-start(f32[2,4,16,1024]{3,2,1,0:T(8,128)} %get-tuple-element.44.refs_1_), channel_id=1, source_target_pairs={{0,8},{4,12},{8,0},{12,4},{16,24},{20,28},{24,16},{28,20},{1,9},{5... | collective-permute-start | bytes 1572872 | tf_op jit(solution)/shard_map/ppermute | solution.py:436
  13.7 0.0 copy-done.1
  13.7 0.1 copy.9
  13.8 0.0 collective-permute-done.refs_3_.refs_5_
  13.8 0.2 matrix.1
  14.0 0.0 collective-permute-done.1.refs_4_
  14.0 0.0 copy-done
  14.1 1.7 %first.1 = (f32[2,4,16,1024]{3,2,1,0:T(8,128)S(1)}, f32[4,16,1024]{2,1,0:T(8,128)S(1)}) custom-call(s32[4]{0:T(128)S(1)} %copy-done, f32[64,128]{1,0:T(8,128)S(1)} %get-tuple-element.42.refs_1_, f32[2,4,8,1024]{3,2,1,0:T(8,128)S(1)} %core.1.refs_2_, f32[2,4,8,1024]{3,2,1,0:T(8,128)} %get-tuple-element.41.refs_3_, ...), custom_call_target="tpu_custom_call" | custom-call | flops 1048576 | bytes 1048576 | tf_op jit(solution)/shard_map/first/pallas_call | solution.py:29
  15.8 1.3 %collective-permute-start.4 = (f32[4,16,1024]{2,1,0:T(8,128)S(1)}, f32[4,16,1024]{2,1,0:T(8,128)S(1)}, u32[]{:S(2)}, u32[]{:S(2)}) collective-permute-start(f32[4,16,1024]{2,1,0:T(8,128)S(1)} %get-tuple-element.47), channel_id=1, source_target_pairs={{0,4},{4,0},{8,12},{12,8},{16,20},{20,16},{24,28},{28,24},{1,5},{5... | collective-permute-start | bytes 786440 | tf_op jit(solution)/shard_map/ppermute | solution.py:435
  17.1 0.0 collective-permute-done.3.refs_4_.refs_3_
  17.1 8.4 %collective-permute-done.2.refs_3_.refs_2_ = f32[2,4,16,1024]{3,2,1,0:T(8,128)} collective-permute-done((f32[2,4,16,1024]{3,2,1,0:T(8,128)}, f32[2,4,16,1024]{3,2,1,0:T(8,128)}, u32[]{:S(2)}, u32[]{:S(2)}) %collective-permute-start.2) | collective-permute-done | bytes 524320 | tf_op jit(solution)/shard_map/ppermute | solution.py:436
  25.5 0.8 send.1
  26.3 0.0 collective-permute-done.4.refs_3_
  26.3 1.3 %collective-permute-start.5 = (f32[2,4,16,1024]{3,2,1,0:T(8,128)S(1)}, f32[2,4,16,1024]{3,2,1,0:T(8,128)S(1)}, u32[]{:S(2)}, u32[]{:S(2)}) collective-permute-start(f32[2,4,16,1024]{3,2,1,0:T(8,128)S(1)} %get-tuple-element.50), channel_id=1, source_target_pairs={{0,4},{4,0},{8,12},{12,8},{16,20},{20,16},{24,28},{28,24},{1,5},{5... | collective-permute-start | bytes 1572872 | tf_op jit(solution)/shard_map/ppermute | solution.py:435
  27.6 0.6 meet2.1.refs_4_
  28.2 1.2 %collective-permute-start.8 = (f32[4,16,1024]{2,1,0:T(8,128)S(1)}, f32[4,16,1024]{2,1,0:T(8,128)S(1)}, u32[]{:S(2)}, u32[]{:S(2)}) collective-permute-start(f32[4,16,1024]{2,1,0:T(8,128)S(1)} %meet2.1.refs_4_), channel_id=1, source_target_pairs={{0,16},{4,20},{8,24},{12,28},{16,0},{20,4},{24,8},{28,12},{1,17},{... | collective-permute-start | bytes 786440 | tf_op jit(solution)/shard_map/ppermute | solution.py:436
  29.4 1.3 %weight_pick.1 = (f32[4,16,1024]{2,1,0:T(8,128)S(1)}, f32[4,16,1024]{2,1,0:T(8,128)S(1)}) custom-call(s32[4]{0:T(128)S(1)} %copy-done, f32[2,4,16,1024]{3,2,1,0:T(8,128)} %get-tuple-element.44.refs_1_, f32[2,4,16,1024]{3,2,1,0:T(8,128)} %collective-permute-done.2.refs_3_.refs_2_, f32[2,4,16,1024]{3,2,1,0:T(8,128)S(1)} %collective-permute-done.3.refs_4_.refs_3_, ...), custom_call_target="tpu_custom_call" | custom-call | flops 262144 | bytes 262144 | tf_op jit(solution)/shard_map/weight_pick/pallas_call | solution.py:29
  30.7 7.8 %collective-permute-done.5.refs_3_ = f32[2,4,16,1024]{3,2,1,0:T(8,128)S(1)} collective-permute-done((f32[2,4,16,1024]{3,2,1,0:T(8,128)S(1)}, f32[2,4,16,1024]{3,2,1,0:T(8,128)S(1)}, u32[]{:S(2)}, u32[]{:S(2)}) %collective-permute-start.5) | collective-permute-done | bytes 524320 | tf_op jit(solution)/shard_map/ppermute | solution.py:435
  38.4 0.7 meet13.1
  39.2 0.9 collective-permute-start.7
  40.0 1.2 %collective-permute-start.9 = (f32[4,16,1024]{2,1,0:T(8,128)S(1)}, f32[4,16,1024]{2,1,0:T(8,128)S(1)}, u32[]{:S(2)}, u32[]{:S(2)}) collective-permute-start(f32[4,16,1024]{2,1,0:T(8,128)S(1)} %get-tuple-element.53), channel_id=1, source_target_pairs={{0,24},{4,28},{8,16},{12,20},{16,8},{20,12},{24,0},{28,4},{1,25},{... | collective-permute-start | bytes 786440 | tf_op jit(solution)/shard_map/ppermute | solution.py:436
  41.2 1.2 %collective-permute-start.6 = (f32[4,16,1024]{2,1,0:T(8,128)S(1)}, f32[4,16,1024]{2,1,0:T(8,128)S(1)}, u32[]{:S(2)}, u32[]{:S(2)}) collective-permute-start(f32[4,16,1024]{2,1,0:T(8,128)S(1)} %get-tuple-element.51), channel_id=1, source_target_pairs={{0,4},{4,0},{8,12},{12,8},{16,20},{20,16},{24,28},{28,24},{1,5},{5... | collective-permute-start | bytes 786440 | tf_op jit(solution)/shard_map/ppermute | solution.py:435
  42.5 0.2 collective-permute-start.10
  42.7 0.0 collective-permute-done.8.refs_5_
  42.7 6.6 %collective-permute-done.7.refs_4_ = f32[4,16,1024]{2,1,0:T(8,128)S(1)} collective-permute-done((f32[4,16,1024]{2,1,0:T(8,128)S(1)}, f32[4,16,1024]{2,1,0:T(8,128)S(1)}, u32[]{:S(2)}, u32[]{:S(2)}) %collective-permute-start.7) | collective-permute-done | bytes 262176 | tf_op jit(solution)/shard_map/ppermute | solution.py:436
  49.3 1.0 %collective-permute-done.9.refs_6_ = f32[4,16,1024]{2,1,0:T(8,128)S(1)} collective-permute-done((f32[4,16,1024]{2,1,0:T(8,128)S(1)}, f32[4,16,1024]{2,1,0:T(8,128)S(1)}, u32[]{:S(2)}, u32[]{:S(2)}) %collective-permute-start.9) | collective-permute-done | bytes 262176 | tf_op jit(solution)/shard_map/ppermute | solution.py:436
  50.4 0.0 collective-permute-done.6.refs_3_
  50.4 1.2 %collective-permute-done.10.refs_8_ = f32[4,16,1024]{2,1,0:T(8,128)S(1)} collective-permute-done((f32[4,16,1024]{2,1,0:T(8,128)S(1)}, f32[4,16,1024]{2,1,0:T(8,128)S(1)}, u32[]{:S(2)}, u32[]{:S(2)}) %collective-permute-start.10) | collective-permute-done | bytes 262176 | tf_op jit(solution)/shard_map/ppermute | solution.py:435
  51.6 0.7 last.1.refs_2_
  52.3 1.3 %collective-permute-start.13 = (f32[4,16,1024]{2,1,0:T(8,128)S(1)}, f32[4,16,1024]{2,1,0:T(8,128)S(1)}, u32[]{:S(2)}, u32[]{:S(2)}) collective-permute-start(f32[4,16,1024]{2,1,0:T(8,128)S(1)} %last.1.refs_2_), channel_id=1, source_target_pairs={{0,4},{4,0},{8,12},{12,8},{16,20},{20,16},{24,28},{28,24},{1,5},{5... | collective-permute-start | bytes 786440 | tf_op jit(solution)/shard_map/ppermute | solution.py:435
  53.6 2.0 %collective-permute-start.12 = (f32[4,16,1024]{2,1,0:T(8,128)S(1)}, f32[4,16,1024]{2,1,0:T(8,128)S(1)}, u32[]{:S(2)}, u32[]{:S(2)}) collective-permute-start(f32[4,16,1024]{2,1,0:T(8,128)S(1)} %last.1.refs_2_), channel_id=1, source_target_pairs={{0,24},{4,28},{8,16},{12,20},{16,8},{20,12},{24,0},{28,4},{1,25},{... | collective-permute-start | bytes 786440 | tf_op jit(solution)/shard_map/ppermute | solution.py:436
  55.6 0.0 collective-permute-start.11
  55.6 2.1 %collective-permute-done.13.refs_2_ = f32[4,16,1024]{2,1,0:T(8,128)S(1)} collective-permute-done((f32[4,16,1024]{2,1,0:T(8,128)S(1)}, f32[4,16,1024]{2,1,0:T(8,128)S(1)}, u32[]{:S(2)}, u32[]{:S(2)}) %collective-permute-start.13) | collective-permute-done | bytes 262176 | tf_op jit(solution)/shard_map/ppermute | solution.py:435
  57.7 3.1 %collective-permute-done.12.refs_4_ = f32[4,16,1024]{2,1,0:T(8,128)S(1)} collective-permute-done((f32[4,16,1024]{2,1,0:T(8,128)S(1)}, f32[4,16,1024]{2,1,0:T(8,128)S(1)}, u32[]{:S(2)}, u32[]{:S(2)}) %collective-permute-start.12) | collective-permute-done | bytes 262176 | tf_op jit(solution)/shard_map/ppermute | solution.py:436
  60.8 6.3 %collective-permute-done.11.refs_3_ = f32[4,16,1024]{2,1,0:T(8,128)S(1)} collective-permute-done((f32[4,16,1024]{2,1,0:T(8,128)S(1)}, f32[4,16,1024]{2,1,0:T(8,128)S(1)}, u32[]{:S(2)}, u32[]{:S(2)}) %collective-permute-start.11) | collective-permute-done | bytes 262176 | tf_op jit(solution)/shard_map/ppermute | solution.py:436
  67.1 0.0 collective-permute-start.14
  67.1 0.2 collective-permute-start.16
  67.4 1.2 %collective-permute-start.17 = (f32[4,16,1024]{2,1,0:T(8,128)S(1)}, f32[4,16,1024]{2,1,0:T(8,128)S(1)}, u32[]{:S(2)}, u32[]{:S(2)}) collective-permute-start(f32[4,16,1024]{2,1,0:T(8,128)S(1)} %collective-permute-done.12.refs_4_), channel_id=1, source_target_pairs={{0,4},{4,0},{8,12},{12,8},{16,20},{20,16},{24,28},{28,24},{1,5},{5... | collective-permute-start | bytes 786440 | tf_op jit(solution)/shard_map/ppermute | solution.py:435
  68.6 10.6 %collective-permute-done.14.refs_4_ = f32[4,16,1024]{2,1,0:T(8,128)S(1)} collective-permute-done((f32[4,16,1024]{2,1,0:T(8,128)S(1)}, f32[4,16,1024]{2,1,0:T(8,128)S(1)}, u32[]{:S(2)}, u32[]{:S(2)}) %collective-permute-start.14) | collective-permute-done | bytes 262176 | tf_op jit(solution)/shard_map/ppermute | solution.py:436
  79.2 0.2 collective-permute-start.15
  79.5 0.6 spread0.2.refs_5_
  80.1 0.8 spread0.3.refs_5_
  80.8 0.0 collective-permute-done.16.refs_2_
  80.8 0.0 collective-permute-done.17.refs_3_
  80.9 0.7 spread1.1.refs_3_
  81.6 3.5 %collective-permute-done.15.refs_2_ = f32[4,16,1024]{2,1,0:T(8,128)S(1)} collective-permute-done((f32[4,16,1024]{2,1,0:T(8,128)S(1)}, f32[4,16,1024]{2,1,0:T(8,128)S(1)}, u32[]{:S(2)}, u32[]{:S(2)}) %collective-permute-start.15) | collective-permute-done | bytes 262176 | tf_op jit(solution)/shard_map/ppermute | solution.py:435
  85.1 1.6 %spread2.1 = (f32[2,4,8,1024]{3,2,1,0:T(8,128)S(1)}, f32[2,4,8,1024]{3,2,1,0:T(8,128)S(1)}, f32[2,4,8,1024]{3,2,1,0:T(8,128)S(1)}, f32[2,4,8,1024]{3,2,1,0:T(8,128)S(1)}, f32[2,4,16,1024]{3,2,1,0:T(8,128)}) custom-call(s32[4]{0:T(128)S(1)} %copy-done, bf16[4,2,2,4,16,1024]{5,4,3,2,1,0:T(8,128)(2,1)S(1)} %get-tuple-element.38.refs_6_.refs_1_, ...), custom_call_target="tpu_custom_call" | custom-call | flops 524288 | bytes 524288 | tf_op jit(solution)/shard_map/spread2/pallas_call | solution.py:29
  86.7 2.9 %collective-permute-start.19 = (f32[2,4,8,1024]{3,2,1,0:T(8,128)S(1)}, f32[2,4,8,1024]{3,2,1,0:T(8,128)S(1)}, u32[]{:S(2)}, u32[]{:S(2)}) collective-permute-start(f32[2,4,8,1024]{3,2,1,0:T(8,128)S(1)} %get-tuple-element.64), channel_id=1, source_target_pairs={{0,1},{1,0},{2,3},{3,2},{4,5},{5,4},{6,7},{7,6},{8,9},{9,8},{10,11... | collective-permute-start | bytes 786440 | tf_op jit(solution)/shard_map/ppermute | solution.py:404
  89.6 5.0 %collective-permute-start.18 = (f32[2,4,8,1024]{3,2,1,0:T(8,128)S(1)}, f32[2,4,8,1024]{3,2,1,0:T(8,128)S(1)}, u32[]{:S(2)}, u32[]{:S(2)}) collective-permute-start(f32[2,4,8,1024]{3,2,1,0:T(8,128)S(1)} %get-tuple-element.62), channel_id=1, source_target_pairs={{1,2},{2,1},{5,6},{6,5},{9,10},{10,9},{13,14},{14,13},{17,18},{18,... | collective-permute-start | bytes 786440 | tf_op jit(solution)/shard_map/ppermute | solution.py:405
  94.6 0.0 collective-permute-done.19.refs_4_
  94.6 1.3 %adjoint0.1.refs_5_ = f32[2,4,8,1024]{3,2,1,0:T(8,128)S(1)} custom-call(s32[8,128]{1,0:T(8,128)S(1)} %get-tuple-element.40.refs_0_, f32[16,17]{1,0:T(8,128)S(1)} %get-tuple-element.36.refs_1_, f32[2,4,16,1024]{3,2,1,0:T(8,128)S(1)} %get-tuple-element.37.refs_2_, f32[2,4,8,1024]{3,2,1,0:T(8,128)S(1)} %get-tuple-element.63.refs_3_, ...), custom_call_target="tpu_custom_call" | custom-call | flops 524288 | bytes 524288 | tf_op jit(solution)/shard_map/adjoint0/pallas_call | solution.py:29
  95.9 2.7 %collective-permute-done.18.refs_4_ = f32[2,4,8,1024]{3,2,1,0:T(8,128)S(1)} collective-permute-done((f32[2,4,8,1024]{3,2,1,0:T(8,128)S(1)}, f32[2,4,8,1024]{3,2,1,0:T(8,128)S(1)}, u32[]{:S(2)}, u32[]{:S(2)}) %collective-permute-start.18) | collective-permute-done | bytes 262176 | tf_op jit(solution)/shard_map/ppermute | solution.py:405
  98.7 2.0 %adjoint1.1 = f32[2,4,16,1024]{3,2,1,0:T(8,128)} custom-call(s32[8,128]{1,0:T(8,128)S(1)} %get-tuple-element.35.refs_0_, f32[16,17]{1,0:T(8,128)S(1)} %get-tuple-element.36.refs_1_, f32[2,4,16,1024]{3,2,1,0:T(8,128)S(1)} %get-tuple-element.37.refs_2_, f32[2,4,8,1024]{3,2,1,0:T(8,128)S(1)} %get-tuple-element.61.refs_3_, ...), custom_call_target="tpu_custom_call" | custom-call | flops 524288 | bytes 524288 | tf_op jit(solution)/shard_map/adjoint1/pallas_call | solution.py:29
Async XLA Ops:
  0.0 13.7 %copy-start.1 = (f32[16,4,4]{0,2,1:T(4,128)S(1)}, f32[16,4,4]{0,2,1:T(4,128)}, u32[]{:S(2)}) copy-start(f32[16,4,4]{0,2,1:T(4,128)} %param.15) | copy-start | bytes 3076
  0.0 14.0 %copy-start = (s32[4]{0:T(128)S(1)}, s32[4]{0:T(128)}, u32[]{:S(2)}) copy-start(s32[4]{0:T(128)} %refs_0_.21) | copy-start | bytes 52
  3.2 10.6 %collective-permute-start = (f32[2,4,8,1024]{3,2,1,0:T(8,128)}, f32[2,4,8,1024]{3,2,1,0:T(8,128)}, u32[]{:S(2)}, u32[]{:S(2)}) collective-permute-start(f32[2,4,8,1024]{3,2,1,0:T(8,128)} %get-tuple-element.41.refs_3_), channel_id=1, source_target_pairs={{1,2},{2,1},{5,6},{6,5},{9,10},{10,9},{13,14},{14,13},{17,18},{18,... | collective-permute-start | bytes 786440 | tf_op jit(solution)/shard_map/ppermute | solution.py:405
  9.0 5.0 %collective-permute-start.1 = (f32[2,4,8,1024]{3,2,1,0:T(8,128)S(1)}, f32[2,4,8,1024]{3,2,1,0:T(8,128)}, u32[]{:S(2)}, u32[]{:S(2)}) collective-permute-start(f32[2,4,8,1024]{3,2,1,0:T(8,128)S(1)} %core.1.refs_2_), channel_id=1, source_target_pairs={{0,1},{1,0},{2,3},{3,2},{4,5},{5,4},{6,7},{7,6},{8,9},{9,8},{10,11... | collective-permute-start | bytes 786440 | tf_op jit(solution)/shard_map/ppermute | solution.py:404
  9.1 8.0 %collective-permute-start.3 = (f32[2,4,16,1024]{3,2,1,0:T(8,128)}, f32[2,4,16,1024]{3,2,1,0:T(8,128)S(1)}, u32[]{:S(2)}, u32[]{:S(2)}) collective-permute-start(f32[2,4,16,1024]{3,2,1,0:T(8,128)} %get-tuple-element.44.refs_1_), channel_id=1, source_target_pairs={{8,16},{12,20},{16,8},{20,12},{9,17},{13,21},{17,9},{21,13},{10,18... | collective-permute-start | bytes 1572872 | tf_op jit(solution)/shard_map/ppermute | solution.py:441
  9.8 15.7 %collective-permute-start.2 = (f32[2,4,16,1024]{3,2,1,0:T(8,128)}, f32[2,4,16,1024]{3,2,1,0:T(8,128)}, u32[]{:S(2)}, u32[]{:S(2)}) collective-permute-start(f32[2,4,16,1024]{3,2,1,0:T(8,128)} %get-tuple-element.44.refs_1_), channel_id=1, source_target_pairs={{0,8},{4,12},{8,0},{12,4},{16,24},{20,28},{24,16},{28,20},{1,9},{5... | collective-permute-start | bytes 1572872 | tf_op jit(solution)/shard_map/ppermute | solution.py:436
  15.8 10.5 %collective-permute-start.4 = (f32[4,16,1024]{2,1,0:T(8,128)S(1)}, f32[4,16,1024]{2,1,0:T(8,128)S(1)}, u32[]{:S(2)}, u32[]{:S(2)}) collective-permute-start(f32[4,16,1024]{2,1,0:T(8,128)S(1)} %get-tuple-element.47), channel_id=1, source_target_pairs={{0,4},{4,0},{8,12},{12,8},{16,20},{20,16},{24,28},{28,24},{1,5},{5... | collective-permute-start | bytes 786440 | tf_op jit(solution)/shard_map/ppermute | solution.py:435
  26.3 12.1 %collective-permute-start.5 = (f32[2,4,16,1024]{3,2,1,0:T(8,128)S(1)}, f32[2,4,16,1024]{3,2,1,0:T(8,128)S(1)}, u32[]{:S(2)}, u32[]{:S(2)}) collective-permute-start(f32[2,4,16,1024]{3,2,1,0:T(8,128)S(1)} %get-tuple-element.50), channel_id=1, source_target_pairs={{0,4},{4,0},{8,12},{12,8},{16,20},{20,16},{24,28},{28,24},{1,5},{5... | collective-permute-start | bytes 1572872 | tf_op jit(solution)/shard_map/ppermute | solution.py:435
  28.2 14.5 %collective-permute-start.8 = (f32[4,16,1024]{2,1,0:T(8,128)S(1)}, f32[4,16,1024]{2,1,0:T(8,128)S(1)}, u32[]{:S(2)}, u32[]{:S(2)}) collective-permute-start(f32[4,16,1024]{2,1,0:T(8,128)S(1)} %meet2.1.refs_4_), channel_id=1, source_target_pairs={{0,16},{4,20},{8,24},{12,28},{16,0},{20,4},{24,8},{28,12},{1,17},{... | collective-permute-start | bytes 786440 | tf_op jit(solution)/shard_map/ppermute | solution.py:436
  39.2 10.2 %collective-permute-start.7 = (f32[4,16,1024]{2,1,0:T(8,128)S(1)}, f32[4,16,1024]{2,1,0:T(8,128)S(1)}, u32[]{:S(2)}, u32[]{:S(2)}) collective-permute-start(f32[4,16,1024]{2,1,0:T(8,128)S(1)} %get-tuple-element.52), channel_id=1, source_target_pairs={{0,8},{4,12},{8,0},{12,4},{16,24},{20,28},{24,16},{28,20},{1,9},{5... | collective-permute-start | bytes 786440 | tf_op jit(solution)/shard_map/ppermute | solution.py:436
  40.0 10.3 %collective-permute-start.9 = (f32[4,16,1024]{2,1,0:T(8,128)S(1)}, f32[4,16,1024]{2,1,0:T(8,128)S(1)}, u32[]{:S(2)}, u32[]{:S(2)}) collective-permute-start(f32[4,16,1024]{2,1,0:T(8,128)S(1)} %get-tuple-element.53), channel_id=1, source_target_pairs={{0,24},{4,28},{8,16},{12,20},{16,8},{20,12},{24,0},{28,4},{1,25},{... | collective-permute-start | bytes 786440 | tf_op jit(solution)/shard_map/ppermute | solution.py:436
  41.2 9.1 %collective-permute-start.6 = (f32[4,16,1024]{2,1,0:T(8,128)S(1)}, f32[4,16,1024]{2,1,0:T(8,128)S(1)}, u32[]{:S(2)}, u32[]{:S(2)}) collective-permute-start(f32[4,16,1024]{2,1,0:T(8,128)S(1)} %get-tuple-element.51), channel_id=1, source_target_pairs={{0,4},{4,0},{8,12},{12,8},{16,20},{20,16},{24,28},{28,24},{1,5},{5... | collective-permute-start | bytes 786440 | tf_op jit(solution)/shard_map/ppermute | solution.py:435
  42.5 9.1 %collective-permute-start.10 = (f32[4,16,1024]{2,1,0:T(8,128)S(1)}, f32[4,16,1024]{2,1,0:T(8,128)S(1)}, u32[]{:S(2)}, u32[]{:S(2)}) collective-permute-start(f32[4,16,1024]{2,1,0:T(8,128)S(1)} %get-tuple-element.55.refs_5_), channel_id=1, source_target_pairs={{0,4},{4,0},{8,12},{12,8},{16,20},{20,16},{24,28},{28,24},{1,5},{5... | collective-permute-start | bytes 786440 | tf_op jit(solution)/shard_map/ppermute | solution.py:435
  52.3 5.4 %collective-permute-start.13 = (f32[4,16,1024]{2,1,0:T(8,128)S(1)}, f32[4,16,1024]{2,1,0:T(8,128)S(1)}, u32[]{:S(2)}, u32[]{:S(2)}) collective-permute-start(f32[4,16,1024]{2,1,0:T(8,128)S(1)} %last.1.refs_2_), channel_id=1, source_target_pairs={{0,4},{4,0},{8,12},{12,8},{16,20},{20,16},{24,28},{28,24},{1,5},{5... | collective-permute-start | bytes 786440 | tf_op jit(solution)/shard_map/ppermute | solution.py:435
  53.6 7.2 %collective-permute-start.12 = (f32[4,16,1024]{2,1,0:T(8,128)S(1)}, f32[4,16,1024]{2,1,0:T(8,128)S(1)}, u32[]{:S(2)}, u32[]{:S(2)}) collective-permute-start(f32[4,16,1024]{2,1,0:T(8,128)S(1)} %last.1.refs_2_), channel_id=1, source_target_pairs={{0,24},{4,28},{8,16},{12,20},{16,8},{20,12},{24,0},{28,4},{1,25},{... | collective-permute-start | bytes 786440 | tf_op jit(solution)/shard_map/ppermute | solution.py:436
  55.6 11.5 %collective-permute-start.11 = (f32[4,16,1024]{2,1,0:T(8,128)S(1)}, f32[4,16,1024]{2,1,0:T(8,128)S(1)}, u32[]{:S(2)}, u32[]{:S(2)}) collective-permute-start(f32[4,16,1024]{2,1,0:T(8,128)S(1)} %last.1.refs_2_), channel_id=1, source_target_pairs={{0,8},{4,12},{8,0},{12,4},{16,24},{20,28},{24,16},{28,20},{1,9},{5... | collective-permute-start | bytes 786440 | tf_op jit(solution)/shard_map/ppermute | solution.py:436
  67.1 12.1 %collective-permute-start.14 = (f32[4,16,1024]{2,1,0:T(8,128)S(1)}, f32[4,16,1024]{2,1,0:T(8,128)S(1)}, u32[]{:S(2)}, u32[]{:S(2)}) collective-permute-start(f32[4,16,1024]{2,1,0:T(8,128)S(1)} %last.1.refs_2_), channel_id=1, source_target_pairs={{0,16},{4,20},{8,24},{12,28},{16,0},{20,4},{24,8},{28,12},{1,17},{... | collective-permute-start | bytes 786440 | tf_op jit(solution)/shard_map/ppermute | solution.py:436
  67.1 13.7 %collective-permute-start.16 = (f32[4,16,1024]{2,1,0:T(8,128)S(1)}, f32[4,16,1024]{2,1,0:T(8,128)S(1)}, u32[]{:S(2)}, u32[]{:S(2)}) collective-permute-start(f32[4,16,1024]{2,1,0:T(8,128)S(1)} %collective-permute-done.11.refs_3_), channel_id=1, source_target_pairs={{0,4},{4,0},{8,12},{12,8},{16,20},{20,16},{24,28},{28,24},{1,5},{5... | collective-permute-start | bytes 786440 | tf_op jit(solution)/shard_map/ppermute | solution.py:435
  67.4 13.5 %collective-permute-start.17 = (f32[4,16,1024]{2,1,0:T(8,128)S(1)}, f32[4,16,1024]{2,1,0:T(8,128)S(1)}, u32[]{:S(2)}, u32[]{:S(2)}) collective-permute-start(f32[4,16,1024]{2,1,0:T(8,128)S(1)} %collective-permute-done.12.refs_4_), channel_id=1, source_target_pairs={{0,4},{4,0},{8,12},{12,8},{16,20},{20,16},{24,28},{28,24},{1,5},{5... | collective-permute-start | bytes 786440 | tf_op jit(solution)/shard_map/ppermute | solution.py:435
  79.2 5.8 %collective-permute-start.15 = (f32[4,16,1024]{2,1,0:T(8,128)S(1)}, f32[4,16,1024]{2,1,0:T(8,128)S(1)}, u32[]{:S(2)}, u32[]{:S(2)}) collective-permute-start(f32[4,16,1024]{2,1,0:T(8,128)S(1)} %collective-permute-done.14.refs_4_), channel_id=1, source_target_pairs={{0,4},{4,0},{8,12},{12,8},{16,20},{20,16},{24,28},{28,24},{1,5},{5... | collective-permute-start | bytes 786440 | tf_op jit(solution)/shard_map/ppermute | solution.py:435
  86.7 7.9 %collective-permute-start.19 = (f32[2,4,8,1024]{3,2,1,0:T(8,128)S(1)}, f32[2,4,8,1024]{3,2,1,0:T(8,128)S(1)}, u32[]{:S(2)}, u32[]{:S(2)}) collective-permute-start(f32[2,4,8,1024]{3,2,1,0:T(8,128)S(1)} %get-tuple-element.64), channel_id=1, source_target_pairs={{0,1},{1,0},{2,3},{3,2},{4,5},{5,4},{6,7},{7,6},{8,9},{9,8},{10,11... | collective-permute-start | bytes 786440 | tf_op jit(solution)/shard_map/ppermute | solution.py:404
  89.6 9.1 %collective-permute-start.18 = (f32[2,4,8,1024]{3,2,1,0:T(8,128)S(1)}, f32[2,4,8,1024]{3,2,1,0:T(8,128)S(1)}, u32[]{:S(2)}, u32[]{:S(2)}) collective-permute-start(f32[2,4,8,1024]{3,2,1,0:T(8,128)S(1)} %get-tuple-element.62), channel_id=1, source_target_pairs={{1,2},{2,1},{5,6},{6,5},{9,10},{10,9},{13,14},{14,13},{17,18},{18,... | collective-permute-start | bytes 786440 | tf_op jit(solution)/shard_map/ppermute | solution.py:405

commit v5 on v4

--- a/solution.py
+++ b/solution.py
@@ -159,6 +159,7 @@
     ]
     moves.append((r["control"].at[:, :, rows_core], r["control_v"].at[:, :, rows_core]))
     moves.append((r["meridional"], r["meridional_v"]))
+    moves.append((r["mixing"], r["mixing_v"]))
     if "obs" in r:
         moves.append((r["obs"].at[0], r["obs_v"]))
     moves.append((r["ens"], r["ens_v"]))
@@ -219,11 +220,16 @@
     for k in range(BAND):
         band = jnp.where(reach == k, taps_ref[:, k : k + 1], band)
     band = jnp.where((block == 3) & alone, 0.0, band)
+    same = lax.broadcasted_iota(jnp.int32, (band_rows, band_rows), 0) == (
+        lax.broadcasted_iota(jnp.int32, (band_rows, band_rows), 1)
+    )
     for a in range(levels):
-        mixing = mixing_ref[a * band_rows : (a + 1) * band_rows, :]
+        mixing = mixing_ref[a]
         factor = jnp.zeros((band_rows, columns), F32)
         for b in range(levels):
-            factor = jnp.where(level == b, mixing[:, b : b + 1], factor)
+            by_lane = jnp.broadcast_to(mixing[b : b + 1, :], (band_rows, band_rows))
+            by_row = jnp.sum(jnp.where(same, by_lane, 0.0), axis=1, keepdims=True)
+            factor = jnp.where(level == b, by_row, factor)
         matrix[a * band_rows : (a + 1) * band_rows, :] = factor * band
     transposed[...] = matrix[...].T
 
@@ -407,6 +413,7 @@
     ins = {
         "shift": zonal_shift, "taps": zonal_taps, "control": control,
         "meridional": meridional_taps, "ens": perturbations,
+        "mixing": jnp.transpose(level_mixing, (1, 2, 0)),
     }
     results = {
         "near_x": shape(*half_shape), "control_v": shape(*field_shape),
@@ -414,6 +421,7 @@
         "shift_x": shape(8, LANES, dtype=jnp.int32),
         "shift_core": shape(8, LANES, dtype=jnp.int32),
         "ens_v": shape(*perturbations.shape, dtype=BF16),
+        "mixing_v": shape(levels, levels, band_rows),
     }
     if direct:
         ins["obs"] = obs_weight
@@ -424,7 +432,7 @@
         *(pltpu.with_memory_space_constraint(v, pltpu.HBM) for v in ins.values()),
         specs=(HBM,) * len(ins),
         scratch=[
-            *tap_room, pltpu.SMEM(zonal_shift.shape, jnp.int32), pltpu.SemaphoreType.DMA((7,)),
+            *tap_room, pltpu.SMEM(zonal_shift.shape, jnp.int32), pltpu.SemaphoreType.DMA((8,)),
         ],
     )
     made = dict(zip(results, made))
@@ -444,11 +452,10 @@
         control_v, specs=(VMEM,) * 3, scratch=tap_room,
     )
     far_core = swap_core(near_core)
-    mixing = jnp.transpose(level_mixing, (1, 0, 2)).reshape(levels * band_rows, levels)
     matrix, transposed = call(
         functools.partial(build_matrix, lat_count),
         (shape(levels * band_rows, 32 * levels), shape(32 * levels, levels * band_rows)),
-        "matrix", 1 << 16, made["meridional_v"], mixing, specs=(VMEM, VMEM), after=(near_core, far_x),
+        "matrix", 1 << 16, made["meridional_v"], made["mixing_v"], specs=(VMEM, VMEM), after=(near_core, far_x),
     )
     parts = (near_core, near_x, far_core, far_x)
 

time: 101 us -> 99.6 us (0.986)
  Pallas kernels: 17.5 us -> 14.9 us
  waiting for transfers between devices: 53.5 us -> 54.9 us
    pallas_call x15, Pallas kernels: 17.5 us -> 14.9 us  [call(): pl.pallas_call(kernel, out_shape=outs, in_specs=list(specs) + [ANY] * ext...]
  transfers between devices with their start and end apart: 20 -> 20, of which waited for: 11 -> 11; matrix products, arithmetic and copies ran while one was open for 0% -> 0% of each run, Pallas kernels for 9% -> 8%
where the time goes in v5:
time: 99.6 us; the launch traced here: 99.4 us
  waiting for transfers between devices  54.9 us (55%)
  starting transfers between devices  29.5 us (30%)
  Pallas kernels  14.9 us (15%)
    ppermute x7, waiting for transfers between devices, per_device(): lax.ppermute(v, 'mem', [(i, i ^ 2 * s) for i in range(mem_count)])  36.9 us
    ppermute x8, waiting for transfers between devices, per_device(): swap_y = lambda v: lax.ppermute(v, 'mem', y_pairs)  15.2 us
    pallas_call x15, Pallas kernels, call(): pl.pallas_call(kernel, out_shape=outs, in_specs=list(specs) + [ANY] * ext...  14.9 us
    ppermute x2, starting transfers between devices, per_device(): swap_x = lambda v: lax.ppermute(v, 'lat', x_pairs)  9.6 us
    ppermute x7, starting transfers between devices, per_device(): lax.ppermute(v, 'mem', [(i, i ^ 2 * s) for i in range(mem_count)])  9.13 us
    ppermute x8, starting transfers between devices, per_device(): swap_y = lambda v: lax.ppermute(v, 'mem', y_pairs)  7.07 us
    ppermute x2, starting transfers between devices, per_device(): swap_core = lambda v: lax.ppermute(v, 'lat', core_pairs)  2.97 us
    ppermute x2, waiting for transfers between devices, per_device(): swap_x = lambda v: lax.ppermute(v, 'lat', x_pairs)  2.74 us
  transfers between devices with their start and end apart: 20, of which 11 were waited for; matrix products, arithmetic and copies ran while one was open for 0% of the time, Pallas kernels for 8%

profile of v5, /device:TPU:1, one launch (start us, length us, event | category | flops | bytes accessed | tf_op | source)
XLA Modules:
  0.0 99.4 jit_solution(13144104281316605508)
XLA Ops:
  0.0 0.0 copy-start
  0.0 2.3 %front.1 = (f32[2,4,8,1024]{3,2,1,0:T(8,128)S(1)}, f32[2,4,16,1024]{3,2,1,0:T(8,128)S(1)}, f32[16,17]{1,0:T(8,128)S(1)}, f32[16,17]{1,0:T(8,128)S(1)}, s32[8,128...) custom-call(s32[16]{0:T(128)} %refs_0_.11, ...), custom_call_target="tpu_custom_call" | custom-call | flops 524288 | bytes 524288 | tf_op jit(solution)/shard_map/front/pallas_call | solution.py:29
  2.3 4.5 %collective-permute-start = (f32[2,4,8,1024]{3,2,1,0:T(8,128)S(1)}, f32[2,4,8,1024]{3,2,1,0:T(8,128)S(1)}, u32[]{:S(2)}, u32[]{:S(2)}) collective-permute-start(f32[2,4,8,1024]{3,2,1,0:T(8,128)S(1)} %get-tuple-element.43.refs_3_), channel_id=1, source_target_pairs={{1,2},{2,1},{5,6},{6,5},{9,10},{10,9},{13,14},{14,13},{17,18},{18,... | collective-permute-start | bytes 786440 | tf_op jit(solution)/shard_map/ppermute | solution.py:411
  6.9 1.3 %core.1.refs_2_ = f32[2,4,8,1024]{3,2,1,0:T(8,128)S(1)} custom-call(s32[8,128]{1,0:T(8,128)S(1)} %get-tuple-element.42.refs_0_, f32[16,17]{1,0:T(8,128)S(1)} %get-tuple-element.37.refs_1_, f32[2,4,16,1024]{3,2,1,0:T(8,128)S(1)} %get-tuple-element.38.refs_2_), custom_call_target="tpu_custom_call" | custom-call | flops 524288 | bytes 524288 | tf_op jit(solution)/shard_map/core/pallas_call | solution.py:29
  8.1 0.1 collective-permute-start.1
  8.2 0.7 collective-permute-start.3
  8.9 3.9 %collective-permute-start.2 = (f32[2,4,16,1024]{3,2,1,0:T(8,128)S(1)}, f32[2,4,16,1024]{3,2,1,0:T(8,128)S(1)}, u32[]{:S(2)}, u32[]{:S(2)}) collective-permute-start(f32[2,4,16,1024]{3,2,1,0:T(8,128)S(1)} %get-tuple-element.46.refs_1_), channel_id=1, source_target_pairs={{0,8},{4,12},{8,0},{12,4},{16,24},{20,28},{24,16},{28,20},{1,9},{5... | collective-permute-start | bytes 1572872 | tf_op jit(solution)/shard_map/ppermute | solution.py:444
  12.8 0.0 collective-permute-done.refs_3_.refs_5_
  12.8 0.3 matrix.1
  13.1 0.0 collective-permute-done.1.refs_4_
  13.2 0.0 copy-done
  13.2 0.6 first.1
  13.8 1.3 %collective-permute-start.4 = (f32[4,16,1024]{2,1,0:T(8,128)S(1)}, f32[4,16,1024]{2,1,0:T(8,128)S(1)}, u32[]{:S(2)}, u32[]{:S(2)}) collective-permute-start(f32[4,16,1024]{2,1,0:T(8,128)S(1)} %get-tuple-element.49), channel_id=1, source_target_pairs={{0,4},{4,0},{8,12},{12,8},{16,20},{20,16},{24,28},{28,24},{1,5},{5... | collective-permute-start | bytes 786440 | tf_op jit(solution)/shard_map/ppermute | solution.py:443
  15.1 0.0 collective-permute-done.3.refs_4_.refs_3_
  15.1 9.2 %collective-permute-done.2.refs_3_.refs_2_ = f32[2,4,16,1024]{3,2,1,0:T(8,128)S(1)} collective-permute-done((f32[2,4,16,1024]{3,2,1,0:T(8,128)S(1)}, f32[2,4,16,1024]{3,2,1,0:T(8,128)S(1)}, u32[]{:S(2)}, u32[]{:S(2)}) %collective-permute-start.2) | collective-permute-done | bytes 524320 | tf_op jit(solution)/shard_map/ppermute | solution.py:444
  24.3 0.7 send.1
  25.0 0.0 collective-permute-done.4.refs_3_
  25.0 1.3 %collective-permute-start.5 = (f32[2,4,16,1024]{3,2,1,0:T(8,128)S(1)}, f32[2,4,16,1024]{3,2,1,0:T(8,128)S(1)}, u32[]{:S(2)}, u32[]{:S(2)}) collective-permute-start(f32[2,4,16,1024]{3,2,1,0:T(8,128)S(1)} %get-tuple-element.52), channel_id=1, source_target_pairs={{0,4},{4,0},{8,12},{12,8},{16,20},{20,16},{24,28},{28,24},{1,5},{5... | collective-permute-start | bytes 1572872 | tf_op jit(solution)/shard_map/ppermute | solution.py:443
  26.4 0.6 meet2.1.refs_4_
  27.0 1.2 %collective-permute-start.8 = (f32[4,16,1024]{2,1,0:T(8,128)S(1)}, f32[4,16,1024]{2,1,0:T(8,128)S(1)}, u32[]{:S(2)}, u32[]{:S(2)}) collective-permute-start(f32[4,16,1024]{2,1,0:T(8,128)S(1)} %meet2.1.refs_4_), channel_id=1, source_target_pairs={{0,16},{4,20},{8,24},{12,28},{16,0},{20,4},{24,8},{28,12},{1,17},{... | collective-permute-start | bytes 786440 | tf_op jit(solution)/shard_map/ppermute | solution.py:444
  28.1 0.6 weight_pick.1
  28.8 8.4 %collective-permute-done.5.refs_3_ = f32[2,4,16,1024]{3,2,1,0:T(8,128)S(1)} collective-permute-done((f32[2,4,16,1024]{3,2,1,0:T(8,128)S(1)}, f32[2,4,16,1024]{3,2,1,0:T(8,128)S(1)}, u32[]{:S(2)}, u32[]{:S(2)}) %collective-permute-start.5) | collective-permute-done | bytes 524320 | tf_op jit(solution)/shard_map/ppermute | solution.py:443
  37.2 0.7 meet13.1
  37.9 0.9 collective-permute-start.7
  38.8 1.2 %collective-permute-start.9 = (f32[4,16,1024]{2,1,0:T(8,128)S(1)}, f32[4,16,1024]{2,1,0:T(8,128)S(1)}, u32[]{:S(2)}, u32[]{:S(2)}) collective-permute-start(f32[4,16,1024]{2,1,0:T(8,128)S(1)} %get-tuple-element.55), channel_id=1, source_target_pairs={{0,24},{4,28},{8,16},{12,20},{16,8},{20,12},{24,0},{28,4},{1,25},{... | collective-permute-start | bytes 786440 | tf_op jit(solution)/shard_map/ppermute | solution.py:444
  40.0 1.2 %collective-permute-start.6 = (f32[4,16,1024]{2,1,0:T(8,128)S(1)}, f32[4,16,1024]{2,1,0:T(8,128)S(1)}, u32[]{:S(2)}, u32[]{:S(2)}) collective-permute-start(f32[4,16,1024]{2,1,0:T(8,128)S(1)} %get-tuple-element.53), channel_id=1, source_target_pairs={{0,4},{4,0},{8,12},{12,8},{16,20},{20,16},{24,28},{28,24},{1,5},{5... | collective-permute-start | bytes 786440 | tf_op jit(solution)/shard_map/ppermute | solution.py:443
  41.2 0.2 collective-permute-start.10
  41.4 0.0 collective-permute-done.8.refs_5_
  41.5 6.6 %collective-permute-done.7.refs_4_ = f32[4,16,1024]{2,1,0:T(8,128)S(1)} collective-permute-done((f32[4,16,1024]{2,1,0:T(8,128)S(1)}, f32[4,16,1024]{2,1,0:T(8,128)S(1)}, u32[]{:S(2)}, u32[]{:S(2)}) %collective-permute-start.7) | collective-permute-done | bytes 262176 | tf_op jit(solution)/shard_map/ppermute | solution.py:444
  48.0 1.1 %collective-permute-done.9.refs_6_ = f32[4,16,1024]{2,1,0:T(8,128)S(1)} collective-permute-done((f32[4,16,1024]{2,1,0:T(8,128)S(1)}, f32[4,16,1024]{2,1,0:T(8,128)S(1)}, u32[]{:S(2)}, u32[]{:S(2)}) %collective-permute-start.9) | collective-permute-done | bytes 262176 | tf_op jit(solution)/shard_map/ppermute | solution.py:444
  49.1 0.0 collective-permute-done.6.refs_3_
  49.1 1.2 %collective-permute-done.10.refs_8_ = f32[4,16,1024]{2,1,0:T(8,128)S(1)} collective-permute-done((f32[4,16,1024]{2,1,0:T(8,128)S(1)}, f32[4,16,1024]{2,1,0:T(8,128)S(1)}, u32[]{:S(2)}, u32[]{:S(2)}) %collective-permute-start.10) | collective-permute-done | bytes 262176 | tf_op jit(solution)/shard_map/ppermute | solution.py:443
  50.3 0.7 last.1.refs_2_
  51.0 1.3 %collective-permute-start.13 = (f32[4,16,1024]{2,1,0:T(8,128)S(1)}, f32[4,16,1024]{2,1,0:T(8,128)S(1)}, u32[]{:S(2)}, u32[]{:S(2)}) collective-permute-start(f32[4,16,1024]{2,1,0:T(8,128)S(1)} %last.1.refs_2_), channel_id=1, source_target_pairs={{0,4},{4,0},{8,12},{12,8},{16,20},{20,16},{24,28},{28,24},{1,5},{5... | collective-permute-start | bytes 786440 | tf_op jit(solution)/shard_map/ppermute | solution.py:443
  52.3 2.0 %collective-permute-start.12 = (f32[4,16,1024]{2,1,0:T(8,128)S(1)}, f32[4,16,1024]{2,1,0:T(8,128)S(1)}, u32[]{:S(2)}, u32[]{:S(2)}) collective-permute-start(f32[4,16,1024]{2,1,0:T(8,128)S(1)} %last.1.refs_2_), channel_id=1, source_target_pairs={{0,24},{4,28},{8,16},{12,20},{16,8},{20,12},{24,0},{28,4},{1,25},{... | collective-permute-start | bytes 786440 | tf_op jit(solution)/shard_map/ppermute | solution.py:444
  54.3 0.0 collective-permute-start.11
  54.3 2.1 %collective-permute-done.13.refs_2_ = f32[4,16,1024]{2,1,0:T(8,128)S(1)} collective-permute-done((f32[4,16,1024]{2,1,0:T(8,128)S(1)}, f32[4,16,1024]{2,1,0:T(8,128)S(1)}, u32[]{:S(2)}, u32[]{:S(2)}) %collective-permute-start.13) | collective-permute-done | bytes 262176 | tf_op jit(solution)/shard_map/ppermute | solution.py:443
  56.4 3.1 %collective-permute-done.12.refs_4_ = f32[4,16,1024]{2,1,0:T(8,128)S(1)} collective-permute-done((f32[4,16,1024]{2,1,0:T(8,128)S(1)}, f32[4,16,1024]{2,1,0:T(8,128)S(1)}, u32[]{:S(2)}, u32[]{:S(2)}) %collective-permute-start.12) | collective-permute-done | bytes 262176 | tf_op jit(solution)/shard_map/ppermute | solution.py:444
  59.5 6.3 %collective-permute-done.11.refs_3_ = f32[4,16,1024]{2,1,0:T(8,128)S(1)} collective-permute-done((f32[4,16,1024]{2,1,0:T(8,128)S(1)}, f32[4,16,1024]{2,1,0:T(8,128)S(1)}, u32[]{:S(2)}, u32[]{:S(2)}) %collective-permute-start.11) | collective-permute-done | bytes 262176 | tf_op jit(solution)/shard_map/ppermute | solution.py:444
  65.8 0.0 collective-permute-start.14
  65.8 0.2 collective-permute-start.16
  66.1 1.2 %collective-permute-start.17 = (f32[4,16,1024]{2,1,0:T(8,128)S(1)}, f32[4,16,1024]{2,1,0:T(8,128)S(1)}, u32[]{:S(2)}, u32[]{:S(2)}) collective-permute-start(f32[4,16,1024]{2,1,0:T(8,128)S(1)} %collective-permute-done.12.refs_4_), channel_id=1, source_target_pairs={{0,4},{4,0},{8,12},{12,8},{16,20},{20,16},{24,28},{28,24},{1,5},{5... | collective-permute-start | bytes 786440 | tf_op jit(solution)/shard_map/ppermute | solution.py:443
  67.3 10.6 %collective-permute-done.14.refs_4_ = f32[4,16,1024]{2,1,0:T(8,128)S(1)} collective-permute-done((f32[4,16,1024]{2,1,0:T(8,128)S(1)}, f32[4,16,1024]{2,1,0:T(8,128)S(1)}, u32[]{:S(2)}, u32[]{:S(2)}) %collective-permute-start.14) | collective-permute-done | bytes 262176 | tf_op jit(solution)/shard_map/ppermute | solution.py:444
  77.9 0.2 collective-permute-start.15
  78.2 0.6 spread0.2.refs_5_
  78.8 0.7 spread0.3.refs_5_
  79.5 0.0 collective-permute-done.16.refs_2_
  79.5 0.0 collective-permute-done.17.refs_3_
  79.5 0.8 spread1.1.refs_3_
  80.3 3.5 %collective-permute-done.15.refs_2_ = f32[4,16,1024]{2,1,0:T(8,128)S(1)} collective-permute-done((f32[4,16,1024]{2,1,0:T(8,128)S(1)}, f32[4,16,1024]{2,1,0:T(8,128)S(1)}, u32[]{:S(2)}, u32[]{:S(2)}) %collective-permute-start.15) | collective-permute-done | bytes 262176 | tf_op jit(solution)/shard_map/ppermute | solution.py:443
  83.8 1.6 %spread2.1 = (f32[2,4,8,1024]{3,2,1,0:T(8,128)S(1)}, f32[2,4,8,1024]{3,2,1,0:T(8,128)S(1)}, f32[2,4,8,1024]{3,2,1,0:T(8,128)S(1)}, f32[2,4,8,1024]{3,2,1,0:T(8,128)S(1)}, f32[2,4,16,1024]{3,2,1,0:T(8,128)}) custom-call(s32[4]{0:T(128)S(1)} %copy-done, bf16[4,2,2,4,16,1024]{5,4,3,2,1,0:T(8,128)(2,1)S(1)} %get-tuple-element.39.refs_6_.refs_1_, ...), custom_call_target="tpu_custom_call" | custom-call | flops 524288 | bytes 524288 | tf_op jit(solution)/shard_map/spread2/pallas_call | solution.py:29
  85.4 2.9 %collective-permute-start.19 = (f32[2,4,8,1024]{3,2,1,0:T(8,128)S(1)}, f32[2,4,8,1024]{3,2,1,0:T(8,128)S(1)}, u32[]{:S(2)}, u32[]{:S(2)}) collective-permute-start(f32[2,4,8,1024]{3,2,1,0:T(8,128)S(1)} %get-tuple-element.66), channel_id=1, source_target_pairs={{0,1},{1,0},{2,3},{3,2},{4,5},{5,4},{6,7},{7,6},{8,9},{9,8},{10,11... | collective-permute-start | bytes 786440 | tf_op jit(solution)/shard_map/ppermute | solution.py:410
  88.3 5.1 %collective-permute-start.18 = (f32[2,4,8,1024]{3,2,1,0:T(8,128)S(1)}, f32[2,4,8,1024]{3,2,1,0:T(8,128)S(1)}, u32[]{:S(2)}, u32[]{:S(2)}) collective-permute-start(f32[2,4,8,1024]{3,2,1,0:T(8,128)S(1)} %get-tuple-element.64), channel_id=1, source_target_pairs={{1,2},{2,1},{5,6},{6,5},{9,10},{10,9},{13,14},{14,13},{17,18},{18,... | collective-permute-start | bytes 786440 | tf_op jit(solution)/shard_map/ppermute | solution.py:411
  93.4 0.0 collective-permute-done.19.refs_4_
  93.4 1.3 %adjoint0.1.refs_5_ = f32[2,4,8,1024]{3,2,1,0:T(8,128)S(1)} custom-call(s32[8,128]{1,0:T(8,128)S(1)} %get-tuple-element.42.refs_0_, f32[16,17]{1,0:T(8,128)S(1)} %get-tuple-element.37.refs_1_, f32[2,4,16,1024]{3,2,1,0:T(8,128)S(1)} %get-tuple-element.38.refs_2_, f32[2,4,8,1024]{3,2,1,0:T(8,128)S(1)} %get-tuple-element.65.refs_3_, ...), custom_call_target="tpu_custom_call" | custom-call | flops 524288 | bytes 524288 | tf_op jit(solution)/shard_map/adjoint0/pallas_call | solution.py:29
  94.7 2.7 %collective-permute-done.18.refs_4_ = f32[2,4,8,1024]{3,2,1,0:T(8,128)S(1)} collective-permute-done((f32[2,4,8,1024]{3,2,1,0:T(8,128)S(1)}, f32[2,4,8,1024]{3,2,1,0:T(8,128)S(1)}, u32[]{:S(2)}, u32[]{:S(2)}) %collective-permute-start.18) | collective-permute-done | bytes 262176 | tf_op jit(solution)/shard_map/ppermute | solution.py:411
  97.4 2.0 %adjoint1.1 = f32[2,4,16,1024]{3,2,1,0:T(8,128)} custom-call(s32[8,128]{1,0:T(8,128)S(1)} %get-tuple-element.36.refs_0_, f32[16,17]{1,0:T(8,128)S(1)} %get-tuple-element.37.refs_1_, f32[2,4,16,1024]{3,2,1,0:T(8,128)S(1)} %get-tuple-element.38.refs_2_, f32[2,4,8,1024]{3,2,1,0:T(8,128)S(1)} %get-tuple-element.63.refs_3_, ...), custom_call_target="tpu_custom_call" | custom-call | flops 524288 | bytes 524288 | tf_op jit(solution)/shard_map/adjoint1/pallas_call | solution.py:29
Async XLA Ops:
  0.0 13.2 %copy-start = (s32[4]{0:T(128)S(1)}, s32[4]{0:T(128)}, u32[]{:S(2)}) copy-start(s32[4]{0:T(128)} %refs_0_.21) | copy-start | bytes 52
  2.3 10.4 %collective-permute-start = (f32[2,4,8,1024]{3,2,1,0:T(8,128)S(1)}, f32[2,4,8,1024]{3,2,1,0:T(8,128)S(1)}, u32[]{:S(2)}, u32[]{:S(2)}) collective-permute-start(f32[2,4,8,1024]{3,2,1,0:T(8,128)S(1)} %get-tuple-element.43.refs_3_), channel_id=1, source_target_pairs={{1,2},{2,1},{5,6},{6,5},{9,10},{10,9},{13,14},{14,13},{17,18},{18,... | collective-permute-start | bytes 786440 | tf_op jit(solution)/shard_map/ppermute | solution.py:411
  8.1 5.0 %collective-permute-start.1 = (f32[2,4,8,1024]{3,2,1,0:T(8,128)S(1)}, f32[2,4,8,1024]{3,2,1,0:T(8,128)S(1)}, u32[]{:S(2)}, u32[]{:S(2)}) collective-permute-start(f32[2,4,8,1024]{3,2,1,0:T(8,128)S(1)} %core.1.refs_2_), channel_id=1, source_target_pairs={{0,1},{1,0},{2,3},{3,2},{4,5},{5,4},{6,7},{7,6},{8,9},{9,8},{10,11... | collective-permute-start | bytes 786440 | tf_op jit(solution)/shard_map/ppermute | solution.py:410
  8.2 6.9 %collective-permute-start.3 = (f32[2,4,16,1024]{3,2,1,0:T(8,128)S(1)}, f32[2,4,16,1024]{3,2,1,0:T(8,128)S(1)}, u32[]{:S(2)}, u32[]{:S(2)}) collective-permute-start(f32[2,4,16,1024]{3,2,1,0:T(8,128)S(1)} %get-tuple-element.46.refs_1_), channel_id=1, source_target_pairs={{8,16},{12,20},{16,8},{20,12},{9,17},{13,21},{17,9},{21,13},{10,18... | collective-permute-start | bytes 1572872 | tf_op jit(solution)/shard_map/ppermute | solution.py:449
  8.9 15.4 %collective-permute-start.2 = (f32[2,4,16,1024]{3,2,1,0:T(8,128)S(1)}, f32[2,4,16,1024]{3,2,1,0:T(8,128)S(1)}, u32[]{:S(2)}, u32[]{:S(2)}) collective-permute-start(f32[2,4,16,1024]{3,2,1,0:T(8,128)S(1)} %get-tuple-element.46.refs_1_), channel_id=1, source_target_pairs={{0,8},{4,12},{8,0},{12,4},{16,24},{20,28},{24,16},{28,20},{1,9},{5... | collective-permute-start | bytes 1572872 | tf_op jit(solution)/shard_map/ppermute | solution.py:444
  13.8 11.2 %collective-permute-start.4 = (f32[4,16,1024]{2,1,0:T(8,128)S(1)}, f32[4,16,1024]{2,1,0:T(8,128)S(1)}, u32[]{:S(2)}, u32[]{:S(2)}) collective-permute-start(f32[4,16,1024]{2,1,0:T(8,128)S(1)} %get-tuple-element.49), channel_id=1, source_target_pairs={{0,4},{4,0},{8,12},{12,8},{16,20},{20,16},{24,28},{28,24},{1,5},{5... | collective-permute-start | bytes 786440 | tf_op jit(solution)/shard_map/ppermute | solution.py:443
  25.0 12.1 %collective-permute-start.5 = (f32[2,4,16,1024]{3,2,1,0:T(8,128)S(1)}, f32[2,4,16,1024]{3,2,1,0:T(8,128)S(1)}, u32[]{:S(2)}, u32[]{:S(2)}) collective-permute-start(f32[2,4,16,1024]{3,2,1,0:T(8,128)S(1)} %get-tuple-element.52), channel_id=1, source_target_pairs={{0,4},{4,0},{8,12},{12,8},{16,20},{20,16},{24,28},{28,24},{1,5},{5... | collective-permute-start | bytes 1572872 | tf_op jit(solution)/shard_map/ppermute | solution.py:443
  27.0 14.5 %collective-permute-start.8 = (f32[4,16,1024]{2,1,0:T(8,128)S(1)}, f32[4,16,1024]{2,1,0:T(8,128)S(1)}, u32[]{:S(2)}, u32[]{:S(2)}) collective-permute-start(f32[4,16,1024]{2,1,0:T(8,128)S(1)} %meet2.1.refs_4_), channel_id=1, source_target_pairs={{0,16},{4,20},{8,24},{12,28},{16,0},{20,4},{24,8},{28,12},{1,17},{... | collective-permute-start | bytes 786440 | tf_op jit(solution)/shard_map/ppermute | solution.py:444
  37.9 10.1 %collective-permute-start.7 = (f32[4,16,1024]{2,1,0:T(8,128)S(1)}, f32[4,16,1024]{2,1,0:T(8,128)S(1)}, u32[]{:S(2)}, u32[]{:S(2)}) collective-permute-start(f32[4,16,1024]{2,1,0:T(8,128)S(1)} %get-tuple-element.54), channel_id=1, source_target_pairs={{0,8},{4,12},{8,0},{12,4},{16,24},{20,28},{24,16},{28,20},{1,9},{5... | collective-permute-start | bytes 786440 | tf_op jit(solution)/shard_map/ppermute | solution.py:444
  38.8 10.3 %collective-permute-start.9 = (f32[4,16,1024]{2,1,0:T(8,128)S(1)}, f32[4,16,1024]{2,1,0:T(8,128)S(1)}, u32[]{:S(2)}, u32[]{:S(2)}) collective-permute-start(f32[4,16,1024]{2,1,0:T(8,128)S(1)} %get-tuple-element.55), channel_id=1, source_target_pairs={{0,24},{4,28},{8,16},{12,20},{16,8},{20,12},{24,0},{28,4},{1,25},{... | collective-permute-start | bytes 786440 | tf_op jit(solution)/shard_map/ppermute | solution.py:444
  40.0 9.1 %collective-permute-start.6 = (f32[4,16,1024]{2,1,0:T(8,128)S(1)}, f32[4,16,1024]{2,1,0:T(8,128)S(1)}, u32[]{:S(2)}, u32[]{:S(2)}) collective-permute-start(f32[4,16,1024]{2,1,0:T(8,128)S(1)} %get-tuple-element.53), channel_id=1, source_target_pairs={{0,4},{4,0},{8,12},{12,8},{16,20},{20,16},{24,28},{28,24},{1,5},{5... | collective-permute-start | bytes 786440 | tf_op jit(solution)/shard_map/ppermute | solution.py:443
  41.2 9.1 %collective-permute-start.10 = (f32[4,16,1024]{2,1,0:T(8,128)S(1)}, f32[4,16,1024]{2,1,0:T(8,128)S(1)}, u32[]{:S(2)}, u32[]{:S(2)}) collective-permute-start(f32[4,16,1024]{2,1,0:T(8,128)S(1)} %get-tuple-element.57.refs_5_), channel_id=1, source_target_pairs={{0,4},{4,0},{8,12},{12,8},{16,20},{20,16},{24,28},{28,24},{1,5},{5... | collective-permute-start | bytes 786440 | tf_op jit(solution)/shard_map/ppermute | solution.py:443
  51.0 5.4 %collective-permute-start.13 = (f32[4,16,1024]{2,1,0:T(8,128)S(1)}, f32[4,16,1024]{2,1,0:T(8,128)S(1)}, u32[]{:S(2)}, u32[]{:S(2)}) collective-permute-start(f32[4,16,1024]{2,1,0:T(8,128)S(1)} %last.1.refs_2_), channel_id=1, source_target_pairs={{0,4},{4,0},{8,12},{12,8},{16,20},{20,16},{24,28},{28,24},{1,5},{5... | collective-permute-start | bytes 786440 | tf_op jit(solution)/shard_map/ppermute | solution.py:443
  52.3 7.2 %collective-permute-start.12 = (f32[4,16,1024]{2,1,0:T(8,128)S(1)}, f32[4,16,1024]{2,1,0:T(8,128)S(1)}, u32[]{:S(2)}, u32[]{:S(2)}) collective-permute-start(f32[4,16,1024]{2,1,0:T(8,128)S(1)} %last.1.refs_2_), channel_id=1, source_target_pairs={{0,24},{4,28},{8,16},{12,20},{16,8},{20,12},{24,0},{28,4},{1,25},{... | collective-permute-start | bytes 786440 | tf_op jit(solution)/shard_map/ppermute | solution.py:444
  54.3 11.5 %collective-permute-start.11 = (f32[4,16,1024]{2,1,0:T(8,128)S(1)}, f32[4,16,1024]{2,1,0:T(8,128)S(1)}, u32[]{:S(2)}, u32[]{:S(2)}) collective-permute-start(f32[4,16,1024]{2,1,0:T(8,128)S(1)} %last.1.refs_2_), channel_id=1, source_target_pairs={{0,8},{4,12},{8,0},{12,4},{16,24},{20,28},{24,16},{28,20},{1,9},{5... | collective-permute-start | bytes 786440 | tf_op jit(solution)/shard_map/ppermute | solution.py:444
  65.8 12.1 %collective-permute-start.14 = (f32[4,16,1024]{2,1,0:T(8,128)S(1)}, f32[4,16,1024]{2,1,0:T(8,128)S(1)}, u32[]{:S(2)}, u32[]{:S(2)}) collective-permute-start(f32[4,16,1024]{2,1,0:T(8,128)S(1)} %last.1.refs_2_), channel_id=1, source_target_pairs={{0,16},{4,20},{8,24},{12,28},{16,0},{20,4},{24,8},{28,12},{1,17},{... | collective-permute-start | bytes 786440 | tf_op jit(solution)/shard_map/ppermute | solution.py:444
  65.8 13.7 %collective-permute-start.16 = (f32[4,16,1024]{2,1,0:T(8,128)S(1)}, f32[4,16,1024]{2,1,0:T(8,128)S(1)}, u32[]{:S(2)}, u32[]{:S(2)}) collective-permute-start(f32[4,16,1024]{2,1,0:T(8,128)S(1)} %collective-permute-done.11.refs_3_), channel_id=1, source_target_pairs={{0,4},{4,0},{8,12},{12,8},{16,20},{20,16},{24,28},{28,24},{1,5},{5... | collective-permute-start | bytes 786440 | tf_op jit(solution)/shard_map/ppermute | solution.py:443
  66.1 13.4 %collective-permute-start.17 = (f32[4,16,1024]{2,1,0:T(8,128)S(1)}, f32[4,16,1024]{2,1,0:T(8,128)S(1)}, u32[]{:S(2)}, u32[]{:S(2)}) collective-permute-start(f32[4,16,1024]{2,1,0:T(8,128)S(1)} %collective-permute-done.12.refs_4_), channel_id=1, source_target_pairs={{0,4},{4,0},{8,12},{12,8},{16,20},{20,16},{24,28},{28,24},{1,5},{5... | collective-permute-start | bytes 786440 | tf_op jit(solution)/shard_map/ppermute | solution.py:443
  77.9 5.8 %collective-permute-start.15 = (f32[4,16,1024]{2,1,0:T(8,128)S(1)}, f32[4,16,1024]{2,1,0:T(8,128)S(1)}, u32[]{:S(2)}, u32[]{:S(2)}) collective-permute-start(f32[4,16,1024]{2,1,0:T(8,128)S(1)} %collective-permute-done.14.refs_4_), channel_id=1, source_target_pairs={{0,4},{4,0},{8,12},{12,8},{16,20},{20,16},{24,28},{28,24},{1,5},{5... | collective-permute-start | bytes 786440 | tf_op jit(solution)/shard_map/ppermute | solution.py:443
  85.4 8.0 %collective-permute-start.19 = (f32[2,4,8,1024]{3,2,1,0:T(8,128)S(1)}, f32[2,4,8,1024]{3,2,1,0:T(8,128)S(1)}, u32[]{:S(2)}, u32[]{:S(2)}) collective-permute-start(f32[2,4,8,1024]{3,2,1,0:T(8,128)S(1)} %get-tuple-element.66), channel_id=1, source_target_pairs={{0,1},{1,0},{2,3},{3,2},{4,5},{5,4},{6,7},{7,6},{8,9},{9,8},{10,11... | collective-permute-start | bytes 786440 | tf_op jit(solution)/shard_map/ppermute | solution.py:410
  88.3 9.1 %collective-permute-start.18 = (f32[2,4,8,1024]{3,2,1,0:T(8,128)S(1)}, f32[2,4,8,1024]{3,2,1,0:T(8,128)S(1)}, u32[]{:S(2)}, u32[]{:S(2)}) collective-permute-start(f32[2,4,8,1024]{3,2,1,0:T(8,128)S(1)} %get-tuple-element.64), channel_id=1, source_target_pairs={{1,2},{2,1},{5,6},{6,5},{9,10},{10,9},{13,14},{14,13},{17,18},{18,... | collective-permute-start | bytes 786440 | tf_op jit(solution)/shard_map/ppermute | solution.py:411

commit v6 on v5

--- a/solution.py
+++ b/solution.py
@@ -157,11 +157,13 @@
         (r["taps"], r["taps_v"]),
         (r["control"].at[:, :, rows_x], r["control_v"].at[:, :, rows_x]),
     ]
+    if "obs" in r:
+        moves.append((r["obs"].at[0, 1 - own_y()], r["weight_sent"]))
     moves.append((r["control"].at[:, :, rows_core], r["control_v"].at[:, :, rows_core]))
     moves.append((r["meridional"], r["meridional_v"]))
     moves.append((r["mixing"], r["mixing_v"]))
     if "obs" in r:
-        moves.append((r["obs"].at[0], r["obs_v"]))
+        moves.append((r["obs"].at[0, own_y()], r["obs_v"]))
     moves.append((r["ens"], r["ens_v"]))
     copies = [pltpu.make_async_copy(a, b, sems.at[i]) for i, (a, b) in enumerate(moves)]
     for copy in copies:
@@ -284,18 +286,17 @@
     return total
 
 
-def weight_pick(owners, here, side, middle, mine, across):
-    place = owner_at(owners, 0) >> 1
-    for found, weights in (
-        (place == own_z(), here),
-        (place == own_z() ^ 1, side),
-        (place == own_z() ^ 3, middle),
-    ):
-
-        @pl.when(found)
-        def _(weights=weights):
-            mine[...] = weights[own_y()]
-            across[...] = weights[1 - own_y()]
+def weight_pick(owners, here, from_y, mine, side, middle):
+    for step, out in ((0, mine), (1, side), (3, middle)):
+        held = (owner_at(owners, step) & 1) == own_y()
+
+        @pl.when(held)
+        def _(out=out):
+            out[...] = here[...]
+
+        @pl.when(jnp.logical_not(held))
+        def _(out=out):
+            out[...] = from_y[...]
 
 
 def first_body(step, owners_hbm, matrix, a, b, c, d, ens, localized, send, owners, sem):
@@ -326,12 +327,17 @@
         meet_body(step, owners, ens, localized, got.at[i], out)
 
 
-def last_body(owners, ens, localized, got_y, got_1, got_2, got_3, mine, from_y, out):
-    slot = slot_at(owners, 0)
-    held = (owner_at(owners, 0) & 1) == own_y()
-    for here, weight in ((held, mine), (jnp.logical_not(held), from_y)):
-
-        @pl.when(here)
+def last_body(
+    owners, ens, localized, got_y, got_1, got_2, got_3, mine, side, middle, out
+):
+    slot, place = slot_at(owners, 0), owner_at(owners, 0) >> 1
+    for found, weight in (
+        (place == own_z(), mine),
+        (place == own_z() ^ 1, side),
+        (place == own_z() ^ 3, middle),
+    ):
+
+        @pl.when(found)
         def _(weight=weight):
             for l in range(localized.shape[1]):
                 out[l] = weight[l] * (
@@ -425,14 +431,14 @@
     }
     if direct:
         ins["obs"] = obs_weight
-        results["obs_v"] = shape(*obs_weight.shape[1:])
+        results["weight_sent"] = results["obs_v"] = piece
     names = (*ins, *results, "taps_x", "shift_s", "sems")
     made = call(
         functools.partial(front_body, names), tuple(results.values()), "front", 1 << 19,
         *(pltpu.with_memory_space_constraint(v, pltpu.HBM) for v in ins.values()),
         specs=(HBM,) * len(ins),
         scratch=[
-            *tap_room, pltpu.SMEM(zonal_shift.shape, jnp.int32), pltpu.SemaphoreType.DMA((8,)),
+            *tap_room, pltpu.SMEM(zonal_shift.shape, jnp.int32), pltpu.SemaphoreType.DMA((9,)),
         ],
     )
     made = dict(zip(results, made))
@@ -444,9 +450,7 @@
         turn_z = lambda v, s: lax.ppermute(
             v, "mem", [(i, i ^ 2 * s) for i in range(mem_count)]
         )
-        middle = [(i, i ^ 6) for i in range(2, mem_count - 2)]
-        from_side = turn_z(made["obs_v"], 1)
-        from_middle = lax.ppermute(made["obs_v"], "mem", middle)
+        from_y = swap_y(made["weight_sent"])
     near_core = call(
         core_body, shape(*half_shape), "core", 1 << 19, made["shift_core"], made["taps_v"],
         control_v, specs=(VMEM,) * 3, scratch=tap_room,
@@ -463,37 +467,42 @@
         localized, first = call(
             functools.partial(first_body, 2), (shape(*field_shape), piece),
             "first", 1 << 20, slot_owner, matrix, *parts, ens,
-            specs=(HBM,) + (VMEM,) * 6,
+            specs=(HBM,) + (VMEM,) * 6, after=(from_y,),
             scratch=[pltpu.SMEM((SLOTS,), jnp.int32), pltpu.SemaphoreType.DMA],
         )
         got_two = swap_y(first)
+        mine, side, middle = call(
+            weight_pick, (piece,) * 3, "weight_pick", 1 << 18, slot_owner, made["obs_v"],
+            from_y, specs=(SMEM,) + (VMEM,) * 2, after=(localized,),
+        )
+        from_side = turn_z(side, 1)
+        pairs = [(i, i ^ 6) for i in range(2, mem_count - 2)]
+        from_middle = lax.ppermute(middle, "mem", pairs)
         pair, single = call(
             send_body, (shape(2, levels, band_rows, width), piece), "send", 1 << 20,
-            slot_owner, ens, localized, specs=(SMEM, VMEM, VMEM), after=(from_side, from_middle),
-        )
-        pair, got_two = lax.optimization_barrier((pair, got_two))
-        got_pair = swap_y(pair)
+            slot_owner, ens, localized, specs=(SMEM, VMEM, VMEM),
+        )
         two = call(
             functools.partial(meet_body, 2), piece, "meet2", 1 << 19,
             slot_owner, ens, localized, got_two, specs=(SMEM,) + (VMEM,) * 3,
         )
         arrived = {2: turn_z(two, 2)}
-        mine, across = call(
-            weight_pick, (piece,) * 2, "weight_pick", 1 << 18, slot_owner, made["obs_v"],
-            from_side, from_middle, specs=(SMEM,) + (VMEM,) * 3, after=(two,),
-        )
+        pair, two, from_side, from_middle = lax.optimization_barrier(
+            (pair, two, from_side, from_middle)
+        )
+        got_pair = swap_y(pair)
         one, three = call(
             meet_pair_body, (piece,) * 2, "meet13", 1 << 19,
             slot_owner, ens, localized, got_pair, specs=(SMEM,) + (VMEM,) * 3,
-            after=(two, across),
+            after=(two,),
         )
         arrived[1], arrived[3] = turn_z(one, 1), turn_z(three, 3)
-        single, across, _ = lax.optimization_barrier((single, across, got_pair))
-        got_own, from_y = swap_y(single), swap_y(across)
+        single, _ = lax.optimization_barrier((single, got_pair))
+        got_own = swap_y(single)
         grad = call(
             last_body, piece, "last", 1 << 19, slot_owner, ens, localized, got_own,
-            arrived[1], arrived[2], arrived[3], mine, from_y,
-            specs=(SMEM,) + (VMEM,) * 8,
+            arrived[1], arrived[2], arrived[3], mine, from_side, from_middle,
+            specs=(SMEM,) + (VMEM,) * 9,
         )
         own = {0: grad, 1: turn_z(grad, 1), 3: turn_z(grad, 3)}
         other = {0: swap_y(grad)}

time: 99.6 us -> 99.8 us (level)
  starting transfers between devices: 29.5 us -> 40.1 us
  waiting for transfers between devices: 54.9 us -> 44.4 us
    ppermute x7, waiting for transfers between devices: 36.9 us -> 24.1 us  [per_device(): lax.ppermute(v, 'mem', [(i, i ^ 2 * s) for i in range(mem_count)])]
    ppermute x7, starting transfers between devices: 9.13 us -> 16.4 us  [per_device(): lax.ppermute(v, 'mem', [(i, i ^ 2 * s) for i in range(mem_count)])]
    ppermute x2, starting transfers between devices: 2.97 us -> 9.24 us  [per_device(): swap_core = lambda v: lax.ppermute(v, 'lat', core_pairs)]
    ppermute x2, starting transfers between devices: 9.6 us -> 6.42 us  [per_device(): swap_x = lambda v: lax.ppermute(v, 'lat', x_pairs)]
    ppermute x2, waiting for transfers between devices: 2.74 us -> 5.85 us  [per_device(): swap_x = lambda v: lax.ppermute(v, 'lat', x_pairs)]
  transfers between devices with their start and end apart: 20 -> 20, of which waited for: 11 -> 12; matrix products, arithmetic and copies ran while one was open for 0% -> 0% of each run, Pallas kernels for 8% -> 7%
where the time goes in v6:
time: 99.8 us; the launch traced here: 99.6 us
  waiting for transfers between devices  44.4 us (44%)
  starting transfers between devices  40.1 us (40%)
  Pallas kernels  14.9 us (15%)
    ppermute x7, waiting for transfers between devices, per_device(): lax.ppermute(v, 'mem', [(i, i ^ 2 * s) for i in range(mem_count)])  24.1 us
    ppermute x7, starting transfers between devices, per_device(): lax.ppermute(v, 'mem', [(i, i ^ 2 * s) for i in range(mem_count)])  16.4 us
    pallas_call x15, Pallas kernels, call(): pl.pallas_call(kernel, out_shape=outs, in_specs=list(specs) + [ANY] * ext...  14.9 us
    ppermute x8, waiting for transfers between devices, per_device(): swap_y = lambda v: lax.ppermute(v, 'mem', y_pairs)  14.5 us
    ppermute x2, starting transfers between devices, per_device(): swap_core = lambda v: lax.ppermute(v, 'lat', core_pairs)  9.24 us
    ppermute x8, starting transfers between devices, per_device(): swap_y = lambda v: lax.ppermute(v, 'mem', y_pairs)  7.35 us
    ppermute x2, starting transfers between devices, per_device(): swap_x = lambda v: lax.ppermute(v, 'lat', x_pairs)  6.42 us
    ppermute x2, waiting for transfers between devices, per_device(): swap_x = lambda v: lax.ppermute(v, 'lat', x_pairs)  5.85 us
  transfers between devices with their start and end apart: 20, of which 12 were waited for; matrix products, arithmetic and copies ran while one was open for 0% of the time, Pallas kernels for 7%

profile of v6, /device:TPU:1, one launch (start us, length us, event | category | flops | bytes accessed | tf_op | source)
XLA Modules:
  0.0 99.6 jit_solution(12685520666182951972)
XLA Ops:
  0.0 0.0 copy-start
  0.0 2.3 %front.1 = (f32[2,4,8,1024]{3,2,1,0:T(8,128)S(1)}, f32[2,4,16,1024]{3,2,1,0:T(8,128)S(1)}, f32[16,17]{1,0:T(8,128)S(1)}, f32[16,17]{1,0:T(8,128)S(1)}, s32[8,128...) custom-call(s32[16]{0:T(128)} %refs_0_.11, ...), custom_call_target="tpu_custom_call" | custom-call | flops 524288 | bytes 524288 | tf_op jit(solution)/shard_map/front/pallas_call | solution.py:29
  2.4 4.5 %collective-permute-start = (f32[2,4,8,1024]{3,2,1,0:T(8,128)S(1)}, f32[2,4,8,1024]{3,2,1,0:T(8,128)S(1)}, u32[]{:S(2)}, u32[]{:S(2)}) collective-permute-start(f32[2,4,8,1024]{3,2,1,0:T(8,128)S(1)} %get-tuple-element.46.refs_3_), channel_id=1, source_target_pairs={{1,2},{2,1},{5,6},{6,5},{9,10},{10,9},{13,14},{14,13},{17,18},{18,... | collective-permute-start | bytes 786440 | tf_op jit(solution)/shard_map/ppermute | solution.py:417
  6.9 1.3 %core.1.refs_2_ = f32[2,4,8,1024]{3,2,1,0:T(8,128)S(1)} custom-call(s32[8,128]{1,0:T(8,128)S(1)} %get-tuple-element.45.refs_0_, f32[16,17]{1,0:T(8,128)S(1)} %get-tuple-element.40.refs_1_, f32[2,4,16,1024]{3,2,1,0:T(8,128)S(1)} %get-tuple-element.41.refs_2_), custom_call_target="tpu_custom_call" | custom-call | flops 524288 | bytes 524288 | tf_op jit(solution)/shard_map/core/pallas_call | solution.py:29
  8.2 0.1 collective-permute-start.1
  8.2 1.3 %collective-permute-start.2 = (f32[4,16,1024]{2,1,0:T(8,128)S(1)}, f32[4,16,1024]{2,1,0:T(8,128)S(1)}, u32[]{:S(2)}, u32[]{:S(2)}) collective-permute-start(f32[4,16,1024]{2,1,0:T(8,128)S(1)} %get-tuple-element.48), channel_id=1, source_target_pairs={{0,4},{4,0},{8,12},{12,8},{16,20},{20,16},{24,28},{28,24},{1,5},{5... | collective-permute-start | bytes 786440 | tf_op jit(solution)/shard_map/ppermute | solution.py:449
  9.5 1.4 %collective-permute-done.refs_3_.refs_5_ = f32[2,4,8,1024]{3,2,1,0:T(8,128)S(1)} collective-permute-done((f32[2,4,8,1024]{3,2,1,0:T(8,128)S(1)}, f32[2,4,8,1024]{3,2,1,0:T(8,128)S(1)}, u32[]{:S(2)}, u32[]{:S(2)}) %collective-permute-start) | collective-permute-done | bytes 262176 | tf_op jit(solution)/shard_map/ppermute | solution.py:417
  10.9 0.3 matrix.1
  11.3 0.0 collective-permute-done.1.refs_4_
  11.3 4.5 %collective-permute-done.2.refs_7_.refs_2_ = f32[4,16,1024]{2,1,0:T(8,128)S(1)} collective-permute-done((f32[4,16,1024]{2,1,0:T(8,128)S(1)}, f32[4,16,1024]{2,1,0:T(8,128)S(1)}, u32[]{:S(2)}, u32[]{:S(2)}) %collective-permute-start.2) | collective-permute-done | bytes 262176 | tf_op jit(solution)/shard_map/ppermute | solution.py:449
  15.7 0.0 copy-done
  15.7 0.6 first.1
  16.4 1.3 %collective-permute-start.3 = (f32[4,16,1024]{2,1,0:T(8,128)S(1)}, f32[4,16,1024]{2,1,0:T(8,128)S(1)}, u32[]{:S(2)}, u32[]{:S(2)}) collective-permute-start(f32[4,16,1024]{2,1,0:T(8,128)S(1)} %get-tuple-element.52), channel_id=1, source_target_pairs={{0,4},{4,0},{8,12},{12,8},{16,20},{20,16},{24,28},{28,24},{1,5},{5... | collective-permute-start | bytes 786440 | tf_op jit(solution)/shard_map/ppermute | solution.py:449
  17.7 0.7 weight_pick.1
  18.4 1.4 %collective-permute-start.4 = (f32[4,16,1024]{2,1,0:T(8,128)S(1)}, f32[4,16,1024]{2,1,0:T(8,128)S(1)}, u32[]{:S(2)}, u32[]{:S(2)}) collective-permute-start(f32[4,16,1024]{2,1,0:T(8,128)S(1)} %get-tuple-element.54), channel_id=1, source_target_pairs={{0,8},{4,12},{8,0},{12,4},{16,24},{20,28},{24,16},{28,20},{1,9},{5... | collective-permute-start | bytes 786440 | tf_op jit(solution)/shard_map/ppermute | solution.py:450
  19.7 0.7 collective-permute-start.5
  20.4 0.7 send.1
  21.1 1.9 %collective-permute-done.3.refs_3_ = f32[4,16,1024]{2,1,0:T(8,128)S(1)} collective-permute-done((f32[4,16,1024]{2,1,0:T(8,128)S(1)}, f32[4,16,1024]{2,1,0:T(8,128)S(1)}, u32[]{:S(2)}, u32[]{:S(2)}) %collective-permute-start.3) | collective-permute-done | bytes 262176 | tf_op jit(solution)/shard_map/ppermute | solution.py:449
  23.0 0.6 meet2.1.refs_4_
  23.6 1.1 %collective-permute-done.4.refs_8_ = f32[4,16,1024]{2,1,0:T(8,128)S(1)} collective-permute-done((f32[4,16,1024]{2,1,0:T(8,128)S(1)}, f32[4,16,1024]{2,1,0:T(8,128)S(1)}, u32[]{:S(2)}, u32[]{:S(2)}) %collective-permute-start.4) | collective-permute-done | bytes 262176 | tf_op jit(solution)/shard_map/ppermute | solution.py:450
  24.7 0.0 collective-permute-done.5.refs_9_
  24.7 0.3 collective-permute-start.6
  24.9 5.2 %collective-permute-start.9 = (f32[4,16,1024]{2,1,0:T(8,128)S(1)}, f32[4,16,1024]{2,1,0:T(8,128)S(1)}, u32[]{:S(2)}, u32[]{:S(2)}) collective-permute-start(f32[4,16,1024]{2,1,0:T(8,128)S(1)} %meet2.1.refs_4_), channel_id=1, source_target_pairs={{0,16},{4,20},{8,24},{12,28},{16,0},{20,4},{24,8},{28,12},{1,17},{... | collective-permute-start | bytes 786440 | tf_op jit(solution)/shard_map/ppermute | solution.py:450
  30.1 5.5 %collective-permute-done.6.refs_3_ = f32[2,4,16,1024]{3,2,1,0:T(8,128)S(1)} collective-permute-done((f32[2,4,16,1024]{3,2,1,0:T(8,128)S(1)}, f32[2,4,16,1024]{3,2,1,0:T(8,128)S(1)}, u32[]{:S(2)}, u32[]{:S(2)}) %collective-permute-start.6) | collective-permute-done | bytes 524320 | tf_op jit(solution)/shard_map/ppermute | solution.py:449
  35.6 0.3 collective-permute-start.7
  35.9 0.7 meet13.1
  36.6 4.3 %collective-permute-start.8 = (f32[4,16,1024]{2,1,0:T(8,128)S(1)}, f32[4,16,1024]{2,1,0:T(8,128)S(1)}, u32[]{:S(2)}, u32[]{:S(2)}) collective-permute-start(f32[4,16,1024]{2,1,0:T(8,128)S(1)} %get-tuple-element.59), channel_id=1, source_target_pairs={{0,8},{4,12},{8,0},{12,4},{16,24},{20,28},{24,16},{28,20},{1,9},{5... | collective-permute-start | bytes 786440 | tf_op jit(solution)/shard_map/ppermute | solution.py:450
  40.9 1.8 %collective-permute-start.10 = (f32[4,16,1024]{2,1,0:T(8,128)S(1)}, f32[4,16,1024]{2,1,0:T(8,128)S(1)}, u32[]{:S(2)}, u32[]{:S(2)}) collective-permute-start(f32[4,16,1024]{2,1,0:T(8,128)S(1)} %get-tuple-element.60), channel_id=1, source_target_pairs={{0,24},{4,28},{8,16},{12,20},{16,8},{20,12},{24,0},{28,4},{1,25},{... | collective-permute-start | bytes 786440 | tf_op jit(solution)/shard_map/ppermute | solution.py:450
  42.7 0.0 collective-permute-done.9.refs_5_
  42.7 0.0 collective-permute-done.7.refs_3_
  42.7 2.5 %collective-permute-done.8.refs_4_ = f32[4,16,1024]{2,1,0:T(8,128)S(1)} collective-permute-done((f32[4,16,1024]{2,1,0:T(8,128)S(1)}, f32[4,16,1024]{2,1,0:T(8,128)S(1)}, u32[]{:S(2)}, u32[]{:S(2)}) %collective-permute-start.8) | collective-permute-done | bytes 262176 | tf_op jit(solution)/shard_map/ppermute | solution.py:450
  45.2 4.6 %collective-permute-done.10.refs_6_ = f32[4,16,1024]{2,1,0:T(8,128)S(1)} collective-permute-done((f32[4,16,1024]{2,1,0:T(8,128)S(1)}, f32[4,16,1024]{2,1,0:T(8,128)S(1)}, u32[]{:S(2)}, u32[]{:S(2)}) %collective-permute-start.10) | collective-permute-done | bytes 262176 | tf_op jit(solution)/shard_map/ppermute | solution.py:450
  49.8 0.7 last.1.refs_2_
  50.5 0.1 collective-permute-start.11
  50.6 2.2 %collective-permute-start.12 = (f32[4,16,1024]{2,1,0:T(8,128)S(1)}, f32[4,16,1024]{2,1,0:T(8,128)S(1)}, u32[]{:S(2)}, u32[]{:S(2)}) collective-permute-start(f32[4,16,1024]{2,1,0:T(8,128)S(1)} %last.1.refs_2_), channel_id=1, source_target_pairs={{0,24},{4,28},{8,16},{12,20},{16,8},{20,12},{24,0},{28,4},{1,25},{... | collective-permute-start | bytes 786440 | tf_op jit(solution)/shard_map/ppermute | solution.py:450
  52.8 1.2 %collective-permute-start.13 = (f32[4,16,1024]{2,1,0:T(8,128)S(1)}, f32[4,16,1024]{2,1,0:T(8,128)S(1)}, u32[]{:S(2)}, u32[]{:S(2)}) collective-permute-start(f32[4,16,1024]{2,1,0:T(8,128)S(1)} %last.1.refs_2_), channel_id=1, source_target_pairs={{0,4},{4,0},{8,12},{12,8},{16,20},{20,16},{24,28},{28,24},{1,5},{5... | collective-permute-start | bytes 786440 | tf_op jit(solution)/shard_map/ppermute | solution.py:449
  54.0 3.7 %collective-permute-done.11.refs_3_ = f32[4,16,1024]{2,1,0:T(8,128)S(1)} collective-permute-done((f32[4,16,1024]{2,1,0:T(8,128)S(1)}, f32[4,16,1024]{2,1,0:T(8,128)S(1)}, u32[]{:S(2)}, u32[]{:S(2)}) %collective-permute-start.11) | collective-permute-done | bytes 262176 | tf_op jit(solution)/shard_map/ppermute | solution.py:450
  57.7 2.9 %collective-permute-done.12.refs_4_ = f32[4,16,1024]{2,1,0:T(8,128)S(1)} collective-permute-done((f32[4,16,1024]{2,1,0:T(8,128)S(1)}, f32[4,16,1024]{2,1,0:T(8,128)S(1)}, u32[]{:S(2)}, u32[]{:S(2)}) %collective-permute-start.12) | collective-permute-done | bytes 262176 | tf_op jit(solution)/shard_map/ppermute | solution.py:450
  60.6 0.0 collective-permute-done.13.refs_2_
  60.6 1.5 %collective-permute-start.14 = (f32[4,16,1024]{2,1,0:T(8,128)S(1)}, f32[4,16,1024]{2,1,0:T(8,128)S(1)}, u32[]{:S(2)}, u32[]{:S(2)}) collective-permute-start(f32[4,16,1024]{2,1,0:T(8,128)S(1)} %last.1.refs_2_), channel_id=1, source_target_pairs={{0,16},{4,20},{8,24},{12,28},{16,0},{20,4},{24,8},{28,12},{1,17},{... | collective-permute-start | bytes 786440 | tf_op jit(solution)/shard_map/ppermute | solution.py:450
  62.1 1.6 %collective-permute-start.16 = (f32[4,16,1024]{2,1,0:T(8,128)S(1)}, f32[4,16,1024]{2,1,0:T(8,128)S(1)}, u32[]{:S(2)}, u32[]{:S(2)}) collective-permute-start(f32[4,16,1024]{2,1,0:T(8,128)S(1)} %collective-permute-done.11.refs_3_), channel_id=1, source_target_pairs={{0,4},{4,0},{8,12},{12,8},{16,20},{20,16},{24,28},{28,24},{1,5},{5... | collective-permute-start | bytes 786440 | tf_op jit(solution)/shard_map/ppermute | solution.py:449
  63.8 0.0 collective-permute-start.17
  63.8 9.2 %collective-permute-done.14.refs_4_ = f32[4,16,1024]{2,1,0:T(8,128)S(1)} collective-permute-done((f32[4,16,1024]{2,1,0:T(8,128)S(1)}, f32[4,16,1024]{2,1,0:T(8,128)S(1)}, u32[]{:S(2)}, u32[]{:S(2)}) %collective-permute-start.14) | collective-permute-done | bytes 262176 | tf_op jit(solution)/shard_map/ppermute | solution.py:450
  73.0 1.3 %collective-permute-start.15 = (f32[4,16,1024]{2,1,0:T(8,128)S(1)}, f32[4,16,1024]{2,1,0:T(8,128)S(1)}, u32[]{:S(2)}, u32[]{:S(2)}) collective-permute-start(f32[4,16,1024]{2,1,0:T(8,128)S(1)} %collective-permute-done.14.refs_4_), channel_id=1, source_target_pairs={{0,4},{4,0},{8,12},{12,8},{16,20},{20,16},{24,28},{28,24},{1,5},{5... | collective-permute-start | bytes 786440 | tf_op jit(solution)/shard_map/ppermute | solution.py:449
  74.3 0.6 spread0.2.refs_5_
  75.0 0.7 spread0.3.refs_5_
  75.7 0.0 collective-permute-done.16.refs_2_
  75.7 0.0 collective-permute-done.17.refs_3_
  75.7 0.8 spread1.1.refs_3_
  76.5 2.6 %collective-permute-done.15.refs_2_ = f32[4,16,1024]{2,1,0:T(8,128)S(1)} collective-permute-done((f32[4,16,1024]{2,1,0:T(8,128)S(1)}, f32[4,16,1024]{2,1,0:T(8,128)S(1)}, u32[]{:S(2)}, u32[]{:S(2)}) %collective-permute-start.15) | collective-permute-done | bytes 262176 | tf_op jit(solution)/shard_map/ppermute | solution.py:449
  79.1 1.6 %spread2.1 = (f32[2,4,8,1024]{3,2,1,0:T(8,128)S(1)}, f32[2,4,8,1024]{3,2,1,0:T(8,128)S(1)}, f32[2,4,8,1024]{3,2,1,0:T(8,128)S(1)}, f32[2,4,8,1024]{3,2,1,0:T(8,128)S(1)}, f32[2,4,16,1024]{3,2,1,0:T(8,128)}) custom-call(s32[4]{0:T(128)S(1)} %copy-done, bf16[4,2,2,4,16,1024]{5,4,3,2,1,0:T(8,128)(2,1)S(1)} %get-tuple-element.42.refs_6_.refs_1_, ...), custom_call_target="tpu_custom_call" | custom-call | flops 524288 | bytes 524288 | tf_op jit(solution)/shard_map/spread2/pallas_call | solution.py:29
  80.8 9.2 %collective-permute-start.19 = (f32[2,4,8,1024]{3,2,1,0:T(8,128)S(1)}, f32[2,4,8,1024]{3,2,1,0:T(8,128)S(1)}, u32[]{:S(2)}, u32[]{:S(2)}) collective-permute-start(f32[2,4,8,1024]{3,2,1,0:T(8,128)S(1)} %get-tuple-element.72), channel_id=1, source_target_pairs={{0,1},{1,0},{2,3},{3,2},{4,5},{5,4},{6,7},{7,6},{8,9},{9,8},{10,11... | collective-permute-start | bytes 786440 | tf_op jit(solution)/shard_map/ppermute | solution.py:416
  89.9 1.9 %collective-permute-start.18 = (f32[2,4,8,1024]{3,2,1,0:T(8,128)S(1)}, f32[2,4,8,1024]{3,2,1,0:T(8,128)S(1)}, u32[]{:S(2)}, u32[]{:S(2)}) collective-permute-start(f32[2,4,8,1024]{3,2,1,0:T(8,128)S(1)} %get-tuple-element.70), channel_id=1, source_target_pairs={{1,2},{2,1},{5,6},{6,5},{9,10},{10,9},{13,14},{14,13},{17,18},{18,... | collective-permute-start | bytes 786440 | tf_op jit(solution)/shard_map/ppermute | solution.py:417
  91.9 0.0 collective-permute-done.19.refs_4_
  91.9 1.3 %adjoint0.1.refs_5_ = f32[2,4,8,1024]{3,2,1,0:T(8,128)S(1)} custom-call(s32[8,128]{1,0:T(8,128)S(1)} %get-tuple-element.45.refs_0_, f32[16,17]{1,0:T(8,128)S(1)} %get-tuple-element.40.refs_1_, f32[2,4,16,1024]{3,2,1,0:T(8,128)S(1)} %get-tuple-element.41.refs_2_, f32[2,4,8,1024]{3,2,1,0:T(8,128)S(1)} %get-tuple-element.71.refs_3_, ...), custom_call_target="tpu_custom_call" | custom-call | flops 524288 | bytes 524288 | tf_op jit(solution)/shard_map/adjoint0/pallas_call | solution.py:29
  93.2 4.5 %collective-permute-done.18.refs_4_ = f32[2,4,8,1024]{3,2,1,0:T(8,128)S(1)} collective-permute-done((f32[2,4,8,1024]{3,2,1,0:T(8,128)S(1)}, f32[2,4,8,1024]{3,2,1,0:T(8,128)S(1)}, u32[]{:S(2)}, u32[]{:S(2)}) %collective-permute-start.18) | collective-permute-done | bytes 262176 | tf_op jit(solution)/shard_map/ppermute | solution.py:417
  97.6 2.0 %adjoint1.1 = f32[2,4,16,1024]{3,2,1,0:T(8,128)} custom-call(s32[8,128]{1,0:T(8,128)S(1)} %get-tuple-element.39.refs_0_, f32[16,17]{1,0:T(8,128)S(1)} %get-tuple-element.40.refs_1_, f32[2,4,16,1024]{3,2,1,0:T(8,128)S(1)} %get-tuple-element.41.refs_2_, f32[2,4,8,1024]{3,2,1,0:T(8,128)S(1)} %get-tuple-element.69.refs_3_, ...), custom_call_target="tpu_custom_call" | custom-call | flops 524288 | bytes 524288 | tf_op jit(solution)/shard_map/adjoint1/pallas_call | solution.py:29
Async XLA Ops:
  0.0 15.7 %copy-start = (s32[4]{0:T(128)S(1)}, s32[4]{0:T(128)}, u32[]{:S(2)}) copy-start(s32[4]{0:T(128)} %refs_0_.21) | copy-start | bytes 52
  2.4 8.6 %collective-permute-start = (f32[2,4,8,1024]{3,2,1,0:T(8,128)S(1)}, f32[2,4,8,1024]{3,2,1,0:T(8,128)S(1)}, u32[]{:S(2)}, u32[]{:S(2)}) collective-permute-start(f32[2,4,8,1024]{3,2,1,0:T(8,128)S(1)} %get-tuple-element.46.refs_3_), channel_id=1, source_target_pairs={{1,2},{2,1},{5,6},{6,5},{9,10},{10,9},{13,14},{14,13},{17,18},{18,... | collective-permute-start | bytes 786440 | tf_op jit(solution)/shard_map/ppermute | solution.py:417
  8.2 3.1 %collective-permute-start.1 = (f32[2,4,8,1024]{3,2,1,0:T(8,128)S(1)}, f32[2,4,8,1024]{3,2,1,0:T(8,128)S(1)}, u32[]{:S(2)}, u32[]{:S(2)}) collective-permute-start(f32[2,4,8,1024]{3,2,1,0:T(8,128)S(1)} %core.1.refs_2_), channel_id=1, source_target_pairs={{0,1},{1,0},{2,3},{3,2},{4,5},{5,4},{6,7},{7,6},{8,9},{9,8},{10,11... | collective-permute-start | bytes 786440 | tf_op jit(solution)/shard_map/ppermute | solution.py:416
  8.2 7.5 %collective-permute-start.2 = (f32[4,16,1024]{2,1,0:T(8,128)S(1)}, f32[4,16,1024]{2,1,0:T(8,128)S(1)}, u32[]{:S(2)}, u32[]{:S(2)}) collective-permute-start(f32[4,16,1024]{2,1,0:T(8,128)S(1)} %get-tuple-element.48), channel_id=1, source_target_pairs={{0,4},{4,0},{8,12},{12,8},{16,20},{20,16},{24,28},{28,24},{1,5},{5... | collective-permute-start | bytes 786440 | tf_op jit(solution)/shard_map/ppermute | solution.py:449
  16.4 6.6 %collective-permute-start.3 = (f32[4,16,1024]{2,1,0:T(8,128)S(1)}, f32[4,16,1024]{2,1,0:T(8,128)S(1)}, u32[]{:S(2)}, u32[]{:S(2)}) collective-permute-start(f32[4,16,1024]{2,1,0:T(8,128)S(1)} %get-tuple-element.52), channel_id=1, source_target_pairs={{0,4},{4,0},{8,12},{12,8},{16,20},{20,16},{24,28},{28,24},{1,5},{5... | collective-permute-start | bytes 786440 | tf_op jit(solution)/shard_map/ppermute | solution.py:449
  18.4 6.3 %collective-permute-start.4 = (f32[4,16,1024]{2,1,0:T(8,128)S(1)}, f32[4,16,1024]{2,1,0:T(8,128)S(1)}, u32[]{:S(2)}, u32[]{:S(2)}) collective-permute-start(f32[4,16,1024]{2,1,0:T(8,128)S(1)} %get-tuple-element.54), channel_id=1, source_target_pairs={{0,8},{4,12},{8,0},{12,4},{16,24},{20,28},{24,16},{28,20},{1,9},{5... | collective-permute-start | bytes 786440 | tf_op jit(solution)/shard_map/ppermute | solution.py:450
  19.7 5.0 %collective-permute-start.5 = (f32[4,16,1024]{2,1,0:T(8,128)S(1)}, f32[4,16,1024]{2,1,0:T(8,128)S(1)}, u32[]{:S(2)}, u32[]{:S(2)}) collective-permute-start(f32[4,16,1024]{2,1,0:T(8,128)S(1)} %get-tuple-element.55), channel_id=1, source_target_pairs={{8,16},{12,20},{16,8},{20,12},{9,17},{13,21},{17,9},{21,13},{10,18... | collective-permute-start | bytes 786440 | tf_op jit(solution)/shard_map/ppermute | solution.py:480
  24.7 10.9 %collective-permute-start.6 = (f32[2,4,16,1024]{3,2,1,0:T(8,128)S(1)}, f32[2,4,16,1024]{3,2,1,0:T(8,128)S(1)}, u32[]{:S(2)}, u32[]{:S(2)}) collective-permute-start(f32[2,4,16,1024]{3,2,1,0:T(8,128)S(1)} %get-tuple-element.56), channel_id=1, source_target_pairs={{0,4},{4,0},{8,12},{12,8},{16,20},{20,16},{24,28},{28,24},{1,5},{5... | collective-permute-start | bytes 1572872 | tf_op jit(solution)/shard_map/ppermute | solution.py:449
  24.9 17.7 %collective-permute-start.9 = (f32[4,16,1024]{2,1,0:T(8,128)S(1)}, f32[4,16,1024]{2,1,0:T(8,128)S(1)}, u32[]{:S(2)}, u32[]{:S(2)}) collective-permute-start(f32[4,16,1024]{2,1,0:T(8,128)S(1)} %meet2.1.refs_4_), channel_id=1, source_target_pairs={{0,16},{4,20},{8,24},{12,28},{16,0},{20,4},{24,8},{28,12},{1,17},{... | collective-permute-start | bytes 786440 | tf_op jit(solution)/shard_map/ppermute | solution.py:450
  35.6 7.1 %collective-permute-start.7 = (f32[4,16,1024]{2,1,0:T(8,128)S(1)}, f32[4,16,1024]{2,1,0:T(8,128)S(1)}, u32[]{:S(2)}, u32[]{:S(2)}) collective-permute-start(f32[4,16,1024]{2,1,0:T(8,128)S(1)} %get-tuple-element.57), channel_id=1, source_target_pairs={{0,4},{4,0},{8,12},{12,8},{16,20},{20,16},{24,28},{28,24},{1,5},{5... | collective-permute-start | bytes 786440 | tf_op jit(solution)/shard_map/ppermute | solution.py:449
  36.6 8.6 %collective-permute-start.8 = (f32[4,16,1024]{2,1,0:T(8,128)S(1)}, f32[4,16,1024]{2,1,0:T(8,128)S(1)}, u32[]{:S(2)}, u32[]{:S(2)}) collective-permute-start(f32[4,16,1024]{2,1,0:T(8,128)S(1)} %get-tuple-element.59), channel_id=1, source_target_pairs={{0,8},{4,12},{8,0},{12,4},{16,24},{20,28},{24,16},{28,20},{1,9},{5... | collective-permute-start | bytes 786440 | tf_op jit(solution)/shard_map/ppermute | solution.py:450
  40.9 8.9 %collective-permute-start.10 = (f32[4,16,1024]{2,1,0:T(8,128)S(1)}, f32[4,16,1024]{2,1,0:T(8,128)S(1)}, u32[]{:S(2)}, u32[]{:S(2)}) collective-permute-start(f32[4,16,1024]{2,1,0:T(8,128)S(1)} %get-tuple-element.60), channel_id=1, source_target_pairs={{0,24},{4,28},{8,16},{12,20},{16,8},{20,12},{24,0},{28,4},{1,25},{... | collective-permute-start | bytes 786440 | tf_op jit(solution)/shard_map/ppermute | solution.py:450
  50.5 7.2 %collective-permute-start.11 = (f32[4,16,1024]{2,1,0:T(8,128)S(1)}, f32[4,16,1024]{2,1,0:T(8,128)S(1)}, u32[]{:S(2)}, u32[]{:S(2)}) collective-permute-start(f32[4,16,1024]{2,1,0:T(8,128)S(1)} %last.1.refs_2_), channel_id=1, source_target_pairs={{0,8},{4,12},{8,0},{12,4},{16,24},{20,28},{24,16},{28,20},{1,9},{5... | collective-permute-start | bytes 786440 | tf_op jit(solution)/shard_map/ppermute | solution.py:450
  50.6 10.0 %collective-permute-start.12 = (f32[4,16,1024]{2,1,0:T(8,128)S(1)}, f32[4,16,1024]{2,1,0:T(8,128)S(1)}, u32[]{:S(2)}, u32[]{:S(2)}) collective-permute-start(f32[4,16,1024]{2,1,0:T(8,128)S(1)} %last.1.refs_2_), channel_id=1, source_target_pairs={{0,24},{4,28},{8,16},{12,20},{16,8},{20,12},{24,0},{28,4},{1,25},{... | collective-permute-start | bytes 786440 | tf_op jit(solution)/shard_map/ppermute | solution.py:450
  52.8 7.8 %collective-permute-start.13 = (f32[4,16,1024]{2,1,0:T(8,128)S(1)}, f32[4,16,1024]{2,1,0:T(8,128)S(1)}, u32[]{:S(2)}, u32[]{:S(2)}) collective-permute-start(f32[4,16,1024]{2,1,0:T(8,128)S(1)} %last.1.refs_2_), channel_id=1, source_target_pairs={{0,4},{4,0},{8,12},{12,8},{16,20},{20,16},{24,28},{28,24},{1,5},{5... | collective-permute-start | bytes 786440 | tf_op jit(solution)/shard_map/ppermute | solution.py:449
  60.6 12.4 %collective-permute-start.14 = (f32[4,16,1024]{2,1,0:T(8,128)S(1)}, f32[4,16,1024]{2,1,0:T(8,128)S(1)}, u32[]{:S(2)}, u32[]{:S(2)}) collective-permute-start(f32[4,16,1024]{2,1,0:T(8,128)S(1)} %last.1.refs_2_), channel_id=1, source_target_pairs={{0,16},{4,20},{8,24},{12,28},{16,0},{20,4},{24,8},{28,12},{1,17},{... | collective-permute-start | bytes 786440 | tf_op jit(solution)/shard_map/ppermute | solution.py:450
  62.1 13.6 %collective-permute-start.16 = (f32[4,16,1024]{2,1,0:T(8,128)S(1)}, f32[4,16,1024]{2,1,0:T(8,128)S(1)}, u32[]{:S(2)}, u32[]{:S(2)}) collective-permute-start(f32[4,16,1024]{2,1,0:T(8,128)S(1)} %collective-permute-done.11.refs_3_), channel_id=1, source_target_pairs={{0,4},{4,0},{8,12},{12,8},{16,20},{20,16},{24,28},{28,24},{1,5},{5... | collective-permute-start | bytes 786440 | tf_op jit(solution)/shard_map/ppermute | solution.py:449
  63.8 11.9 %collective-permute-start.17 = (f32[4,16,1024]{2,1,0:T(8,128)S(1)}, f32[4,16,1024]{2,1,0:T(8,128)S(1)}, u32[]{:S(2)}, u32[]{:S(2)}) collective-permute-start(f32[4,16,1024]{2,1,0:T(8,128)S(1)} %collective-permute-done.12.refs_4_), channel_id=1, source_target_pairs={{0,4},{4,0},{8,12},{12,8},{16,20},{20,16},{24,28},{28,24},{1,5},{5... | collective-permute-start | bytes 786440 | tf_op jit(solution)/shard_map/ppermute | solution.py:449
  73.0 6.1 %collective-permute-start.15 = (f32[4,16,1024]{2,1,0:T(8,128)S(1)}, f32[4,16,1024]{2,1,0:T(8,128)S(1)}, u32[]{:S(2)}, u32[]{:S(2)}) collective-permute-start(f32[4,16,1024]{2,1,0:T(8,128)S(1)} %collective-permute-done.14.refs_4_), channel_id=1, source_target_pairs={{0,4},{4,0},{8,12},{12,8},{16,20},{20,16},{24,28},{28,24},{1,5},{5... | collective-permute-start | bytes 786440 | tf_op jit(solution)/shard_map/ppermute | solution.py:449
  80.8 11.1 %collective-permute-start.19 = (f32[2,4,8,1024]{3,2,1,0:T(8,128)S(1)}, f32[2,4,8,1024]{3,2,1,0:T(8,128)S(1)}, u32[]{:S(2)}, u32[]{:S(2)}) collective-permute-start(f32[2,4,8,1024]{3,2,1,0:T(8,128)S(1)} %get-tuple-element.72), channel_id=1, source_target_pairs={{0,1},{1,0},{2,3},{3,2},{4,5},{5,4},{6,7},{7,6},{8,9},{9,8},{10,11... | collective-permute-start | bytes 786440 | tf_op jit(solution)/shard_map/ppermute | solution.py:416
  89.9 7.7 %collective-permute-start.18 = (f32[2,4,8,1024]{3,2,1,0:T(8,128)S(1)}, f32[2,4,8,1024]{3,2,1,0:T(8,128)S(1)}, u32[]{:S(2)}, u32[]{:S(2)}) collective-permute-start(f32[2,4,8,1024]{3,2,1,0:T(8,128)S(1)} %get-tuple-element.70), channel_id=1, source_target_pairs={{1,2},{2,1},{5,6},{6,5},{9,10},{10,9},{13,14},{14,13},{17,18},{18,... | collective-permute-start | bytes 786440 | tf_op jit(solution)/shard_map/ppermute | solution.py:417

commit v7 on v5

--- a/solution.py
+++ b/solution.py
@@ -495,25 +495,28 @@
             arrived[1], arrived[2], arrived[3], mine, from_y,
             specs=(SMEM,) + (VMEM,) * 8,
         )
-        own = {0: grad, 1: turn_z(grad, 1), 3: turn_z(grad, 3)}
-        other = {0: swap_y(grad)}
-        later, own[1], own[3], other[0] = lax.optimization_barrier((grad, own[1], own[3], other[0]))
+        own = {0: grad, 3: turn_z(grad, 3), 1: turn_z(grad, 1)}
+        weighted = call(
+            functools.partial(spread_body, ((0, 0),), True, False), shape(*field_shape),
+            "spread", 1 << 19, slot_owner, ens, grad, specs=(SMEM,) + (VMEM,) * 2,
+        )
+        other, weighted = lax.optimization_barrier((grad, weighted))
+        other = {0: swap_y(other)}
+        later, own[3], other[0] = lax.optimization_barrier((grad, own[3], other[0]))
         own[2] = turn_z(later, 2)
         other.update({s: swap_y(own[s]) for s in (1, 3, 2)})
-        weighted = None
-        groups = (((0, 0),), ((0, 1), (1, 0), (3, 0)), ((1, 1), (3, 1), (2, 0)), ((2, 1),))
+        groups = (((0, 1), (1, 0), (3, 0)), ((1, 1), (3, 1), (2, 0)), ((2, 1),))
         for group in groups:
             final = group == groups[-1]
             grads = [other[s] if o else own[s] for s, o in group]
             pieces = tuple(group)
-            before = () if weighted is None else (weighted,)
             extra = (transposed,) if final else ()
             result = call(
-                functools.partial(spread_body, pieces, weighted is None, final),
+                functools.partial(spread_body, pieces, False, final),
                 (shape(*half_shape),) * 4 + (shape(*field_shape),) if final else shape(*field_shape),
                 "spread%d" % group[0][0], 1 << 19,
-                slot_owner, ens, *grads, *before, *extra,
-                specs=(SMEM,) + (VMEM,) * (1 + len(grads) + len(before) + len(extra)),
+                slot_owner, ens, *grads, weighted, *extra,
+                specs=(SMEM,) + (VMEM,) * (2 + len(grads) + len(extra)),
             )
             weighted = result
         own_core, own_x, to_core, to_x = result[:4]

time: 99.6 us -> 96.1 us (0.965)
  waiting for transfers between devices: 54.9 us -> 45.1 us
  starting transfers between devices: 29.5 us -> 35.7 us
    ppermute x7, waiting for transfers between devices: 36.9 us -> 26.7 us  [per_device(): lax.ppermute(v, 'mem', [(i, i ^ 2 * s) for i in range(mem_count)])]
    ppermute x2, starting transfers between devices: 2.97 us -> 6.29 us  [per_device(): swap_core = lambda v: lax.ppermute(v, 'lat', core_pairs)]
    ppermute x8, starting transfers between devices: 7.07 us -> 9.15 us  [per_device(): swap_y = lambda v: lax.ppermute(v, 'mem', y_pairs)]
    ppermute x7, starting transfers between devices: 9.13 us -> 11.1 us  [per_device(): lax.ppermute(v, 'mem', [(i, i ^ 2 * s) for i in range(mem_count)])]
    ppermute x2, starting transfers between devices: 9.6 us -> 8.49 us  [per_device(): swap_x = lambda v: lax.ppermute(v, 'lat', x_pairs)]
where the time goes in v7:
time: 96.1 us; the launch traced here: 95.9 us
  waiting for transfers between devices  45.1 us (47%)
  starting transfers between devices  35.7 us (37%)
  Pallas kernels  14.9 us (16%)
    ppermute x7, waiting for transfers between devices, per_device(): lax.ppermute(v, 'mem', [(i, i ^ 2 * s) for i in range(mem_count)])  26.7 us
    ppermute x8, waiting for transfers between devices, per_device(): swap_y = lambda v: lax.ppermute(v, 'mem', y_pairs)  15.7 us
    pallas_call x15, Pallas kernels, call(): pl.pallas_call(kernel, out_shape=outs, in_specs=list(specs) + [ANY] * ext...  14.9 us
    ppermute x7, starting transfers between devices, per_device(): lax.ppermute(v, 'mem', [(i, i ^ 2 * s) for i in range(mem_count)])  11.1 us
    ppermute x8, starting transfers between devices, per_device(): swap_y = lambda v: lax.ppermute(v, 'mem', y_pairs)  9.15 us
    ppermute x2, starting transfers between devices, per_device(): swap_x = lambda v: lax.ppermute(v, 'lat', x_pairs)  8.49 us
    ppermute x2, starting transfers between devices, per_device(): swap_core = lambda v: lax.ppermute(v, 'lat', core_pairs)  6.29 us
    ppermute x2, waiting for transfers between devices, per_device(): swap_x = lambda v: lax.ppermute(v, 'lat', x_pairs)  2.74 us
  transfers between devices with their start and end apart: 20, of which 11 were waited for; matrix products, arithmetic and copies ran while one was open for 0% of the time, Pallas kernels for 8%

profile of v7, /device:TPU:1, one launch (start us, length us, event | category | flops | bytes accessed | tf_op | source)
XLA Modules:
  0.0 95.9 jit_solution(6550346834271576665)
XLA Ops:
  0.0 0.0 copy-start
  0.0 2.3 %front.1 = (f32[2,4,8,1024]{3,2,1,0:T(8,128)S(1)}, f32[2,4,16,1024]{3,2,1,0:T(8,128)S(1)}, f32[16,17]{1,0:T(8,128)S(1)}, f32[16,17]{1,0:T(8,128)S(1)}, s32[8,128...) custom-call(s32[16]{0:T(128)} %refs_0_.11, ...), custom_call_target="tpu_custom_call" | custom-call | flops 524288 | bytes 524288 | tf_op jit(solution)/shard_map/front/pallas_call | solution.py:29
  2.3 4.5 %collective-permute-start = (f32[2,4,8,1024]{3,2,1,0:T(8,128)S(1)}, f32[2,4,8,1024]{3,2,1,0:T(8,128)S(1)}, u32[]{:S(2)}, u32[]{:S(2)}) collective-permute-start(f32[2,4,8,1024]{3,2,1,0:T(8,128)S(1)} %get-tuple-element.44.refs_3_), channel_id=1, source_target_pairs={{1,2},{2,1},{5,6},{6,5},{9,10},{10,9},{13,14},{14,13},{17,18},{18,... | collective-permute-start | bytes 786440 | tf_op jit(solution)/shard_map/ppermute | solution.py:411
  6.9 1.3 %core.1.refs_2_ = f32[2,4,8,1024]{3,2,1,0:T(8,128)S(1)} custom-call(s32[8,128]{1,0:T(8,128)S(1)} %get-tuple-element.43.refs_0_, f32[16,17]{1,0:T(8,128)S(1)} %get-tuple-element.38.refs_1_, f32[2,4,16,1024]{3,2,1,0:T(8,128)S(1)} %get-tuple-element.39.refs_2_), custom_call_target="tpu_custom_call" | custom-call | flops 524288 | bytes 524288 | tf_op jit(solution)/shard_map/core/pallas_call | solution.py:29
  8.1 0.1 collective-permute-start.1
  8.2 0.7 collective-permute-start.3
  8.9 3.9 %collective-permute-start.2 = (f32[2,4,16,1024]{3,2,1,0:T(8,128)S(1)}, f32[2,4,16,1024]{3,2,1,0:T(8,128)S(1)}, u32[]{:S(2)}, u32[]{:S(2)}) collective-permute-start(f32[2,4,16,1024]{3,2,1,0:T(8,128)S(1)} %get-tuple-element.47.refs_1_), channel_id=1, source_target_pairs={{0,8},{4,12},{8,0},{12,4},{16,24},{20,28},{24,16},{28,20},{1,9},{5... | collective-permute-start | bytes 1572872 | tf_op jit(solution)/shard_map/ppermute | solution.py:444
  12.8 0.0 collective-permute-done.refs_3_.refs_5_
  12.8 0.3 matrix.1
  13.1 0.0 collective-permute-done.1.refs_4_
  13.2 0.0 copy-done
  13.2 0.6 first.1
  13.8 1.3 %collective-permute-start.4 = (f32[4,16,1024]{2,1,0:T(8,128)S(1)}, f32[4,16,1024]{2,1,0:T(8,128)S(1)}, u32[]{:S(2)}, u32[]{:S(2)}) collective-permute-start(f32[4,16,1024]{2,1,0:T(8,128)S(1)} %get-tuple-element.50), channel_id=1, source_target_pairs={{0,4},{4,0},{8,12},{12,8},{16,20},{20,16},{24,28},{28,24},{1,5},{5... | collective-permute-start | bytes 786440 | tf_op jit(solution)/shard_map/ppermute | solution.py:443
  15.1 0.0 collective-permute-done.3.refs_4_.refs_3_
  15.1 9.2 %collective-permute-done.2.refs_3_.refs_2_ = f32[2,4,16,1024]{3,2,1,0:T(8,128)S(1)} collective-permute-done((f32[2,4,16,1024]{3,2,1,0:T(8,128)S(1)}, f32[2,4,16,1024]{3,2,1,0:T(8,128)S(1)}, u32[]{:S(2)}, u32[]{:S(2)}) %collective-permute-start.2) | collective-permute-done | bytes 524320 | tf_op jit(solution)/shard_map/ppermute | solution.py:444
  24.3 0.7 send.1
  25.0 0.0 collective-permute-done.4.refs_3_
  25.0 1.3 %collective-permute-start.5 = (f32[2,4,16,1024]{3,2,1,0:T(8,128)S(1)}, f32[2,4,16,1024]{3,2,1,0:T(8,128)S(1)}, u32[]{:S(2)}, u32[]{:S(2)}) collective-permute-start(f32[2,4,16,1024]{3,2,1,0:T(8,128)S(1)} %get-tuple-element.53), channel_id=1, source_target_pairs={{0,4},{4,0},{8,12},{12,8},{16,20},{20,16},{24,28},{28,24},{1,5},{5... | collective-permute-start | bytes 1572872 | tf_op jit(solution)/shard_map/ppermute | solution.py:443
  26.4 0.6 meet2.1.refs_4_
  27.0 1.2 %collective-permute-start.8 = (f32[4,16,1024]{2,1,0:T(8,128)S(1)}, f32[4,16,1024]{2,1,0:T(8,128)S(1)}, u32[]{:S(2)}, u32[]{:S(2)}) collective-permute-start(f32[4,16,1024]{2,1,0:T(8,128)S(1)} %meet2.1.refs_4_), channel_id=1, source_target_pairs={{0,16},{4,20},{8,24},{12,28},{16,0},{20,4},{24,8},{28,12},{1,17},{... | collective-permute-start | bytes 786440 | tf_op jit(solution)/shard_map/ppermute | solution.py:444
  28.1 0.6 weight_pick.1
  28.8 8.4 %collective-permute-done.5.refs_3_ = f32[2,4,16,1024]{3,2,1,0:T(8,128)S(1)} collective-permute-done((f32[2,4,16,1024]{3,2,1,0:T(8,128)S(1)}, f32[2,4,16,1024]{3,2,1,0:T(8,128)S(1)}, u32[]{:S(2)}, u32[]{:S(2)}) %collective-permute-start.5) | collective-permute-done | bytes 524320 | tf_op jit(solution)/shard_map/ppermute | solution.py:443
  37.2 0.7 meet13.1
  37.9 0.9 collective-permute-start.7
  38.8 1.2 %collective-permute-start.9 = (f32[4,16,1024]{2,1,0:T(8,128)S(1)}, f32[4,16,1024]{2,1,0:T(8,128)S(1)}, u32[]{:S(2)}, u32[]{:S(2)}) collective-permute-start(f32[4,16,1024]{2,1,0:T(8,128)S(1)} %get-tuple-element.56), channel_id=1, source_target_pairs={{0,24},{4,28},{8,16},{12,20},{16,8},{20,12},{24,0},{28,4},{1,25},{... | collective-permute-start | bytes 786440 | tf_op jit(solution)/shard_map/ppermute | solution.py:444
  40.0 1.2 %collective-permute-start.6 = (f32[4,16,1024]{2,1,0:T(8,128)S(1)}, f32[4,16,1024]{2,1,0:T(8,128)S(1)}, u32[]{:S(2)}, u32[]{:S(2)}) collective-permute-start(f32[4,16,1024]{2,1,0:T(8,128)S(1)} %get-tuple-element.54), channel_id=1, source_target_pairs={{0,4},{4,0},{8,12},{12,8},{16,20},{20,16},{24,28},{28,24},{1,5},{5... | collective-permute-start | bytes 786440 | tf_op jit(solution)/shard_map/ppermute | solution.py:443
  41.2 0.2 collective-permute-start.10
  41.4 0.0 collective-permute-done.8.refs_5_
  41.5 6.6 %collective-permute-done.7.refs_4_ = f32[4,16,1024]{2,1,0:T(8,128)S(1)} collective-permute-done((f32[4,16,1024]{2,1,0:T(8,128)S(1)}, f32[4,16,1024]{2,1,0:T(8,128)S(1)}, u32[]{:S(2)}, u32[]{:S(2)}) %collective-permute-start.7) | collective-permute-done | bytes 262176 | tf_op jit(solution)/shard_map/ppermute | solution.py:444
  48.0 1.1 %collective-permute-done.9.refs_6_ = f32[4,16,1024]{2,1,0:T(8,128)S(1)} collective-permute-done((f32[4,16,1024]{2,1,0:T(8,128)S(1)}, f32[4,16,1024]{2,1,0:T(8,128)S(1)}, u32[]{:S(2)}, u32[]{:S(2)}) %collective-permute-start.9) | collective-permute-done | bytes 262176 | tf_op jit(solution)/shard_map/ppermute | solution.py:444
  49.1 0.0 collective-permute-done.6.refs_3_
  49.1 1.2 %collective-permute-done.10.refs_8_ = f32[4,16,1024]{2,1,0:T(8,128)S(1)} collective-permute-done((f32[4,16,1024]{2,1,0:T(8,128)S(1)}, f32[4,16,1024]{2,1,0:T(8,128)S(1)}, u32[]{:S(2)}, u32[]{:S(2)}) %collective-permute-start.10) | collective-permute-done | bytes 262176 | tf_op jit(solution)/shard_map/ppermute | solution.py:443
  50.3 0.7 last.1.refs_2_
  51.0 2.1 %collective-permute-start.11 = (f32[4,16,1024]{2,1,0:T(8,128)S(1)}, f32[4,16,1024]{2,1,0:T(8,128)S(1)}, u32[]{:S(2)}, u32[]{:S(2)}) collective-permute-start(f32[4,16,1024]{2,1,0:T(8,128)S(1)} %last.1.refs_2_), channel_id=1, source_target_pairs={{0,24},{4,28},{8,16},{12,20},{16,8},{20,12},{24,0},{28,4},{1,25},{... | collective-permute-start | bytes 786440 | tf_op jit(solution)/shard_map/ppermute | solution.py:444
  53.1 0.6 spread.1.refs_5_
  53.7 1.3 %collective-permute-start.12 = (f32[4,16,1024]{2,1,0:T(8,128)S(1)}, f32[4,16,1024]{2,1,0:T(8,128)S(1)}, u32[]{:S(2)}, u32[]{:S(2)}) collective-permute-start(f32[4,16,1024]{2,1,0:T(8,128)S(1)} %last.1.refs_2_), channel_id=1, source_target_pairs={{0,4},{4,0},{8,12},{12,8},{16,20},{20,16},{24,28},{28,24},{1,5},{5... | collective-permute-start | bytes 786440 | tf_op jit(solution)/shard_map/ppermute | solution.py:443
  55.0 0.0 collective-permute-start.15
  55.0 3.3 %collective-permute-done.11.refs_4_ = f32[4,16,1024]{2,1,0:T(8,128)S(1)} collective-permute-done((f32[4,16,1024]{2,1,0:T(8,128)S(1)}, f32[4,16,1024]{2,1,0:T(8,128)S(1)}, u32[]{:S(2)}, u32[]{:S(2)}) %collective-permute-start.11) | collective-permute-done | bytes 262176 | tf_op jit(solution)/shard_map/ppermute | solution.py:444
  58.3 0.7 collective-permute-done.12.refs_2_
  59.0 1.9 %collective-permute-start.13 = (f32[4,16,1024]{2,1,0:T(8,128)S(1)}, f32[4,16,1024]{2,1,0:T(8,128)S(1)}, u32[]{:S(2)}, u32[]{:S(2)}) collective-permute-start(f32[4,16,1024]{2,1,0:T(8,128)S(1)} %last.1.refs_2_), channel_id=1, source_target_pairs={{0,16},{4,20},{8,24},{12,28},{16,0},{20,4},{24,8},{28,12},{1,17},{... | collective-permute-start | bytes 786440 | tf_op jit(solution)/shard_map/ppermute | solution.py:444
  60.9 1.5 %collective-permute-done.15.refs_3_ = f32[4,16,1024]{2,1,0:T(8,128)S(1)} collective-permute-done((f32[4,16,1024]{2,1,0:T(8,128)S(1)}, f32[4,16,1024]{2,1,0:T(8,128)S(1)}, u32[]{:S(2)}, u32[]{:S(2)}) %collective-permute-start.15) | collective-permute-done | bytes 262176 | tf_op jit(solution)/shard_map/ppermute | solution.py:444
  62.4 2.5 %collective-permute-start.16 = (f32[4,16,1024]{2,1,0:T(8,128)S(1)}, f32[4,16,1024]{2,1,0:T(8,128)S(1)}, u32[]{:S(2)}, u32[]{:S(2)}) collective-permute-start(f32[4,16,1024]{2,1,0:T(8,128)S(1)} %collective-permute-done.15.refs_3_), channel_id=1, source_target_pairs={{0,4},{4,0},{8,12},{12,8},{16,20},{20,16},{24,28},{28,24},{1,5},{5... | collective-permute-start | bytes 786440 | tf_op jit(solution)/shard_map/ppermute | solution.py:443
  64.9 0.0 collective-permute-start.17
  65.0 4.9 %collective-permute-done.13.refs_4_ = f32[4,16,1024]{2,1,0:T(8,128)S(1)} collective-permute-done((f32[4,16,1024]{2,1,0:T(8,128)S(1)}, f32[4,16,1024]{2,1,0:T(8,128)S(1)}, u32[]{:S(2)}, u32[]{:S(2)}) %collective-permute-start.13) | collective-permute-done | bytes 262176 | tf_op jit(solution)/shard_map/ppermute | solution.py:444
  69.9 1.2 %collective-permute-start.14 = (f32[4,16,1024]{2,1,0:T(8,128)S(1)}, f32[4,16,1024]{2,1,0:T(8,128)S(1)}, u32[]{:S(2)}, u32[]{:S(2)}) collective-permute-start(f32[4,16,1024]{2,1,0:T(8,128)S(1)} %collective-permute-done.13.refs_4_), channel_id=1, source_target_pairs={{0,4},{4,0},{8,12},{12,8},{16,20},{20,16},{24,28},{28,24},{1,5},{5... | collective-permute-start | bytes 786440 | tf_op jit(solution)/shard_map/ppermute | solution.py:443
  71.2 0.7 spread0.1.refs_5_
  71.9 0.0 collective-permute-done.16.refs_2_
  71.9 0.0 collective-permute-done.17.refs_3_
  71.9 0.8 spread1.1.refs_3_
  72.7 5.4 %collective-permute-done.14.refs_2_ = f32[4,16,1024]{2,1,0:T(8,128)S(1)} collective-permute-done((f32[4,16,1024]{2,1,0:T(8,128)S(1)}, f32[4,16,1024]{2,1,0:T(8,128)S(1)}, u32[]{:S(2)}, u32[]{:S(2)}) %collective-permute-start.14) | collective-permute-done | bytes 262176 | tf_op jit(solution)/shard_map/ppermute | solution.py:443
  78.1 1.6 %spread2.1 = (f32[2,4,8,1024]{3,2,1,0:T(8,128)S(1)}, f32[2,4,8,1024]{3,2,1,0:T(8,128)S(1)}, f32[2,4,8,1024]{3,2,1,0:T(8,128)S(1)}, f32[2,4,8,1024]{3,2,1,0:T(8,128)S(1)}, f32[2,4,16,1024]{3,2,1,0:T(8,128)}) custom-call(s32[4]{0:T(128)S(1)} %copy-done, bf16[4,2,2,4,16,1024]{5,4,3,2,1,0:T(8,128)(2,1)S(1)} %get-tuple-element.40.refs_6_.refs_1_, ...), custom_call_target="tpu_custom_call" | custom-call | flops 524288 | bytes 524288 | tf_op jit(solution)/shard_map/spread2/pallas_call | solution.py:29
  79.7 6.2 %collective-permute-start.19 = (f32[2,4,8,1024]{3,2,1,0:T(8,128)S(1)}, f32[2,4,8,1024]{3,2,1,0:T(8,128)S(1)}, u32[]{:S(2)}, u32[]{:S(2)}) collective-permute-start(f32[2,4,8,1024]{3,2,1,0:T(8,128)S(1)} %get-tuple-element.68), channel_id=1, source_target_pairs={{0,1},{1,0},{2,3},{3,2},{4,5},{5,4},{6,7},{7,6},{8,9},{9,8},{10,11... | collective-permute-start | bytes 786440 | tf_op jit(solution)/shard_map/ppermute | solution.py:410
  85.9 4.0 %collective-permute-start.18 = (f32[2,4,8,1024]{3,2,1,0:T(8,128)S(1)}, f32[2,4,8,1024]{3,2,1,0:T(8,128)S(1)}, u32[]{:S(2)}, u32[]{:S(2)}) collective-permute-start(f32[2,4,8,1024]{3,2,1,0:T(8,128)S(1)} %get-tuple-element.66), channel_id=1, source_target_pairs={{1,2},{2,1},{5,6},{6,5},{9,10},{10,9},{13,14},{14,13},{17,18},{18,... | collective-permute-start | bytes 786440 | tf_op jit(solution)/shard_map/ppermute | solution.py:411
  89.9 0.0 collective-permute-done.19.refs_4_
  89.9 1.3 %adjoint0.1.refs_5_ = f32[2,4,8,1024]{3,2,1,0:T(8,128)S(1)} custom-call(s32[8,128]{1,0:T(8,128)S(1)} %get-tuple-element.43.refs_0_, f32[16,17]{1,0:T(8,128)S(1)} %get-tuple-element.38.refs_1_, f32[2,4,16,1024]{3,2,1,0:T(8,128)S(1)} %get-tuple-element.39.refs_2_, f32[2,4,8,1024]{3,2,1,0:T(8,128)S(1)} %get-tuple-element.67.refs_3_, ...), custom_call_target="tpu_custom_call" | custom-call | flops 524288 | bytes 524288 | tf_op jit(solution)/shard_map/adjoint0/pallas_call | solution.py:29
  91.2 2.7 %collective-permute-done.18.refs_4_ = f32[2,4,8,1024]{3,2,1,0:T(8,128)S(1)} collective-permute-done((f32[2,4,8,1024]{3,2,1,0:T(8,128)S(1)}, f32[2,4,8,1024]{3,2,1,0:T(8,128)S(1)}, u32[]{:S(2)}, u32[]{:S(2)}) %collective-permute-start.18) | collective-permute-done | bytes 262176 | tf_op jit(solution)/shard_map/ppermute | solution.py:411
  93.9 2.0 %adjoint1.1 = f32[2,4,16,1024]{3,2,1,0:T(8,128)} custom-call(s32[8,128]{1,0:T(8,128)S(1)} %get-tuple-element.37.refs_0_, f32[16,17]{1,0:T(8,128)S(1)} %get-tuple-element.38.refs_1_, f32[2,4,16,1024]{3,2,1,0:T(8,128)S(1)} %get-tuple-element.39.refs_2_, f32[2,4,8,1024]{3,2,1,0:T(8,128)S(1)} %get-tuple-element.65.refs_3_, ...), custom_call_target="tpu_custom_call" | custom-call | flops 524288 | bytes 524288 | tf_op jit(solution)/shard_map/adjoint1/pallas_call | solution.py:29
Async XLA Ops:
  0.0 13.2 %copy-start = (s32[4]{0:T(128)S(1)}, s32[4]{0:T(128)}, u32[]{:S(2)}) copy-start(s32[4]{0:T(128)} %refs_0_.21) | copy-start | bytes 52
  2.3 10.4 %collective-permute-start = (f32[2,4,8,1024]{3,2,1,0:T(8,128)S(1)}, f32[2,4,8,1024]{3,2,1,0:T(8,128)S(1)}, u32[]{:S(2)}, u32[]{:S(2)}) collective-permute-start(f32[2,4,8,1024]{3,2,1,0:T(8,128)S(1)} %get-tuple-element.44.refs_3_), channel_id=1, source_target_pairs={{1,2},{2,1},{5,6},{6,5},{9,10},{10,9},{13,14},{14,13},{17,18},{18,... | collective-permute-start | bytes 786440 | tf_op jit(solution)/shard_map/ppermute | solution.py:411
  8.1 5.0 %collective-permute-start.1 = (f32[2,4,8,1024]{3,2,1,0:T(8,128)S(1)}, f32[2,4,8,1024]{3,2,1,0:T(8,128)S(1)}, u32[]{:S(2)}, u32[]{:S(2)}) collective-permute-start(f32[2,4,8,1024]{3,2,1,0:T(8,128)S(1)} %core.1.refs_2_), channel_id=1, source_target_pairs={{0,1},{1,0},{2,3},{3,2},{4,5},{5,4},{6,7},{7,6},{8,9},{9,8},{10,11... | collective-permute-start | bytes 786440 | tf_op jit(solution)/shard_map/ppermute | solution.py:410
  8.2 6.9 %collective-permute-start.3 = (f32[2,4,16,1024]{3,2,1,0:T(8,128)S(1)}, f32[2,4,16,1024]{3,2,1,0:T(8,128)S(1)}, u32[]{:S(2)}, u32[]{:S(2)}) collective-permute-start(f32[2,4,16,1024]{3,2,1,0:T(8,128)S(1)} %get-tuple-element.47.refs_1_), channel_id=1, source_target_pairs={{8,16},{12,20},{16,8},{20,12},{9,17},{13,21},{17,9},{21,13},{10,18... | collective-permute-start | bytes 1572872 | tf_op jit(solution)/shard_map/ppermute | solution.py:449
  8.9 15.4 %collective-permute-start.2 = (f32[2,4,16,1024]{3,2,1,0:T(8,128)S(1)}, f32[2,4,16,1024]{3,2,1,0:T(8,128)S(1)}, u32[]{:S(2)}, u32[]{:S(2)}) collective-permute-start(f32[2,4,16,1024]{3,2,1,0:T(8,128)S(1)} %get-tuple-element.47.refs_1_), channel_id=1, source_target_pairs={{0,8},{4,12},{8,0},{12,4},{16,24},{20,28},{24,16},{28,20},{1,9},{5... | collective-permute-start | bytes 1572872 | tf_op jit(solution)/shard_map/ppermute | solution.py:444
  13.8 11.2 %collective-permute-start.4 = (f32[4,16,1024]{2,1,0:T(8,128)S(1)}, f32[4,16,1024]{2,1,0:T(8,128)S(1)}, u32[]{:S(2)}, u32[]{:S(2)}) collective-permute-start(f32[4,16,1024]{2,1,0:T(8,128)S(1)} %get-tuple-element.50), channel_id=1, source_target_pairs={{0,4},{4,0},{8,12},{12,8},{16,20},{20,16},{24,28},{28,24},{1,5},{5... | collective-permute-start | bytes 786440 | tf_op jit(solution)/shard_map/ppermute | solution.py:443
  25.0 12.1 %collective-permute-start.5 = (f32[2,4,16,1024]{3,2,1,0:T(8,128)S(1)}, f32[2,4,16,1024]{3,2,1,0:T(8,128)S(1)}, u32[]{:S(2)}, u32[]{:S(2)}) collective-permute-start(f32[2,4,16,1024]{3,2,1,0:T(8,128)S(1)} %get-tuple-element.53), channel_id=1, source_target_pairs={{0,4},{4,0},{8,12},{12,8},{16,20},{20,16},{24,28},{28,24},{1,5},{5... | collective-permute-start | bytes 1572872 | tf_op jit(solution)/shard_map/ppermute | solution.py:443
  27.0 14.5 %collective-permute-start.8 = (f32[4,16,1024]{2,1,0:T(8,128)S(1)}, f32[4,16,1024]{2,1,0:T(8,128)S(1)}, u32[]{:S(2)}, u32[]{:S(2)}) collective-permute-start(f32[4,16,1024]{2,1,0:T(8,128)S(1)} %meet2.1.refs_4_), channel_id=1, source_target_pairs={{0,16},{4,20},{8,24},{12,28},{16,0},{20,4},{24,8},{28,12},{1,17},{... | collective-permute-start | bytes 786440 | tf_op jit(solution)/shard_map/ppermute | solution.py:444
  37.9 10.1 %collective-permute-start.7 = (f32[4,16,1024]{2,1,0:T(8,128)S(1)}, f32[4,16,1024]{2,1,0:T(8,128)S(1)}, u32[]{:S(2)}, u32[]{:S(2)}) collective-permute-start(f32[4,16,1024]{2,1,0:T(8,128)S(1)} %get-tuple-element.55), channel_id=1, source_target_pairs={{0,8},{4,12},{8,0},{12,4},{16,24},{20,28},{24,16},{28,20},{1,9},{5... | collective-permute-start | bytes 786440 | tf_op jit(solution)/shard_map/ppermute | solution.py:444
  38.8 10.3 %collective-permute-start.9 = (f32[4,16,1024]{2,1,0:T(8,128)S(1)}, f32[4,16,1024]{2,1,0:T(8,128)S(1)}, u32[]{:S(2)}, u32[]{:S(2)}) collective-permute-start(f32[4,16,1024]{2,1,0:T(8,128)S(1)} %get-tuple-element.56), channel_id=1, source_target_pairs={{0,24},{4,28},{8,16},{12,20},{16,8},{20,12},{24,0},{28,4},{1,25},{... | collective-permute-start | bytes 786440 | tf_op jit(solution)/shard_map/ppermute | solution.py:444
  40.0 9.1 %collective-permute-start.6 = (f32[4,16,1024]{2,1,0:T(8,128)S(1)}, f32[4,16,1024]{2,1,0:T(8,128)S(1)}, u32[]{:S(2)}, u32[]{:S(2)}) collective-permute-start(f32[4,16,1024]{2,1,0:T(8,128)S(1)} %get-tuple-element.54), channel_id=1, source_target_pairs={{0,4},{4,0},{8,12},{12,8},{16,20},{20,16},{24,28},{28,24},{1,5},{5... | collective-permute-start | bytes 786440 | tf_op jit(solution)/shard_map/ppermute | solution.py:443
  41.2 9.1 %collective-permute-start.10 = (f32[4,16,1024]{2,1,0:T(8,128)S(1)}, f32[4,16,1024]{2,1,0:T(8,128)S(1)}, u32[]{:S(2)}, u32[]{:S(2)}) collective-permute-start(f32[4,16,1024]{2,1,0:T(8,128)S(1)} %get-tuple-element.58.refs_5_), channel_id=1, source_target_pairs={{0,4},{4,0},{8,12},{12,8},{16,20},{20,16},{24,28},{28,24},{1,5},{5... | collective-permute-start | bytes 786440 | tf_op jit(solution)/shard_map/ppermute | solution.py:443
  51.0 7.3 %collective-permute-start.11 = (f32[4,16,1024]{2,1,0:T(8,128)S(1)}, f32[4,16,1024]{2,1,0:T(8,128)S(1)}, u32[]{:S(2)}, u32[]{:S(2)}) collective-permute-start(f32[4,16,1024]{2,1,0:T(8,128)S(1)} %last.1.refs_2_), channel_id=1, source_target_pairs={{0,24},{4,28},{8,16},{12,20},{16,8},{20,12},{24,0},{28,4},{1,25},{... | collective-permute-start | bytes 786440 | tf_op jit(solution)/shard_map/ppermute | solution.py:444
  53.7 5.3 %collective-permute-start.12 = (f32[4,16,1024]{2,1,0:T(8,128)S(1)}, f32[4,16,1024]{2,1,0:T(8,128)S(1)}, u32[]{:S(2)}, u32[]{:S(2)}) collective-permute-start(f32[4,16,1024]{2,1,0:T(8,128)S(1)} %last.1.refs_2_), channel_id=1, source_target_pairs={{0,4},{4,0},{8,12},{12,8},{16,20},{20,16},{24,28},{28,24},{1,5},{5... | collective-permute-start | bytes 786440 | tf_op jit(solution)/shard_map/ppermute | solution.py:443
  55.0 7.4 %collective-permute-start.15 = (f32[4,16,1024]{2,1,0:T(8,128)S(1)}, f32[4,16,1024]{2,1,0:T(8,128)S(1)}, u32[]{:S(2)}, u32[]{:S(2)}) collective-permute-start(f32[4,16,1024]{2,1,0:T(8,128)S(1)} %last.1.refs_2_), channel_id=1, source_target_pairs={{0,8},{4,12},{8,0},{12,4},{16,24},{20,28},{24,16},{28,20},{1,9},{5... | collective-permute-start | bytes 786440 | tf_op jit(solution)/shard_map/ppermute | solution.py:444
  59.0 10.9 %collective-permute-start.13 = (f32[4,16,1024]{2,1,0:T(8,128)S(1)}, f32[4,16,1024]{2,1,0:T(8,128)S(1)}, u32[]{:S(2)}, u32[]{:S(2)}) collective-permute-start(f32[4,16,1024]{2,1,0:T(8,128)S(1)} %last.1.refs_2_), channel_id=1, source_target_pairs={{0,16},{4,20},{8,24},{12,28},{16,0},{20,4},{24,8},{28,12},{1,17},{... | collective-permute-start | bytes 786440 | tf_op jit(solution)/shard_map/ppermute | solution.py:444
  62.4 9.5 %collective-permute-start.16 = (f32[4,16,1024]{2,1,0:T(8,128)S(1)}, f32[4,16,1024]{2,1,0:T(8,128)S(1)}, u32[]{:S(2)}, u32[]{:S(2)}) collective-permute-start(f32[4,16,1024]{2,1,0:T(8,128)S(1)} %collective-permute-done.15.refs_3_), channel_id=1, source_target_pairs={{0,4},{4,0},{8,12},{12,8},{16,20},{20,16},{24,28},{28,24},{1,5},{5... | collective-permute-start | bytes 786440 | tf_op jit(solution)/shard_map/ppermute | solution.py:443
  64.9 7.0 %collective-permute-start.17 = (f32[4,16,1024]{2,1,0:T(8,128)S(1)}, f32[4,16,1024]{2,1,0:T(8,128)S(1)}, u32[]{:S(2)}, u32[]{:S(2)}) collective-permute-start(f32[4,16,1024]{2,1,0:T(8,128)S(1)} %collective-permute-done.11.refs_4_), channel_id=1, source_target_pairs={{0,4},{4,0},{8,12},{12,8},{16,20},{20,16},{24,28},{28,24},{1,5},{5... | collective-permute-start | bytes 786440 | tf_op jit(solution)/shard_map/ppermute | solution.py:443
  69.9 8.1 %collective-permute-start.14 = (f32[4,16,1024]{2,1,0:T(8,128)S(1)}, f32[4,16,1024]{2,1,0:T(8,128)S(1)}, u32[]{:S(2)}, u32[]{:S(2)}) collective-permute-start(f32[4,16,1024]{2,1,0:T(8,128)S(1)} %collective-permute-done.13.refs_4_), channel_id=1, source_target_pairs={{0,4},{4,0},{8,12},{12,8},{16,20},{20,16},{24,28},{28,24},{1,5},{5... | collective-permute-start | bytes 786440 | tf_op jit(solution)/shard_map/ppermute | solution.py:443
  79.7 10.2 %collective-permute-start.19 = (f32[2,4,8,1024]{3,2,1,0:T(8,128)S(1)}, f32[2,4,8,1024]{3,2,1,0:T(8,128)S(1)}, u32[]{:S(2)}, u32[]{:S(2)}) collective-permute-start(f32[2,4,8,1024]{3,2,1,0:T(8,128)S(1)} %get-tuple-element.68), channel_id=1, source_target_pairs={{0,1},{1,0},{2,3},{3,2},{4,5},{5,4},{6,7},{7,6},{8,9},{9,8},{10,11... | collective-permute-start | bytes 786440 | tf_op jit(solution)/shard_map/ppermute | solution.py:410
  85.9 8.0 %collective-permute-start.18 = (f32[2,4,8,1024]{3,2,1,0:T(8,128)S(1)}, f32[2,4,8,1024]{3,2,1,0:T(8,128)S(1)}, u32[]{:S(2)}, u32[]{:S(2)}) collective-permute-start(f32[2,4,8,1024]{3,2,1,0:T(8,128)S(1)} %get-tuple-element.66), channel_id=1, source_target_pairs={{1,2},{2,1},{5,6},{6,5},{9,10},{10,9},{13,14},{14,13},{17,18},{18,... | collective-permute-start | bytes 786440 | tf_op jit(solution)/shard_map/ppermute | solution.py:411

commit v8 on v7

--- a/solution.py
+++ b/solution.py
@@ -182,16 +182,21 @@
     zonal_forward(first, shifts, taps, control, out)
 
 
-def zonal_adjoint(which, shifts, taps_v, control, own, got, *refs):
+def zonal_adjoint(lat_count, which, shifts, taps_v, control, own, got, *refs):
     other, out, taps = (None, *refs) if which == 0 else refs
     members, levels, _, width = control.shape
     first = half_start(which)
     amount = (shifts[...] - HALF) & (width - 1)
     spread_taps(taps_v, first, taps)
+    lat = lax.axis_index("lat")
+    alone = (which == 1) & ((lat == 0) | (lat == lat_count - 1))
 
     def step(m, carry):
         for l in range(levels):
-            columns = [own[m, l, :, cut] + got[m, l, :, cut] for cut in tiles(width)]
+            columns = [
+                own[m, l, :, cut] + jnp.where(alone, 0.0, got[m, l, :, cut])
+                for cut in tiles(width)
+            ]
             result = circle_filter(columns, amount, lambda k: taps[k])
             for cut, value in zip(tiles(width), result):
                 total = control[m, l, pl.ds(first, 8), cut] + value
@@ -262,9 +267,10 @@
                 out[m, l, :, cut] = result[l * band_rows : (l + 1) * band_rows]
 
 
-def delocalize(matrix, weighted, parts):
+def delocalize(matrix, weighted, first, parts):
     members, levels, band_rows, width = weighted.shape
-    left = halves(matrix[...])
+    rows = slice(first * levels * 8, (first + len(parts)) * levels * 8)
+    left = halves(matrix[rows, :])
     for m in range(members):
         for c in range(0, width, CHUNK):
             cut = slice(c, c + CHUNK)
@@ -274,6 +280,10 @@
                 for l in range(levels):
                     start = (p * levels + l) * 8
                     part[m, l, :, cut] = result[start : start + 8]
+
+
+def blocks_body(first, matrix, weighted, *parts):
+    delocalize(matrix, weighted, first, parts)
 
 
 def increment(ens, localized, slot, field, l):
@@ -359,7 +369,7 @@
                 total = term if total is None else total + term
             out[m, l] = total
     if final:
-        delocalize(matrix, out, refs[:4])
+        delocalize(matrix, out, 3, refs[:1])
 
 
 def all_increments(ens, localized, out):
@@ -383,7 +393,7 @@
                     term = ens[slot, field, m, l].astype(F32) * grad[slot, field, l]
                     total = term if total is None else total + term
             out[m, l] = total
-    delocalize(matrix, out, (a, b, c, d))
+    delocalize(matrix, out, 0, (a, b, c, d))
 
 
 def per_device(
@@ -405,10 +415,15 @@
     half_shape = (members, levels, 8, width)
     piece = shape(levels, band_rows, width)
     core_pairs = [(i, i ^ 1) for i in range(lat_count)]
-    x_pairs = [(i, i + 1) for i in range(1, lat_count - 1, 2)]
-    x_pairs += [(j, i) for i, j in x_pairs]
+    x_swaps = [
+        (m * lat_count + i, (m ^ 1) * lat_count + i)
+        if i in (0, lat_count - 1)
+        else (m * lat_count + i, m * lat_count + ((i - 1) ^ 1) + 1)
+        for m in range(mem_count)
+        for i in range(lat_count)
+    ]
     swap_core = lambda v: lax.ppermute(v, "lat", core_pairs)
-    swap_x = lambda v: lax.ppermute(v, "lat", x_pairs)
+    swap_x = lambda v: lax.ppermute(v, ("mem", "lat"), x_swaps)
     tap_room = [pltpu.VMEM((BAND, 8, LANES), F32)]
     ins = {
         "shift": zonal_shift, "taps": zonal_taps, "control": control,
@@ -513,13 +528,17 @@
             extra = (transposed,) if final else ()
             result = call(
                 functools.partial(spread_body, pieces, False, final),
-                (shape(*half_shape),) * 4 + (shape(*field_shape),) if final else shape(*field_shape),
+                (shape(*half_shape), shape(*field_shape)) if final else shape(*field_shape),
                 "spread%d" % group[0][0], 1 << 19,
                 slot_owner, ens, *grads, weighted, *extra,
                 specs=(SMEM,) + (VMEM,) * (2 + len(grads) + len(extra)),
             )
             weighted = result
-        own_core, own_x, to_core, to_x = result[:4]
+        to_x, weighted = result
+        own_core, own_x, to_core = call(
+            functools.partial(blocks_body, 0), (shape(*half_shape),) * 3, "blocks", 1 << 19,
+            transposed, weighted, specs=(VMEM,) * 2,
+        )
     else:
         localized = call(
             localize_body, shape(*field_shape), "localize", 1 << 20, matrix, *parts,
@@ -550,12 +569,12 @@
         )
     got_x, got_core = swap_x(to_x), swap_core(to_core)
     half = call(
-        functools.partial(zonal_adjoint, 0), shape(*half_shape), "adjoint0", 1 << 19,
+        functools.partial(zonal_adjoint, lat_count, 0), shape(*half_shape), "adjoint0", 1 << 19,
         made["shift_core"], made["taps_v"], control_v, own_core, got_core,
         specs=(VMEM,) * 5, scratch=tap_room,
     )
     return call(
-        functools.partial(zonal_adjoint, 1), shape(*field_shape), "adjoint1", 1 << 19,
+        functools.partial(zonal_adjoint, lat_count, 1), shape(*field_shape), "adjoint1", 1 << 19,
         made["shift_x"], made["taps_v"], control_v, own_x, got_x, half,
         specs=(VMEM,) * 6, scratch=tap_room,
     )

time: 96.1 us -> 94.9 us (0.988)
  starting transfers between devices: 35.7 us -> 25.5 us
  waiting for transfers between devices: 45.1 us -> 54.1 us
    ppermute x2, starting transfers between devices: 8.49 us -> 2.67 us  [per_device(): swap_x = lambda v: lax.ppermute(v, ('mem', 'lat'), x_swaps)]
    ppermute x8, starting transfers between devices: 9.15 us -> 4.32 us  [per_device(): swap_y = lambda v: lax.ppermute(v, 'mem', y_pairs)]
    ppermute x7, waiting for transfers between devices: 26.7 us -> 30.3 us  [per_device(): lax.ppermute(v, 'mem', [(i, i ^ 2 * s) for i in range(mem_count)])]
    ppermute x8, waiting for transfers between devices: 15.7 us -> 19 us  [per_device(): swap_y = lambda v: lax.ppermute(v, 'mem', y_pairs)]
    ppermute x2, waiting for transfers between devices: 0.01 us -> 1.16 us  [per_device(): swap_core = lambda v: lax.ppermute(v, 'lat', core_pairs)]
    pallas_call x15 -> x16, Pallas kernels: 14.9 us -> 14.5 us  [call(): pl.pallas_call(kernel, out_shape=outs, in_specs=list(specs) + [ANY] * ext...]
  transfers between devices with their start and end apart: 20 -> 20, of which waited for: 11 -> 13; matrix products, arithmetic and copies ran while one was open for 0% -> 0% of each run, Pallas kernels for 8% -> 8%
where the time goes in v8:
time: 94.9 us; the launch traced here: 94.4 us
  waiting for transfers between devices  54.1 us (57%)
  starting transfers between devices  25.5 us (27%)
  Pallas kernels  14.5 us (15%)
    ppermute x7, waiting for transfers between devices, per_device(): lax.ppermute(v, 'mem', [(i, i ^ 2 * s) for i in range(mem_count)])  30.3 us
    ppermute x8, waiting for transfers between devices, per_device(): swap_y = lambda v: lax.ppermute(v, 'mem', y_pairs)  19 us
    pallas_call x16, Pallas kernels, call(): pl.pallas_call(kernel, out_shape=outs, in_specs=list(specs) + [ANY] * ext...  14.5 us
    ppermute x7, starting transfers between devices, per_device(): lax.ppermute(v, 'mem', [(i, i ^ 2 * s) for i in range(mem_count)])  11.4 us
    ppermute x2, starting transfers between devices, per_device(): swap_core = lambda v: lax.ppermute(v, 'lat', core_pairs)  6.42 us
    ppermute x8, starting transfers between devices, per_device(): swap_y = lambda v: lax.ppermute(v, 'mem', y_pairs)  4.32 us
    ppermute x2, waiting for transfers between devices, per_device(): swap_x = lambda v: lax.ppermute(v, ('mem', 'lat'), x_swaps)  3.61 us
    ppermute x2, starting transfers between devices, per_device(): swap_x = lambda v: lax.ppermute(v, ('mem', 'lat'), x_swaps)  2.67 us
  transfers between devices with their start and end apart: 20, of which 13 were waited for; matrix products, arithmetic and copies ran while one was open for 0% of the time, Pallas kernels for 8%

profile of v8, /device:TPU:1, one launch (start us, length us, event | category | flops | bytes accessed | tf_op | source)
XLA Modules:
  0.0 94.4 jit_solution(1067573801063699161)
XLA Ops:
  0.0 0.0 copy-start
  0.0 2.3 %front.1 = (f32[2,4,8,1024]{3,2,1,0:T(8,128)S(1)}, f32[2,4,16,1024]{3,2,1,0:T(8,128)S(1)}, f32[16,17]{1,0:T(8,128)S(1)}, f32[16,17]{1,0:T(8,128)S(1)}, s32[8,128...) custom-call(s32[16]{0:T(128)} %refs_0_.11, ...), custom_call_target="tpu_custom_call" | custom-call | flops 524288 | bytes 524288 | tf_op jit(solution)/shard_map/front/pallas_call | solution.py:29
  2.3 2.7 %collective-permute-start = (f32[2,4,8,1024]{3,2,1,0:T(8,128)S(1)}, f32[2,4,8,1024]{3,2,1,0:T(8,128)S(1)}, u32[]{:S(2)}, u32[]{:S(2)}) collective-permute-start(f32[2,4,8,1024]{3,2,1,0:T(8,128)S(1)} %get-tuple-element.44.refs_3_), channel_id=1, source_target_pairs={{0,4},{1,2},{2,1},{3,7},{4,0},{5,6},{6,5},{7,3},{8,12},{9,10},{10,... | collective-permute-start | bytes 786440 | tf_op jit(solution)/shard_map/ppermute | solution.py:426
  5.0 1.3 %core.1.refs_2_ = f32[2,4,8,1024]{3,2,1,0:T(8,128)S(1)} custom-call(s32[8,128]{1,0:T(8,128)S(1)} %get-tuple-element.43.refs_0_, f32[16,17]{1,0:T(8,128)S(1)} %get-tuple-element.39.refs_1_, f32[2,4,16,1024]{3,2,1,0:T(8,128)S(1)} %get-tuple-element.40.refs_2_), custom_call_target="tpu_custom_call" | custom-call | flops 524288 | bytes 524288 | tf_op jit(solution)/shard_map/core/pallas_call | solution.py:29
  6.3 0.5 collective-permute-start.1
  6.8 0.7 collective-permute-start.3
  7.5 3.9 %collective-permute-start.2 = (f32[2,4,16,1024]{3,2,1,0:T(8,128)S(1)}, f32[2,4,16,1024]{3,2,1,0:T(8,128)S(1)}, u32[]{:S(2)}, u32[]{:S(2)}) collective-permute-start(f32[2,4,16,1024]{3,2,1,0:T(8,128)S(1)} %get-tuple-element.49.refs_1_), channel_id=1, source_target_pairs={{0,8},{4,12},{8,0},{12,4},{16,24},{20,28},{24,16},{28,20},{1,9},{5... | collective-permute-start | bytes 1572872 | tf_op jit(solution)/shard_map/ppermute | solution.py:459
  11.3 0.0 collective-permute-done.refs_3_.refs_5_
  11.3 0.3 matrix.1
  11.7 0.0 collective-permute-done.1.refs_4_
  11.7 0.0 copy-done
  11.7 0.6 first.1
  12.3 0.9 collective-permute-start.4
  13.2 0.0 collective-permute-done.3.refs_4_.refs_3_
  13.2 10.1 %collective-permute-done.2.refs_3_.refs_2_ = f32[2,4,16,1024]{3,2,1,0:T(8,128)S(1)} collective-permute-done((f32[2,4,16,1024]{3,2,1,0:T(8,128)S(1)}, f32[2,4,16,1024]{3,2,1,0:T(8,128)S(1)}, u32[]{:S(2)}, u32[]{:S(2)}) %collective-permute-start.2) | collective-permute-done | bytes 524320 | tf_op jit(solution)/shard_map/ppermute | solution.py:459
  23.4 0.7 send.1
  24.1 0.0 collective-permute-done.4.refs_3_
  24.1 0.4 collective-permute-start.5
  24.5 0.6 meet2.1.refs_4_
  25.1 1.2 %collective-permute-start.8 = (f32[4,16,1024]{2,1,0:T(8,128)S(1)}, f32[4,16,1024]{2,1,0:T(8,128)S(1)}, u32[]{:S(2)}, u32[]{:S(2)}) collective-permute-start(f32[4,16,1024]{2,1,0:T(8,128)S(1)} %meet2.1.refs_4_), channel_id=1, source_target_pairs={{0,16},{4,20},{8,24},{12,28},{16,0},{20,4},{24,8},{28,12},{1,17},{... | collective-permute-start | bytes 786440 | tf_op jit(solution)/shard_map/ppermute | solution.py:459
  26.3 0.6 weight_pick.1
  26.9 9.8 %collective-permute-done.5.refs_3_ = f32[2,4,16,1024]{3,2,1,0:T(8,128)S(1)} collective-permute-done((f32[2,4,16,1024]{3,2,1,0:T(8,128)S(1)}, f32[2,4,16,1024]{3,2,1,0:T(8,128)S(1)}, u32[]{:S(2)}, u32[]{:S(2)}) %collective-permute-start.5) | collective-permute-done | bytes 524320 | tf_op jit(solution)/shard_map/ppermute | solution.py:458
  36.7 0.7 meet13.1
  37.4 0.9 collective-permute-start.7
  38.3 1.2 %collective-permute-start.9 = (f32[4,16,1024]{2,1,0:T(8,128)S(1)}, f32[4,16,1024]{2,1,0:T(8,128)S(1)}, u32[]{:S(2)}, u32[]{:S(2)}) collective-permute-start(f32[4,16,1024]{2,1,0:T(8,128)S(1)} %get-tuple-element.58), channel_id=1, source_target_pairs={{0,24},{4,28},{8,16},{12,20},{16,8},{20,12},{24,0},{28,4},{1,25},{... | collective-permute-start | bytes 786440 | tf_op jit(solution)/shard_map/ppermute | solution.py:459
  39.5 0.0 collective-permute-start.6
  39.5 1.5 %collective-permute-start.10 = (f32[4,16,1024]{2,1,0:T(8,128)S(1)}, f32[4,16,1024]{2,1,0:T(8,128)S(1)}, u32[]{:S(2)}, u32[]{:S(2)}) collective-permute-start(f32[4,16,1024]{2,1,0:T(8,128)S(1)} %get-tuple-element.60.refs_5_), channel_id=1, source_target_pairs={{0,4},{4,0},{8,12},{12,8},{16,20},{20,16},{24,28},{28,24},{1,5},{5... | collective-permute-start | bytes 786440 | tf_op jit(solution)/shard_map/ppermute | solution.py:458
  40.9 0.0 collective-permute-done.8.refs_5_
  40.9 2.6 %collective-permute-done.7.refs_4_ = f32[4,16,1024]{2,1,0:T(8,128)S(1)} collective-permute-done((f32[4,16,1024]{2,1,0:T(8,128)S(1)}, f32[4,16,1024]{2,1,0:T(8,128)S(1)}, u32[]{:S(2)}, u32[]{:S(2)}) %collective-permute-start.7) | collective-permute-done | bytes 262176 | tf_op jit(solution)/shard_map/ppermute | solution.py:459
  43.5 5.9 %collective-permute-done.9.refs_6_ = f32[4,16,1024]{2,1,0:T(8,128)S(1)} collective-permute-done((f32[4,16,1024]{2,1,0:T(8,128)S(1)}, f32[4,16,1024]{2,1,0:T(8,128)S(1)}, u32[]{:S(2)}, u32[]{:S(2)}) %collective-permute-start.9) | collective-permute-done | bytes 262176 | tf_op jit(solution)/shard_map/ppermute | solution.py:459
  49.4 0.0 collective-permute-done.6.refs_3_
  49.4 0.9 collective-permute-done.10.refs_8_
  50.3 0.7 last.1.refs_2_
  51.0 2.1 %collective-permute-start.11 = (f32[4,16,1024]{2,1,0:T(8,128)S(1)}, f32[4,16,1024]{2,1,0:T(8,128)S(1)}, u32[]{:S(2)}, u32[]{:S(2)}) collective-permute-start(f32[4,16,1024]{2,1,0:T(8,128)S(1)} %last.1.refs_2_), channel_id=1, source_target_pairs={{0,24},{4,28},{8,16},{12,20},{16,8},{20,12},{24,0},{28,4},{1,25},{... | collective-permute-start | bytes 786440 | tf_op jit(solution)/shard_map/ppermute | solution.py:459
  53.0 0.6 spread.1.refs_5_
  53.6 0.1 collective-permute-start.12
  53.7 0.1 collective-permute-start.15
  53.8 4.4 %collective-permute-done.11.refs_4_ = f32[4,16,1024]{2,1,0:T(8,128)S(1)} collective-permute-done((f32[4,16,1024]{2,1,0:T(8,128)S(1)}, f32[4,16,1024]{2,1,0:T(8,128)S(1)}, u32[]{:S(2)}, u32[]{:S(2)}) %collective-permute-start.11) | collective-permute-done | bytes 262176 | tf_op jit(solution)/shard_map/ppermute | solution.py:459
  58.2 0.7 collective-permute-done.12.refs_2_
  58.9 2.2 %collective-permute-start.13 = (f32[4,16,1024]{2,1,0:T(8,128)S(1)}, f32[4,16,1024]{2,1,0:T(8,128)S(1)}, u32[]{:S(2)}, u32[]{:S(2)}) collective-permute-start(f32[4,16,1024]{2,1,0:T(8,128)S(1)} %last.1.refs_2_), channel_id=1, source_target_pairs={{0,16},{4,20},{8,24},{12,28},{16,0},{20,4},{24,8},{28,12},{1,17},{... | collective-permute-start | bytes 786440 | tf_op jit(solution)/shard_map/ppermute | solution.py:459
  61.1 3.9 %collective-permute-done.15.refs_3_ = f32[4,16,1024]{2,1,0:T(8,128)S(1)} collective-permute-done((f32[4,16,1024]{2,1,0:T(8,128)S(1)}, f32[4,16,1024]{2,1,0:T(8,128)S(1)}, u32[]{:S(2)}, u32[]{:S(2)}) %collective-permute-start.15) | collective-permute-done | bytes 262176 | tf_op jit(solution)/shard_map/ppermute | solution.py:459
  65.0 0.0 collective-permute-start.16
  65.0 1.5 %collective-permute-start.17 = (f32[4,16,1024]{2,1,0:T(8,128)S(1)}, f32[4,16,1024]{2,1,0:T(8,128)S(1)}, u32[]{:S(2)}, u32[]{:S(2)}) collective-permute-start(f32[4,16,1024]{2,1,0:T(8,128)S(1)} %collective-permute-done.11.refs_4_), channel_id=1, source_target_pairs={{0,4},{4,0},{8,12},{12,8},{16,20},{20,16},{24,28},{28,24},{1,5},{5... | collective-permute-start | bytes 786440 | tf_op jit(solution)/shard_map/ppermute | solution.py:458
  66.5 3.4 %collective-permute-done.13.refs_4_ = f32[4,16,1024]{2,1,0:T(8,128)S(1)} collective-permute-done((f32[4,16,1024]{2,1,0:T(8,128)S(1)}, f32[4,16,1024]{2,1,0:T(8,128)S(1)}, u32[]{:S(2)}, u32[]{:S(2)}) %collective-permute-start.13) | collective-permute-done | bytes 262176 | tf_op jit(solution)/shard_map/ppermute | solution.py:459
  69.9 0.0 collective-permute-start.14
  69.9 0.7 spread0.1.refs_5_
  70.7 0.0 collective-permute-done.16.refs_2_
  70.7 2.8 %collective-permute-done.17.refs_3_ = f32[4,16,1024]{2,1,0:T(8,128)S(1)} collective-permute-done((f32[4,16,1024]{2,1,0:T(8,128)S(1)}, f32[4,16,1024]{2,1,0:T(8,128)S(1)}, u32[]{:S(2)}, u32[]{:S(2)}) %collective-permute-start.17) | collective-permute-done | bytes 262176 | tf_op jit(solution)/shard_map/ppermute | solution.py:458
  73.5 0.8 spread1.1.refs_3_
  74.3 4.8 %collective-permute-done.14.refs_2_ = f32[4,16,1024]{2,1,0:T(8,128)S(1)} collective-permute-done((f32[4,16,1024]{2,1,0:T(8,128)S(1)}, f32[4,16,1024]{2,1,0:T(8,128)S(1)}, u32[]{:S(2)}, u32[]{:S(2)}) %collective-permute-start.14) | collective-permute-done | bytes 262176 | tf_op jit(solution)/shard_map/ppermute | solution.py:458
  79.1 0.8 spread2.1
  79.9 0.5 blocks.1
  80.4 5.9 %collective-permute-start.19 = (f32[2,4,8,1024]{3,2,1,0:T(8,128)S(1)}, f32[2,4,8,1024]{3,2,1,0:T(8,128)S(1)}, u32[]{:S(2)}, u32[]{:S(2)}) collective-permute-start(f32[2,4,8,1024]{3,2,1,0:T(8,128)S(1)} %get-tuple-element.70), channel_id=1, source_target_pairs={{0,1},{1,0},{2,3},{3,2},{4,5},{5,4},{6,7},{7,6},{8,9},{9,8},{10,11... | collective-permute-start | bytes 786440 | tf_op jit(solution)/shard_map/ppermute | solution.py:425
  86.3 0.0 collective-permute-start.18
  86.3 1.2 %collective-permute-done.19.refs_4_ = f32[2,4,8,1024]{3,2,1,0:T(8,128)S(1)} collective-permute-done((f32[2,4,8,1024]{3,2,1,0:T(8,128)S(1)}, f32[2,4,8,1024]{3,2,1,0:T(8,128)S(1)}, u32[]{:S(2)}, u32[]{:S(2)}) %collective-permute-start.19) | collective-permute-done | bytes 262176 | tf_op jit(solution)/shard_map/ppermute | solution.py:425
  87.5 1.3 %adjoint0.1.refs_5_ = f32[2,4,8,1024]{3,2,1,0:T(8,128)S(1)} custom-call(s32[8,128]{1,0:T(8,128)S(1)} %get-tuple-element.43.refs_0_, f32[16,17]{1,0:T(8,128)S(1)} %get-tuple-element.39.refs_1_, f32[2,4,16,1024]{3,2,1,0:T(8,128)S(1)} %get-tuple-element.40.refs_2_, f32[2,4,8,1024]{3,2,1,0:T(8,128)S(1)} %get-tuple-element.69.refs_3_, ...), custom_call_target="tpu_custom_call" | custom-call | flops 524288 | bytes 524288 | tf_op jit(solution)/shard_map/adjoint0/pallas_call | solution.py:29
  88.8 3.6 %collective-permute-done.18.refs_4_ = f32[2,4,8,1024]{3,2,1,0:T(8,128)S(1)} collective-permute-done((f32[2,4,8,1024]{3,2,1,0:T(8,128)S(1)}, f32[2,4,8,1024]{3,2,1,0:T(8,128)S(1)}, u32[]{:S(2)}, u32[]{:S(2)}) %collective-permute-start.18) | collective-permute-done | bytes 262176 | tf_op jit(solution)/shard_map/ppermute | solution.py:426
  92.4 2.0 %adjoint1.1 = f32[2,4,16,1024]{3,2,1,0:T(8,128)} custom-call(s32[8,128]{1,0:T(8,128)S(1)} %get-tuple-element.38.refs_0_, f32[16,17]{1,0:T(8,128)S(1)} %get-tuple-element.39.refs_1_, f32[2,4,16,1024]{3,2,1,0:T(8,128)S(1)} %get-tuple-element.40.refs_2_, f32[2,4,8,1024]{3,2,1,0:T(8,128)S(1)} %get-tuple-element.67.refs_3_, ...), custom_call_target="tpu_custom_call" | custom-call | flops 524288 | bytes 524288 | tf_op jit(solution)/shard_map/adjoint1/pallas_call | solution.py:29
Async XLA Ops:
  0.0 11.7 %copy-start = (s32[4]{0:T(128)S(1)}, s32[4]{0:T(128)}, u32[]{:S(2)}) copy-start(s32[4]{0:T(128)} %refs_0_.21) | copy-start | bytes 52
  2.3 9.0 %collective-permute-start = (f32[2,4,8,1024]{3,2,1,0:T(8,128)S(1)}, f32[2,4,8,1024]{3,2,1,0:T(8,128)S(1)}, u32[]{:S(2)}, u32[]{:S(2)}) collective-permute-start(f32[2,4,8,1024]{3,2,1,0:T(8,128)S(1)} %get-tuple-element.44.refs_3_), channel_id=1, source_target_pairs={{0,4},{1,2},{2,1},{3,7},{4,0},{5,6},{6,5},{7,3},{8,12},{9,10},{10,... | collective-permute-start | bytes 786440 | tf_op jit(solution)/shard_map/ppermute | solution.py:426
  6.3 5.4 %collective-permute-start.1 = (f32[2,4,8,1024]{3,2,1,0:T(8,128)S(1)}, f32[2,4,8,1024]{3,2,1,0:T(8,128)S(1)}, u32[]{:S(2)}, u32[]{:S(2)}) collective-permute-start(f32[2,4,8,1024]{3,2,1,0:T(8,128)S(1)} %core.1.refs_2_), channel_id=1, source_target_pairs={{0,1},{1,0},{2,3},{3,2},{4,5},{5,4},{6,7},{7,6},{8,9},{9,8},{10,11... | collective-permute-start | bytes 786440 | tf_op jit(solution)/shard_map/ppermute | solution.py:425
  6.8 6.5 %collective-permute-start.3 = (f32[2,4,16,1024]{3,2,1,0:T(8,128)S(1)}, f32[2,4,16,1024]{3,2,1,0:T(8,128)S(1)}, u32[]{:S(2)}, u32[]{:S(2)}) collective-permute-start(f32[2,4,16,1024]{3,2,1,0:T(8,128)S(1)} %get-tuple-element.49.refs_1_), channel_id=1, source_target_pairs={{8,16},{12,20},{16,8},{20,12},{9,17},{13,21},{17,9},{21,13},{10,18... | collective-permute-start | bytes 1572872 | tf_op jit(solution)/shard_map/ppermute | solution.py:464
  7.5 15.9 %collective-permute-start.2 = (f32[2,4,16,1024]{3,2,1,0:T(8,128)S(1)}, f32[2,4,16,1024]{3,2,1,0:T(8,128)S(1)}, u32[]{:S(2)}, u32[]{:S(2)}) collective-permute-start(f32[2,4,16,1024]{3,2,1,0:T(8,128)S(1)} %get-tuple-element.49.refs_1_), channel_id=1, source_target_pairs={{0,8},{4,12},{8,0},{12,4},{16,24},{20,28},{24,16},{28,20},{1,9},{5... | collective-permute-start | bytes 1572872 | tf_op jit(solution)/shard_map/ppermute | solution.py:459
  12.3 11.7 %collective-permute-start.4 = (f32[4,16,1024]{2,1,0:T(8,128)S(1)}, f32[4,16,1024]{2,1,0:T(8,128)S(1)}, u32[]{:S(2)}, u32[]{:S(2)}) collective-permute-start(f32[4,16,1024]{2,1,0:T(8,128)S(1)} %get-tuple-element.52), channel_id=1, source_target_pairs={{0,4},{4,0},{8,12},{12,8},{16,20},{20,16},{24,28},{28,24},{1,5},{5... | collective-permute-start | bytes 786440 | tf_op jit(solution)/shard_map/ppermute | solution.py:458
  24.1 12.6 %collective-permute-start.5 = (f32[2,4,16,1024]{3,2,1,0:T(8,128)S(1)}, f32[2,4,16,1024]{3,2,1,0:T(8,128)S(1)}, u32[]{:S(2)}, u32[]{:S(2)}) collective-permute-start(f32[2,4,16,1024]{3,2,1,0:T(8,128)S(1)} %get-tuple-element.55), channel_id=1, source_target_pairs={{0,4},{4,0},{8,12},{12,8},{16,20},{20,16},{24,28},{28,24},{1,5},{5... | collective-permute-start | bytes 1572872 | tf_op jit(solution)/shard_map/ppermute | solution.py:458
  25.1 15.8 %collective-permute-start.8 = (f32[4,16,1024]{2,1,0:T(8,128)S(1)}, f32[4,16,1024]{2,1,0:T(8,128)S(1)}, u32[]{:S(2)}, u32[]{:S(2)}) collective-permute-start(f32[4,16,1024]{2,1,0:T(8,128)S(1)} %meet2.1.refs_4_), channel_id=1, source_target_pairs={{0,16},{4,20},{8,24},{12,28},{16,0},{20,4},{24,8},{28,12},{1,17},{... | collective-permute-start | bytes 786440 | tf_op jit(solution)/shard_map/ppermute | solution.py:459
  37.4 6.1 %collective-permute-start.7 = (f32[4,16,1024]{2,1,0:T(8,128)S(1)}, f32[4,16,1024]{2,1,0:T(8,128)S(1)}, u32[]{:S(2)}, u32[]{:S(2)}) collective-permute-start(f32[4,16,1024]{2,1,0:T(8,128)S(1)} %get-tuple-element.57), channel_id=1, source_target_pairs={{0,8},{4,12},{8,0},{12,4},{16,24},{20,28},{24,16},{28,20},{1,9},{5... | collective-permute-start | bytes 786440 | tf_op jit(solution)/shard_map/ppermute | solution.py:459
  38.3 11.1 %collective-permute-start.9 = (f32[4,16,1024]{2,1,0:T(8,128)S(1)}, f32[4,16,1024]{2,1,0:T(8,128)S(1)}, u32[]{:S(2)}, u32[]{:S(2)}) collective-permute-start(f32[4,16,1024]{2,1,0:T(8,128)S(1)} %get-tuple-element.58), channel_id=1, source_target_pairs={{0,24},{4,28},{8,16},{12,20},{16,8},{20,12},{24,0},{28,4},{1,25},{... | collective-permute-start | bytes 786440 | tf_op jit(solution)/shard_map/ppermute | solution.py:459
  39.5 9.9 %collective-permute-start.6 = (f32[4,16,1024]{2,1,0:T(8,128)S(1)}, f32[4,16,1024]{2,1,0:T(8,128)S(1)}, u32[]{:S(2)}, u32[]{:S(2)}) collective-permute-start(f32[4,16,1024]{2,1,0:T(8,128)S(1)} %get-tuple-element.56), channel_id=1, source_target_pairs={{0,4},{4,0},{8,12},{12,8},{16,20},{20,16},{24,28},{28,24},{1,5},{5... | collective-permute-start | bytes 786440 | tf_op jit(solution)/shard_map/ppermute | solution.py:458
  39.5 10.8 %collective-permute-start.10 = (f32[4,16,1024]{2,1,0:T(8,128)S(1)}, f32[4,16,1024]{2,1,0:T(8,128)S(1)}, u32[]{:S(2)}, u32[]{:S(2)}) collective-permute-start(f32[4,16,1024]{2,1,0:T(8,128)S(1)} %get-tuple-element.60.refs_5_), channel_id=1, source_target_pairs={{0,4},{4,0},{8,12},{12,8},{16,20},{20,16},{24,28},{28,24},{1,5},{5... | collective-permute-start | bytes 786440 | tf_op jit(solution)/shard_map/ppermute | solution.py:458
  51.0 7.3 %collective-permute-start.11 = (f32[4,16,1024]{2,1,0:T(8,128)S(1)}, f32[4,16,1024]{2,1,0:T(8,128)S(1)}, u32[]{:S(2)}, u32[]{:S(2)}) collective-permute-start(f32[4,16,1024]{2,1,0:T(8,128)S(1)} %last.1.refs_2_), channel_id=1, source_target_pairs={{0,24},{4,28},{8,16},{12,20},{16,8},{20,12},{24,0},{28,4},{1,25},{... | collective-permute-start | bytes 786440 | tf_op jit(solution)/shard_map/ppermute | solution.py:459
  53.6 5.3 %collective-permute-start.12 = (f32[4,16,1024]{2,1,0:T(8,128)S(1)}, f32[4,16,1024]{2,1,0:T(8,128)S(1)}, u32[]{:S(2)}, u32[]{:S(2)}) collective-permute-start(f32[4,16,1024]{2,1,0:T(8,128)S(1)} %last.1.refs_2_), channel_id=1, source_target_pairs={{0,4},{4,0},{8,12},{12,8},{16,20},{20,16},{24,28},{28,24},{1,5},{5... | collective-permute-start | bytes 786440 | tf_op jit(solution)/shard_map/ppermute | solution.py:458
  53.7 11.3 %collective-permute-start.15 = (f32[4,16,1024]{2,1,0:T(8,128)S(1)}, f32[4,16,1024]{2,1,0:T(8,128)S(1)}, u32[]{:S(2)}, u32[]{:S(2)}) collective-permute-start(f32[4,16,1024]{2,1,0:T(8,128)S(1)} %last.1.refs_2_), channel_id=1, source_target_pairs={{0,8},{4,12},{8,0},{12,4},{16,24},{20,28},{24,16},{28,20},{1,9},{5... | collective-permute-start | bytes 786440 | tf_op jit(solution)/shard_map/ppermute | solution.py:459
  58.9 11.0 %collective-permute-start.13 = (f32[4,16,1024]{2,1,0:T(8,128)S(1)}, f32[4,16,1024]{2,1,0:T(8,128)S(1)}, u32[]{:S(2)}, u32[]{:S(2)}) collective-permute-start(f32[4,16,1024]{2,1,0:T(8,128)S(1)} %last.1.refs_2_), channel_id=1, source_target_pairs={{0,16},{4,20},{8,24},{12,28},{16,0},{20,4},{24,8},{28,12},{1,17},{... | collective-permute-start | bytes 786440 | tf_op jit(solution)/shard_map/ppermute | solution.py:459
  65.0 5.6 %collective-permute-start.16 = (f32[4,16,1024]{2,1,0:T(8,128)S(1)}, f32[4,16,1024]{2,1,0:T(8,128)S(1)}, u32[]{:S(2)}, u32[]{:S(2)}) collective-permute-start(f32[4,16,1024]{2,1,0:T(8,128)S(1)} %collective-permute-done.15.refs_3_), channel_id=1, source_target_pairs={{0,4},{4,0},{8,12},{12,8},{16,20},{20,16},{24,28},{28,24},{1,5},{5... | collective-permute-start | bytes 786440 | tf_op jit(solution)/shard_map/ppermute | solution.py:458
  65.0 8.5 %collective-permute-start.17 = (f32[4,16,1024]{2,1,0:T(8,128)S(1)}, f32[4,16,1024]{2,1,0:T(8,128)S(1)}, u32[]{:S(2)}, u32[]{:S(2)}) collective-permute-start(f32[4,16,1024]{2,1,0:T(8,128)S(1)} %collective-permute-done.11.refs_4_), channel_id=1, source_target_pairs={{0,4},{4,0},{8,12},{12,8},{16,20},{20,16},{24,28},{28,24},{1,5},{5... | collective-permute-start | bytes 786440 | tf_op jit(solution)/shard_map/ppermute | solution.py:458
  69.9 9.2 %collective-permute-start.14 = (f32[4,16,1024]{2,1,0:T(8,128)S(1)}, f32[4,16,1024]{2,1,0:T(8,128)S(1)}, u32[]{:S(2)}, u32[]{:S(2)}) collective-permute-start(f32[4,16,1024]{2,1,0:T(8,128)S(1)} %collective-permute-done.13.refs_4_), channel_id=1, source_target_pairs={{0,4},{4,0},{8,12},{12,8},{16,20},{20,16},{24,28},{28,24},{1,5},{5... | collective-permute-start | bytes 786440 | tf_op jit(solution)/shard_map/ppermute | solution.py:458
  80.4 7.1 %collective-permute-start.19 = (f32[2,4,8,1024]{3,2,1,0:T(8,128)S(1)}, f32[2,4,8,1024]{3,2,1,0:T(8,128)S(1)}, u32[]{:S(2)}, u32[]{:S(2)}) collective-permute-start(f32[2,4,8,1024]{3,2,1,0:T(8,128)S(1)} %get-tuple-element.70), channel_id=1, source_target_pairs={{0,1},{1,0},{2,3},{3,2},{4,5},{5,4},{6,7},{7,6},{8,9},{9,8},{10,11... | collective-permute-start | bytes 786440 | tf_op jit(solution)/shard_map/ppermute | solution.py:425
  86.3 6.1 %collective-permute-start.18 = (f32[2,4,8,1024]{3,2,1,0:T(8,128)S(1)}, f32[2,4,8,1024]{3,2,1,0:T(8,128)S(1)}, u32[]{:S(2)}, u32[]{:S(2)}) collective-permute-start(f32[2,4,8,1024]{3,2,1,0:T(8,128)S(1)} %get-tuple-element.68), channel_id=1, source_target_pairs={{0,4},{1,2},{2,1},{3,7},{4,0},{5,6},{6,5},{7,3},{8,12},{9,10},{10,... | collective-permute-start | bytes 786440 | tf_op jit(solution)/shard_map/ppermute | solution.py:426

commit v9 on v8

--- a/solution.py
+++ b/solution.py
@@ -318,22 +318,25 @@
         send[l] = increment(ens, localized, slot, 1 - own_y(), l)
 
 
-def send_body(owners, ens, localized, pair, single):
-    for step, send in ((1, pair.at[0]), (3, pair.at[1]), (0, single)):
+def send_body(owners, ens, localized, three, one):
+    for step, field, send in (
+        (3, 1 - own_y(), three), (1, own_y(), one.at[0]), (1, 1 - own_y(), one.at[1])
+    ):
         slot = slot_at(owners, step)
         for l in range(localized.shape[1]):
-            send[l] = increment(ens, localized, slot, 1 - own_y(), l)
+            send[l] = increment(ens, localized, slot, field, l)
+
+
+def cross_body(owners, ens, localized, got, out):
+    slot = slot_at(owners, 0)
+    for l in range(localized.shape[1]):
+        out[l] = increment(ens, localized, slot, 1 - own_y(), l) + got[1, l]
 
 
 def meet_body(step, owners, ens, localized, got, out):
     slot = slot_at(owners, step)
     for l in range(localized.shape[1]):
         out[l] = increment(ens, localized, slot, own_y(), l) + got[l]
-
-
-def meet_pair_body(owners, ens, localized, got, *outs):
-    for i, (step, out) in enumerate(zip((1, 3), outs)):
-        meet_body(step, owners, ens, localized, got.at[i], out)
 
 
 def last_body(owners, ens, localized, got_y, got_1, got_2, got_3, mine, from_y, out):
@@ -347,7 +350,7 @@
                 out[l] = weight[l] * (
                     increment(ens, localized, slot, own_y(), l)
                     + got_y[l]
-                    + (got_1[l] + got_2[l] + got_3[l])
+                    + (got_1[0, l] + got_2[l] + got_3[l])
                 )
 
 
@@ -482,29 +485,34 @@
             scratch=[pltpu.SMEM((SLOTS,), jnp.int32), pltpu.SemaphoreType.DMA],
         )
         got_two = swap_y(first)
-        pair, single = call(
-            send_body, (shape(2, levels, band_rows, width), piece), "send", 1 << 20,
+        three, one = call(
+            send_body, (piece, shape(2, levels, band_rows, width)), "send", 1 << 20,
             slot_owner, ens, localized, specs=(SMEM, VMEM, VMEM), after=(from_side, from_middle),
         )
-        pair, got_two = lax.optimization_barrier((pair, got_two))
-        got_pair = swap_y(pair)
-        two = call(
-            functools.partial(meet_body, 2), piece, "meet2", 1 << 19,
-            slot_owner, ens, localized, got_two, specs=(SMEM,) + (VMEM,) * 3,
-        )
-        arrived = {2: turn_z(two, 2)}
+
+        def meet(s, got, after):
+            return call(
+                functools.partial(meet_body, s), piece, "meet%d" % s, 1 << 19,
+                slot_owner, ens, localized, got, specs=(SMEM,) + (VMEM,) * 3, after=after,
+            )
+
+        three, got_two = lax.optimization_barrier((three, got_two))
+        got_three = swap_y(three)
+        two = meet(2, got_two, ())
+        arrived = {2: turn_z(two, 2), 1: turn_z(one, 1)}
         mine, across = call(
             weight_pick, (piece,) * 2, "weight_pick", 1 << 18, slot_owner, made["obs_v"],
             from_side, from_middle, specs=(SMEM,) + (VMEM,) * 3, after=(two,),
         )
-        one, three = call(
-            meet_pair_body, (piece,) * 2, "meet13", 1 << 19,
-            slot_owner, ens, localized, got_pair, specs=(SMEM,) + (VMEM,) * 3,
-            after=(two, across),
-        )
-        arrived[1], arrived[3] = turn_z(one, 1), turn_z(three, 3)
-        single, across, _ = lax.optimization_barrier((single, across, got_pair))
-        got_own, from_y = swap_y(single), swap_y(across)
+        three = meet(3, got_three, (two, across))
+        arrived[3] = turn_z(three, 3)
+        across, _ = lax.optimization_barrier((across, got_three))
+        from_y = swap_y(across)
+        cross = call(
+            cross_body, piece, "cross", 1 << 19, slot_owner, ens, localized, arrived[1],
+            specs=(SMEM,) + (VMEM,) * 3, after=(three,),
+        )
+        got_own = swap_y(cross)
         grad = call(
             last_body, piece, "last", 1 << 19, slot_owner, ens, localized, got_own,
             arrived[1], arrived[2], arrived[3], mine, from_y,
@@ -519,7 +527,9 @@
         other = {0: swap_y(other)}
         later, own[3], other[0] = lax.optimization_barrier((grad, own[3], other[0]))
         own[2] = turn_z(later, 2)
-        other.update({s: swap_y(own[s]) for s in (1, 3, 2)})
+        along, own[1] = lax.optimization_barrier((other[0], own[1]))
+        other[1] = turn_z(along, 1)
+        other.update({s: swap_y(own[s]) for s in (3, 2)})
         groups = (((0, 1), (1, 0), (3, 0)), ((1, 1), (3, 1), (2, 0)), ((2, 1),))
         for group in groups:
             final = group == groups[-1]

time: 94.9 us -> 90.8 us (0.957)
  waiting for transfers between devices: 54.1 us -> 39.4 us
  starting transfers between devices: 25.5 us -> 35.7 us
    ppermute x7 -> x8, starting transfers between devices: 11.4 us -> 21.6 us  [per_device(): lax.ppermute(v, 'mem', [(i, i ^ 2 * s) for i in range(mem_count)])]
    ppermute x7 -> x8, waiting for transfers between devices: 30.3 us -> 21.4 us  [per_device(): lax.ppermute(v, 'mem', [(i, i ^ 2 * s) for i in range(mem_count)])]
    ppermute x8 -> x7, waiting for transfers between devices: 19 us -> 10.7 us  [per_device(): swap_y = lambda v: lax.ppermute(v, 'mem', y_pairs)]
    ppermute x8 -> x7, starting transfers between devices: 4.32 us -> 7.03 us  [per_device(): swap_y = lambda v: lax.ppermute(v, 'mem', y_pairs)]
    ppermute x2, waiting for transfers between devices: 3.61 us -> 6.2 us  [per_device(): swap_x = lambda v: lax.ppermute(v, ('mem', 'lat'), x_swaps)]
    ppermute x2, starting transfers between devices: 6.42 us -> 3.97 us  [per_device(): swap_core = lambda v: lax.ppermute(v, 'lat', core_pairs)]
    pallas_call x16 -> x17, Pallas kernels: 14.5 us -> 15.1 us  [call(): pl.pallas_call(kernel, out_shape=outs, in_specs=list(specs) + [ANY] * ext...]
  transfers between devices with their start and end apart: 20 -> 20, of which waited for: 13 -> 11; matrix products, arithmetic and copies ran while one was open for 0% -> 0% of each run, Pallas kernels for 8% -> 9%
where the time goes in v9:
time: 90.8 us; the launch traced here: 90.3 us
  waiting for transfers between devices  39.4 us (43%)
  starting transfers between devices  35.7 us (39%)
  Pallas kernels  15.1 us (17%)
    ppermute x8, starting transfers between devices, per_device(): lax.ppermute(v, 'mem', [(i, i ^ 2 * s) for i in range(mem_count)])  21.6 us
    ppermute x8, waiting for transfers between devices, per_device(): lax.ppermute(v, 'mem', [(i, i ^ 2 * s) for i in range(mem_count)])  21.4 us
    pallas_call x17, Pallas kernels, call(): pl.pallas_call(kernel, out_shape=outs, in_specs=list(specs) + [ANY] * ext...  15.1 us
    ppermute x7, waiting for transfers between devices, per_device(): swap_y = lambda v: lax.ppermute(v, 'mem', y_pairs)  10.7 us
    ppermute x7, starting transfers between devices, per_device(): swap_y = lambda v: lax.ppermute(v, 'mem', y_pairs)  7.03 us
    ppermute x2, waiting for transfers between devices, per_device(): swap_x = lambda v: lax.ppermute(v, ('mem', 'lat'), x_swaps)  6.2 us
    ppermute x2, starting transfers between devices, per_device(): swap_core = lambda v: lax.ppermute(v, 'lat', core_pairs)  3.97 us
    ppermute x2, starting transfers between devices, per_device(): swap_x = lambda v: lax.ppermute(v, ('mem', 'lat'), x_swaps)  2.38 us
  transfers between devices with their start and end apart: 20, of which 11 were waited for; matrix products, arithmetic and copies ran while one was open for 0% of the time, Pallas kernels for 9%

profile of v9, /device:TPU:1, one launch (start us, length us, event | category | flops | bytes accessed | tf_op | source)
XLA Modules:
  0.0 90.3 jit_solution(11515988384209448850)
XLA Ops:
  0.0 0.0 copy-start
  0.0 2.3 %front.1 = (f32[2,4,8,1024]{3,2,1,0:T(8,128)S(1)}, f32[2,4,16,1024]{3,2,1,0:T(8,128)S(1)}, f32[16,17]{1,0:T(8,128)S(1)}, f32[16,17]{1,0:T(8,128)S(1)}, s32[8,128...) custom-call(s32[16]{0:T(128)} %refs_0_.12, ...), custom_call_target="tpu_custom_call" | custom-call | flops 524288 | bytes 524288 | tf_op jit(solution)/shard_map/front/pallas_call | solution.py:29
  2.3 0.7 collective-permute-start.3
  3.0 4.7 %collective-permute-start.2 = (f32[2,4,16,1024]{3,2,1,0:T(8,128)S(1)}, f32[2,4,16,1024]{3,2,1,0:T(8,128)S(1)}, u32[]{:S(2)}, u32[]{:S(2)}) collective-permute-start(f32[2,4,16,1024]{3,2,1,0:T(8,128)S(1)} %get-tuple-element.48.refs_1_), channel_id=1, source_target_pairs={{0,8},{4,12},{8,0},{12,4},{16,24},{20,28},{24,16},{28,20},{1,9},{5... | collective-permute-start | bytes 1572872 | tf_op jit(solution)/shard_map/ppermute | solution.py:462
  7.7 2.3 %collective-permute-start = (f32[2,4,8,1024]{3,2,1,0:T(8,128)S(1)}, f32[2,4,8,1024]{3,2,1,0:T(8,128)S(1)}, u32[]{:S(2)}, u32[]{:S(2)}) collective-permute-start(f32[2,4,8,1024]{3,2,1,0:T(8,128)S(1)} %get-tuple-element.43.refs_3_), channel_id=1, source_target_pairs={{0,4},{1,2},{2,1},{3,7},{4,0},{5,6},{6,5},{7,3},{8,12},{9,10},{10,... | collective-permute-start | bytes 786440 | tf_op jit(solution)/shard_map/ppermute | solution.py:429
  10.1 1.3 %core.1.refs_2_ = f32[2,4,8,1024]{3,2,1,0:T(8,128)S(1)} custom-call(s32[8,128]{1,0:T(8,128)S(1)} %get-tuple-element.42.refs_0_, f32[16,17]{1,0:T(8,128)S(1)} %get-tuple-element.38.refs_1_, f32[2,4,16,1024]{3,2,1,0:T(8,128)S(1)} %get-tuple-element.39.refs_2_), custom_call_target="tpu_custom_call" | custom-call | flops 524288 | bytes 524288 | tf_op jit(solution)/shard_map/core/pallas_call | solution.py:29
  11.3 0.5 collective-permute-start.1
  11.8 2.6 %collective-permute-done.refs_3_.refs_5_ = f32[2,4,8,1024]{3,2,1,0:T(8,128)S(1)} collective-permute-done((f32[2,4,8,1024]{3,2,1,0:T(8,128)S(1)}, f32[2,4,8,1024]{3,2,1,0:T(8,128)S(1)}, u32[]{:S(2)}, u32[]{:S(2)}) %collective-permute-start) | collective-permute-done | bytes 262176 | tf_op jit(solution)/shard_map/ppermute | solution.py:429
  14.4 0.3 matrix.1
  14.8 0.0 collective-permute-done.1.refs_4_
  14.8 0.0 copy-done
  14.8 0.6 first.1
  15.4 1.3 %collective-permute-start.5 = (f32[4,16,1024]{2,1,0:T(8,128)S(1)}, f32[4,16,1024]{2,1,0:T(8,128)S(1)}, u32[]{:S(2)}, u32[]{:S(2)}) collective-permute-start(f32[4,16,1024]{2,1,0:T(8,128)S(1)} %get-tuple-element.51), channel_id=1, source_target_pairs={{0,4},{4,0},{8,12},{12,8},{16,20},{20,16},{24,28},{28,24},{1,5},{5... | collective-permute-start | bytes 786440 | tf_op jit(solution)/shard_map/ppermute | solution.py:461
  16.7 0.0 collective-permute-done.3.refs_4_.refs_3_
  16.7 2.3 %collective-permute-done.2.refs_3_.refs_2_ = f32[2,4,16,1024]{3,2,1,0:T(8,128)S(1)} collective-permute-done((f32[2,4,16,1024]{3,2,1,0:T(8,128)S(1)}, f32[2,4,16,1024]{3,2,1,0:T(8,128)S(1)}, u32[]{:S(2)}, u32[]{:S(2)}) %collective-permute-start.2) | collective-permute-done | bytes 524320 | tf_op jit(solution)/shard_map/ppermute | solution.py:462
  19.1 0.7 send.1
  19.8 1.2 %collective-permute-start.4 = (f32[2,4,16,1024]{3,2,1,0:T(8,128)S(1)}, f32[2,4,16,1024]{3,2,1,0:T(8,128)S(1)}, u32[]{:S(2)}, u32[]{:S(2)}) collective-permute-start(f32[2,4,16,1024]{3,2,1,0:T(8,128)S(1)} %get-tuple-element.49), channel_id=1, source_target_pairs={{0,8},{4,12},{8,0},{12,4},{16,24},{20,28},{24,16},{28,20},{1,9},{5... | collective-permute-start | bytes 1572872 | tf_op jit(solution)/shard_map/ppermute | solution.py:462
  21.0 1.4 %collective-permute-done.5.refs_3_ = f32[4,16,1024]{2,1,0:T(8,128)S(1)} collective-permute-done((f32[4,16,1024]{2,1,0:T(8,128)S(1)}, f32[4,16,1024]{2,1,0:T(8,128)S(1)}, u32[]{:S(2)}, u32[]{:S(2)}) %collective-permute-start.5) | collective-permute-done | bytes 262176 | tf_op jit(solution)/shard_map/ppermute | solution.py:461
  22.4 1.2 %collective-permute-start.6 = (f32[4,16,1024]{2,1,0:T(8,128)S(1)}, f32[4,16,1024]{2,1,0:T(8,128)S(1)}, u32[]{:S(2)}, u32[]{:S(2)}) collective-permute-start(f32[4,16,1024]{2,1,0:T(8,128)S(1)} %get-tuple-element.52), channel_id=1, source_target_pairs={{0,4},{4,0},{8,12},{12,8},{16,20},{20,16},{24,28},{28,24},{1,5},{5... | collective-permute-start | bytes 786440 | tf_op jit(solution)/shard_map/ppermute | solution.py:461
  23.6 0.6 meet2.1.refs_4_
  24.2 0.1 collective-permute-start.8
  24.3 0.6 weight_pick.1
  24.9 3.4 %collective-permute-done.6.refs_3_ = f32[4,16,1024]{2,1,0:T(8,128)S(1)} collective-permute-done((f32[4,16,1024]{2,1,0:T(8,128)S(1)}, f32[4,16,1024]{2,1,0:T(8,128)S(1)}, u32[]{:S(2)}, u32[]{:S(2)}) %collective-permute-start.6) | collective-permute-done | bytes 262176 | tf_op jit(solution)/shard_map/ppermute | solution.py:461
  28.4 1.2 %collective-permute-start.10 = (f32[4,16,1024]{2,1,0:T(8,128)S(1)}, f32[4,16,1024]{2,1,0:T(8,128)S(1)}, u32[]{:S(2)}, u32[]{:S(2)}) collective-permute-start(f32[4,16,1024]{2,1,0:T(8,128)S(1)} %get-tuple-element.56.refs_5_), channel_id=1, source_target_pairs={{0,4},{4,0},{8,12},{12,8},{16,20},{20,16},{24,28},{28,24},{1,5},{5... | collective-permute-start | bytes 786440 | tf_op jit(solution)/shard_map/ppermute | solution.py:461
  29.6 0.6 meet3.1.refs_4_
  30.2 1.1 %collective-permute-start.9 = (f32[4,16,1024]{2,1,0:T(8,128)S(1)}, f32[4,16,1024]{2,1,0:T(8,128)S(1)}, u32[]{:S(2)}, u32[]{:S(2)}) collective-permute-start(f32[4,16,1024]{2,1,0:T(8,128)S(1)} %meet3.1.refs_4_), channel_id=1, source_target_pairs={{0,24},{4,28},{8,16},{12,20},{16,8},{20,12},{24,0},{28,4},{1,25},{... | collective-permute-start | bytes 786440 | tf_op jit(solution)/shard_map/ppermute | solution.py:462
  31.4 6.0 %collective-permute-done.4.refs_3_.refs_4_ = f32[2,4,16,1024]{3,2,1,0:T(8,128)S(1)} collective-permute-done((f32[2,4,16,1024]{3,2,1,0:T(8,128)S(1)}, f32[2,4,16,1024]{3,2,1,0:T(8,128)S(1)}, u32[]{:S(2)}, u32[]{:S(2)}) %collective-permute-start.4) | collective-permute-done | bytes 524320 | tf_op jit(solution)/shard_map/ppermute | solution.py:462
  37.3 0.6 cross.1
  38.0 1.3 %collective-permute-start.7 = (f32[4,16,1024]{2,1,0:T(8,128)S(1)}, f32[4,16,1024]{2,1,0:T(8,128)S(1)}, u32[]{:S(2)}, u32[]{:S(2)}) collective-permute-start(f32[4,16,1024]{2,1,0:T(8,128)S(1)} %cross.1), channel_id=1, source_target_pairs={{0,4},{4,0},{8,12},{12,8},{16,20},{20,16},{24,28},{28,24},{1,5},{5... | collective-permute-start | bytes 786440 | tf_op jit(solution)/shard_map/ppermute | solution.py:461
  39.3 0.0 collective-permute-done.8.refs_5_
  39.3 0.0 collective-permute-done.10.refs_8_
  39.3 4.3 %collective-permute-done.9.refs_6_ = f32[4,16,1024]{2,1,0:T(8,128)S(1)} collective-permute-done((f32[4,16,1024]{2,1,0:T(8,128)S(1)}, f32[4,16,1024]{2,1,0:T(8,128)S(1)}, u32[]{:S(2)}, u32[]{:S(2)}) %collective-permute-start.9) | collective-permute-done | bytes 262176 | tf_op jit(solution)/shard_map/ppermute | solution.py:462
  43.6 0.0 collective-permute-done.7.refs_3_
  43.6 0.7 last.1.refs_2_
  44.2 2.1 %collective-permute-start.11 = (f32[4,16,1024]{2,1,0:T(8,128)S(1)}, f32[4,16,1024]{2,1,0:T(8,128)S(1)}, u32[]{:S(2)}, u32[]{:S(2)}) collective-permute-start(f32[4,16,1024]{2,1,0:T(8,128)S(1)} %last.1.refs_2_), channel_id=1, source_target_pairs={{0,24},{4,28},{8,16},{12,20},{16,8},{20,12},{24,0},{28,4},{1,25},{... | collective-permute-start | bytes 786440 | tf_op jit(solution)/shard_map/ppermute | solution.py:462
  46.4 0.6 spread.1.refs_5_
  47.0 1.3 %collective-permute-start.12 = (f32[4,16,1024]{2,1,0:T(8,128)S(1)}, f32[4,16,1024]{2,1,0:T(8,128)S(1)}, u32[]{:S(2)}, u32[]{:S(2)}) collective-permute-start(f32[4,16,1024]{2,1,0:T(8,128)S(1)} %last.1.refs_2_), channel_id=1, source_target_pairs={{0,4},{4,0},{8,12},{12,8},{16,20},{20,16},{24,28},{28,24},{1,5},{5... | collective-permute-start | bytes 786440 | tf_op jit(solution)/shard_map/ppermute | solution.py:461
  48.3 5.6 %collective-permute-start.15 = (f32[4,16,1024]{2,1,0:T(8,128)S(1)}, f32[4,16,1024]{2,1,0:T(8,128)S(1)}, u32[]{:S(2)}, u32[]{:S(2)}) collective-permute-start(f32[4,16,1024]{2,1,0:T(8,128)S(1)} %last.1.refs_2_), channel_id=1, source_target_pairs={{0,8},{4,12},{8,0},{12,4},{16,24},{20,28},{24,16},{28,20},{1,9},{5... | collective-permute-start | bytes 786440 | tf_op jit(solution)/shard_map/ppermute | solution.py:462
  53.9 0.0 collective-permute-done.11.refs_4_
  53.9 0.0 collective-permute-done.12.refs_2_
  53.9 6.3 %collective-permute-start.13 = (f32[4,16,1024]{2,1,0:T(8,128)S(1)}, f32[4,16,1024]{2,1,0:T(8,128)S(1)}, u32[]{:S(2)}, u32[]{:S(2)}) collective-permute-start(f32[4,16,1024]{2,1,0:T(8,128)S(1)} %last.1.refs_2_), channel_id=1, source_target_pairs={{0,16},{4,20},{8,24},{12,28},{16,0},{20,4},{24,8},{28,12},{1,17},{... | collective-permute-start | bytes 786440 | tf_op jit(solution)/shard_map/ppermute | solution.py:462
  60.2 0.0 collective-permute-done.15.refs_3_
  60.2 0.4 collective-permute-start.16
  60.7 0.6 collective-permute-start.17
  61.3 8.1 %collective-permute-done.13.refs_4_ = f32[4,16,1024]{2,1,0:T(8,128)S(1)} collective-permute-done((f32[4,16,1024]{2,1,0:T(8,128)S(1)}, f32[4,16,1024]{2,1,0:T(8,128)S(1)}, u32[]{:S(2)}, u32[]{:S(2)}) %collective-permute-start.13) | collective-permute-done | bytes 262176 | tf_op jit(solution)/shard_map/ppermute | solution.py:462
  69.4 0.0 collective-permute-start.14
  69.4 0.7 spread0.1.refs_5_
  70.1 0.7 collective-permute-done.16.refs_2_
  70.8 0.0 collective-permute-done.17.refs_3_
  70.8 0.8 spread1.1.refs_3_
  71.6 5.9 %collective-permute-done.14.refs_2_ = f32[4,16,1024]{2,1,0:T(8,128)S(1)} collective-permute-done((f32[4,16,1024]{2,1,0:T(8,128)S(1)}, f32[4,16,1024]{2,1,0:T(8,128)S(1)}, u32[]{:S(2)}, u32[]{:S(2)}) %collective-permute-start.14) | collective-permute-done | bytes 262176 | tf_op jit(solution)/shard_map/ppermute | solution.py:461
  77.5 0.8 spread2.1
  78.4 0.5 blocks.1
  78.8 3.5 %collective-permute-start.19 = (f32[2,4,8,1024]{3,2,1,0:T(8,128)S(1)}, f32[2,4,8,1024]{3,2,1,0:T(8,128)S(1)}, u32[]{:S(2)}, u32[]{:S(2)}) collective-permute-start(f32[2,4,8,1024]{3,2,1,0:T(8,128)S(1)} %get-tuple-element.68), channel_id=1, source_target_pairs={{0,1},{1,0},{2,3},{3,2},{4,5},{5,4},{6,7},{7,6},{8,9},{9,8},{10,11... | collective-permute-start | bytes 786440 | tf_op jit(solution)/shard_map/ppermute | solution.py:428
  82.3 0.0 collective-permute-start.18
  82.4 1.1 %collective-permute-done.19.refs_4_ = f32[2,4,8,1024]{3,2,1,0:T(8,128)S(1)} collective-permute-done((f32[2,4,8,1024]{3,2,1,0:T(8,128)S(1)}, f32[2,4,8,1024]{3,2,1,0:T(8,128)S(1)}, u32[]{:S(2)}, u32[]{:S(2)}) %collective-permute-start.19) | collective-permute-done | bytes 262176 | tf_op jit(solution)/shard_map/ppermute | solution.py:428
  83.5 1.3 %adjoint0.1.refs_5_ = f32[2,4,8,1024]{3,2,1,0:T(8,128)S(1)} custom-call(s32[8,128]{1,0:T(8,128)S(1)} %get-tuple-element.42.refs_0_, f32[16,17]{1,0:T(8,128)S(1)} %get-tuple-element.38.refs_1_, f32[2,4,16,1024]{3,2,1,0:T(8,128)S(1)} %get-tuple-element.39.refs_2_, f32[2,4,8,1024]{3,2,1,0:T(8,128)S(1)} %get-tuple-element.67.refs_3_, ...), custom_call_target="tpu_custom_call" | custom-call | flops 524288 | bytes 524288 | tf_op jit(solution)/shard_map/adjoint0/pallas_call | solution.py:29
  84.8 3.6 %collective-permute-done.18.refs_4_ = f32[2,4,8,1024]{3,2,1,0:T(8,128)S(1)} collective-permute-done((f32[2,4,8,1024]{3,2,1,0:T(8,128)S(1)}, f32[2,4,8,1024]{3,2,1,0:T(8,128)S(1)}, u32[]{:S(2)}, u32[]{:S(2)}) %collective-permute-start.18) | collective-permute-done | bytes 262176 | tf_op jit(solution)/shard_map/ppermute | solution.py:429
  88.4 2.0 %adjoint1.1 = f32[2,4,16,1024]{3,2,1,0:T(8,128)} custom-call(s32[8,128]{1,0:T(8,128)S(1)} %get-tuple-element.37.refs_0_, f32[16,17]{1,0:T(8,128)S(1)} %get-tuple-element.38.refs_1_, f32[2,4,16,1024]{3,2,1,0:T(8,128)S(1)} %get-tuple-element.39.refs_2_, f32[2,4,8,1024]{3,2,1,0:T(8,128)S(1)} %get-tuple-element.65.refs_3_, ...), custom_call_target="tpu_custom_call" | custom-call | flops 524288 | bytes 524288 | tf_op jit(solution)/shard_map/adjoint1/pallas_call | solution.py:29
Async XLA Ops:
  0.0 14.8 %copy-start = (s32[4]{0:T(128)S(1)}, s32[4]{0:T(128)}, u32[]{:S(2)}) copy-start(s32[4]{0:T(128)} %refs_0_.23) | copy-start | bytes 52
  2.3 14.4 %collective-permute-start.3 = (f32[2,4,16,1024]{3,2,1,0:T(8,128)S(1)}, f32[2,4,16,1024]{3,2,1,0:T(8,128)S(1)}, u32[]{:S(2)}, u32[]{:S(2)}) collective-permute-start(f32[2,4,16,1024]{3,2,1,0:T(8,128)S(1)} %get-tuple-element.48.refs_1_), channel_id=1, source_target_pairs={{8,16},{12,20},{16,8},{20,12},{9,17},{13,21},{17,9},{21,13},{10,18... | collective-permute-start | bytes 1572872 | tf_op jit(solution)/shard_map/ppermute | solution.py:467
  3.0 16.0 %collective-permute-start.2 = (f32[2,4,16,1024]{3,2,1,0:T(8,128)S(1)}, f32[2,4,16,1024]{3,2,1,0:T(8,128)S(1)}, u32[]{:S(2)}, u32[]{:S(2)}) collective-permute-start(f32[2,4,16,1024]{3,2,1,0:T(8,128)S(1)} %get-tuple-element.48.refs_1_), channel_id=1, source_target_pairs={{0,8},{4,12},{8,0},{12,4},{16,24},{20,28},{24,16},{28,20},{1,9},{5... | collective-permute-start | bytes 1572872 | tf_op jit(solution)/shard_map/ppermute | solution.py:462
  7.7 6.7 %collective-permute-start = (f32[2,4,8,1024]{3,2,1,0:T(8,128)S(1)}, f32[2,4,8,1024]{3,2,1,0:T(8,128)S(1)}, u32[]{:S(2)}, u32[]{:S(2)}) collective-permute-start(f32[2,4,8,1024]{3,2,1,0:T(8,128)S(1)} %get-tuple-element.43.refs_3_), channel_id=1, source_target_pairs={{0,4},{1,2},{2,1},{3,7},{4,0},{5,6},{6,5},{7,3},{8,12},{9,10},{10,... | collective-permute-start | bytes 786440 | tf_op jit(solution)/shard_map/ppermute | solution.py:429
  11.3 3.4 %collective-permute-start.1 = (f32[2,4,8,1024]{3,2,1,0:T(8,128)S(1)}, f32[2,4,8,1024]{3,2,1,0:T(8,128)S(1)}, u32[]{:S(2)}, u32[]{:S(2)}) collective-permute-start(f32[2,4,8,1024]{3,2,1,0:T(8,128)S(1)} %core.1.refs_2_), channel_id=1, source_target_pairs={{0,1},{1,0},{2,3},{3,2},{4,5},{5,4},{6,7},{7,6},{8,9},{9,8},{10,11... | collective-permute-start | bytes 786440 | tf_op jit(solution)/shard_map/ppermute | solution.py:428
  15.4 7.0 %collective-permute-start.5 = (f32[4,16,1024]{2,1,0:T(8,128)S(1)}, f32[4,16,1024]{2,1,0:T(8,128)S(1)}, u32[]{:S(2)}, u32[]{:S(2)}) collective-permute-start(f32[4,16,1024]{2,1,0:T(8,128)S(1)} %get-tuple-element.51), channel_id=1, source_target_pairs={{0,4},{4,0},{8,12},{12,8},{16,20},{20,16},{24,28},{28,24},{1,5},{5... | collective-permute-start | bytes 786440 | tf_op jit(solution)/shard_map/ppermute | solution.py:461
  19.8 17.5 %collective-permute-start.4 = (f32[2,4,16,1024]{3,2,1,0:T(8,128)S(1)}, f32[2,4,16,1024]{3,2,1,0:T(8,128)S(1)}, u32[]{:S(2)}, u32[]{:S(2)}) collective-permute-start(f32[2,4,16,1024]{3,2,1,0:T(8,128)S(1)} %get-tuple-element.49), channel_id=1, source_target_pairs={{0,8},{4,12},{8,0},{12,4},{16,24},{20,28},{24,16},{28,20},{1,9},{5... | collective-permute-start | bytes 1572872 | tf_op jit(solution)/shard_map/ppermute | solution.py:462
  22.4 6.0 %collective-permute-start.6 = (f32[4,16,1024]{2,1,0:T(8,128)S(1)}, f32[4,16,1024]{2,1,0:T(8,128)S(1)}, u32[]{:S(2)}, u32[]{:S(2)}) collective-permute-start(f32[4,16,1024]{2,1,0:T(8,128)S(1)} %get-tuple-element.52), channel_id=1, source_target_pairs={{0,4},{4,0},{8,12},{12,8},{16,20},{20,16},{24,28},{28,24},{1,5},{5... | collective-permute-start | bytes 786440 | tf_op jit(solution)/shard_map/ppermute | solution.py:461
  24.2 15.0 %collective-permute-start.8 = (f32[4,16,1024]{2,1,0:T(8,128)S(1)}, f32[4,16,1024]{2,1,0:T(8,128)S(1)}, u32[]{:S(2)}, u32[]{:S(2)}) collective-permute-start(f32[4,16,1024]{2,1,0:T(8,128)S(1)} %meet2.1.refs_4_), channel_id=1, source_target_pairs={{0,16},{4,20},{8,24},{12,28},{16,0},{20,4},{24,8},{28,12},{1,17},{... | collective-permute-start | bytes 786440 | tf_op jit(solution)/shard_map/ppermute | solution.py:462
  28.4 10.9 %collective-permute-start.10 = (f32[4,16,1024]{2,1,0:T(8,128)S(1)}, f32[4,16,1024]{2,1,0:T(8,128)S(1)}, u32[]{:S(2)}, u32[]{:S(2)}) collective-permute-start(f32[4,16,1024]{2,1,0:T(8,128)S(1)} %get-tuple-element.56.refs_5_), channel_id=1, source_target_pairs={{0,4},{4,0},{8,12},{12,8},{16,20},{20,16},{24,28},{28,24},{1,5},{5... | collective-permute-start | bytes 786440 | tf_op jit(solution)/shard_map/ppermute | solution.py:461
  30.2 13.3 %collective-permute-start.9 = (f32[4,16,1024]{2,1,0:T(8,128)S(1)}, f32[4,16,1024]{2,1,0:T(8,128)S(1)}, u32[]{:S(2)}, u32[]{:S(2)}) collective-permute-start(f32[4,16,1024]{2,1,0:T(8,128)S(1)} %meet3.1.refs_4_), channel_id=1, source_target_pairs={{0,24},{4,28},{8,16},{12,20},{16,8},{20,12},{24,0},{28,4},{1,25},{... | collective-permute-start | bytes 786440 | tf_op jit(solution)/shard_map/ppermute | solution.py:462
  38.0 5.6 %collective-permute-start.7 = (f32[4,16,1024]{2,1,0:T(8,128)S(1)}, f32[4,16,1024]{2,1,0:T(8,128)S(1)}, u32[]{:S(2)}, u32[]{:S(2)}) collective-permute-start(f32[4,16,1024]{2,1,0:T(8,128)S(1)} %cross.1), channel_id=1, source_target_pairs={{0,4},{4,0},{8,12},{12,8},{16,20},{20,16},{24,28},{28,24},{1,5},{5... | collective-permute-start | bytes 786440 | tf_op jit(solution)/shard_map/ppermute | solution.py:461
  44.2 9.7 %collective-permute-start.11 = (f32[4,16,1024]{2,1,0:T(8,128)S(1)}, f32[4,16,1024]{2,1,0:T(8,128)S(1)}, u32[]{:S(2)}, u32[]{:S(2)}) collective-permute-start(f32[4,16,1024]{2,1,0:T(8,128)S(1)} %last.1.refs_2_), channel_id=1, source_target_pairs={{0,24},{4,28},{8,16},{12,20},{16,8},{20,12},{24,0},{28,4},{1,25},{... | collective-permute-start | bytes 786440 | tf_op jit(solution)/shard_map/ppermute | solution.py:462
  47.0 7.0 %collective-permute-start.12 = (f32[4,16,1024]{2,1,0:T(8,128)S(1)}, f32[4,16,1024]{2,1,0:T(8,128)S(1)}, u32[]{:S(2)}, u32[]{:S(2)}) collective-permute-start(f32[4,16,1024]{2,1,0:T(8,128)S(1)} %last.1.refs_2_), channel_id=1, source_target_pairs={{0,4},{4,0},{8,12},{12,8},{16,20},{20,16},{24,28},{28,24},{1,5},{5... | collective-permute-start | bytes 786440 | tf_op jit(solution)/shard_map/ppermute | solution.py:461
  48.3 12.0 %collective-permute-start.15 = (f32[4,16,1024]{2,1,0:T(8,128)S(1)}, f32[4,16,1024]{2,1,0:T(8,128)S(1)}, u32[]{:S(2)}, u32[]{:S(2)}) collective-permute-start(f32[4,16,1024]{2,1,0:T(8,128)S(1)} %last.1.refs_2_), channel_id=1, source_target_pairs={{0,8},{4,12},{8,0},{12,4},{16,24},{20,28},{24,16},{28,20},{1,9},{5... | collective-permute-start | bytes 786440 | tf_op jit(solution)/shard_map/ppermute | solution.py:462
  53.9 15.5 %collective-permute-start.13 = (f32[4,16,1024]{2,1,0:T(8,128)S(1)}, f32[4,16,1024]{2,1,0:T(8,128)S(1)}, u32[]{:S(2)}, u32[]{:S(2)}) collective-permute-start(f32[4,16,1024]{2,1,0:T(8,128)S(1)} %last.1.refs_2_), channel_id=1, source_target_pairs={{0,16},{4,20},{8,24},{12,28},{16,0},{20,4},{24,8},{28,12},{1,17},{... | collective-permute-start | bytes 786440 | tf_op jit(solution)/shard_map/ppermute | solution.py:462
  60.2 10.6 %collective-permute-start.16 = (f32[4,16,1024]{2,1,0:T(8,128)S(1)}, f32[4,16,1024]{2,1,0:T(8,128)S(1)}, u32[]{:S(2)}, u32[]{:S(2)}) collective-permute-start(f32[4,16,1024]{2,1,0:T(8,128)S(1)} %collective-permute-done.12.refs_2_), channel_id=1, source_target_pairs={{0,8},{4,12},{8,0},{12,4},{16,24},{20,28},{24,16},{28,20},{1,9},{5... | collective-permute-start | bytes 786440 | tf_op jit(solution)/shard_map/ppermute | solution.py:462
  60.7 10.1 %collective-permute-start.17 = (f32[4,16,1024]{2,1,0:T(8,128)S(1)}, f32[4,16,1024]{2,1,0:T(8,128)S(1)}, u32[]{:S(2)}, u32[]{:S(2)}) collective-permute-start(f32[4,16,1024]{2,1,0:T(8,128)S(1)} %collective-permute-done.11.refs_4_), channel_id=1, source_target_pairs={{0,4},{4,0},{8,12},{12,8},{16,20},{20,16},{24,28},{28,24},{1,5},{5... | collective-permute-start | bytes 786440 | tf_op jit(solution)/shard_map/ppermute | solution.py:461
  69.4 8.1 %collective-permute-start.14 = (f32[4,16,1024]{2,1,0:T(8,128)S(1)}, f32[4,16,1024]{2,1,0:T(8,128)S(1)}, u32[]{:S(2)}, u32[]{:S(2)}) collective-permute-start(f32[4,16,1024]{2,1,0:T(8,128)S(1)} %collective-permute-done.13.refs_4_), channel_id=1, source_target_pairs={{0,4},{4,0},{8,12},{12,8},{16,20},{20,16},{24,28},{28,24},{1,5},{5... | collective-permute-start | bytes 786440 | tf_op jit(solution)/shard_map/ppermute | solution.py:461
  78.8 4.6 %collective-permute-start.19 = (f32[2,4,8,1024]{3,2,1,0:T(8,128)S(1)}, f32[2,4,8,1024]{3,2,1,0:T(8,128)S(1)}, u32[]{:S(2)}, u32[]{:S(2)}) collective-permute-start(f32[2,4,8,1024]{3,2,1,0:T(8,128)S(1)} %get-tuple-element.68), channel_id=1, source_target_pairs={{0,1},{1,0},{2,3},{3,2},{4,5},{5,4},{6,7},{7,6},{8,9},{9,8},{10,11... | collective-permute-start | bytes 786440 | tf_op jit(solution)/shard_map/ppermute | solution.py:428
  82.3 6.1 %collective-permute-start.18 = (f32[2,4,8,1024]{3,2,1,0:T(8,128)S(1)}, f32[2,4,8,1024]{3,2,1,0:T(8,128)S(1)}, u32[]{:S(2)}, u32[]{:S(2)}) collective-permute-start(f32[2,4,8,1024]{3,2,1,0:T(8,128)S(1)} %get-tuple-element.66), channel_id=1, source_target_pairs={{0,4},{1,2},{2,1},{3,7},{4,0},{5,6},{6,5},{7,3},{8,12},{9,10},{10,... | collective-permute-start | bytes 786440 | tf_op jit(solution)/shard_map/ppermute | solution.py:429

commit v10 on v9

--- a/solution.py
+++ b/solution.py
@@ -518,7 +518,7 @@
             arrived[1], arrived[2], arrived[3], mine, from_y,
             specs=(SMEM,) + (VMEM,) * 8,
         )
-        own = {0: grad, 3: turn_z(grad, 3), 1: turn_z(grad, 1)}
+        own = {0: grad, 3: turn_z(grad, 3)}
         weighted = call(
             functools.partial(spread_body, ((0, 0),), True, False), shape(*field_shape),
             "spread", 1 << 19, slot_owner, ens, grad, specs=(SMEM,) + (VMEM,) * 2,
@@ -527,8 +527,8 @@
         other = {0: swap_y(other)}
         later, own[3], other[0] = lax.optimization_barrier((grad, own[3], other[0]))
         own[2] = turn_z(later, 2)
-        along, own[1] = lax.optimization_barrier((other[0], own[1]))
-        other[1] = turn_z(along, 1)
+        along, near = lax.optimization_barrier((other[0], grad))
+        own[1], other[1] = turn_z(near, 1), turn_z(along, 1)
         other.update({s: swap_y(own[s]) for s in (3, 2)})
         groups = (((0, 1), (1, 0), (3, 0)), ((1, 1), (3, 1), (2, 0)), ((2, 1),))
         for group in groups:

time: 90.8 us -> 90.3 us (level)
  waiting for transfers between devices: 39.4 us -> 37.6 us
  starting transfers between devices: 35.7 us -> 37.3 us
    ppermute x8, waiting for transfers between devices: 21.4 us -> 26.6 us  [per_device(): lax.ppermute(v, 'mem', [(i, i ^ 2 * s) for i in range(mem_count)])]
    ppermute x7, waiting for transfers between devices: 10.7 us -> 5.64 us  [per_device(): swap_y = lambda v: lax.ppermute(v, 'mem', y_pairs)]
    ppermute x8, starting transfers between devices: 21.6 us -> 18.7 us  [per_device(): lax.ppermute(v, 'mem', [(i, i ^ 2 * s) for i in range(mem_count)])]
    ppermute x2, starting transfers between devices: 2.38 us -> 4.82 us  [per_device(): swap_x = lambda v: lax.ppermute(v, ('mem', 'lat'), x_swaps)]
    ppermute x7, starting transfers between devices: 7.03 us -> 9.03 us  [per_device(): swap_y = lambda v: lax.ppermute(v, 'mem', y_pairs)]
    ppermute x2, waiting for transfers between devices: 1.12 us -> 0.01 us  [per_device(): swap_core = lambda v: lax.ppermute(v, 'lat', core_pairs)]
where the time goes in v10:
time: 90.3 us; the launch traced here: 90.2 us
  waiting for transfers between devices  37.6 us (42%)
  starting transfers between devices  37.3 us (41%)
  Pallas kernels  15.1 us (17%)
    ppermute x8, waiting for transfers between devices, per_device(): lax.ppermute(v, 'mem', [(i, i ^ 2 * s) for i in range(mem_count)])  26.6 us
    ppermute x8, starting transfers between devices, per_device(): lax.ppermute(v, 'mem', [(i, i ^ 2 * s) for i in range(mem_count)])  18.7 us
    pallas_call x17, Pallas kernels, call(): pl.pallas_call(kernel, out_shape=outs, in_specs=list(specs) + [ANY] * ext...  15.1 us
    ppermute x7, starting transfers between devices, per_device(): swap_y = lambda v: lax.ppermute(v, 'mem', y_pairs)  9.03 us
    ppermute x7, waiting for transfers between devices, per_device(): swap_y = lambda v: lax.ppermute(v, 'mem', y_pairs)  5.64 us
    ppermute x2, waiting for transfers between devices, per_device(): swap_x = lambda v: lax.ppermute(v, ('mem', 'lat'), x_swaps)  5.36 us
    ppermute x2, starting transfers between devices, per_device(): swap_x = lambda v: lax.ppermute(v, ('mem', 'lat'), x_swaps)  4.82 us
    ppermute x2, starting transfers between devices, per_device(): swap_core = lambda v: lax.ppermute(v, 'lat', core_pairs)  4.08 us
  transfers between devices with their start and end apart: 20, of which 11 were waited for; matrix products, arithmetic and copies ran while one was open for 0% of the time, Pallas kernels for 9%

profile of v10, /device:TPU:1, one launch (start us, length us, event | category | flops | bytes accessed | tf_op | source)
XLA Modules:
  0.0 90.2 jit_solution(5684931147214902348)
XLA Ops:
  0.0 0.0 copy-start
  0.0 2.3 %front.1 = (f32[2,4,8,1024]{3,2,1,0:T(8,128)S(1)}, f32[2,4,16,1024]{3,2,1,0:T(8,128)S(1)}, f32[16,17]{1,0:T(8,128)S(1)}, f32[16,17]{1,0:T(8,128)S(1)}, s32[8,128...) custom-call(s32[16]{0:T(128)} %refs_0_.12, ...), custom_call_target="tpu_custom_call" | custom-call | flops 524288 | bytes 524288 | tf_op jit(solution)/shard_map/front/pallas_call | solution.py:29
  2.3 0.7 collective-permute-start.3
  3.0 4.7 %collective-permute-start.2 = (f32[2,4,16,1024]{3,2,1,0:T(8,128)S(1)}, f32[2,4,16,1024]{3,2,1,0:T(8,128)S(1)}, u32[]{:S(2)}, u32[]{:S(2)}) collective-permute-start(f32[2,4,16,1024]{3,2,1,0:T(8,128)S(1)} %get-tuple-element.48.refs_1_), channel_id=1, source_target_pairs={{0,8},{4,12},{8,0},{12,4},{16,24},{20,28},{24,16},{28,20},{1,9},{5... | collective-permute-start | bytes 1572872 | tf_op jit(solution)/shard_map/ppermute | solution.py:462
  7.7 2.3 %collective-permute-start = (f32[2,4,8,1024]{3,2,1,0:T(8,128)S(1)}, f32[2,4,8,1024]{3,2,1,0:T(8,128)S(1)}, u32[]{:S(2)}, u32[]{:S(2)}) collective-permute-start(f32[2,4,8,1024]{3,2,1,0:T(8,128)S(1)} %get-tuple-element.43.refs_3_), channel_id=1, source_target_pairs={{0,4},{1,2},{2,1},{3,7},{4,0},{5,6},{6,5},{7,3},{8,12},{9,10},{10,... | collective-permute-start | bytes 786440 | tf_op jit(solution)/shard_map/ppermute | solution.py:429
  10.1 1.3 %core.1.refs_2_ = f32[2,4,8,1024]{3,2,1,0:T(8,128)S(1)} custom-call(s32[8,128]{1,0:T(8,128)S(1)} %get-tuple-element.42.refs_0_, f32[16,17]{1,0:T(8,128)S(1)} %get-tuple-element.38.refs_1_, f32[2,4,16,1024]{3,2,1,0:T(8,128)S(1)} %get-tuple-element.39.refs_2_), custom_call_target="tpu_custom_call" | custom-call | flops 524288 | bytes 524288 | tf_op jit(solution)/shard_map/core/pallas_call | solution.py:29
  11.3 0.5 collective-permute-start.1
  11.8 2.6 %collective-permute-done.refs_3_.refs_5_ = f32[2,4,8,1024]{3,2,1,0:T(8,128)S(1)} collective-permute-done((f32[2,4,8,1024]{3,2,1,0:T(8,128)S(1)}, f32[2,4,8,1024]{3,2,1,0:T(8,128)S(1)}, u32[]{:S(2)}, u32[]{:S(2)}) %collective-permute-start) | collective-permute-done | bytes 262176 | tf_op jit(solution)/shard_map/ppermute | solution.py:429
  14.4 0.3 matrix.1
  14.8 0.0 collective-permute-done.1.refs_4_
  14.8 0.0 copy-done
  14.8 0.6 first.1
  15.4 1.3 %collective-permute-start.5 = (f32[4,16,1024]{2,1,0:T(8,128)S(1)}, f32[4,16,1024]{2,1,0:T(8,128)S(1)}, u32[]{:S(2)}, u32[]{:S(2)}) collective-permute-start(f32[4,16,1024]{2,1,0:T(8,128)S(1)} %get-tuple-element.51), channel_id=1, source_target_pairs={{0,4},{4,0},{8,12},{12,8},{16,20},{20,16},{24,28},{28,24},{1,5},{5... | collective-permute-start | bytes 786440 | tf_op jit(solution)/shard_map/ppermute | solution.py:461
  16.7 0.0 collective-permute-done.3.refs_4_.refs_3_
  16.7 2.3 %collective-permute-done.2.refs_3_.refs_2_ = f32[2,4,16,1024]{3,2,1,0:T(8,128)S(1)} collective-permute-done((f32[2,4,16,1024]{3,2,1,0:T(8,128)S(1)}, f32[2,4,16,1024]{3,2,1,0:T(8,128)S(1)}, u32[]{:S(2)}, u32[]{:S(2)}) %collective-permute-start.2) | collective-permute-done | bytes 524320 | tf_op jit(solution)/shard_map/ppermute | solution.py:462
  19.1 0.7 send.1
  19.8 1.2 %collective-permute-start.4 = (f32[2,4,16,1024]{3,2,1,0:T(8,128)S(1)}, f32[2,4,16,1024]{3,2,1,0:T(8,128)S(1)}, u32[]{:S(2)}, u32[]{:S(2)}) collective-permute-start(f32[2,4,16,1024]{3,2,1,0:T(8,128)S(1)} %get-tuple-element.49), channel_id=1, source_target_pairs={{0,8},{4,12},{8,0},{12,4},{16,24},{20,28},{24,16},{28,20},{1,9},{5... | collective-permute-start | bytes 1572872 | tf_op jit(solution)/shard_map/ppermute | solution.py:462
  21.0 1.4 %collective-permute-done.5.refs_3_ = f32[4,16,1024]{2,1,0:T(8,128)S(1)} collective-permute-done((f32[4,16,1024]{2,1,0:T(8,128)S(1)}, f32[4,16,1024]{2,1,0:T(8,128)S(1)}, u32[]{:S(2)}, u32[]{:S(2)}) %collective-permute-start.5) | collective-permute-done | bytes 262176 | tf_op jit(solution)/shard_map/ppermute | solution.py:461
  22.4 1.2 %collective-permute-start.6 = (f32[4,16,1024]{2,1,0:T(8,128)S(1)}, f32[4,16,1024]{2,1,0:T(8,128)S(1)}, u32[]{:S(2)}, u32[]{:S(2)}) collective-permute-start(f32[4,16,1024]{2,1,0:T(8,128)S(1)} %get-tuple-element.52), channel_id=1, source_target_pairs={{0,4},{4,0},{8,12},{12,8},{16,20},{20,16},{24,28},{28,24},{1,5},{5... | collective-permute-start | bytes 786440 | tf_op jit(solution)/shard_map/ppermute | solution.py:461
  23.6 0.6 meet2.1.refs_4_
  24.2 0.1 collective-permute-start.8
  24.3 0.6 weight_pick.1
  24.9 3.4 %collective-permute-done.6.refs_3_ = f32[4,16,1024]{2,1,0:T(8,128)S(1)} collective-permute-done((f32[4,16,1024]{2,1,0:T(8,128)S(1)}, f32[4,16,1024]{2,1,0:T(8,128)S(1)}, u32[]{:S(2)}, u32[]{:S(2)}) %collective-permute-start.6) | collective-permute-done | bytes 262176 | tf_op jit(solution)/shard_map/ppermute | solution.py:461
  28.4 1.2 %collective-permute-start.10 = (f32[4,16,1024]{2,1,0:T(8,128)S(1)}, f32[4,16,1024]{2,1,0:T(8,128)S(1)}, u32[]{:S(2)}, u32[]{:S(2)}) collective-permute-start(f32[4,16,1024]{2,1,0:T(8,128)S(1)} %get-tuple-element.56.refs_5_), channel_id=1, source_target_pairs={{0,4},{4,0},{8,12},{12,8},{16,20},{20,16},{24,28},{28,24},{1,5},{5... | collective-permute-start | bytes 786440 | tf_op jit(solution)/shard_map/ppermute | solution.py:461
  29.6 0.6 meet3.1.refs_4_
  30.2 1.1 %collective-permute-start.9 = (f32[4,16,1024]{2,1,0:T(8,128)S(1)}, f32[4,16,1024]{2,1,0:T(8,128)S(1)}, u32[]{:S(2)}, u32[]{:S(2)}) collective-permute-start(f32[4,16,1024]{2,1,0:T(8,128)S(1)} %meet3.1.refs_4_), channel_id=1, source_target_pairs={{0,24},{4,28},{8,16},{12,20},{16,8},{20,12},{24,0},{28,4},{1,25},{... | collective-permute-start | bytes 786440 | tf_op jit(solution)/shard_map/ppermute | solution.py:462
  31.4 6.0 %collective-permute-done.4.refs_3_.refs_4_ = f32[2,4,16,1024]{3,2,1,0:T(8,128)S(1)} collective-permute-done((f32[2,4,16,1024]{3,2,1,0:T(8,128)S(1)}, f32[2,4,16,1024]{3,2,1,0:T(8,128)S(1)}, u32[]{:S(2)}, u32[]{:S(2)}) %collective-permute-start.4) | collective-permute-done | bytes 524320 | tf_op jit(solution)/shard_map/ppermute | solution.py:462
  37.3 0.6 cross.1
  38.0 1.3 %collective-permute-start.7 = (f32[4,16,1024]{2,1,0:T(8,128)S(1)}, f32[4,16,1024]{2,1,0:T(8,128)S(1)}, u32[]{:S(2)}, u32[]{:S(2)}) collective-permute-start(f32[4,16,1024]{2,1,0:T(8,128)S(1)} %cross.1), channel_id=1, source_target_pairs={{0,4},{4,0},{8,12},{12,8},{16,20},{20,16},{24,28},{28,24},{1,5},{5... | collective-permute-start | bytes 786440 | tf_op jit(solution)/shard_map/ppermute | solution.py:461
  39.3 0.0 collective-permute-done.8.refs_5_
  39.3 0.0 collective-permute-done.10.refs_8_
  39.3 4.3 %collective-permute-done.9.refs_6_ = f32[4,16,1024]{2,1,0:T(8,128)S(1)} collective-permute-done((f32[4,16,1024]{2,1,0:T(8,128)S(1)}, f32[4,16,1024]{2,1,0:T(8,128)S(1)}, u32[]{:S(2)}, u32[]{:S(2)}) %collective-permute-start.9) | collective-permute-done | bytes 262176 | tf_op jit(solution)/shard_map/ppermute | solution.py:462
  43.6 0.0 collective-permute-done.7.refs_3_
  43.6 0.7 last.1.refs_2_
  44.2 2.1 %collective-permute-start.11 = (f32[4,16,1024]{2,1,0:T(8,128)S(1)}, f32[4,16,1024]{2,1,0:T(8,128)S(1)}, u32[]{:S(2)}, u32[]{:S(2)}) collective-permute-start(f32[4,16,1024]{2,1,0:T(8,128)S(1)} %last.1.refs_2_), channel_id=1, source_target_pairs={{0,24},{4,28},{8,16},{12,20},{16,8},{20,12},{24,0},{28,4},{1,25},{... | collective-permute-start | bytes 786440 | tf_op jit(solution)/shard_map/ppermute | solution.py:462
  46.4 0.6 spread.1.refs_5_
  47.0 1.3 %collective-permute-start.12 = (f32[4,16,1024]{2,1,0:T(8,128)S(1)}, f32[4,16,1024]{2,1,0:T(8,128)S(1)}, u32[]{:S(2)}, u32[]{:S(2)}) collective-permute-start(f32[4,16,1024]{2,1,0:T(8,128)S(1)} %last.1.refs_2_), channel_id=1, source_target_pairs={{0,4},{4,0},{8,12},{12,8},{16,20},{20,16},{24,28},{28,24},{1,5},{5... | collective-permute-start | bytes 786440 | tf_op jit(solution)/shard_map/ppermute | solution.py:461
  48.3 3.1 %collective-permute-done.11.refs_4_ = f32[4,16,1024]{2,1,0:T(8,128)S(1)} collective-permute-done((f32[4,16,1024]{2,1,0:T(8,128)S(1)}, f32[4,16,1024]{2,1,0:T(8,128)S(1)}, u32[]{:S(2)}, u32[]{:S(2)}) %collective-permute-start.11) | collective-permute-done | bytes 262176 | tf_op jit(solution)/shard_map/ppermute | solution.py:462
  51.4 0.8 collective-permute-done.12.refs_2_
  52.3 8.0 %collective-permute-start.13 = (f32[4,16,1024]{2,1,0:T(8,128)S(1)}, f32[4,16,1024]{2,1,0:T(8,128)S(1)}, u32[]{:S(2)}, u32[]{:S(2)}) collective-permute-start(f32[4,16,1024]{2,1,0:T(8,128)S(1)} %last.1.refs_2_), channel_id=1, source_target_pairs={{0,16},{4,20},{8,24},{12,28},{16,0},{20,4},{24,8},{28,12},{1,17},{... | collective-permute-start | bytes 786440 | tf_op jit(solution)/shard_map/ppermute | solution.py:462
  60.2 0.4 collective-permute-start.17
  60.6 1.1 %collective-permute-start.15 = (f32[4,16,1024]{2,1,0:T(8,128)S(1)}, f32[4,16,1024]{2,1,0:T(8,128)S(1)}, u32[]{:S(2)}, u32[]{:S(2)}) collective-permute-start(f32[4,16,1024]{2,1,0:T(8,128)S(1)} %collective-permute-done.12.refs_2_), channel_id=1, source_target_pairs={{0,8},{4,12},{8,0},{12,4},{16,24},{20,28},{24,16},{28,20},{1,9},{5... | collective-permute-start | bytes 786440 | tf_op jit(solution)/shard_map/ppermute | solution.py:462
  61.7 1.0 %collective-permute-start.16 = (f32[4,16,1024]{2,1,0:T(8,128)S(1)}, f32[4,16,1024]{2,1,0:T(8,128)S(1)}, u32[]{:S(2)}, u32[]{:S(2)}) collective-permute-start(f32[4,16,1024]{2,1,0:T(8,128)S(1)} %collective-permute-done.11.refs_4_), channel_id=1, source_target_pairs={{0,4},{4,0},{8,12},{12,8},{16,20},{20,16},{24,28},{28,24},{1,5},{5... | collective-permute-start | bytes 786440 | tf_op jit(solution)/shard_map/ppermute | solution.py:461
  62.8 6.8 %collective-permute-done.13.refs_4_ = f32[4,16,1024]{2,1,0:T(8,128)S(1)} collective-permute-done((f32[4,16,1024]{2,1,0:T(8,128)S(1)}, f32[4,16,1024]{2,1,0:T(8,128)S(1)}, u32[]{:S(2)}, u32[]{:S(2)}) %collective-permute-start.13) | collective-permute-done | bytes 262176 | tf_op jit(solution)/shard_map/ppermute | solution.py:462
  69.5 1.6 %collective-permute-start.14 = (f32[4,16,1024]{2,1,0:T(8,128)S(1)}, f32[4,16,1024]{2,1,0:T(8,128)S(1)}, u32[]{:S(2)}, u32[]{:S(2)}) collective-permute-start(f32[4,16,1024]{2,1,0:T(8,128)S(1)} %collective-permute-done.13.refs_4_), channel_id=1, source_target_pairs={{0,4},{4,0},{8,12},{12,8},{16,20},{20,16},{24,28},{28,24},{1,5},{5... | collective-permute-start | bytes 786440 | tf_op jit(solution)/shard_map/ppermute | solution.py:461
  71.1 0.0 collective-permute-done.17.refs_3_
  71.1 0.8 spread0.1.refs_5_
  71.9 4.1 %collective-permute-done.15.refs_2_ = f32[4,16,1024]{2,1,0:T(8,128)S(1)} collective-permute-done((f32[4,16,1024]{2,1,0:T(8,128)S(1)}, f32[4,16,1024]{2,1,0:T(8,128)S(1)}, u32[]{:S(2)}, u32[]{:S(2)}) %collective-permute-start.15) | collective-permute-done | bytes 262176 | tf_op jit(solution)/shard_map/ppermute | solution.py:462
  76.0 0.0 collective-permute-done.16.refs_3_
  76.0 0.8 spread1.1.refs_3_
  76.7 0.0 collective-permute-done.14.refs_2_
  76.8 0.8 spread2.1
  77.6 0.5 blocks.1
  78.1 3.6 %collective-permute-start.19 = (f32[2,4,8,1024]{3,2,1,0:T(8,128)S(1)}, f32[2,4,8,1024]{3,2,1,0:T(8,128)S(1)}, u32[]{:S(2)}, u32[]{:S(2)}) collective-permute-start(f32[2,4,8,1024]{3,2,1,0:T(8,128)S(1)} %get-tuple-element.68), channel_id=1, source_target_pairs={{0,1},{1,0},{2,3},{3,2},{4,5},{5,4},{6,7},{7,6},{8,9},{9,8},{10,11... | collective-permute-start | bytes 786440 | tf_op jit(solution)/shard_map/ppermute | solution.py:428
  81.7 2.5 %collective-permute-start.18 = (f32[2,4,8,1024]{3,2,1,0:T(8,128)S(1)}, f32[2,4,8,1024]{3,2,1,0:T(8,128)S(1)}, u32[]{:S(2)}, u32[]{:S(2)}) collective-permute-start(f32[2,4,8,1024]{3,2,1,0:T(8,128)S(1)} %get-tuple-element.66), channel_id=1, source_target_pairs={{0,4},{1,2},{2,1},{3,7},{4,0},{5,6},{6,5},{7,3},{8,12},{9,10},{10,... | collective-permute-start | bytes 786440 | tf_op jit(solution)/shard_map/ppermute | solution.py:429
  84.1 0.0 collective-permute-done.19.refs_4_
  84.2 1.3 %adjoint0.1.refs_5_ = f32[2,4,8,1024]{3,2,1,0:T(8,128)S(1)} custom-call(s32[8,128]{1,0:T(8,128)S(1)} %get-tuple-element.42.refs_0_, f32[16,17]{1,0:T(8,128)S(1)} %get-tuple-element.38.refs_1_, f32[2,4,16,1024]{3,2,1,0:T(8,128)S(1)} %get-tuple-element.39.refs_2_, f32[2,4,8,1024]{3,2,1,0:T(8,128)S(1)} %get-tuple-element.67.refs_3_, ...), custom_call_target="tpu_custom_call" | custom-call | flops 524288 | bytes 524288 | tf_op jit(solution)/shard_map/adjoint0/pallas_call | solution.py:29
  85.4 2.8 %collective-permute-done.18.refs_4_ = f32[2,4,8,1024]{3,2,1,0:T(8,128)S(1)} collective-permute-done((f32[2,4,8,1024]{3,2,1,0:T(8,128)S(1)}, f32[2,4,8,1024]{3,2,1,0:T(8,128)S(1)}, u32[]{:S(2)}, u32[]{:S(2)}) %collective-permute-start.18) | collective-permute-done | bytes 262176 | tf_op jit(solution)/shard_map/ppermute | solution.py:429
  88.2 2.0 %adjoint1.1 = f32[2,4,16,1024]{3,2,1,0:T(8,128)} custom-call(s32[8,128]{1,0:T(8,128)S(1)} %get-tuple-element.37.refs_0_, f32[16,17]{1,0:T(8,128)S(1)} %get-tuple-element.38.refs_1_, f32[2,4,16,1024]{3,2,1,0:T(8,128)S(1)} %get-tuple-element.39.refs_2_, f32[2,4,8,1024]{3,2,1,0:T(8,128)S(1)} %get-tuple-element.65.refs_3_, ...), custom_call_target="tpu_custom_call" | custom-call | flops 524288 | bytes 524288 | tf_op jit(solution)/shard_map/adjoint1/pallas_call | solution.py:29
Async XLA Ops:
  0.0 14.8 %copy-start = (s32[4]{0:T(128)S(1)}, s32[4]{0:T(128)}, u32[]{:S(2)}) copy-start(s32[4]{0:T(128)} %refs_0_.23) | copy-start | bytes 52
  2.3 14.4 %collective-permute-start.3 = (f32[2,4,16,1024]{3,2,1,0:T(8,128)S(1)}, f32[2,4,16,1024]{3,2,1,0:T(8,128)S(1)}, u32[]{:S(2)}, u32[]{:S(2)}) collective-permute-start(f32[2,4,16,1024]{3,2,1,0:T(8,128)S(1)} %get-tuple-element.48.refs_1_), channel_id=1, source_target_pairs={{8,16},{12,20},{16,8},{20,12},{9,17},{13,21},{17,9},{21,13},{10,18... | collective-permute-start | bytes 1572872 | tf_op jit(solution)/shard_map/ppermute | solution.py:467
  3.0 16.0 %collective-permute-start.2 = (f32[2,4,16,1024]{3,2,1,0:T(8,128)S(1)}, f32[2,4,16,1024]{3,2,1,0:T(8,128)S(1)}, u32[]{:S(2)}, u32[]{:S(2)}) collective-permute-start(f32[2,4,16,1024]{3,2,1,0:T(8,128)S(1)} %get-tuple-element.48.refs_1_), channel_id=1, source_target_pairs={{0,8},{4,12},{8,0},{12,4},{16,24},{20,28},{24,16},{28,20},{1,9},{5... | collective-permute-start | bytes 1572872 | tf_op jit(solution)/shard_map/ppermute | solution.py:462
  7.7 6.7 %collective-permute-start = (f32[2,4,8,1024]{3,2,1,0:T(8,128)S(1)}, f32[2,4,8,1024]{3,2,1,0:T(8,128)S(1)}, u32[]{:S(2)}, u32[]{:S(2)}) collective-permute-start(f32[2,4,8,1024]{3,2,1,0:T(8,128)S(1)} %get-tuple-element.43.refs_3_), channel_id=1, source_target_pairs={{0,4},{1,2},{2,1},{3,7},{4,0},{5,6},{6,5},{7,3},{8,12},{9,10},{10,... | collective-permute-start | bytes 786440 | tf_op jit(solution)/shard_map/ppermute | solution.py:429
  11.3 3.4 %collective-permute-start.1 = (f32[2,4,8,1024]{3,2,1,0:T(8,128)S(1)}, f32[2,4,8,1024]{3,2,1,0:T(8,128)S(1)}, u32[]{:S(2)}, u32[]{:S(2)}) collective-permute-start(f32[2,4,8,1024]{3,2,1,0:T(8,128)S(1)} %core.1.refs_2_), channel_id=1, source_target_pairs={{0,1},{1,0},{2,3},{3,2},{4,5},{5,4},{6,7},{7,6},{8,9},{9,8},{10,11... | collective-permute-start | bytes 786440 | tf_op jit(solution)/shard_map/ppermute | solution.py:428
  15.4 7.0 %collective-permute-start.5 = (f32[4,16,1024]{2,1,0:T(8,128)S(1)}, f32[4,16,1024]{2,1,0:T(8,128)S(1)}, u32[]{:S(2)}, u32[]{:S(2)}) collective-permute-start(f32[4,16,1024]{2,1,0:T(8,128)S(1)} %get-tuple-element.51), channel_id=1, source_target_pairs={{0,4},{4,0},{8,12},{12,8},{16,20},{20,16},{24,28},{28,24},{1,5},{5... | collective-permute-start | bytes 786440 | tf_op jit(solution)/shard_map/ppermute | solution.py:461
  19.8 17.5 %collective-permute-start.4 = (f32[2,4,16,1024]{3,2,1,0:T(8,128)S(1)}, f32[2,4,16,1024]{3,2,1,0:T(8,128)S(1)}, u32[]{:S(2)}, u32[]{:S(2)}) collective-permute-start(f32[2,4,16,1024]{3,2,1,0:T(8,128)S(1)} %get-tuple-element.49), channel_id=1, source_target_pairs={{0,8},{4,12},{8,0},{12,4},{16,24},{20,28},{24,16},{28,20},{1,9},{5... | collective-permute-start | bytes 1572872 | tf_op jit(solution)/shard_map/ppermute | solution.py:462
  22.4 6.0 %collective-permute-start.6 = (f32[4,16,1024]{2,1,0:T(8,128)S(1)}, f32[4,16,1024]{2,1,0:T(8,128)S(1)}, u32[]{:S(2)}, u32[]{:S(2)}) collective-permute-start(f32[4,16,1024]{2,1,0:T(8,128)S(1)} %get-tuple-element.52), channel_id=1, source_target_pairs={{0,4},{4,0},{8,12},{12,8},{16,20},{20,16},{24,28},{28,24},{1,5},{5... | collective-permute-start | bytes 786440 | tf_op jit(solution)/shard_map/ppermute | solution.py:461
  24.2 15.0 %collective-permute-start.8 = (f32[4,16,1024]{2,1,0:T(8,128)S(1)}, f32[4,16,1024]{2,1,0:T(8,128)S(1)}, u32[]{:S(2)}, u32[]{:S(2)}) collective-permute-start(f32[4,16,1024]{2,1,0:T(8,128)S(1)} %meet2.1.refs_4_), channel_id=1, source_target_pairs={{0,16},{4,20},{8,24},{12,28},{16,0},{20,4},{24,8},{28,12},{1,17},{... | collective-permute-start | bytes 786440 | tf_op jit(solution)/shard_map/ppermute | solution.py:462
  28.4 10.9 %collective-permute-start.10 = (f32[4,16,1024]{2,1,0:T(8,128)S(1)}, f32[4,16,1024]{2,1,0:T(8,128)S(1)}, u32[]{:S(2)}, u32[]{:S(2)}) collective-permute-start(f32[4,16,1024]{2,1,0:T(8,128)S(1)} %get-tuple-element.56.refs_5_), channel_id=1, source_target_pairs={{0,4},{4,0},{8,12},{12,8},{16,20},{20,16},{24,28},{28,24},{1,5},{5... | collective-permute-start | bytes 786440 | tf_op jit(solution)/shard_map/ppermute | solution.py:461
  30.2 13.3 %collective-permute-start.9 = (f32[4,16,1024]{2,1,0:T(8,128)S(1)}, f32[4,16,1024]{2,1,0:T(8,128)S(1)}, u32[]{:S(2)}, u32[]{:S(2)}) collective-permute-start(f32[4,16,1024]{2,1,0:T(8,128)S(1)} %meet3.1.refs_4_), channel_id=1, source_target_pairs={{0,24},{4,28},{8,16},{12,20},{16,8},{20,12},{24,0},{28,4},{1,25},{... | collective-permute-start | bytes 786440 | tf_op jit(solution)/shard_map/ppermute | solution.py:462
  38.0 5.6 %collective-permute-start.7 = (f32[4,16,1024]{2,1,0:T(8,128)S(1)}, f32[4,16,1024]{2,1,0:T(8,128)S(1)}, u32[]{:S(2)}, u32[]{:S(2)}) collective-permute-start(f32[4,16,1024]{2,1,0:T(8,128)S(1)} %cross.1), channel_id=1, source_target_pairs={{0,4},{4,0},{8,12},{12,8},{16,20},{20,16},{24,28},{28,24},{1,5},{5... | collective-permute-start | bytes 786440 | tf_op jit(solution)/shard_map/ppermute | solution.py:461
  44.2 7.2 %collective-permute-start.11 = (f32[4,16,1024]{2,1,0:T(8,128)S(1)}, f32[4,16,1024]{2,1,0:T(8,128)S(1)}, u32[]{:S(2)}, u32[]{:S(2)}) collective-permute-start(f32[4,16,1024]{2,1,0:T(8,128)S(1)} %last.1.refs_2_), channel_id=1, source_target_pairs={{0,24},{4,28},{8,16},{12,20},{16,8},{20,12},{24,0},{28,4},{1,25},{... | collective-permute-start | bytes 786440 | tf_op jit(solution)/shard_map/ppermute | solution.py:462
  47.0 5.3 %collective-permute-start.12 = (f32[4,16,1024]{2,1,0:T(8,128)S(1)}, f32[4,16,1024]{2,1,0:T(8,128)S(1)}, u32[]{:S(2)}, u32[]{:S(2)}) collective-permute-start(f32[4,16,1024]{2,1,0:T(8,128)S(1)} %last.1.refs_2_), channel_id=1, source_target_pairs={{0,4},{4,0},{8,12},{12,8},{16,20},{20,16},{24,28},{28,24},{1,5},{5... | collective-permute-start | bytes 786440 | tf_op jit(solution)/shard_map/ppermute | solution.py:461
  52.3 17.3 %collective-permute-start.13 = (f32[4,16,1024]{2,1,0:T(8,128)S(1)}, f32[4,16,1024]{2,1,0:T(8,128)S(1)}, u32[]{:S(2)}, u32[]{:S(2)}) collective-permute-start(f32[4,16,1024]{2,1,0:T(8,128)S(1)} %last.1.refs_2_), channel_id=1, source_target_pairs={{0,16},{4,20},{8,24},{12,28},{16,0},{20,4},{24,8},{28,12},{1,17},{... | collective-permute-start | bytes 786440 | tf_op jit(solution)/shard_map/ppermute | solution.py:462
  60.2 10.9 %collective-permute-start.17 = (f32[4,16,1024]{2,1,0:T(8,128)S(1)}, f32[4,16,1024]{2,1,0:T(8,128)S(1)}, u32[]{:S(2)}, u32[]{:S(2)}) collective-permute-start(f32[4,16,1024]{2,1,0:T(8,128)S(1)} %last.1.refs_2_), channel_id=1, source_target_pairs={{0,8},{4,12},{8,0},{12,4},{16,24},{20,28},{24,16},{28,20},{1,9},{5... | collective-permute-start | bytes 786440 | tf_op jit(solution)/shard_map/ppermute | solution.py:462
  60.6 15.4 %collective-permute-start.15 = (f32[4,16,1024]{2,1,0:T(8,128)S(1)}, f32[4,16,1024]{2,1,0:T(8,128)S(1)}, u32[]{:S(2)}, u32[]{:S(2)}) collective-permute-start(f32[4,16,1024]{2,1,0:T(8,128)S(1)} %collective-permute-done.12.refs_2_), channel_id=1, source_target_pairs={{0,8},{4,12},{8,0},{12,4},{16,24},{20,28},{24,16},{28,20},{1,9},{5... | collective-permute-start | bytes 786440 | tf_op jit(solution)/shard_map/ppermute | solution.py:462
  61.7 14.3 %collective-permute-start.16 = (f32[4,16,1024]{2,1,0:T(8,128)S(1)}, f32[4,16,1024]{2,1,0:T(8,128)S(1)}, u32[]{:S(2)}, u32[]{:S(2)}) collective-permute-start(f32[4,16,1024]{2,1,0:T(8,128)S(1)} %collective-permute-done.11.refs_4_), channel_id=1, source_target_pairs={{0,4},{4,0},{8,12},{12,8},{16,20},{20,16},{24,28},{28,24},{1,5},{5... | collective-permute-start | bytes 786440 | tf_op jit(solution)/shard_map/ppermute | solution.py:461
  69.5 7.2 %collective-permute-start.14 = (f32[4,16,1024]{2,1,0:T(8,128)S(1)}, f32[4,16,1024]{2,1,0:T(8,128)S(1)}, u32[]{:S(2)}, u32[]{:S(2)}) collective-permute-start(f32[4,16,1024]{2,1,0:T(8,128)S(1)} %collective-permute-done.13.refs_4_), channel_id=1, source_target_pairs={{0,4},{4,0},{8,12},{12,8},{16,20},{20,16},{24,28},{28,24},{1,5},{5... | collective-permute-start | bytes 786440 | tf_op jit(solution)/shard_map/ppermute | solution.py:461
  78.1 6.1 %collective-permute-start.19 = (f32[2,4,8,1024]{3,2,1,0:T(8,128)S(1)}, f32[2,4,8,1024]{3,2,1,0:T(8,128)S(1)}, u32[]{:S(2)}, u32[]{:S(2)}) collective-permute-start(f32[2,4,8,1024]{3,2,1,0:T(8,128)S(1)} %get-tuple-element.68), channel_id=1, source_target_pairs={{0,1},{1,0},{2,3},{3,2},{4,5},{5,4},{6,7},{7,6},{8,9},{9,8},{10,11... | collective-permute-start | bytes 786440 | tf_op jit(solution)/shard_map/ppermute | solution.py:428
  81.7 6.5 %collective-permute-start.18 = (f32[2,4,8,1024]{3,2,1,0:T(8,128)S(1)}, f32[2,4,8,1024]{3,2,1,0:T(8,128)S(1)}, u32[]{:S(2)}, u32[]{:S(2)}) collective-permute-start(f32[2,4,8,1024]{3,2,1,0:T(8,128)S(1)} %get-tuple-element.66), channel_id=1, source_target_pairs={{0,4},{1,2},{2,1},{3,7},{4,0},{5,6},{6,5},{7,3},{8,12},{9,10},{10,... | collective-permute-start | bytes 786440 | tf_op jit(solution)/shard_map/ppermute | solution.py:429

commit v11 on v10

--- a/solution.py
+++ b/solution.py
@@ -250,7 +250,7 @@
     return dot(lh, rh) + (dot(lh, rl) + dot(ll, rh))
 
 
-CHUNK = 256
+CHUNK = 512
 
 
 def localize(matrix, parts, out):
@@ -510,7 +510,7 @@
         from_y = swap_y(across)
         cross = call(
             cross_body, piece, "cross", 1 << 19, slot_owner, ens, localized, arrived[1],
-            specs=(SMEM,) + (VMEM,) * 3, after=(three,),
+            specs=(SMEM,) + (VMEM,) * 3,
         )
         got_own = swap_y(cross)
         grad = call(
@@ -525,7 +525,7 @@
         )
         other, weighted = lax.optimization_barrier((grad, weighted))
         other = {0: swap_y(other)}
-        later, own[3], other[0] = lax.optimization_barrier((grad, own[3], other[0]))
+        later, own[3], other[0], weighted = lax.optimization_barrier((grad, own[3], other[0], weighted))
         own[2] = turn_z(later, 2)
         along, near = lax.optimization_barrier((other[0], grad))
         own[1], other[1] = turn_z(near, 1), turn_z(along, 1)

time: 90.3 us -> 90.3 us (level)
  no operation moved by 1% of the time
where the time goes in v11:
time: 90.3 us; the launch traced here: 90.2 us
  waiting for transfers between devices  37.6 us (42%)
  starting transfers between devices  37.3 us (41%)
  Pallas kernels  15.1 us (17%)
    ppermute x8, waiting for transfers between devices, per_device(): lax.ppermute(v, 'mem', [(i, i ^ 2 * s) for i in range(mem_count)])  26.6 us
    ppermute x8, starting transfers between devices, per_device(): lax.ppermute(v, 'mem', [(i, i ^ 2 * s) for i in range(mem_count)])  18.7 us
    pallas_call x17, Pallas kernels, call(): pl.pallas_call(kernel, out_shape=outs, in_specs=list(specs) + [ANY] * ext...  15.1 us
    ppermute x7, starting transfers between devices, per_device(): swap_y = lambda v: lax.ppermute(v, 'mem', y_pairs)  9.03 us
    ppermute x7, waiting for transfers between devices, per_device(): swap_y = lambda v: lax.ppermute(v, 'mem', y_pairs)  5.64 us
    ppermute x2, waiting for transfers between devices, per_device(): swap_x = lambda v: lax.ppermute(v, ('mem', 'lat'), x_swaps)  5.36 us
    ppermute x2, starting transfers between devices, per_device(): swap_x = lambda v: lax.ppermute(v, ('mem', 'lat'), x_swaps)  4.82 us
    ppermute x2, starting transfers between devices, per_device(): swap_core = lambda v: lax.ppermute(v, 'lat', core_pairs)  4.08 us
  transfers between devices with their start and end apart: 20, of which 11 were waited for; matrix products, arithmetic and copies ran while one was open for 0% of the time, Pallas kernels for 9%

profile of v11, /device:TPU:1, one launch (start us, length us, event | category | flops | bytes accessed | tf_op | source)
XLA Modules:
  0.0 90.2 jit_solution(5490504749293841072)
XLA Ops:
  0.0 0.0 copy-start
  0.0 2.3 %front.1 = (f32[2,4,8,1024]{3,2,1,0:T(8,128)S(1)}, f32[2,4,16,1024]{3,2,1,0:T(8,128)S(1)}, f32[16,17]{1,0:T(8,128)S(1)}, f32[16,17]{1,0:T(8,128)S(1)}, s32[8,128...) custom-call(s32[16]{0:T(128)} %refs_0_.12, ...), custom_call_target="tpu_custom_call" | custom-call | flops 524288 | bytes 524288 | tf_op jit(solution)/shard_map/front/pallas_call | solution.py:29
  2.3 0.7 collective-permute-start.3
  3.0 4.7 %collective-permute-start.2 = (f32[2,4,16,1024]{3,2,1,0:T(8,128)S(1)}, f32[2,4,16,1024]{3,2,1,0:T(8,128)S(1)}, u32[]{:S(2)}, u32[]{:S(2)}) collective-permute-start(f32[2,4,16,1024]{3,2,1,0:T(8,128)S(1)} %get-tuple-element.49.refs_1_), channel_id=1, source_target_pairs={{0,8},{4,12},{8,0},{12,4},{16,24},{20,28},{24,16},{28,20},{1,9},{5... | collective-permute-start | bytes 1572872 | tf_op jit(solution)/shard_map/ppermute | solution.py:462
  7.7 2.3 %collective-permute-start = (f32[2,4,8,1024]{3,2,1,0:T(8,128)S(1)}, f32[2,4,8,1024]{3,2,1,0:T(8,128)S(1)}, u32[]{:S(2)}, u32[]{:S(2)}) collective-permute-start(f32[2,4,8,1024]{3,2,1,0:T(8,128)S(1)} %get-tuple-element.44.refs_3_), channel_id=1, source_target_pairs={{0,4},{1,2},{2,1},{3,7},{4,0},{5,6},{6,5},{7,3},{8,12},{9,10},{10,... | collective-permute-start | bytes 786440 | tf_op jit(solution)/shard_map/ppermute | solution.py:429
  10.1 1.3 %core.1.refs_2_ = f32[2,4,8,1024]{3,2,1,0:T(8,128)S(1)} custom-call(s32[8,128]{1,0:T(8,128)S(1)} %get-tuple-element.43.refs_0_, f32[16,17]{1,0:T(8,128)S(1)} %get-tuple-element.39.refs_1_, f32[2,4,16,1024]{3,2,1,0:T(8,128)S(1)} %get-tuple-element.40.refs_2_), custom_call_target="tpu_custom_call" | custom-call | flops 524288 | bytes 524288 | tf_op jit(solution)/shard_map/core/pallas_call | solution.py:29
  11.3 0.5 collective-permute-start.1
  11.8 2.6 %collective-permute-done.refs_3_.refs_5_ = f32[2,4,8,1024]{3,2,1,0:T(8,128)S(1)} collective-permute-done((f32[2,4,8,1024]{3,2,1,0:T(8,128)S(1)}, f32[2,4,8,1024]{3,2,1,0:T(8,128)S(1)}, u32[]{:S(2)}, u32[]{:S(2)}) %collective-permute-start) | collective-permute-done | bytes 262176 | tf_op jit(solution)/shard_map/ppermute | solution.py:429
  14.4 0.3 matrix.1
  14.8 0.0 collective-permute-done.1.refs_4_
  14.8 0.0 copy-done
  14.8 0.6 first.1
  15.4 1.3 %collective-permute-start.6 = (f32[4,16,1024]{2,1,0:T(8,128)S(1)}, f32[4,16,1024]{2,1,0:T(8,128)S(1)}, u32[]{:S(2)}, u32[]{:S(2)}) collective-permute-start(f32[4,16,1024]{2,1,0:T(8,128)S(1)} %get-tuple-element.52), channel_id=1, source_target_pairs={{0,4},{4,0},{8,12},{12,8},{16,20},{20,16},{24,28},{28,24},{1,5},{5... | collective-permute-start | bytes 786440 | tf_op jit(solution)/shard_map/ppermute | solution.py:461
  16.7 0.0 collective-permute-done.3.refs_4_.refs_3_
  16.7 2.3 %collective-permute-done.2.refs_3_.refs_2_ = f32[2,4,16,1024]{3,2,1,0:T(8,128)S(1)} collective-permute-done((f32[2,4,16,1024]{3,2,1,0:T(8,128)S(1)}, f32[2,4,16,1024]{3,2,1,0:T(8,128)S(1)}, u32[]{:S(2)}, u32[]{:S(2)}) %collective-permute-start.2) | collective-permute-done | bytes 524320 | tf_op jit(solution)/shard_map/ppermute | solution.py:462
  19.1 0.7 send.1
  19.8 1.2 %collective-permute-start.4 = (f32[2,4,16,1024]{3,2,1,0:T(8,128)S(1)}, f32[2,4,16,1024]{3,2,1,0:T(8,128)S(1)}, u32[]{:S(2)}, u32[]{:S(2)}) collective-permute-start(f32[2,4,16,1024]{3,2,1,0:T(8,128)S(1)} %get-tuple-element.50), channel_id=1, source_target_pairs={{0,8},{4,12},{8,0},{12,4},{16,24},{20,28},{24,16},{28,20},{1,9},{5... | collective-permute-start | bytes 1572872 | tf_op jit(solution)/shard_map/ppermute | solution.py:462
  21.0 1.4 %collective-permute-done.6.refs_3_ = f32[4,16,1024]{2,1,0:T(8,128)S(1)} collective-permute-done((f32[4,16,1024]{2,1,0:T(8,128)S(1)}, f32[4,16,1024]{2,1,0:T(8,128)S(1)}, u32[]{:S(2)}, u32[]{:S(2)}) %collective-permute-start.6) | collective-permute-done | bytes 262176 | tf_op jit(solution)/shard_map/ppermute | solution.py:461
  22.4 1.2 %collective-permute-start.8 = (f32[4,16,1024]{2,1,0:T(8,128)S(1)}, f32[4,16,1024]{2,1,0:T(8,128)S(1)}, u32[]{:S(2)}, u32[]{:S(2)}) collective-permute-start(f32[4,16,1024]{2,1,0:T(8,128)S(1)} %get-tuple-element.54), channel_id=1, source_target_pairs={{0,4},{4,0},{8,12},{12,8},{16,20},{20,16},{24,28},{28,24},{1,5},{5... | collective-permute-start | bytes 786440 | tf_op jit(solution)/shard_map/ppermute | solution.py:461
  23.6 0.6 meet2.1.refs_4_
  24.2 0.1 collective-permute-start.7
  24.3 0.6 weight_pick.1
  24.9 3.4 %collective-permute-done.8.refs_3_ = f32[4,16,1024]{2,1,0:T(8,128)S(1)} collective-permute-done((f32[4,16,1024]{2,1,0:T(8,128)S(1)}, f32[4,16,1024]{2,1,0:T(8,128)S(1)}, u32[]{:S(2)}, u32[]{:S(2)}) %collective-permute-start.8) | collective-permute-done | bytes 262176 | tf_op jit(solution)/shard_map/ppermute | solution.py:461
  28.4 1.2 %collective-permute-start.10 = (f32[4,16,1024]{2,1,0:T(8,128)S(1)}, f32[4,16,1024]{2,1,0:T(8,128)S(1)}, u32[]{:S(2)}, u32[]{:S(2)}) collective-permute-start(f32[4,16,1024]{2,1,0:T(8,128)S(1)} %get-tuple-element.57.refs_5_), channel_id=1, source_target_pairs={{0,4},{4,0},{8,12},{12,8},{16,20},{20,16},{24,28},{28,24},{1,5},{5... | collective-permute-start | bytes 786440 | tf_op jit(solution)/shard_map/ppermute | solution.py:461
  29.6 0.6 meet3.1
  30.2 1.1 %collective-permute-start.9 = (f32[4,16,1024]{2,1,0:T(8,128)S(1)}, f32[4,16,1024]{2,1,0:T(8,128)S(1)}, u32[]{:S(2)}, u32[]{:S(2)}) collective-permute-start(f32[4,16,1024]{2,1,0:T(8,128)S(1)} %meet3.1), channel_id=1, source_target_pairs={{0,24},{4,28},{8,16},{12,20},{16,8},{20,12},{24,0},{28,4},{1,25},{... | collective-permute-start | bytes 786440 | tf_op jit(solution)/shard_map/ppermute | solution.py:462
  31.4 6.0 %collective-permute-done.4.refs_3_.refs_4_ = f32[2,4,16,1024]{3,2,1,0:T(8,128)S(1)} collective-permute-done((f32[2,4,16,1024]{3,2,1,0:T(8,128)S(1)}, f32[2,4,16,1024]{3,2,1,0:T(8,128)S(1)}, u32[]{:S(2)}, u32[]{:S(2)}) %collective-permute-start.4) | collective-permute-done | bytes 524320 | tf_op jit(solution)/shard_map/ppermute | solution.py:462
  37.3 0.6 cross.1
  38.0 1.3 %collective-permute-start.5 = (f32[4,16,1024]{2,1,0:T(8,128)S(1)}, f32[4,16,1024]{2,1,0:T(8,128)S(1)}, u32[]{:S(2)}, u32[]{:S(2)}) collective-permute-start(f32[4,16,1024]{2,1,0:T(8,128)S(1)} %cross.1), channel_id=1, source_target_pairs={{0,4},{4,0},{8,12},{12,8},{16,20},{20,16},{24,28},{28,24},{1,5},{5... | collective-permute-start | bytes 786440 | tf_op jit(solution)/shard_map/ppermute | solution.py:461
  39.3 0.0 collective-permute-done.7.refs_5_
  39.3 0.0 collective-permute-done.10.refs_8_
  39.3 4.3 %collective-permute-done.9.refs_6_ = f32[4,16,1024]{2,1,0:T(8,128)S(1)} collective-permute-done((f32[4,16,1024]{2,1,0:T(8,128)S(1)}, f32[4,16,1024]{2,1,0:T(8,128)S(1)}, u32[]{:S(2)}, u32[]{:S(2)}) %collective-permute-start.9) | collective-permute-done | bytes 262176 | tf_op jit(solution)/shard_map/ppermute | solution.py:462
  43.6 0.0 collective-permute-done.5.refs_3_
  43.6 0.7 last.1.refs_2_
  44.2 2.1 %collective-permute-start.11 = (f32[4,16,1024]{2,1,0:T(8,128)S(1)}, f32[4,16,1024]{2,1,0:T(8,128)S(1)}, u32[]{:S(2)}, u32[]{:S(2)}) collective-permute-start(f32[4,16,1024]{2,1,0:T(8,128)S(1)} %last.1.refs_2_), channel_id=1, source_target_pairs={{0,24},{4,28},{8,16},{12,20},{16,8},{20,12},{24,0},{28,4},{1,25},{... | collective-permute-start | bytes 786440 | tf_op jit(solution)/shard_map/ppermute | solution.py:462
  46.4 0.6 spread.1.refs_5_
  47.0 1.3 %collective-permute-start.12 = (f32[4,16,1024]{2,1,0:T(8,128)S(1)}, f32[4,16,1024]{2,1,0:T(8,128)S(1)}, u32[]{:S(2)}, u32[]{:S(2)}) collective-permute-start(f32[4,16,1024]{2,1,0:T(8,128)S(1)} %last.1.refs_2_), channel_id=1, source_target_pairs={{0,4},{4,0},{8,12},{12,8},{16,20},{20,16},{24,28},{28,24},{1,5},{5... | collective-permute-start | bytes 786440 | tf_op jit(solution)/shard_map/ppermute | solution.py:461
  48.3 3.1 %collective-permute-done.11.refs_4_ = f32[4,16,1024]{2,1,0:T(8,128)S(1)} collective-permute-done((f32[4,16,1024]{2,1,0:T(8,128)S(1)}, f32[4,16,1024]{2,1,0:T(8,128)S(1)}, u32[]{:S(2)}, u32[]{:S(2)}) %collective-permute-start.11) | collective-permute-done | bytes 262176 | tf_op jit(solution)/shard_map/ppermute | solution.py:462
  51.4 0.8 collective-permute-done.12.refs_2_
  52.3 8.0 %collective-permute-start.13 = (f32[4,16,1024]{2,1,0:T(8,128)S(1)}, f32[4,16,1024]{2,1,0:T(8,128)S(1)}, u32[]{:S(2)}, u32[]{:S(2)}) collective-permute-start(f32[4,16,1024]{2,1,0:T(8,128)S(1)} %last.1.refs_2_), channel_id=1, source_target_pairs={{0,16},{4,20},{8,24},{12,28},{16,0},{20,4},{24,8},{28,12},{1,17},{... | collective-permute-start | bytes 786440 | tf_op jit(solution)/shard_map/ppermute | solution.py:462
  60.2 0.4 collective-permute-start.17
  60.6 1.1 %collective-permute-start.15 = (f32[4,16,1024]{2,1,0:T(8,128)S(1)}, f32[4,16,1024]{2,1,0:T(8,128)S(1)}, u32[]{:S(2)}, u32[]{:S(2)}) collective-permute-start(f32[4,16,1024]{2,1,0:T(8,128)S(1)} %collective-permute-done.12.refs_2_), channel_id=1, source_target_pairs={{0,8},{4,12},{8,0},{12,4},{16,24},{20,28},{24,16},{28,20},{1,9},{5... | collective-permute-start | bytes 786440 | tf_op jit(solution)/shard_map/ppermute | solution.py:462
  61.7 1.0 %collective-permute-start.16 = (f32[4,16,1024]{2,1,0:T(8,128)S(1)}, f32[4,16,1024]{2,1,0:T(8,128)S(1)}, u32[]{:S(2)}, u32[]{:S(2)}) collective-permute-start(f32[4,16,1024]{2,1,0:T(8,128)S(1)} %collective-permute-done.11.refs_4_), channel_id=1, source_target_pairs={{0,4},{4,0},{8,12},{12,8},{16,20},{20,16},{24,28},{28,24},{1,5},{5... | collective-permute-start | bytes 786440 | tf_op jit(solution)/shard_map/ppermute | solution.py:461
  62.8 6.8 %collective-permute-done.13.refs_4_ = f32[4,16,1024]{2,1,0:T(8,128)S(1)} collective-permute-done((f32[4,16,1024]{2,1,0:T(8,128)S(1)}, f32[4,16,1024]{2,1,0:T(8,128)S(1)}, u32[]{:S(2)}, u32[]{:S(2)}) %collective-permute-start.13) | collective-permute-done | bytes 262176 | tf_op jit(solution)/shard_map/ppermute | solution.py:462
  69.5 1.6 %collective-permute-start.14 = (f32[4,16,1024]{2,1,0:T(8,128)S(1)}, f32[4,16,1024]{2,1,0:T(8,128)S(1)}, u32[]{:S(2)}, u32[]{:S(2)}) collective-permute-start(f32[4,16,1024]{2,1,0:T(8,128)S(1)} %collective-permute-done.13.refs_4_), channel_id=1, source_target_pairs={{0,4},{4,0},{8,12},{12,8},{16,20},{20,16},{24,28},{28,24},{1,5},{5... | collective-permute-start | bytes 786440 | tf_op jit(solution)/shard_map/ppermute | solution.py:461
  71.1 0.0 collective-permute-done.17.refs_3_
  71.1 0.8 spread0.1.refs_5_
  71.9 4.1 %collective-permute-done.15.refs_2_ = f32[4,16,1024]{2,1,0:T(8,128)S(1)} collective-permute-done((f32[4,16,1024]{2,1,0:T(8,128)S(1)}, f32[4,16,1024]{2,1,0:T(8,128)S(1)}, u32[]{:S(2)}, u32[]{:S(2)}) %collective-permute-start.15) | collective-permute-done | bytes 262176 | tf_op jit(solution)/shard_map/ppermute | solution.py:462
  76.0 0.0 collective-permute-done.16.refs_3_
  76.0 0.8 spread1.1.refs_3_
  76.7 0.0 collective-permute-done.14.refs_2_
  76.8 0.8 spread2.1
  77.6 0.5 blocks.1
  78.1 3.6 %collective-permute-start.19 = (f32[2,4,8,1024]{3,2,1,0:T(8,128)S(1)}, f32[2,4,8,1024]{3,2,1,0:T(8,128)S(1)}, u32[]{:S(2)}, u32[]{:S(2)}) collective-permute-start(f32[2,4,8,1024]{3,2,1,0:T(8,128)S(1)} %get-tuple-element.70), channel_id=1, source_target_pairs={{0,1},{1,0},{2,3},{3,2},{4,5},{5,4},{6,7},{7,6},{8,9},{9,8},{10,11... | collective-permute-start | bytes 786440 | tf_op jit(solution)/shard_map/ppermute | solution.py:428
  81.7 2.5 %collective-permute-start.18 = (f32[2,4,8,1024]{3,2,1,0:T(8,128)S(1)}, f32[2,4,8,1024]{3,2,1,0:T(8,128)S(1)}, u32[]{:S(2)}, u32[]{:S(2)}) collective-permute-start(f32[2,4,8,1024]{3,2,1,0:T(8,128)S(1)} %get-tuple-element.68), channel_id=1, source_target_pairs={{0,4},{1,2},{2,1},{3,7},{4,0},{5,6},{6,5},{7,3},{8,12},{9,10},{10,... | collective-permute-start | bytes 786440 | tf_op jit(solution)/shard_map/ppermute | solution.py:429
  84.1 0.0 collective-permute-done.19.refs_4_
  84.2 1.3 %adjoint0.1.refs_5_ = f32[2,4,8,1024]{3,2,1,0:T(8,128)S(1)} custom-call(s32[8,128]{1,0:T(8,128)S(1)} %get-tuple-element.43.refs_0_, f32[16,17]{1,0:T(8,128)S(1)} %get-tuple-element.39.refs_1_, f32[2,4,16,1024]{3,2,1,0:T(8,128)S(1)} %get-tuple-element.40.refs_2_, f32[2,4,8,1024]{3,2,1,0:T(8,128)S(1)} %get-tuple-element.69.refs_3_, ...), custom_call_target="tpu_custom_call" | custom-call | flops 524288 | bytes 524288 | tf_op jit(solution)/shard_map/adjoint0/pallas_call | solution.py:29
  85.4 2.8 %collective-permute-done.18.refs_4_ = f32[2,4,8,1024]{3,2,1,0:T(8,128)S(1)} collective-permute-done((f32[2,4,8,1024]{3,2,1,0:T(8,128)S(1)}, f32[2,4,8,1024]{3,2,1,0:T(8,128)S(1)}, u32[]{:S(2)}, u32[]{:S(2)}) %collective-permute-start.18) | collective-permute-done | bytes 262176 | tf_op jit(solution)/shard_map/ppermute | solution.py:429
  88.2 2.0 %adjoint1.1 = f32[2,4,16,1024]{3,2,1,0:T(8,128)} custom-call(s32[8,128]{1,0:T(8,128)S(1)} %get-tuple-element.38.refs_0_, f32[16,17]{1,0:T(8,128)S(1)} %get-tuple-element.39.refs_1_, f32[2,4,16,1024]{3,2,1,0:T(8,128)S(1)} %get-tuple-element.40.refs_2_, f32[2,4,8,1024]{3,2,1,0:T(8,128)S(1)} %get-tuple-element.67.refs_3_, ...), custom_call_target="tpu_custom_call" | custom-call | flops 524288 | bytes 524288 | tf_op jit(solution)/shard_map/adjoint1/pallas_call | solution.py:29
Async XLA Ops:
  0.0 14.8 %copy-start = (s32[4]{0:T(128)S(1)}, s32[4]{0:T(128)}, u32[]{:S(2)}) copy-start(s32[4]{0:T(128)} %refs_0_.23) | copy-start | bytes 52
  2.3 14.4 %collective-permute-start.3 = (f32[2,4,16,1024]{3,2,1,0:T(8,128)S(1)}, f32[2,4,16,1024]{3,2,1,0:T(8,128)S(1)}, u32[]{:S(2)}, u32[]{:S(2)}) collective-permute-start(f32[2,4,16,1024]{3,2,1,0:T(8,128)S(1)} %get-tuple-element.49.refs_1_), channel_id=1, source_target_pairs={{8,16},{12,20},{16,8},{20,12},{9,17},{13,21},{17,9},{21,13},{10,18... | collective-permute-start | bytes 1572872 | tf_op jit(solution)/shard_map/ppermute | solution.py:467
  3.0 16.0 %collective-permute-start.2 = (f32[2,4,16,1024]{3,2,1,0:T(8,128)S(1)}, f32[2,4,16,1024]{3,2,1,0:T(8,128)S(1)}, u32[]{:S(2)}, u32[]{:S(2)}) collective-permute-start(f32[2,4,16,1024]{3,2,1,0:T(8,128)S(1)} %get-tuple-element.49.refs_1_), channel_id=1, source_target_pairs={{0,8},{4,12},{8,0},{12,4},{16,24},{20,28},{24,16},{28,20},{1,9},{5... | collective-permute-start | bytes 1572872 | tf_op jit(solution)/shard_map/ppermute | solution.py:462
  7.7 6.7 %collective-permute-start = (f32[2,4,8,1024]{3,2,1,0:T(8,128)S(1)}, f32[2,4,8,1024]{3,2,1,0:T(8,128)S(1)}, u32[]{:S(2)}, u32[]{:S(2)}) collective-permute-start(f32[2,4,8,1024]{3,2,1,0:T(8,128)S(1)} %get-tuple-element.44.refs_3_), channel_id=1, source_target_pairs={{0,4},{1,2},{2,1},{3,7},{4,0},{5,6},{6,5},{7,3},{8,12},{9,10},{10,... | collective-permute-start | bytes 786440 | tf_op jit(solution)/shard_map/ppermute | solution.py:429
  11.3 3.4 %collective-permute-start.1 = (f32[2,4,8,1024]{3,2,1,0:T(8,128)S(1)}, f32[2,4,8,1024]{3,2,1,0:T(8,128)S(1)}, u32[]{:S(2)}, u32[]{:S(2)}) collective-permute-start(f32[2,4,8,1024]{3,2,1,0:T(8,128)S(1)} %core.1.refs_2_), channel_id=1, source_target_pairs={{0,1},{1,0},{2,3},{3,2},{4,5},{5,4},{6,7},{7,6},{8,9},{9,8},{10,11... | collective-permute-start | bytes 786440 | tf_op jit(solution)/shard_map/ppermute | solution.py:428
  15.4 7.0 %collective-permute-start.6 = (f32[4,16,1024]{2,1,0:T(8,128)S(1)}, f32[4,16,1024]{2,1,0:T(8,128)S(1)}, u32[]{:S(2)}, u32[]{:S(2)}) collective-permute-start(f32[4,16,1024]{2,1,0:T(8,128)S(1)} %get-tuple-element.52), channel_id=1, source_target_pairs={{0,4},{4,0},{8,12},{12,8},{16,20},{20,16},{24,28},{28,24},{1,5},{5... | collective-permute-start | bytes 786440 | tf_op jit(solution)/shard_map/ppermute | solution.py:461
  19.8 17.5 %collective-permute-start.4 = (f32[2,4,16,1024]{3,2,1,0:T(8,128)S(1)}, f32[2,4,16,1024]{3,2,1,0:T(8,128)S(1)}, u32[]{:S(2)}, u32[]{:S(2)}) collective-permute-start(f32[2,4,16,1024]{3,2,1,0:T(8,128)S(1)} %get-tuple-element.50), channel_id=1, source_target_pairs={{0,8},{4,12},{8,0},{12,4},{16,24},{20,28},{24,16},{28,20},{1,9},{5... | collective-permute-start | bytes 1572872 | tf_op jit(solution)/shard_map/ppermute | solution.py:462
  22.4 6.0 %collective-permute-start.8 = (f32[4,16,1024]{2,1,0:T(8,128)S(1)}, f32[4,16,1024]{2,1,0:T(8,128)S(1)}, u32[]{:S(2)}, u32[]{:S(2)}) collective-permute-start(f32[4,16,1024]{2,1,0:T(8,128)S(1)} %get-tuple-element.54), channel_id=1, source_target_pairs={{0,4},{4,0},{8,12},{12,8},{16,20},{20,16},{24,28},{28,24},{1,5},{5... | collective-permute-start | bytes 786440 | tf_op jit(solution)/shard_map/ppermute | solution.py:461
  24.2 15.0 %collective-permute-start.7 = (f32[4,16,1024]{2,1,0:T(8,128)S(1)}, f32[4,16,1024]{2,1,0:T(8,128)S(1)}, u32[]{:S(2)}, u32[]{:S(2)}) collective-permute-start(f32[4,16,1024]{2,1,0:T(8,128)S(1)} %meet2.1.refs_4_), channel_id=1, source_target_pairs={{0,16},{4,20},{8,24},{12,28},{16,0},{20,4},{24,8},{28,12},{1,17},{... | collective-permute-start | bytes 786440 | tf_op jit(solution)/shard_map/ppermute | solution.py:462
  28.4 10.9 %collective-permute-start.10 = (f32[4,16,1024]{2,1,0:T(8,128)S(1)}, f32[4,16,1024]{2,1,0:T(8,128)S(1)}, u32[]{:S(2)}, u32[]{:S(2)}) collective-permute-start(f32[4,16,1024]{2,1,0:T(8,128)S(1)} %get-tuple-element.57.refs_5_), channel_id=1, source_target_pairs={{0,4},{4,0},{8,12},{12,8},{16,20},{20,16},{24,28},{28,24},{1,5},{5... | collective-permute-start | bytes 786440 | tf_op jit(solution)/shard_map/ppermute | solution.py:461
  30.2 13.3 %collective-permute-start.9 = (f32[4,16,1024]{2,1,0:T(8,128)S(1)}, f32[4,16,1024]{2,1,0:T(8,128)S(1)}, u32[]{:S(2)}, u32[]{:S(2)}) collective-permute-start(f32[4,16,1024]{2,1,0:T(8,128)S(1)} %meet3.1), channel_id=1, source_target_pairs={{0,24},{4,28},{8,16},{12,20},{16,8},{20,12},{24,0},{28,4},{1,25},{... | collective-permute-start | bytes 786440 | tf_op jit(solution)/shard_map/ppermute | solution.py:462
  38.0 5.6 %collective-permute-start.5 = (f32[4,16,1024]{2,1,0:T(8,128)S(1)}, f32[4,16,1024]{2,1,0:T(8,128)S(1)}, u32[]{:S(2)}, u32[]{:S(2)}) collective-permute-start(f32[4,16,1024]{2,1,0:T(8,128)S(1)} %cross.1), channel_id=1, source_target_pairs={{0,4},{4,0},{8,12},{12,8},{16,20},{20,16},{24,28},{28,24},{1,5},{5... | collective-permute-start | bytes 786440 | tf_op jit(solution)/shard_map/ppermute | solution.py:461
  44.2 7.2 %collective-permute-start.11 = (f32[4,16,1024]{2,1,0:T(8,128)S(1)}, f32[4,16,1024]{2,1,0:T(8,128)S(1)}, u32[]{:S(2)}, u32[]{:S(2)}) collective-permute-start(f32[4,16,1024]{2,1,0:T(8,128)S(1)} %last.1.refs_2_), channel_id=1, source_target_pairs={{0,24},{4,28},{8,16},{12,20},{16,8},{20,12},{24,0},{28,4},{1,25},{... | collective-permute-start | bytes 786440 | tf_op jit(solution)/shard_map/ppermute | solution.py:462
  47.0 5.3 %collective-permute-start.12 = (f32[4,16,1024]{2,1,0:T(8,128)S(1)}, f32[4,16,1024]{2,1,0:T(8,128)S(1)}, u32[]{:S(2)}, u32[]{:S(2)}) collective-permute-start(f32[4,16,1024]{2,1,0:T(8,128)S(1)} %last.1.refs_2_), channel_id=1, source_target_pairs={{0,4},{4,0},{8,12},{12,8},{16,20},{20,16},{24,28},{28,24},{1,5},{5... | collective-permute-start | bytes 786440 | tf_op jit(solution)/shard_map/ppermute | solution.py:461
  52.3 17.3 %collective-permute-start.13 = (f32[4,16,1024]{2,1,0:T(8,128)S(1)}, f32[4,16,1024]{2,1,0:T(8,128)S(1)}, u32[]{:S(2)}, u32[]{:S(2)}) collective-permute-start(f32[4,16,1024]{2,1,0:T(8,128)S(1)} %last.1.refs_2_), channel_id=1, source_target_pairs={{0,16},{4,20},{8,24},{12,28},{16,0},{20,4},{24,8},{28,12},{1,17},{... | collective-permute-start | bytes 786440 | tf_op jit(solution)/shard_map/ppermute | solution.py:462
  60.2 10.9 %collective-permute-start.17 = (f32[4,16,1024]{2,1,0:T(8,128)S(1)}, f32[4,16,1024]{2,1,0:T(8,128)S(1)}, u32[]{:S(2)}, u32[]{:S(2)}) collective-permute-start(f32[4,16,1024]{2,1,0:T(8,128)S(1)} %last.1.refs_2_), channel_id=1, source_target_pairs={{0,8},{4,12},{8,0},{12,4},{16,24},{20,28},{24,16},{28,20},{1,9},{5... | collective-permute-start | bytes 786440 | tf_op jit(solution)/shard_map/ppermute | solution.py:462
  60.6 15.4 %collective-permute-start.15 = (f32[4,16,1024]{2,1,0:T(8,128)S(1)}, f32[4,16,1024]{2,1,0:T(8,128)S(1)}, u32[]{:S(2)}, u32[]{:S(2)}) collective-permute-start(f32[4,16,1024]{2,1,0:T(8,128)S(1)} %collective-permute-done.12.refs_2_), channel_id=1, source_target_pairs={{0,8},{4,12},{8,0},{12,4},{16,24},{20,28},{24,16},{28,20},{1,9},{5... | collective-permute-start | bytes 786440 | tf_op jit(solution)/shard_map/ppermute | solution.py:462
  61.7 14.3 %collective-permute-start.16 = (f32[4,16,1024]{2,1,0:T(8,128)S(1)}, f32[4,16,1024]{2,1,0:T(8,128)S(1)}, u32[]{:S(2)}, u32[]{:S(2)}) collective-permute-start(f32[4,16,1024]{2,1,0:T(8,128)S(1)} %collective-permute-done.11.refs_4_), channel_id=1, source_target_pairs={{0,4},{4,0},{8,12},{12,8},{16,20},{20,16},{24,28},{28,24},{1,5},{5... | collective-permute-start | bytes 786440 | tf_op jit(solution)/shard_map/ppermute | solution.py:461
  69.5 7.2 %collective-permute-start.14 = (f32[4,16,1024]{2,1,0:T(8,128)S(1)}, f32[4,16,1024]{2,1,0:T(8,128)S(1)}, u32[]{:S(2)}, u32[]{:S(2)}) collective-permute-start(f32[4,16,1024]{2,1,0:T(8,128)S(1)} %collective-permute-done.13.refs_4_), channel_id=1, source_target_pairs={{0,4},{4,0},{8,12},{12,8},{16,20},{20,16},{24,28},{28,24},{1,5},{5... | collective-permute-start | bytes 786440 | tf_op jit(solution)/shard_map/ppermute | solution.py:461
  78.1 6.1 %collective-permute-start.19 = (f32[2,4,8,1024]{3,2,1,0:T(8,128)S(1)}, f32[2,4,8,1024]{3,2,1,0:T(8,128)S(1)}, u32[]{:S(2)}, u32[]{:S(2)}) collective-permute-start(f32[2,4,8,1024]{3,2,1,0:T(8,128)S(1)} %get-tuple-element.70), channel_id=1, source_target_pairs={{0,1},{1,0},{2,3},{3,2},{4,5},{5,4},{6,7},{7,6},{8,9},{9,8},{10,11... | collective-permute-start | bytes 786440 | tf_op jit(solution)/shard_map/ppermute | solution.py:428
  81.7 6.5 %collective-permute-start.18 = (f32[2,4,8,1024]{3,2,1,0:T(8,128)S(1)}, f32[2,4,8,1024]{3,2,1,0:T(8,128)S(1)}, u32[]{:S(2)}, u32[]{:S(2)}) collective-permute-start(f32[2,4,8,1024]{3,2,1,0:T(8,128)S(1)} %get-tuple-element.68), channel_id=1, source_target_pairs={{0,4},{1,2},{2,1},{3,7},{4,0},{5,6},{6,5},{7,3},{8,12},{9,10},{10,... | collective-permute-start | bytes 786440 | tf_op jit(solution)/shard_map/ppermute | solution.py:429
